TPU v7x, 128 devices: a whole 4x4x4 slice. The times are simulated.
128 devices in a mesh: kv: 16 (over x, y), tp: 8 (over z, core).
Axes of the slice: x: 4, y: 4, z: 4, core: 2. Of those that a mesh axis runs over, the one named last changes fastest.
Arguments:
- activations: bfloat16 [256, 5120], P(('kv', 'tp')), may hold values from -27 to 27
- queries: bfloat16 [256, 5120], P('kv', 'tp'), may hold values from -16 to 16
- tree_cache_keys: bfloat16 [16384, 1024], P('kv', 'tp'), may hold values from -16 to 16
- tree_cache_values: bfloat16 [16384, 1024], P('kv', 'tp'), may hold values from -8 to 8
- parents: int32 [13], replicated, may hold values from 0 to 4, as said below
- node_lengths: int32 [13], replicated, may hold values from 1 to 4096, as said below
- token_leaf: int32 [256], replicated, may hold values from 5 to 12
- out_weight: bfloat16 [5120, 5120], P('tp'), may hold values from -0.078125 to 0.078125
- norm_gain: float32 [5120], replicated, may hold values from 0.5 to 1.5
- gate_weight: bfloat16 [5120, 27648], P(None, ('kv', 'tp')), may hold values from -0.078125 to 0.078125
- up_weight: bfloat16 [5120, 27648], P(None, ('kv', 'tp')), may hold values from -0.078125 to 0.078125
- down_weight: bfloat16 [27648, 5120], P(('kv', 'tp')), may hold values from -0.0390625 to 0.0390625
Outputs:
- output: bfloat16 [256, 5120], P(('kv', 'tp'))
Inputs may be any that keep to these rules, and one draw needn't show every extreme that they name: Node 0 is the root, nodes 1 to 4 are tenants, the rest are leaves. parents[0] = 0, every tenant's parent is 0, every leaf's parent is a tenant, and every tenant is the parent of some leaf. `node_lengths`: the root holds exactly 4096 slots, every tenant at most 2048 and one tenant exactly that many, every leaf at most 512 and one leaf exactly that many. The nodes' slots follow one another in node order from slot 0.
All inputs are finite; a program needn't handle non-finite values.
Results may differ from a plain program's by a relative error of at most 0.017.
Values may be sent and summed in bfloat16 or wider, within the bound.
No kernel may reach another device: no remote copies, remote signals or barrier semaphores. Data moves between devices by JAX's collectives and lax.ppermute only.
A program may use at most 128 MiB of HBM per device.

v0:
```python
import math

import jax
import jax.numpy as jnp
from jax import lax
from jax.sharding import PartitionSpec as P

QUERY_HEADS = 40
KEY_VALUE_HEADS = 8
HEAD_WIDTH = 128


LOWEST = -1e30
EPSILON = 1e-06


def merged_2(value, axis, combine):
    everything = jax.tree.map(
        lambda part, kind: lax.all_gather(part.astype(kind), axis),
        value,
        jax.tree.map(lambda a: jnp.bfloat16 if a.dtype == jnp.float32 else a.dtype, value),
    )

    def take(k):
        return jax.tree.map(lambda part, own: part[k].astype(own.dtype), everything, value)

    return lax.fori_loop(
        1, lax.axis_size(axis), lambda k, so_far: combine(so_far, take(k)), take(0)
    )


def slot_owner(node_lengths, first_slot, slot_total):
    node_ends = jnp.cumsum(node_lengths)
    node_starts = node_ends - node_lengths
    slot_ids = first_slot + jnp.arange(slot_total, dtype=jnp.int32)
    inside = (slot_ids[:, None] >= node_starts[None, :]) & (slot_ids[:, None] < node_ends[None, :])
    labels = jnp.arange(node_lengths.shape[0], dtype=jnp.int32)
    holder = jnp.sum(jnp.where(inside, labels[None, :], 0), axis=1)
    return jnp.where(jnp.any(inside, axis=1), holder, -1)


def parent_of(node_ids, parents):
    labels = jnp.arange(parents.shape[0], dtype=jnp.int32)
    return jnp.sum(jnp.where(node_ids[:, None] == labels[None, :], parents[None, :], 0), axis=1)


def combine(earlier, later):
    highest = jnp.maximum(earlier[0], later[0])
    weight_early = jnp.exp(earlier[0] - highest)
    weight_late = jnp.exp(later[0] - highest)
    return (
        highest,
        earlier[1] * weight_early + later[1] * weight_late,
        earlier[2] * weight_early[..., None] + later[2] * weight_late[..., None],
    )


def attend_rows(
    carried,
    query_head_rows,
    leaf_ids,
    tenant_ids,
    key_rows,
    value_rows,
    node_lengths,
    first_slot,
    score_scale,
):
    row_total = key_rows.shape[0]
    block_length = math.gcd(row_total, 512)
    count_of_blocks = row_total // block_length
    kv_local = query_head_rows.shape[1]
    head_size = query_head_rows.shape[3]
    slot_node = slot_owner(node_lengths, first_slot, row_total).reshape(
        count_of_blocks, block_length
    )
    key_blocks = key_rows.reshape(count_of_blocks, block_length, kv_local, head_size)
    value_blocks = value_rows.reshape(count_of_blocks, block_length, kv_local, head_size)

    def one_block(running, sliced):
        key_block, value_block, node_block = sliced
        scores = (
            jnp.einsum(
                "tkgd,skd->tkgs", query_head_rows, key_block, preferred_element_type=jnp.float32
            )
            * score_scale
        )
        allowed = (
            (node_block[None, :] == 0)
            | (node_block[None, :] == tenant_ids[:, None])
            | (node_block[None, :] == leaf_ids[:, None])
        )
        allowed = allowed[:, None, None, :]
        highest = jnp.maximum(running[0], jnp.max(jnp.where(allowed, scores, LOWEST), axis=3))
        weights = jnp.exp(jnp.where(allowed, scores - highest[..., None], -jnp.inf))
        shrink = jnp.exp(running[0] - highest)
        denominator = running[1] * shrink + jnp.sum(weights, axis=3)
        weighted = running[2] * shrink[..., None] + jnp.einsum(
            "tkgs,skd->tkgd",
            weights.astype(jnp.bfloat16),
            value_block,
            preferred_element_type=jnp.float32,
        )
        return ((highest, denominator, weighted), None)

    result, unused = lax.scan(one_block, carried, (key_blocks, value_blocks, slot_node))
    return result


def local(
    activations,
    queries,
    tree_cache_keys,
    tree_cache_values,
    parents,
    node_lengths,
    token_leaf,
    out_weight,
    norm_gain,
    gate_weight,
    up_weight,
    down_weight,
):
    head_size = HEAD_WIDTH
    heads_per_group = QUERY_HEADS // KEY_VALUE_HEADS
    kv_local = tree_cache_keys.shape[1] // head_size
    tok_group = queries.shape[0]
    keys_local = tree_cache_keys.shape[0]
    score_scale = 1.0 / math.sqrt(head_size)
    group_index = lax.axis_index("kv")
    tenant_all = parent_of(token_leaf, parents)
    gathered = lax.all_gather(queries, "kv", axis=0, tiled=True)
    all_heads = gathered.reshape(gathered.shape[0], kv_local, heads_per_group, head_size)
    row_count = gathered.shape[0]
    partial_value = attend_rows(
        (
            jnp.full((row_count, kv_local, heads_per_group), LOWEST, jnp.float32),
            jnp.zeros((row_count, kv_local, heads_per_group), jnp.float32),
            jnp.zeros((row_count, kv_local, heads_per_group, head_size), jnp.float32),
        ),
        all_heads,
        token_leaf,
        tenant_all,
        tree_cache_keys,
        tree_cache_values,
        node_lengths,
        group_index * keys_local,
        score_scale,
    )
    merged = merged_2(partial_value, "kv", combine)
    highest, denominator, weighted = [
        lax.dynamic_slice_in_dim(member, group_index * tok_group, tok_group, 0) for member in merged
    ]
    context = (
        (weighted / denominator[..., None])
        .astype(jnp.bfloat16)
        .reshape(tok_group, kv_local * heads_per_group * head_size)
    )
    picked = context
    attended = lax.psum_scatter(
        jnp.dot(picked, out_weight, preferred_element_type=jnp.float32).astype(jnp.bfloat16),
        "tp",
        scatter_dimension=0,
        tiled=True,
    ).astype(jnp.float32)
    residual = (activations.astype(jnp.float32) + attended).astype(jnp.bfloat16)
    widened = residual.astype(jnp.float32)
    normed = (
        widened
        * lax.rsqrt(jnp.mean(widened * widened, axis=1, keepdims=True) + EPSILON)
        * norm_gain
    ).astype(jnp.bfloat16)
    piece = lax.all_gather(normed, ("kv", "tp"), axis=0, tiled=True)
    gate_proj = jnp.dot(piece, gate_weight, preferred_element_type=jnp.float32)
    up_proj = jnp.dot(piece, up_weight, preferred_element_type=jnp.float32)
    hidden = (jax.nn.silu(gate_proj) * up_proj).astype(jnp.bfloat16)
    picked = hidden
    mixed = lax.psum_scatter(
        jnp.dot(picked, down_weight, preferred_element_type=jnp.float32),
        ("kv", "tp"),
        scatter_dimension=0,
        tiled=True,
    )
    return (widened + mixed).astype(jnp.bfloat16)


def solution(mesh):
    return jax.shard_map(
        local,
        mesh=mesh,
        in_specs=(
            P(("kv", "tp"), None),
            P("kv", "tp"),
            P("kv", "tp"),
            P("kv", "tp"),
            P(),
            P(),
            P(),
            P("tp", None),
            P(),
            P(None, ("kv", "tp")),
            P(None, ("kv", "tp")),
            P(("kv", "tp"), None),
        ),
        out_specs=P(("kv", "tp"), None),
        check_vma=False,
    )
```

profile of v0, /device:TPU:0, one launch (start us, length us, event | category | flops | bytes accessed | tf_op | source)
XLA Modules:
  0.0 484.7 jit_solution(7227337852958654434)
XLA Ops:
  6.5 1.0 reduce-window.8
  7.5 0.7 bitcast_subtract_fusion.1
  8.4 24.3 %all_gather.24 = bf16[256,640]{1,0:T(8,128)(2,1)S(1)} all-gather(bf16[16,640]{1,0:T(8,128)(2,1)} %param.17), channel_id=1, replica_groups=mesh['kv'=16,'tp'=8] {'kv'}, dimensions={0}, use_global_device_ids=true | all-gather | bytes 348160 | tf_op jit(solution)/shard_map/all_gather | solution.py:132
  33.1 0.8 select_reduce_fusion.1
  33.9 14.7 %while.35 = (s32[]{:T(128)}, f32[256,1,5]{0,2,1:T(8,128)S(1)}, f32[256,1,5]{0,2,1:T(8,128)S(1)}, f32[256,1,5,128]{0,3,2,1:T(8,128)S(1)}, s32[2,512]{1,0:T(2,128)...) while((s32[]{:T(128)}, f32[256,1,5]{0,2,1:T(8,128)S(1)}, ...), condition=%wide.region_7.8_spmd.clone, body=%wide.region_4.7_spmd.clone.sunk | while | flops 343777280 | bytes 20867232 | solution.py:106
  33.9 0.9 compare_or_fusion.2
  34.8 3.0 fusion.73
  37.8 2.8 fusion.76
  40.6 0.6 fusion.75
  41.3 0.9 compare_or_fusion.2
  42.2 3.0 fusion.73
  45.1 2.8 fusion.76
  48.0 0.6 fusion.75
  48.6 0.7 convert_element_type.151
  49.4 23.0 %all-gather.1 = bf16[4096,1,5]{0,2,1:T(8,128)(2,1)S(1)} all-gather(bf16[256,1,5]{0,2,1:T(8,128)(2,1)S(1)} %convert_element_type.148), channel_id=3, replica_groups=mesh['kv'=16,'tp'=8] {'kv'}, dimensions={0}, use_global_device_ids=true | all-gather | bytes 43520 | tf_op jit(solution)/shard_map/all_gather | solution.py:19
  72.4 0.6 copy.82
  73.0 21.6 %all-gather = bf16[4096,1,5]{0,2,1:T(8,128)(2,1)S(1)} all-gather(bf16[256,1,5]{0,2,1:T(8,128)(2,1)S(1)} %convert_element_type.145), channel_id=2, replica_groups=mesh['kv'=16,'tp'=8] {'kv'}, dimensions={0}, use_global_device_ids=true | all-gather | bytes 43520 | tf_op jit(solution)/shard_map/all_gather | solution.py:19
  94.6 0.6 copy.83
  95.3 17.0 %all-gather.7.cloned.1.call-done = bf16[4096,1,5,128]{0,3,2,1:T(8,128)(2,1)} async-done(((bf16[256,1,5,128]{0,3,2,1:T(8,128)(2,1)}), bf16[4096,1,5,128]{0,3,2,1:T(8,128)(2,1)}) %all-gather.7.cloned.1.call-update) | async-done | bytes 5242896 | tf_op jit(solution)/shard_map/all_gather | solution.py:19
  112.3 1.9 slice_convert_fusion
  114.1 1.5 copy.60
  115.6 11.1 %copy.69 = bf16[4096,1,5,128]{3,2,0,1:T(8,128)(2,1)} copy(bf16[4096,1,5,128]{0,3,2,1:T(8,128)(2,1)} %all-gather.7.cloned.1.call-done) | data formatting | bytes 10485760 | tf_op jit(solution)/shard_map/while | solution.py:27
  126.8 46.7 %while.34 = (s32[]{:T(128)}, f32[256,1,5]{0,1,2:T(1,128)S(1)}, f32[256,1,5]{0,1,2:T(1,128)S(1)}, f32[256,1,5,128]{3,2,1,0:T(8,128)S(1)}, bf16[16,256,1,5]{1,0,3,...) while((s32[]{:T(128)}, f32[256,1,5]{0,1,2:T(1,128)S(1)}, ...), condition=%wide.region_9.10_spmd, body=%wide.region_8.9_spmd.sunk | while | flops 665605 | bytes 1705111 | solution.py:27
  126.8 0.8 fusion.69
  127.8 2.0 fusion.70
  129.9 0.8 fusion.69
  131.0 2.0 fusion.70
  133.0 0.8 fusion.69
  134.1 2.0 fusion.70
  136.1 0.8 fusion.69
  137.2 2.0 fusion.70
  139.2 0.8 fusion.69
  140.3 2.0 fusion.70
  142.3 0.8 fusion.69
  143.4 2.0 fusion.70
  145.5 0.8 fusion.69
  146.5 2.0 fusion.70
  148.6 0.8 fusion.69
  149.7 2.0 fusion.70
  151.7 0.8 fusion.69
  152.8 2.0 fusion.70
  154.8 0.8 fusion.69
  155.9 2.0 fusion.70
  157.9 0.8 fusion.69
  159.0 2.0 fusion.70
  161.0 0.8 fusion.69
  162.1 2.0 fusion.70
  164.2 0.8 fusion.69
  165.2 2.0 fusion.70
  167.3 0.8 fusion.69
  168.3 2.0 fusion.70
  170.4 0.8 fusion.69
  171.5 2.0 fusion.70
  173.8 4.5 convolution_convert_fusion
  178.4 0.6 dynamic-slice
  179.6 56.4 %all-reduce.5.cloned.1.call-done = bf16[16,5120]{1,0:T(8,128)(2,1)} async-done(((bf16[16,5120]{1,0:T(8,128)(2,1)}), bf16[16,5120]{1,0:T(8,128)(2,1)}) %all-reduce.5.cloned.1.call-update) | async-done | bytes 163856
  236.1 1.0 fusion.44
  237.1 0.7 fusion.50
  238.1 67.0 %all-gather.9.cloned.1.call-done = bf16[128,2,5120]{2,1,0:T(2,128)(2,1)} async-done(((bf16[1,2,5120]{2,1,0:T(2,128)(2,1)}), bf16[128,2,5120]{2,1,0:T(2,128)(2,1)}) %all-gather.9.cloned.1.call-update) | async-done | bytes 2621456 | tf_op jit(solution)/shard_map/all_gather | solution.py:173
  305.1 6.5 %reshape.293 = bf16[256,5120]{1,0:T(8,128)(2,1)} reshape(bf16[128,2,5120]{2,1,0:T(2,128)(2,1)} %all-gather.9.cloned.1.call-done) | data formatting | bytes 5242880
  311.6 3.4 fusion.54
  315.0 7.8 %fusion.36 = f32[256,5120]{1,0:T(8,128)} fusion(bf16[216,5120]{1,0:T(8,128)(2,1)S(1)} %copy-done, bf16[256,5120]{1,0:T(8,128)(2,1)} %reshape.293, bf16[5120,216]{0,1:T(8,128)(2,1)} %param.26, f32[256,216]{0,1:T(8,128)S(1)} %fusion.54), kind=kOutput, calls=%fused_computation.47 | convolution fusion | flops 1132793856 | bytes 12509184 | tf_op jit(solution)/shard_map/dot_general | solution.py:179
  322.8 153.8 %all-reduce.7.cloned.1.call-done = f32[256,5120]{1,0:T(8,128)} async-done(((f32[256,5120]{1,0:T(8,128)}), f32[256,5120]{1,0:T(8,128)}) %all-reduce.7.cloned.1.call-update) | async-done | bytes 5242896
  476.6 1.6 fusion.47
  (79 shorter events, 5.4 us)
Async XLA Ops:
  6.5 308.4 %copy-start = (bf16[216,5120]{1,0:T(8,128)(2,1)S(1)}, bf16[216,5120]{1,0:T(8,128)(2,1)}, u32[]{:S(2)}) copy-start(bf16[216,5120]{1,0:T(8,128)(2,1)} %param.27) | copy-start | bytes 6635524
  6.5 105.7 %all-gather.7.cloned.1.call-start = ((), (), s32[]{:S(2)}) async-start(), calls=%async_computation | async-start | bytes 5570560 | tf_op jit(solution)/shard_map/all_gather | solution.py:19
  37.8 2.9 copy-start.1
  45.1 2.9 copy-start.1
  49.4 186.7 %all-reduce.5.cloned.1.call-start = ((), (), s32[]{:S(2)}) async-start(), calls=%async_computation.2 | async-start | bytes 327680
  173.8 4.6 copy-start.4
  173.8 62.3 %copy-start.2 = (bf16[2,5120]{1,0:T(2,128)(2,1)S(1)}, bf16[2,5120]{1,0:T(2,128)(2,1)}, u32[]{:S(2)}) copy-start(bf16[2,5120]{1,0:T(2,128)(2,1)} %param.16) | copy-start | bytes 61444
  173.8 63.3 %copy-start.3 = (f32[5120]{0:T(1024)S(1)}, f32[5120]{0:T(1024)}, u32[]{:S(2)}) copy-start(f32[5120]{0:T(1024)} %param.24) | copy-start | bytes 61444
  178.3 126.8 %all-gather.9.cloned.1.call-start = ((), (), s32[]{:S(2)}) async-start(), calls=%async_computation.1 | async-start | bytes 2641920 | tf_op jit(solution)/shard_map/all_gather | solution.py:173
  237.8 238.8 %all-reduce.7.cloned.1.call-start = ((), (), s32[]{:S(2)}) async-start(), calls=%async_computation.3 | async-start | bytes 10485760
Sparse Core Ops, SparseCore 0:
  49.5 62.7 all-gather.6
  178.4 57.5 all-reduce.4
  239.7 65.3 all-gather.8
  322.9 153.6 all-reduce.6
where the time goes:
time: 488 us; the launch traced here: 485 us
  waiting for transfers between devices  294 us (60%)
  blocking collectives  68.8 us (14%)
  other arithmetic  53.7 us (11%)
  matrix products  27.3 us (6%)
  local copies, waits for them, and re-layouts  25.6 us (5%)
  between operations  14 us (3%)
    unnamed x6, waiting for transfers between devices  210 us
    all_gather x1, waiting for transfers between devices, local(): piece = lax.all_gather(normed, ('kv', 'tp'), axis=0, tiled=True)  67 us
    all_gather x2, blocking collectives, merged_2(): lax.all_gather(part.astype(kind), axis)  44.5 us
    add x15, other arithmetic, combine(): earlier[2] * weight_early[..., None] + later[2] * weight_late[..., None]  30.2 us
    all_gather x1, blocking collectives, local(): gathered = lax.all_gather(queries, 'kv', axis=0, tiled=True)  24.3 us
    all_gather x1, waiting for transfers between devices, merged_2(): lax.all_gather(part.astype(kind), axis)  17 us
    while x5, local copies, waits for them, and re-layouts, merged_2(): lax.fori_loop(1, lax.axis_size(axis), lambda k, so_far: combine(so_far, t...  12.7 us
    add x15, other arithmetic, combine(): earlier[1] * weight_early + later[1] * weight_late  11.8 us
  transfers between devices with their start and end apart: 4, of which 4 were waited for; matrix products, arithmetic and copies ran while one was open for 0% of the time, Pallas kernels for 0%

commit v1 on v0

v1 whole, which is shorter than its diff:
```python
import math

import jax
import jax.numpy as jnp
from jax import lax
from jax.sharding import PartitionSpec as P

QUERY_HEADS = 40
KEY_VALUE_HEADS = 8
HEAD_WIDTH = 128
GROUP = QUERY_HEADS // KEY_VALUE_HEADS
LOWEST = -1e30
EPSILON = 1e-06
BF = jnp.bfloat16
F32 = jnp.float32


def move_x(value, k):
    pairs = [(x * 4 + y, (x + k) % 4 * 4 + y) for x in range(4) for y in range(4)]
    return lax.ppermute(value, "kv", pairs)


def move_y(value, k):
    pairs = [(x * 4 + y, x * 4 + (y + k) % 4) for x in range(4) for y in range(4)]
    return lax.ppermute(value, "kv", pairs)


def move_z(value, k):
    pairs = [(z * 2 + c, (z + k) % 4 * 2 + c) for z in range(4) for c in range(2)]
    return lax.ppermute(value, "tp", pairs)


def move_core(value):
    return lax.ppermute(value, "tp", [(i, i ^ 1) for i in range(8)])


def spread(value, move):
    return jnp.concatenate([value] + [move(value, k) for k in (1, 2, 3)], axis=0)


def collect(value, move):
    rows = value.shape[0] // 4
    sent = [move(value[k * rows : (k + 1) * rows].astype(BF), -k) for k in (1, 2, 3)]
    total = value[:rows].astype(F32)
    for part in sent:
        total = total + part.astype(F32)
    return total


def slot_owner(node_lengths, first_slot, slot_total):
    node_ends = jnp.cumsum(node_lengths)
    node_starts = node_ends - node_lengths
    slot_ids = first_slot + jnp.arange(slot_total, dtype=jnp.int32)
    inside = (slot_ids[:, None] >= node_starts[None, :]) & (slot_ids[:, None] < node_ends[None, :])
    labels = jnp.arange(node_lengths.shape[0], dtype=jnp.int32)
    holder = jnp.sum(jnp.where(inside, labels[None, :], 0), axis=1)
    return jnp.where(jnp.any(inside, axis=1), holder, -1)


def parent_of(node_ids, parents):
    labels = jnp.arange(parents.shape[0], dtype=jnp.int32)
    return jnp.sum(jnp.where(node_ids[:, None] == labels[None, :], parents[None, :], 0), axis=1)


def pack(o, m, l):
    n = o.shape[0]
    high = l.astype(BF)
    low = (l - high.astype(F32)).astype(BF)
    stats = jnp.concatenate(
        [m.astype(BF), high, low, jnp.zeros((n, 128 - 3 * GROUP), BF)], axis=1
    )
    return jnp.concatenate([o.astype(BF).reshape(n, GROUP * HEAD_WIDTH), stats], axis=1)


def unpack(packed):
    n = packed.shape[0]
    o = packed[:, : GROUP * HEAD_WIDTH].astype(F32).reshape(n, GROUP, HEAD_WIDTH)
    s = packed[:, GROUP * HEAD_WIDTH :].astype(F32)
    return o, s[:, :GROUP], s[:, GROUP : 2 * GROUP] + s[:, 2 * GROUP : 3 * GROUP]


def merge(parts):
    parts = [unpack(p) for p in parts]
    top = parts[0][1]
    for p in parts[1:]:
        top = jnp.maximum(top, p[1])
    o, l = 0.0, 0.0
    for p in parts:
        scale = jnp.exp(p[1] - top)
        o = o + p[0] * scale[..., None]
        l = l + p[2] * scale
    return o, top, l


def collect_softmax(packed, move):
    rows = packed.shape[0] // 4
    blocks = [packed[k * rows : (k + 1) * rows] for k in range(4)]
    return merge([blocks[0]] + [move(blocks[k], -k) for k in (1, 2, 3)])


def local(
    activations,
    queries,
    keys,
    values,
    parents,
    node_lengths,
    token_leaf,
    out_weight,
    norm_gain,
    gate_weight,
    up_weight,
    down_weight,
):
    scale = 1.0 / math.sqrt(HEAD_WIDTH)
    kv = lax.axis_index("kv")
    tp = lax.axis_index("tp")
    x, y, z, c = kv // 4, kv % 4, tp // 2, tp % 2
    slot_total = keys.shape[0]

    i16 = jnp.arange(16, dtype=jnp.int32)
    row_order = (z + 4 - i16 // 2 % 4) % 4 * 4 + (c ^ (i16 // 8)) * 2 + i16 % 2
    pick = (row_order[:, None] == i16[None, :])
    block_order = (x + 4 - i16 // 4) % 4 * 4 + (y + 4 - i16 % 4) % 4
    tokens = (block_order[:, None] * 16 + row_order[None, :]).reshape(256)
    leaf = jnp.sum(
        jnp.where(tokens[:, None] == jnp.arange(256, dtype=jnp.int32)[None, :], token_leaf[None, :], 0), axis=1
    )
    tenant = parent_of(leaf, parents)
    slot_node = slot_owner(node_lengths, kv * slot_total, slot_total)

    q = jnp.dot(pick.astype(BF), queries, preferred_element_type=F32).astype(BF)
    q = spread(spread(q, move_y), move_x)
    q = q.reshape(256, GROUP, HEAD_WIDTH)
    scores = jnp.einsum("tgd,sd->tgs", q, keys, preferred_element_type=F32) * scale
    allowed = (
        (slot_node[None, :] == 0)
        | (slot_node[None, :] == tenant[:, None])
        | (slot_node[None, :] == leaf[:, None])
    )[:, None, :]
    top = jnp.max(jnp.where(allowed, scores, LOWEST), axis=2)
    top = lax.reduce_precision(top, 8, 7)
    weights = jnp.exp(jnp.where(allowed, scores - top[..., None], -jnp.inf))
    mass = jnp.sum(weights, axis=2)
    weighted = jnp.einsum("tgs,sd->tgd", weights.astype(BF), values, preferred_element_type=F32)

    packed = pack(weighted, top, mass)
    packed = pack(*collect_softmax(packed, move_x))
    o, top, mass = collect_softmax(packed, move_y)
    context = (o / mass[..., None]).astype(BF).reshape(16, GROUP * HEAD_WIDTH)

    attended = jnp.dot(context, out_weight, preferred_element_type=F32)
    attended = attended[:8] + move_core(attended[8:].astype(BF)).astype(F32)
    attended = collect(attended, move_z)
    residual = (activations.astype(F32) + attended).astype(BF)
    widened = residual.astype(F32)
    normed = (
        widened
        * lax.rsqrt(jnp.mean(widened * widened, axis=1, keepdims=True) + EPSILON)
        * norm_gain
    ).astype(BF)

    rows = spread(spread(spread(normed, move_z), move_y), move_x)
    rows = jnp.concatenate([rows, move_core(rows)], axis=0)
    gate = jnp.dot(rows, gate_weight, preferred_element_type=F32)
    up = jnp.dot(rows, up_weight, preferred_element_type=F32)
    hidden = (jax.nn.silu(gate) * up).astype(BF)
    mixed = jnp.dot(hidden, down_weight, preferred_element_type=F32)
    mixed = mixed[:128] + move_core(mixed[128:].astype(BF)).astype(F32)
    mixed = collect(collect(collect(mixed, move_x), move_y), move_z)
    return (widened + mixed).astype(BF)


def solution(mesh):
    return jax.shard_map(
        local,
        mesh=mesh,
        in_specs=(
            P(("kv", "tp"), None),
            P("kv", "tp"),
            P("kv", "tp"),
            P("kv", "tp"),
            P(),
            P(),
            P(),
            P("tp", None),
            P(),
            P(None, ("kv", "tp")),
            P(None, ("kv", "tp")),
            P(("kv", "tp"), None),
        ),
        out_specs=P(("kv", "tp"), None),
        check_vma=False,
    )
```

time: 488 us -> 177 us (0.36)
  waiting for transfers between devices: 294 us -> 76.3 us
  blocking collectives: 68.8 us -> 0 us
  other arithmetic: 53.7 us -> 10.3 us
  starting transfers between devices: 0.31 us -> 42.6 us
  between operations: 14 us -> 0.37 us
  matrix products: 27.3 us -> 19.7 us
    unnamed x6 -> x0, waiting for transfers between devices: 210 us -> none
    all_gather x2 -> x0, waiting for transfers between devices: 84 us -> none  [the longest x1 67 us: local(): piece = lax.all_gather(normed, ('kv', 'tp'), axis=0, tiled=True)]
    ppermute x0 -> x36, waiting for transfers between devices: none -> 76.3 us  [the longest x12 39.7 us: move_x(): return lax.ppermute(value, 'kv', pairs)]
    all_gather x3 -> x0, blocking collectives: 68.8 us -> none  [the longest x2 44.5 us: merged_2(): lax.all_gather(part.astype(kind), axis)]
    ppermute x0 -> x36, starting transfers between devices: none -> 42.6 us  [the longest x12 14.8 us: move_y(): return lax.ppermute(value, 'kv', pairs)]
    add x32 -> x3, other arithmetic: 42.1 us -> 0.11 us  [the longest x1 0.07 us: local(): tokens = (block_order[:, None] * 16 + row_order[None, :]).reshape(256)]
    concatenate x0 -> x7, local copies, waits for them, and re-layouts: none -> 23.7 us  [the longest x1 13 us: local(): rows = jnp.concatenate([rows, move_core(rows)], axis=0)]
    while x11 -> x0, local copies, waits for them, and re-layouts: 12.7 us -> none  [the longest x5 12.7 us: merged_2(): lax.fori_loop(1, lax.axis_size(axis), lambda k, so_far: combine(so_far, t...]
  transfers between devices with their start and end apart: 4 -> 36, of which waited for: 4 -> 26; matrix products, arithmetic and copies ran while one was open for 0% -> 2% of each run, Pallas kernels for 0% -> 0%
where the time goes in v1:
time: 177 us
  waiting for transfers between devices  76.3 us (43%)
  starting transfers between devices  42.6 us (24%)
  local copies, waits for them, and re-layouts  27.4 us (15%)
  matrix products  19.7 us (11%)
  other arithmetic  10.3 us (6%)
    ppermute x12, waiting for transfers between devices, move_x(): return lax.ppermute(value, 'kv', pairs)  39.7 us
    ppermute x12, waiting for transfers between devices, move_y(): return lax.ppermute(value, 'kv', pairs)  17.8 us
    ppermute x12, starting transfers between devices, move_y(): return lax.ppermute(value, 'kv', pairs)  14.8 us
    ppermute x9, starting transfers between devices, move_z(): return lax.ppermute(value, 'tp', pairs)  14.1 us
    ppermute x12, starting transfers between devices, move_x(): return lax.ppermute(value, 'kv', pairs)  13.3 us
    concatenate x1, local copies, waits for them, and re-layouts, local(): rows = jnp.concatenate([rows, move_core(rows)], axis=0)  13 us
    ppermute x9, waiting for transfers between devices, move_z(): return lax.ppermute(value, 'tp', pairs)  11.3 us
    concatenate x4, local copies, waits for them, and re-layouts, spread(): jnp.concatenate([value] + [move(value, k) for k in (1, 2, 3)], axis=0)  9.48 us
  transfers between devices with their start and end apart: 36, of which 26 were waited for; matrix products, arithmetic and copies ran while one was open for 2% of the time, Pallas kernels for 0%

profile of v1, /device:TPU:0, one launch (start us, length us, event | category | flops | bytes accessed | tf_op | source)
XLA Modules:
  0.0 176.7 jit_solution(4017754382312666890)
XLA Ops:
  0.0 1.1 constant_dynamic-update-slice_fusion.6
  1.1 3.1 %collective-permute-start.2 = (bf16[16,640]{1,0:T(8,128)(2,1)S(1)}, bf16[16,640]{1,0:T(8,128)(2,1)S(1)}, u32[]{:S(2)}, u32[]{:S(2)}) collective-permute-start(bf16[16,640]{1,0:T(8,128)(2,1)S(1)} %get-tuple-element.53), channel_id=1, source_target_pairs={{0,24},{8,0},{16,8},{24,16},{32,56},{40,32},{48,40},{56,48},{64,88... | collective-permute-start | bytes 61448 | tf_op jit(solution)/shard_map/ppermute | solution.py:25
  4.8 1.0 collective-permute-start
  5.8 0.8 reduce-window.8
  7.6 0.9 select_reduce_fusion.1
  8.5 0.7 select_reduce_fusion.3
  9.8 2.8 %collective-permute-start.5 = (bf16[64,640]{1,0:T(8,128)(2,1)S(1)}, bf16[64,640]{1,0:T(8,128)(2,1)S(1)}, u32[]{:S(2)}, u32[]{:S(2)}) collective-permute-start(bf16[64,640]{1,0:T(8,128)(2,1)S(1)} %pad_maximum_fusion), channel_id=1, source_target_pairs={{0,96},{8,104},{16,112},{24,120},{32,0},{40,8},{48,16},{56,24},{64... | collective-permute-start | bytes 245768 | tf_op jit(solution)/shard_map/ppermute | solution.py:20
  12.7 0.8 collective-permute-start.4
  13.5 0.9 collective-permute-start.3
  14.4 5.1 %collective-permute-done.3 = bf16[64,640]{1,0:T(8,128)(2,1)S(1)} collective-permute-done((bf16[64,640]{1,0:T(8,128)(2,1)S(1)}, bf16[64,640]{1,0:T(8,128)(2,1)S(1)}, u32[]{:S(2)}, u32[]{:S(2)}) %collective-permute-start.3) | collective-permute-done | bytes 81952 | tf_op jit(solution)/shard_map/ppermute | solution.py:20
  19.7 2.2 %select_reduce_fusion = (f32[256,5]{0,1:T(8,128)S(1)}, f32[256,5,1024]{2,0,1:T(8,128)S(1)}) fusion(pred[256,1024]{1,0:T(8,128)(4,1)S(1)} %compare_or_fusion, bf16[256,5,128]{0,2,1:T(8,128)(2,1)S(1)} %bitcast.68, bf16[1024,128]{1,0:T(8,128)(2,1)} %param.14), kind=kOutput, calls=%fused_computation.1 | convolution fusion | flops 339475200 | bytes 6099968 | tf_op jit(solution)/shard_map/tgd,sd->tgs/dot_general | solution.py:135
  22.0 1.6 fusion
  23.5 1.4 fusion.5
  25.2 0.7 concatenate.37
  26.7 1.5 collective-permute-start.8
  28.2 1.1 collective-permute-start.7
  29.3 3.4 %collective-permute-done.6 = bf16[64,768]{0,1:T(8,128)(2,1)S(1)} collective-permute-done((bf16[64,768]{0,1:T(8,128)(2,1)S(1)}, bf16[64,768]{0,1:T(8,128)(2,1)S(1)}, u32[]{:S(2)}, u32[]{:S(2)}) %collective-permute-start.6) | collective-permute-done | bytes 98336 | tf_op jit(solution)/shard_map/ppermute | solution.py:20
  32.7 3.6 %collective-permute-done.8 = bf16[64,768]{0,1:T(8,128)(2,1)S(1)} collective-permute-done((bf16[64,768]{0,1:T(8,128)(2,1)S(1)}, bf16[64,768]{0,1:T(8,128)(2,1)S(1)}, u32[]{:S(2)}, u32[]{:S(2)}) %collective-permute-start.8) | collective-permute-done | bytes 98336 | tf_op jit(solution)/shard_map/ppermute | solution.py:20
  37.4 1.1 fusion.15
  39.2 2.3 %collective-permute-start.9 = (bf16[16,768]{0,1:T(8,128)(2,1)S(1)}, bf16[16,768]{0,1:T(8,128)(2,1)S(1)}, u32[]{:S(2)}, u32[]{:S(2)}) collective-permute-start(bf16[16,768]{0,1:T(8,128)(2,1)S(1)} %get-tuple-element.39), channel_id=1, source_target_pairs={{0,24},{8,0},{16,8},{24,16},{32,56},{40,32},{48,40},{56,48},{64,88... | collective-permute-start | bytes 73736 | tf_op jit(solution)/shard_map/ppermute | solution.py:25
  41.6 2.0 %collective-permute-start.10 = (bf16[16,768]{0,1:T(8,128)(2,1)S(1)}, bf16[16,768]{0,1:T(8,128)(2,1)S(1)}, u32[]{:S(2)}, u32[]{:S(2)}) collective-permute-start(bf16[16,768]{0,1:T(8,128)(2,1)S(1)} %get-tuple-element.41), channel_id=1, source_target_pairs={{0,16},{8,24},{16,0},{24,8},{32,48},{40,56},{48,32},{56,40},{64,80... | collective-permute-start | bytes 73736 | tf_op jit(solution)/shard_map/ppermute | solution.py:25
  43.5 2.8 %collective-permute-done.9 = bf16[16,768]{0,1:T(8,128)(2,1)S(1)} collective-permute-done((bf16[16,768]{0,1:T(8,128)(2,1)S(1)}, bf16[16,768]{0,1:T(8,128)(2,1)S(1)}, u32[]{:S(2)}, u32[]{:S(2)}) %collective-permute-start.9) | collective-permute-done | bytes 24608 | tf_op jit(solution)/shard_map/ppermute | solution.py:25
  46.3 4.2 %collective-permute-done.11 = bf16[16,768]{0,1:T(8,128)(2,1)S(1)} collective-permute-done((bf16[16,768]{0,1:T(8,128)(2,1)S(1)}, bf16[16,768]{0,1:T(8,128)(2,1)S(1)}, u32[]{:S(2)}, u32[]{:S(2)}) %collective-permute-start.11) | collective-permute-done | bytes 24608 | tf_op jit(solution)/shard_map/ppermute | solution.py:25
  50.8 3.9 %fusion.95 = f32[16,5120]{1,0:T(8,128)S(1)} fusion(bf16[16,640]{0,1:T(8,128)(2,1)S(1)} %fusion.10, bf16[640,5120]{1,0:T(8,128)(2,1)} %param.19), kind=kOutput, calls=%fused_computation.190 | convolution fusion | flops 104857600 | bytes 6901760 | tf_op jit(solution)/shard_map/dot_general | solution.py:152
  55.0 1.3 collective-permute-done.12
  56.3 4.1 %collective-permute-start.13 = (bf16[2,5120]{1,0:T(2,128)(2,1)S(1)}, bf16[2,5120]{1,0:T(2,128)(2,1)S(1)}, u32[]{:S(2)}, u32[]{:S(2)}) collective-permute-start(bf16[2,5120]{1,0:T(2,128)(2,1)S(1)} %get-tuple-element.45), channel_id=1, source_target_pairs={{0,6},{1,7},{2,0},{3,1},{4,2},{5,3},{6,4},{7,5},{8,14},{9,15},{10,... | collective-permute-start | bytes 61448 | tf_op jit(solution)/shard_map/ppermute | solution.py:30
  60.4 1.9 %collective-permute-start.14 = (bf16[2,5120]{1,0:T(2,128)(2,1)S(1)}, bf16[2,5120]{1,0:T(2,128)(2,1)S(1)}, u32[]{:S(2)}, u32[]{:S(2)}) collective-permute-start(bf16[2,5120]{1,0:T(2,128)(2,1)S(1)} %get-tuple-element.47), channel_id=1, source_target_pairs={{0,4},{1,5},{2,6},{3,7},{4,0},{5,1},{6,2},{7,3},{8,12},{9,13},{10,... | collective-permute-start | bytes 61448 | tf_op jit(solution)/shard_map/ppermute | solution.py:30
  62.3 3.1 %collective-permute-done.15 = bf16[2,5120]{1,0:T(2,128)(2,1)S(1)} collective-permute-done((bf16[2,5120]{1,0:T(2,128)(2,1)S(1)}, bf16[2,5120]{1,0:T(2,128)(2,1)S(1)}, u32[]{:S(2)}, u32[]{:S(2)}) %collective-permute-start.15) | collective-permute-done | bytes 20512 | tf_op jit(solution)/shard_map/ppermute | solution.py:30
  66.0 3.3 %collective-permute-start.18 = (bf16[2,5120]{1,0:T(2,128)(2,1)S(1)}, bf16[2,5120]{1,0:T(2,128)(2,1)S(1)}, u32[]{:S(2)}, u32[]{:S(2)}) collective-permute-start(bf16[2,5120]{1,0:T(2,128)(2,1)S(1)} %fusion.28), channel_id=1, source_target_pairs={{0,6},{1,7},{2,0},{3,1},{4,2},{5,3},{6,4},{7,5},{8,14},{9,15},{10,... | collective-permute-start | bytes 61448 | tf_op jit(solution)/shard_map/ppermute | solution.py:30
  69.3 0.9 collective-permute-start.16
  70.8 3.8 %collective-permute-done.17 = bf16[2,5120]{1,0:T(2,128)(2,1)S(1)} collective-permute-done((bf16[2,5120]{1,0:T(2,128)(2,1)S(1)}, bf16[2,5120]{1,0:T(2,128)(2,1)S(1)}, u32[]{:S(2)}, u32[]{:S(2)}) %collective-permute-start.17) | collective-permute-done | bytes 20512 | tf_op jit(solution)/shard_map/ppermute | solution.py:30
  74.7 1.5 collective-permute-start.21
  77.1 2.1 %collective-permute-done.21 = bf16[8,5120]{1,0:T(8,128)(2,1)S(1)} collective-permute-done((bf16[8,5120]{1,0:T(8,128)(2,1)S(1)}, bf16[8,5120]{1,0:T(8,128)(2,1)S(1)}, u32[]{:S(2)}, u32[]{:S(2)}) %collective-permute-start.21) | collective-permute-done | bytes 81952 | tf_op jit(solution)/shard_map/ppermute | solution.py:25
  79.2 3.0 %collective-permute-done.20 = bf16[8,5120]{1,0:T(8,128)(2,1)S(1)} collective-permute-done((bf16[8,5120]{1,0:T(8,128)(2,1)S(1)}, bf16[8,5120]{1,0:T(8,128)(2,1)S(1)}, u32[]{:S(2)}, u32[]{:S(2)}) %collective-permute-start.20) | collective-permute-done | bytes 81952 | tf_op jit(solution)/shard_map/ppermute | solution.py:25
  82.2 0.8 collective-permute-done.19
  83.0 2.6 %concatenate.41 = bf16[32,5120]{1,0:T(8,128)(2,1)} concatenate(bf16[2,5120]{1,0:T(2,128)(2,1)S(1)} %fusion.28, bf16[2,5120]{1,0:T(2,128)(2,1)S(1)} %collective-permute-done.16, bf16[2,5120]{1,0:T(2,128)(2,1)S(1)} %collective-permute-done.17, bf16[2,5120]{1,0:T(2,128)(2,1)S(1)} %collective-permute-done.18, bf16[8,5120]{1,0:T(8,128)(2,1)S(1)} %collective-permute-done.19, ...), dimensions={0} | concatenate | bytes 655360 | tf_op jit(solution)/shard_map/concatenate | solution.py:38
  85.6 1.1 collective-permute-start.24
  87.2 1.3 collective-permute-start.22
  88.5 6.0 %collective-permute-done.24 = bf16[32,5120]{1,0:T(8,128)(2,1)S(1)} collective-permute-done((bf16[32,5120]{1,0:T(8,128)(2,1)}, bf16[32,5120]{1,0:T(8,128)(2,1)S(1)}, u32[]{:S(2)}, u32[]{:S(2)}) %collective-permute-start.24) | collective-permute-done | bytes 327712 | tf_op jit(solution)/shard_map/ppermute | solution.py:20
  94.5 2.5 %collective-permute-done.23 = bf16[32,5120]{1,0:T(8,128)(2,1)S(1)} collective-permute-done((bf16[32,5120]{1,0:T(8,128)(2,1)}, bf16[32,5120]{1,0:T(8,128)(2,1)S(1)}, u32[]{:S(2)}, u32[]{:S(2)}) %collective-permute-start.23) | collective-permute-done | bytes 327712 | tf_op jit(solution)/shard_map/ppermute | solution.py:20
  96.9 3.4 %collective-permute-done.22 = bf16[32,5120]{1,0:T(8,128)(2,1)S(1)} collective-permute-done((bf16[32,5120]{1,0:T(8,128)(2,1)}, bf16[32,5120]{1,0:T(8,128)(2,1)S(1)}, u32[]{:S(2)}, u32[]{:S(2)}) %collective-permute-start.22) | collective-permute-done | bytes 327712 | tf_op jit(solution)/shard_map/ppermute | solution.py:20
  100.3 6.6 %concatenate.42 = bf16[128,5120]{1,0:T(8,128)(2,1)} concatenate(bf16[2,5120]{1,0:T(2,128)(2,1)S(1)} %fusion.28, bf16[2,5120]{1,0:T(2,128)(2,1)S(1)} %collective-permute-done.16, bf16[2,5120]{1,0:T(2,128)(2,1)S(1)} %collective-permute-done.17, bf16[2,5120]{1,0:T(2,128)(2,1)S(1)} %collective-permute-done.18, bf16[8,5120]{1,0:T(8,128)(2,1)S(1)} %collective-permute-done.19, ...), dimensions={0} | concatenate | bytes 2621440 | tf_op jit(solution)/shard_map/concatenate | solution.py:38
  106.9 3.4 %collective-permute-done.25 = bf16[128,5120]{1,0:T(8,128)(2,1)} collective-permute-done((bf16[128,5120]{1,0:T(8,128)(2,1)}, bf16[128,5120]{1,0:T(8,128)(2,1)}, u32[]{:S(2)}, u32[]{:S(2)}) %collective-permute-start.25) | collective-permute-done | bytes 1310752 | tf_op jit(solution)/shard_map/ppermute | solution.py:34
  110.3 13.0 %concatenate.43 = bf16[256,5120]{1,0:T(8,128)(2,1)} concatenate(bf16[2,5120]{1,0:T(2,128)(2,1)S(1)} %fusion.28, bf16[2,5120]{1,0:T(2,128)(2,1)S(1)} %collective-permute-done.16, bf16[2,5120]{1,0:T(2,128)(2,1)S(1)} %collective-permute-done.17, bf16[2,5120]{1,0:T(2,128)(2,1)S(1)} %collective-permute-done.18, bf16[8,5120]{1,0:T(8,128)(2,1)S(1)} %collective-permute-done.19, ...), dimensions={0} | concatenate | bytes 5242880 | tf_op jit(solution)/shard_map/concatenate | solution.py:164
  123.3 3.4 %fusion.96 = f32[256,216]{0,1:T(8,128)S(1)} fusion(bf16[256,5120]{1,0:T(8,128)(2,1)} %concatenate.43, bf16[5120,216]{0,1:T(8,128)(2,1)} %param.21), kind=kOutput, calls=%fused_computation.191 | convolution fusion | flops 566231040 | bytes 5054464 | tf_op jit(solution)/shard_map/dot_general | solution.py:165
  126.7 7.8 %fusion.23 = f32[256,5120]{1,0:T(8,128)} fusion(bf16[216,5120]{1,0:T(8,128)(2,1)S(1)} %copy-done, f32[256,216]{0,1:T(8,128)S(1)} %fusion.96, bf16[256,5120]{1,0:T(8,128)(2,1)} %concatenate.43, bf16[5120,216]{0,1:T(8,128)(2,1)} %param.22), kind=kOutput, calls=%fused_computation.42 | convolution fusion | flops 1132793856 | bytes 12509184 | tf_op jit(solution)/shard_map/dot_general | solution.py:168
  134.5 1.9 %slice.447 = bf16[128,5120]{1,0:T(8,128)(2,1)S(1)} slice(f32[256,5120]{1,0:T(8,128)} %fusion.23), slice={[128:256], [0:5120]} | slice | bytes 2621440 | tf_op jit(solution)/shard_map/slice | solution.py:169
  136.7 2.9 %collective-permute-done.26 = bf16[128,5120]{1,0:T(8,128)(2,1)S(1)} collective-permute-done((bf16[128,5120]{1,0:T(8,128)(2,1)S(1)}, bf16[128,5120]{1,0:T(8,128)(2,1)S(1)}, u32[]{:S(2)}, u32[]{:S(2)}) %collective-permute-start.26) | collective-permute-done | bytes 1310752 | tf_op jit(solution)/shard_map/ppermute | solution.py:34
  139.6 2.2 %fusion.80 = (bf16[128,5120]{1,0:T(8,128)(2,1)S(1)}, f32[128,5120]{1,0:T(8,128)S(1)}) fusion(bf16[128,5120]{1,0:T(8,128)(2,1)S(1)} %collective-permute-done.26, f32[256,5120]{1,0:T(8,128)} %fusion.23), kind=kLoop, calls=%fused_computation.181 | loop fusion | flops 1966080 | bytes 7864320 | tf_op jit(solution)/shard_map/convert.8
  141.9 0.7 collective-permute-start.27
  142.6 1.4 collective-permute-start.29
  144.6 7.9 %collective-permute-done.27 = bf16[32,5120]{1,0:T(8,128)(2,1)S(1)} collective-permute-done((bf16[32,5120]{1,0:T(8,128)(2,1)S(1)}, bf16[32,5120]{1,0:T(8,128)(2,1)S(1)}, u32[]{:S(2)}, u32[]{:S(2)}) %collective-permute-start.27) | collective-permute-done | bytes 327712 | tf_op jit(solution)/shard_map/ppermute | solution.py:20
  152.5 7.8 %collective-permute-done.29 = bf16[32,5120]{1,0:T(8,128)(2,1)S(1)} collective-permute-done((bf16[32,5120]{1,0:T(8,128)(2,1)S(1)}, bf16[32,5120]{1,0:T(8,128)(2,1)S(1)}, u32[]{:S(2)}, u32[]{:S(2)}) %collective-permute-start.29) | collective-permute-done | bytes 327712 | tf_op jit(solution)/shard_map/ppermute | solution.py:20
  160.5 0.8 collective-permute-start.30
  161.3 1.3 collective-permute-start.32
  162.6 1.3 collective-permute-start.31
  163.8 1.8 %collective-permute-done.30 = bf16[8,5120]{1,0:T(8,128)(2,1)S(1)} collective-permute-done((bf16[8,5120]{1,0:T(8,128)(2,1)S(1)}, bf16[8,5120]{1,0:T(8,128)(2,1)S(1)}, u32[]{:S(2)}, u32[]{:S(2)}) %collective-permute-start.30) | collective-permute-done | bytes 81952 | tf_op jit(solution)/shard_map/ppermute | solution.py:25
  165.6 1.6 collective-permute-done.32
  167.2 1.3 collective-permute-done.31
  168.6 0.8 collective-permute-start.33
  169.5 1.2 collective-permute-start.35
  170.7 1.7 collective-permute-start.34
  172.5 2.0 %collective-permute-done.35 = bf16[2,5120]{1,0:T(2,128)(2,1)S(1)} collective-permute-done((bf16[2,5120]{1,0:T(2,128)(2,1)S(1)}, bf16[2,5120]{1,0:T(2,128)(2,1)S(1)}, u32[]{:S(2)}, u32[]{:S(2)}) %collective-permute-start.35) | collective-permute-done | bytes 20512 | tf_op jit(solution)/shard_map/ppermute | solution.py:30
  174.5 1.5 collective-permute-done.34
  (87 shorter events, 10.3 us)
Async XLA Ops:
  0.0 126.7 %copy-start = (bf16[216,5120]{1,0:T(8,128)(2,1)S(1)}, bf16[216,5120]{1,0:T(8,128)(2,1)}, u32[]{:S(2)}) copy-start(bf16[216,5120]{1,0:T(8,128)(2,1)} %param.23) | copy-start | bytes 6635524
  1.1 8.5 %collective-permute-start.2 = (bf16[16,640]{1,0:T(8,128)(2,1)S(1)}, bf16[16,640]{1,0:T(8,128)(2,1)S(1)}, u32[]{:S(2)}, u32[]{:S(2)}) collective-permute-start(bf16[16,640]{1,0:T(8,128)(2,1)S(1)} %get-tuple-element.53), channel_id=1, source_target_pairs={{0,24},{8,0},{16,8},{24,16},{32,56},{40,32},{48,40},{56,48},{64,88... | collective-permute-start | bytes 61448 | tf_op jit(solution)/shard_map/ppermute | solution.py:25
  4.2 5.4 %collective-permute-start.1 = (bf16[16,640]{1,0:T(8,128)(2,1)S(1)}, bf16[16,640]{1,0:T(8,128)(2,1)S(1)}, u32[]{:S(2)}, u32[]{:S(2)}) collective-permute-start(bf16[16,640]{1,0:T(8,128)(2,1)S(1)} %get-tuple-element.53), channel_id=1, source_target_pairs={{0,16},{8,24},{16,0},{24,8},{32,48},{40,56},{48,32},{56,40},{64,80... | collective-permute-start | bytes 61448 | tf_op jit(solution)/shard_map/ppermute | solution.py:25
  4.8 5.0 %collective-permute-start = (bf16[16,640]{1,0:T(8,128)(2,1)S(1)}, bf16[16,640]{1,0:T(8,128)(2,1)S(1)}, u32[]{:S(2)}, u32[]{:S(2)}) collective-permute-start(bf16[16,640]{1,0:T(8,128)(2,1)S(1)} %get-tuple-element.53), channel_id=1, source_target_pairs={{0,8},{8,16},{16,24},{24,0},{32,40},{40,48},{48,56},{56,32},{64,72... | collective-permute-start | bytes 61448 | tf_op jit(solution)/shard_map/ppermute | solution.py:25
  9.8 9.7 %collective-permute-start.5 = (bf16[64,640]{1,0:T(8,128)(2,1)S(1)}, bf16[64,640]{1,0:T(8,128)(2,1)S(1)}, u32[]{:S(2)}, u32[]{:S(2)}) collective-permute-start(bf16[64,640]{1,0:T(8,128)(2,1)S(1)} %pad_maximum_fusion), channel_id=1, source_target_pairs={{0,96},{8,104},{16,112},{24,120},{32,0},{40,8},{48,16},{56,24},{64... | collective-permute-start | bytes 245768 | tf_op jit(solution)/shard_map/ppermute | solution.py:20
  12.7 6.8 %collective-permute-start.4 = (bf16[64,640]{1,0:T(8,128)(2,1)S(1)}, bf16[64,640]{1,0:T(8,128)(2,1)S(1)}, u32[]{:S(2)}, u32[]{:S(2)}) collective-permute-start(bf16[64,640]{1,0:T(8,128)(2,1)S(1)} %pad_maximum_fusion), channel_id=1, source_target_pairs={{0,64},{8,72},{16,80},{24,88},{32,96},{40,104},{48,112},{56,120},{... | collective-permute-start | bytes 245768 | tf_op jit(solution)/shard_map/ppermute | solution.py:20
  13.5 6.0 %collective-permute-start.3 = (bf16[64,640]{1,0:T(8,128)(2,1)S(1)}, bf16[64,640]{1,0:T(8,128)(2,1)S(1)}, u32[]{:S(2)}, u32[]{:S(2)}) collective-permute-start(bf16[64,640]{1,0:T(8,128)(2,1)S(1)} %pad_maximum_fusion), channel_id=1, source_target_pairs={{0,32},{8,40},{16,48},{24,56},{32,64},{40,72},{48,80},{56,88},{64,... | collective-permute-start | bytes 245768 | tf_op jit(solution)/shard_map/ppermute | solution.py:20
  21.9 1.6 copy-start.5
  26.1 6.6 %collective-permute-start.6 = (bf16[64,768]{0,1:T(8,128)(2,1)S(1)}, bf16[64,768]{0,1:T(8,128)(2,1)S(1)}, u32[]{:S(2)}, u32[]{:S(2)}) collective-permute-start(bf16[64,768]{0,1:T(8,128)(2,1)S(1)} %get-tuple-element.33), channel_id=1, source_target_pairs={{0,96},{8,104},{16,112},{24,120},{32,0},{40,8},{48,16},{56,24},{64... | collective-permute-start | bytes 294920 | tf_op jit(solution)/shard_map/ppermute | solution.py:20
  26.7 9.6 %collective-permute-start.8 = (bf16[64,768]{0,1:T(8,128)(2,1)S(1)}, bf16[64,768]{0,1:T(8,128)(2,1)S(1)}, u32[]{:S(2)}, u32[]{:S(2)}) collective-permute-start(bf16[64,768]{0,1:T(8,128)(2,1)S(1)} %get-tuple-element.34), channel_id=1, source_target_pairs={{0,32},{8,40},{16,48},{24,56},{32,64},{40,72},{48,80},{56,88},{64,... | collective-permute-start | bytes 294920 | tf_op jit(solution)/shard_map/ppermute | solution.py:20
  28.2 8.2 %collective-permute-start.7 = (bf16[64,768]{0,1:T(8,128)(2,1)S(1)}, bf16[64,768]{0,1:T(8,128)(2,1)S(1)}, u32[]{:S(2)}, u32[]{:S(2)}) collective-permute-start(bf16[64,768]{0,1:T(8,128)(2,1)S(1)} %get-tuple-element.35), channel_id=1, source_target_pairs={{0,64},{8,72},{16,80},{24,88},{32,96},{40,104},{48,112},{56,120},{... | collective-permute-start | bytes 294920 | tf_op jit(solution)/shard_map/ppermute | solution.py:20
  36.3 0.7 copy-start.1
  36.4 0.7 copy-start.2
  39.2 7.1 %collective-permute-start.9 = (bf16[16,768]{0,1:T(8,128)(2,1)S(1)}, bf16[16,768]{0,1:T(8,128)(2,1)S(1)}, u32[]{:S(2)}, u32[]{:S(2)}) collective-permute-start(bf16[16,768]{0,1:T(8,128)(2,1)S(1)} %get-tuple-element.39), channel_id=1, source_target_pairs={{0,24},{8,0},{16,8},{24,16},{32,56},{40,32},{48,40},{56,48},{64,88... | collective-permute-start | bytes 73736 | tf_op jit(solution)/shard_map/ppermute | solution.py:25
  41.6 9.0 %collective-permute-start.11 = (bf16[16,768]{0,1:T(8,128)(2,1)S(1)}, bf16[16,768]{0,1:T(8,128)(2,1)S(1)}, u32[]{:S(2)}, u32[]{:S(2)}) collective-permute-start(bf16[16,768]{0,1:T(8,128)(2,1)S(1)} %get-tuple-element.40), channel_id=1, source_target_pairs={{0,8},{8,16},{16,24},{24,0},{32,40},{40,48},{48,56},{56,32},{64,72... | collective-permute-start | bytes 73736 | tf_op jit(solution)/shard_map/ppermute | solution.py:25
  41.6 9.0 %collective-permute-start.10 = (bf16[16,768]{0,1:T(8,128)(2,1)S(1)}, bf16[16,768]{0,1:T(8,128)(2,1)S(1)}, u32[]{:S(2)}, u32[]{:S(2)}) collective-permute-start(bf16[16,768]{0,1:T(8,128)(2,1)S(1)} %get-tuple-element.41), channel_id=1, source_target_pairs={{0,16},{8,24},{16,0},{24,8},{32,48},{40,56},{48,32},{56,40},{64,80... | collective-permute-start | bytes 73736 | tf_op jit(solution)/shard_map/ppermute | solution.py:25
  50.8 14.9 %copy-start.3 = (bf16[2,5120]{1,0:T(2,128)(2,1)S(1)}, bf16[2,5120]{1,0:T(2,128)(2,1)}, u32[]{:S(2)}) copy-start(bf16[2,5120]{1,0:T(2,128)(2,1)} %param.12) | copy-start | bytes 61444
  50.8 15.1 %copy-start.4 = (f32[5120]{0:T(1024)S(1)}, f32[5120]{0:T(1024)}, u32[]{:S(2)}) copy-start(f32[5120]{0:T(1024)} %param.20) | copy-start | bytes 61444
  54.7 1.5 collective-permute-start.12
  56.3 6.0 %collective-permute-start.13 = (bf16[2,5120]{1,0:T(2,128)(2,1)S(1)}, bf16[2,5120]{1,0:T(2,128)(2,1)S(1)}, u32[]{:S(2)}, u32[]{:S(2)}) collective-permute-start(bf16[2,5120]{1,0:T(2,128)(2,1)S(1)} %get-tuple-element.45), channel_id=1, source_target_pairs={{0,6},{1,7},{2,0},{3,1},{4,2},{5,3},{6,4},{7,5},{8,14},{9,15},{10,... | collective-permute-start | bytes 61448 | tf_op jit(solution)/shard_map/ppermute | solution.py:30
  60.4 5.0 %collective-permute-start.15 = (bf16[2,5120]{1,0:T(2,128)(2,1)S(1)}, bf16[2,5120]{1,0:T(2,128)(2,1)S(1)}, u32[]{:S(2)}, u32[]{:S(2)}) collective-permute-start(bf16[2,5120]{1,0:T(2,128)(2,1)S(1)} %get-tuple-element.46), channel_id=1, source_target_pairs={{0,2},{1,3},{2,4},{3,5},{4,6},{5,7},{6,0},{7,1},{8,10},{9,11},{10,... | collective-permute-start | bytes 61448 | tf_op jit(solution)/shard_map/ppermute | solution.py:30
  60.4 5.3 %collective-permute-start.14 = (bf16[2,5120]{1,0:T(2,128)(2,1)S(1)}, bf16[2,5120]{1,0:T(2,128)(2,1)S(1)}, u32[]{:S(2)}, u32[]{:S(2)}) collective-permute-start(bf16[2,5120]{1,0:T(2,128)(2,1)S(1)} %get-tuple-element.47), channel_id=1, source_target_pairs={{0,4},{1,5},{2,6},{3,7},{4,0},{5,1},{6,2},{7,3},{8,12},{9,13},{10,... | collective-permute-start | bytes 61448 | tf_op jit(solution)/shard_map/ppermute | solution.py:30
  66.0 4.8 %collective-permute-start.18 = (bf16[2,5120]{1,0:T(2,128)(2,1)S(1)}, bf16[2,5120]{1,0:T(2,128)(2,1)S(1)}, u32[]{:S(2)}, u32[]{:S(2)}) collective-permute-start(bf16[2,5120]{1,0:T(2,128)(2,1)S(1)} %fusion.28), channel_id=1, source_target_pairs={{0,6},{1,7},{2,0},{3,1},{4,2},{5,3},{6,4},{7,5},{8,14},{9,15},{10,... | collective-permute-start | bytes 61448 | tf_op jit(solution)/shard_map/ppermute | solution.py:30
  69.3 5.3 %collective-permute-start.17 = (bf16[2,5120]{1,0:T(2,128)(2,1)S(1)}, bf16[2,5120]{1,0:T(2,128)(2,1)S(1)}, u32[]{:S(2)}, u32[]{:S(2)}) collective-permute-start(bf16[2,5120]{1,0:T(2,128)(2,1)S(1)} %fusion.28), channel_id=1, source_target_pairs={{0,4},{1,5},{2,6},{3,7},{4,0},{5,1},{6,2},{7,3},{8,12},{9,13},{10,... | collective-permute-start | bytes 61448 | tf_op jit(solution)/shard_map/ppermute | solution.py:30
  69.3 5.3 %collective-permute-start.16 = (bf16[2,5120]{1,0:T(2,128)(2,1)S(1)}, bf16[2,5120]{1,0:T(2,128)(2,1)S(1)}, u32[]{:S(2)}, u32[]{:S(2)}) collective-permute-start(bf16[2,5120]{1,0:T(2,128)(2,1)S(1)} %fusion.28), channel_id=1, source_target_pairs={{0,2},{1,3},{2,4},{3,5},{4,6},{5,7},{6,0},{7,1},{8,10},{9,11},{10,... | collective-permute-start | bytes 61448 | tf_op jit(solution)/shard_map/ppermute | solution.py:30
  74.7 4.5 %collective-permute-start.21 = (bf16[8,5120]{1,0:T(8,128)(2,1)S(1)}, bf16[8,5120]{1,0:T(8,128)(2,1)S(1)}, u32[]{:S(2)}, u32[]{:S(2)}) collective-permute-start(bf16[8,5120]{1,0:T(8,128)(2,1)S(1)} %pad_maximum_fusion.1), channel_id=1, source_target_pairs={{0,24},{8,0},{16,8},{24,16},{32,56},{40,32},{48,40},{56,48},{64,88... | collective-permute-start | bytes 245768 | tf_op jit(solution)/shard_map/ppermute | solution.py:25
  76.2 6.0 %collective-permute-start.20 = (bf16[8,5120]{1,0:T(8,128)(2,1)S(1)}, bf16[8,5120]{1,0:T(8,128)(2,1)S(1)}, u32[]{:S(2)}, u32[]{:S(2)}) collective-permute-start(bf16[8,5120]{1,0:T(8,128)(2,1)S(1)} %pad_maximum_fusion.1), channel_id=1, source_target_pairs={{0,16},{8,24},{16,0},{24,8},{32,48},{40,56},{48,32},{56,40},{64,80... | collective-permute-start | bytes 245768 | tf_op jit(solution)/shard_map/ppermute | solution.py:25
  76.6 6.3 %collective-permute-start.19 = (bf16[8,5120]{1,0:T(8,128)(2,1)S(1)}, bf16[8,5120]{1,0:T(8,128)(2,1)S(1)}, u32[]{:S(2)}, u32[]{:S(2)}) collective-permute-start(bf16[8,5120]{1,0:T(8,128)(2,1)S(1)} %pad_maximum_fusion.1), channel_id=1, source_target_pairs={{0,8},{8,16},{16,24},{24,0},{32,40},{40,48},{48,56},{56,32},{64,72... | collective-permute-start | bytes 245768 | tf_op jit(solution)/shard_map/ppermute | solution.py:25
  85.6 8.8 %collective-permute-start.24 = (bf16[32,5120]{1,0:T(8,128)(2,1)}, bf16[32,5120]{1,0:T(8,128)(2,1)S(1)}, u32[]{:S(2)}, u32[]{:S(2)}) collective-permute-start(bf16[32,5120]{1,0:T(8,128)(2,1)} %concatenate.41), channel_id=1, source_target_pairs={{0,96},{8,104},{16,112},{24,120},{32,0},{40,8},{48,16},{56,24},{64... | collective-permute-start | bytes 983048 | tf_op jit(solution)/shard_map/ppermute | solution.py:20
  86.7 10.2 %collective-permute-start.23 = (bf16[32,5120]{1,0:T(8,128)(2,1)}, bf16[32,5120]{1,0:T(8,128)(2,1)S(1)}, u32[]{:S(2)}, u32[]{:S(2)}) collective-permute-start(bf16[32,5120]{1,0:T(8,128)(2,1)} %concatenate.41), channel_id=1, source_target_pairs={{0,64},{8,72},{16,80},{24,88},{32,96},{40,104},{48,112},{56,120},{... | collective-permute-start | bytes 983048 | tf_op jit(solution)/shard_map/ppermute | solution.py:20
  87.2 13.1 %collective-permute-start.22 = (bf16[32,5120]{1,0:T(8,128)(2,1)}, bf16[32,5120]{1,0:T(8,128)(2,1)S(1)}, u32[]{:S(2)}, u32[]{:S(2)}) collective-permute-start(bf16[32,5120]{1,0:T(8,128)(2,1)} %concatenate.41), channel_id=1, source_target_pairs={{0,32},{8,40},{16,48},{24,56},{32,64},{40,72},{48,80},{56,88},{64,... | collective-permute-start | bytes 983048 | tf_op jit(solution)/shard_map/ppermute | solution.py:20
  106.9 3.4 %collective-permute-start.25 = (bf16[128,5120]{1,0:T(8,128)(2,1)}, bf16[128,5120]{1,0:T(8,128)(2,1)}, u32[]{:S(2)}, u32[]{:S(2)}) collective-permute-start(bf16[128,5120]{1,0:T(8,128)(2,1)} %concatenate.42), channel_id=1, source_target_pairs={{0,1},{1,0},{2,3},{3,2},{4,5},{5,4},{6,7},{7,6},{8,9},{9,8},{10,11... | collective-permute-start | bytes 3932168 | tf_op jit(solution)/shard_map/ppermute | solution.py:34
  136.4 3.1 %collective-permute-start.26 = (bf16[128,5120]{1,0:T(8,128)(2,1)S(1)}, bf16[128,5120]{1,0:T(8,128)(2,1)S(1)}, u32[]{:S(2)}, u32[]{:S(2)}) collective-permute-start(bf16[128,5120]{1,0:T(8,128)(2,1)S(1)} %slice.447), channel_id=1, source_target_pairs={{0,1},{1,0},{2,3},{3,2},{4,5},{5,4},{6,7},{7,6},{8,9},{9,8},{10,11... | collective-permute-start | bytes 3932168 | tf_op jit(solution)/shard_map/ppermute | solution.py:34
  141.9 10.6 %collective-permute-start.27 = (bf16[32,5120]{1,0:T(8,128)(2,1)S(1)}, bf16[32,5120]{1,0:T(8,128)(2,1)S(1)}, u32[]{:S(2)}, u32[]{:S(2)}) collective-permute-start(bf16[32,5120]{1,0:T(8,128)(2,1)S(1)} %get-tuple-element.30), channel_id=1, source_target_pairs={{0,96},{8,104},{16,112},{24,120},{32,0},{40,8},{48,16},{56,24},{64... | collective-permute-start | bytes 983048 | tf_op jit(solution)/shard_map/ppermute | solution.py:20
  142.6 17.7 %collective-permute-start.29 = (bf16[32,5120]{1,0:T(8,128)(2,1)S(1)}, bf16[32,5120]{1,0:T(8,128)(2,1)S(1)}, u32[]{:S(2)}, u32[]{:S(2)}) collective-permute-start(bf16[32,5120]{1,0:T(8,128)(2,1)S(1)} %get-tuple-element.31), channel_id=1, source_target_pairs={{0,32},{8,40},{16,48},{24,56},{32,64},{40,72},{48,80},{56,88},{64,... | collective-permute-start | bytes 983048 | tf_op jit(solution)/shard_map/ppermute | solution.py:20
  144.0 16.3 %collective-permute-start.28 = (bf16[32,5120]{1,0:T(8,128)(2,1)S(1)}, bf16[32,5120]{1,0:T(8,128)(2,1)S(1)}, u32[]{:S(2)}, u32[]{:S(2)}) collective-permute-start(bf16[32,5120]{1,0:T(8,128)(2,1)S(1)} %get-tuple-element.32), channel_id=1, source_target_pairs={{0,64},{8,72},{16,80},{24,88},{32,96},{40,104},{48,112},{56,120},{... | collective-permute-start | bytes 983048 | tf_op jit(solution)/shard_map/ppermute | solution.py:20
  160.5 5.1 %collective-permute-start.30 = (bf16[8,5120]{1,0:T(8,128)(2,1)S(1)}, bf16[8,5120]{1,0:T(8,128)(2,1)S(1)}, u32[]{:S(2)}, u32[]{:S(2)}) collective-permute-start(bf16[8,5120]{1,0:T(8,128)(2,1)S(1)} %get-tuple-element.36), channel_id=1, source_target_pairs={{0,24},{8,0},{16,8},{24,16},{32,56},{40,32},{48,40},{56,48},{64,88... | collective-permute-start | bytes 245768 | tf_op jit(solution)/shard_map/ppermute | solution.py:25
  161.3 5.9 %collective-permute-start.32 = (bf16[8,5120]{1,0:T(8,128)(2,1)S(1)}, bf16[8,5120]{1,0:T(8,128)(2,1)S(1)}, u32[]{:S(2)}, u32[]{:S(2)}) collective-permute-start(bf16[8,5120]{1,0:T(8,128)(2,1)S(1)} %get-tuple-element.37), channel_id=1, source_target_pairs={{0,8},{8,16},{16,24},{24,0},{32,40},{40,48},{48,56},{56,32},{64,72... | collective-permute-start | bytes 245768 | tf_op jit(solution)/shard_map/ppermute | solution.py:25
  162.6 5.9 %collective-permute-start.31 = (bf16[8,5120]{1,0:T(8,128)(2,1)S(1)}, bf16[8,5120]{1,0:T(8,128)(2,1)S(1)}, u32[]{:S(2)}, u32[]{:S(2)}) collective-permute-start(bf16[8,5120]{1,0:T(8,128)(2,1)S(1)} %get-tuple-element.38), channel_id=1, source_target_pairs={{0,16},{8,24},{16,0},{24,8},{32,48},{40,56},{48,32},{56,40},{64,80... | collective-permute-start | bytes 245768 | tf_op jit(solution)/shard_map/ppermute | solution.py:25
  168.6 3.9 %collective-permute-start.33 = (bf16[2,5120]{1,0:T(2,128)(2,1)S(1)}, bf16[2,5120]{1,0:T(2,128)(2,1)S(1)}, u32[]{:S(2)}, u32[]{:S(2)}) collective-permute-start(bf16[2,5120]{1,0:T(2,128)(2,1)S(1)} %get-tuple-element.42), channel_id=1, source_target_pairs={{0,6},{1,7},{2,0},{3,1},{4,2},{5,3},{6,4},{7,5},{8,14},{9,15},{10,... | collective-permute-start | bytes 61448 | tf_op jit(solution)/shard_map/ppermute | solution.py:30
  169.5 5.0 %collective-permute-start.35 = (bf16[2,5120]{1,0:T(2,128)(2,1)S(1)}, bf16[2,5120]{1,0:T(2,128)(2,1)S(1)}, u32[]{:S(2)}, u32[]{:S(2)}) collective-permute-start(bf16[2,5120]{1,0:T(2,128)(2,1)S(1)} %get-tuple-element.43), channel_id=1, source_target_pairs={{0,2},{1,3},{2,4},{3,5},{4,6},{5,7},{6,0},{7,1},{8,10},{9,11},{10,... | collective-permute-start | bytes 61448 | tf_op jit(solution)/shard_map/ppermute | solution.py:30
  170.7 5.3 %collective-permute-start.34 = (bf16[2,5120]{1,0:T(2,128)(2,1)S(1)}, bf16[2,5120]{1,0:T(2,128)(2,1)S(1)}, u32[]{:S(2)}, u32[]{:S(2)}) collective-permute-start(bf16[2,5120]{1,0:T(2,128)(2,1)S(1)} %get-tuple-element.44), channel_id=1, source_target_pairs={{0,4},{1,5},{2,6},{3,7},{4,0},{5,1},{6,2},{7,3},{8,12},{9,13},{10,... | collective-permute-start | bytes 61448 | tf_op jit(solution)/shard_map/ppermute | solution.py:30

commit v2 on v1

v2 whole, which is shorter than its diff:
```python
import functools
import math

import jax
import jax.numpy as jnp
from jax import lax
from jax.experimental import pallas as pl
from jax.experimental.pallas import tpu as pltpu
from jax.sharding import PartitionSpec as P

QUERY_HEADS = 40
KEY_VALUE_HEADS = 8
HEAD_WIDTH = 128
GROUP = QUERY_HEADS // KEY_VALUE_HEADS
LOWEST = -(2.0**100)
SCALE = 1.0 / math.sqrt(HEAD_WIDTH)
EPSILON = 1e-06
BF = jnp.bfloat16
F32 = jnp.float32
D = 5120
VM = pltpu.VMEM
SM = pltpu.SMEM


def call(kernel, out_shape, in_spaces, scratch=(), limit=48 << 20, **kw):
    outs = out_shape if isinstance(out_shape, (list, tuple)) else [out_shape]
    specs = [pl.BlockSpec(memory_space=VM) for _ in outs]
    return pl.pallas_call(
        kernel,
        out_shape=out_shape,
        in_specs=[pl.BlockSpec(memory_space=s) for s in in_spaces],
        out_specs=specs if isinstance(out_shape, (list, tuple)) else specs[0],
        scratch_shapes=list(scratch),
        compiler_params=pltpu.CompilerParams(vmem_limit_bytes=limit),
        **kw,
    )


def nt(a, b):
    return lax.dot_general(a, b, (((1,), (1,)), ((), ())), preferred_element_type=F32)


def mm(a, b):
    return lax.dot_general(a, b, (((1,), (0,)), ((), ())), preferred_element_type=F32)


def attend_kernel(lengths, parents, first, leaf, q, keys, values, out, starts):
    nodes = lengths.shape[0]
    slots = keys.shape[0]
    tokens = q.shape[0]
    running = jnp.int32(0)
    for n in range(nodes):
        starts[n] = running
        running = running + lengths[n]
    lane = lax.broadcasted_iota(jnp.int32, (1, 128), 1)
    zero = jnp.zeros((1, 128), jnp.int32)
    own_lo, own_hi, up_lo, up_hi = zero, zero, zero, zero
    for n in range(nodes):
        lo = starts[n]
        up = parents[n]
        here = lane == n
        own_lo = jnp.where(here, lo, own_lo)
        own_hi = jnp.where(here, lo + lengths[n], own_hi)
        up_lo = jnp.where(here, starts[up], up_lo)
        up_hi = jnp.where(here, starts[up] + lengths[up], up_hi)
    slot = first[0] + lax.broadcasted_iota(jnp.int32, (slots, 128), 0)
    seen = (
        (slot < lengths[0])
        | ((slot >= own_lo) & (slot < own_hi))
        | ((slot >= up_lo) & (slot < up_hi))
    )
    bias = jnp.where(seen, 0.0, LOWEST).astype(BF)
    node = lax.broadcasted_iota(jnp.int32, (128, tokens), 0)
    onehot = jnp.where(node == leaf[...], 1.0, 0.0).astype(F32).T.astype(BF)
    keys_wide = jnp.concatenate([keys[...], bias], axis=1)

    lane_t = lax.broadcasted_iota(jnp.int32, (tokens, 128), 1)
    stats = jnp.zeros((tokens, 128), F32)
    for g in range(GROUP):
        cols = pl.ds(g * HEAD_WIDTH, HEAD_WIDTH)
        q_wide = jnp.concatenate([q[:, cols], onehot], axis=1)
        scores = nt(q_wide, keys_wide)
        top = jnp.max(scores, axis=1, keepdims=True).astype(BF).astype(F32)
        weights = jnp.exp((scores - top) * SCALE)
        mass = jnp.sum(weights, axis=1, keepdims=True)
        out[:, cols] = mm(weights.astype(BF), values[...]).astype(BF)
        high = mass.astype(BF).astype(F32)
        stats = jnp.where(lane_t == g, top, stats)
        stats = jnp.where(lane_t == GROUP + g, high, stats)
        stats = jnp.where(lane_t == 2 * GROUP + g, mass - high, stats)
    out[:, GROUP * HEAD_WIDTH :] = stats.astype(BF)


def project_kernel(core, parts, weight, own, other):
    sources = parts.shape[0]
    width = GROUP * HEAD_WIDTH
    stats = [parts[s, :, width:].astype(F32) for s in range(sources)]
    top = stats[0]
    for s in stats[1:]:
        top = jnp.maximum(top, s)
    scales = [jnp.exp((s - top) * SCALE) for s in stats]
    heads = []
    for g in range(GROUP):
        total = jnp.zeros((16, HEAD_WIDTH), F32)
        mass = jnp.zeros((16, 1), F32)
        for s in range(sources):
            scale = scales[s][:, g : g + 1]
            part = parts[s, :, g * HEAD_WIDTH : (g + 1) * HEAD_WIDTH].astype(F32)
            total = total + part * scale
            low = stats[s][:, GROUP + g : GROUP + g + 1] + stats[s][:, 2 * GROUP + g : 2 * GROUP + g + 1]
            mass = mass + low * scale
        heads.append((total / mass).astype(BF))
    context = jnp.concatenate(heads, axis=1)
    row = lax.broadcasted_iota(jnp.int32, (16, 16), 0)
    col = lax.broadcasted_iota(jnp.int32, (16, 16), 1)
    half = jnp.where(row < 8, core[0], 1 - core[0])
    source = (row % 8) // 2 * 4 + half * 2 + row % 2
    pick = jnp.where(col == source, 1.0, 0.0).astype(BF)
    context = mm(pick, context).astype(BF)
    result = mm(context, weight[...])
    own[...] = result[:8]
    other[...] = result[8:].astype(BF)


def hidden_of(rows, gate, up):
    g = nt(rows, gate)
    u = nt(rows, up)
    return (g / (1.0 + jnp.exp(-g)) * u).astype(BF)


def hidden_kernel(rows, gate, up, out):
    out[...] = hidden_of(rows[...], gate[...], up[...])


def mlp_kernel(rows, gate, up, down, out):
    out[...] = mm(hidden_of(rows[...], gate[...], up[...]), down[...]).astype(out.dtype)


def down_kernel(hidden, down, out):
    out[...] = mm(hidden[...], down[...]).astype(out.dtype)


def move_z(value, k):
    pairs = [(z * 2 + c, (z + k) % 4 * 2 + c) for z in range(4) for c in range(2)]
    return lax.ppermute(value, "tp", pairs)


def move_core(value):
    return lax.ppermute(value, "tp", [(i, i ^ 1) for i in range(8)])


def local(
    activations,
    queries,
    keys,
    values,
    parents,
    node_lengths,
    token_leaf,
    out_weight,
    norm_gain,
    gate_weight,
    up_weight,
    down_weight,
):
    kv = lax.axis_index("kv")
    tp = lax.axis_index("tp")
    z, c = tp // 2, tp % 2
    slots = keys.shape[0]
    gate_t, up_t = gate_weight.T, up_weight.T
    shape = jax.ShapeDtypeStruct

    q = lax.all_to_all(jnp.broadcast_to(queries[None], (16, 16, 640)), "kv", 0, 0)
    packed = call(
        attend_kernel,
        shape((256, 768), BF),
        [SM, SM, SM, VM, VM, VM, VM],
        [pltpu.SMEM((16,), jnp.int32)],
    )(node_lengths, parents, (kv * slots)[None], token_leaf[None, :], q.reshape(256, 640), keys, values)
    parts = lax.all_to_all(packed.reshape(16, 16, 768), "kv", 0, 0)
    own, other = call(project_kernel, [shape((8, D), F32), shape((8, D), BF)], [SM, VM, VM])(
        c[None], parts, out_weight
    )

    mine = (jnp.arange(8) // 2 == z)[:, None]
    act = jnp.where(mine, jnp.tile(activations, (4, 1)), 0).astype(F32)
    attended = own + move_core(other).astype(F32) + act
    sent = attended.astype(BF)
    for part in [move_z(sent, k) for k in (1, 3, 2)]:
        attended = attended + part.astype(F32)
    residual = attended.astype(BF)
    widened = residual.astype(F32)
    normed = (
        widened
        * lax.rsqrt(jnp.mean(widened * widened, axis=1, keepdims=True) + EPSILON)
        * norm_gain
    ).astype(BF)

    rows = lax.all_to_all(jnp.broadcast_to(normed[None], (16, 8, D)), "kv", 0, 0).reshape(128, D)
    rows_other = move_core(rows)
    hidden = call(hidden_kernel, shape((128, 216), BF), [VM, VM, VM])(rows, gate_t, up_t)
    y_other = call(mlp_kernel, shape((128, D), BF), [VM, VM, VM, VM])(rows_other, gate_t, up_t, down_weight)
    back = move_core(y_other)
    y_own = call(down_kernel, shape((128, D), F32), [VM, VM])(hidden, down_weight)
    mixed = (y_own + back.astype(F32)).astype(BF).reshape(64, 2, D)
    groups = [[i for i in range(128) if i % 2 == k] for k in range(2)]
    mixed = lax.all_to_all(mixed, ("kv", "tp"), 0, 0, axis_index_groups=groups)
    final = lax.dynamic_slice_in_dim(widened, z * 2, 2, 0) + jnp.sum(mixed.astype(F32), axis=0)
    return final.astype(BF)


def solution(mesh):
    return jax.shard_map(
        local,
        mesh=mesh,
        in_specs=(
            P(("kv", "tp"), None),
            P("kv", "tp"),
            P("kv", "tp"),
            P("kv", "tp"),
            P(),
            P(),
            P(),
            P("tp", None),
            P(),
            P(None, ("kv", "tp")),
            P(None, ("kv", "tp")),
            P(("kv", "tp"), None),
        ),
        out_specs=P(("kv", "tp"), None),
        check_vma=False,
    )
```

time: 177 us -> 121 us (0.68)
  waiting for transfers between devices: 76.3 us -> 49.2 us
  blocking collectives: 0 us -> 22 us
  local copies, waits for them, and re-layouts: 27.4 us -> 6.97 us
  matrix products: 19.7 us -> 0 us
  starting transfers between devices: 42.6 us -> 24.3 us
  Pallas kernels: 0 us -> 15.3 us
  other arithmetic: 10.3 us -> 2.38 us
    ppermute x24 -> x0, waiting for transfers between devices: 57.5 us -> none  [the longest x12 39.7 us: move_x(): return lax.ppermute(value, 'kv', pairs)]
    all_to_all x0 -> x3, waiting for transfers between devices: none -> 39.9 us  [the longest x1 21.8 us: local(): mixed = lax.all_to_all(mixed, ('kv', 'tp'), 0, 0, axis_index_groups=groups)]
    ppermute x24 -> x0, starting transfers between devices: 28.1 us -> none  [the longest x12 14.8 us: move_y(): return lax.ppermute(value, 'kv', pairs)]
    concatenate x7 -> x0, local copies, waits for them, and re-layouts: 23.7 us -> none  [the longest x1 13 us: local(): rows = jnp.concatenate([rows, move_core(rows)], axis=0)]
    all_to_all x0 -> x1, blocking collectives: none -> 22 us  [local(): lax.all_to_all(jnp.broadcast_to(normed[None], (16, 8, D)), 'kv', 0, 0)]
    dot_general x6 -> x0, matrix products: 19.7 us -> none  [the longest x1 7.79 us: local(): mixed = jnp.dot(hidden, down_weight, preferred_element_type=F32)]
    all_to_all x0 -> x3, starting transfers between devices: none -> 18.1 us  [the longest x1 7.25 us: local(): lax.all_to_all(jnp.broadcast_to(queries[None], (16, 16, 640)), 'kv', 0, 0)]
    pallas_call x0 -> x5, Pallas kernels: none -> 15.3 us  [the longest x1 4.56 us: local(): call(mlp_kernel, shape((128, D), BF), [VM, VM, VM, VM])]
  transfers between devices with their start and end apart: 36 -> 9, of which waited for: 26 -> 9; matrix products, arithmetic and copies ran while one was open for 2% -> 0% of each run, Pallas kernels for 0% -> 2%
where the time goes in v2:
time: 121 us; the launch traced here: 120 us
  waiting for transfers between devices  49.2 us (41%)
  starting transfers between devices  24.3 us (20%)
  blocking collectives  22 us (18%)
  Pallas kernels  15.3 us (13%)
  local copies, waits for them, and re-layouts  6.97 us (6%)
  other arithmetic  2.38 us (2%)
    all_to_all x1, blocking collectives, local(): lax.all_to_all(jnp.broadcast_to(normed[None], (16, 8, D)), 'kv', 0, 0)  22 us
    all_to_all x1, waiting for transfers between devices, local(): mixed = lax.all_to_all(mixed, ('kv', 'tp'), 0, 0, axis_index_groups=groups)  21.8 us
    all_to_all x1, waiting for transfers between devices, local(): lax.all_to_all(jnp.broadcast_to(queries[None], (16, 16, 640)), 'kv', 0, 0)  9.16 us
    all_to_all x1, waiting for transfers between devices, local(): parts = lax.all_to_all(packed.reshape(16, 16, 768), 'kv', 0, 0)  8.99 us
    all_to_all x1, starting transfers between devices, local(): lax.all_to_all(jnp.broadcast_to(queries[None], (16, 16, 640)), 'kv', 0, 0)  7.25 us
    all_to_all x1, starting transfers between devices, local(): mixed = lax.all_to_all(mixed, ('kv', 'tp'), 0, 0, axis_index_groups=groups)  7.19 us
    ppermute x3, starting transfers between devices, move_z(): return lax.ppermute(value, 'tp', pairs)  5.98 us
    ppermute x3, waiting for transfers between devices, move_core(): return lax.ppermute(value, 'tp', [(i, i ^ 1) for i in range(8)])  4.99 us
  transfers between devices with their start and end apart: 9, of which 9 were waited for; matrix products, arithmetic and copies ran while one was open for 0% of the time, Pallas kernels for 2%

profile of v2, /device:TPU:0, one launch (start us, length us, event | category | flops | bytes accessed | tf_op | source)
XLA Modules:
  0.0 120.4 jit_solution(848831491469866421)
XLA Ops:
  0.0 1.5 %broadcast_in_dim.39 = bf16[16,16,640]{2,1,0:T(8,128)(2,1)} broadcast(bf16[16,640]{1,0:T(8,128)(2,1)} %param.13), dimensions={1,2} | broadcast | bytes 348160 | tf_op jit(solution)/shard_map/broadcast_in_dim | solution.py:173
  1.5 0.0 copy-start.9
  1.5 7.2 %all-to-all-start = ((bf16[16,16,640]{2,1,0:T(8,128)(2,1)}), bf16[16,16,640]{2,1,0:T(8,128)(2,1)S(1)}, u32[]{:S(2)}, u32[]{:S(2)}) async-start(bf16[16,16,640]{2,1,0:T(8,128)(2,1)} %broadcast_in_dim.39), calls=%async_computation | async-start | bytes 655360 | tf_op jit(solution)/shard_map/all_to_all | solution.py:173
  8.7 9.2 %all-to-all-done = bf16[16,16,640]{2,1,0:T(8,128)(2,1)S(1)} async-done(((bf16[16,16,640]{2,1,0:T(8,128)(2,1)}), bf16[16,16,640]{2,1,0:T(8,128)(2,1)S(1)}, u32[]{:S(2)}, u32[]{:S(2)}) %all-to-all-start) | async-done | bytes 327712 | tf_op jit(solution)/shard_map/all_to_all | solution.py:173
  17.9 0.0 copy-start.3
  17.9 0.9 copy-done.3
  18.9 0.0 copy-start.4
  18.9 0.9 copy-done.4
  19.8 0.0 copy-start.5
  19.8 0.7 copy-done.5
  20.5 0.0 copy-start.6
  20.5 0.7 copy-done.6
  21.1 0.0 copy-start.7
  21.1 0.7 copy-done.7
  21.8 4.3 %shard_map.118 = bf16[256,768]{1,0:T(8,128)(2,1)} custom-call(s32[13]{0:T(128)S(1)} %copy-done.6, s32[13]{0:T(128)S(1)} %copy-done.7, s32[1]{0:T(128)} %bitcast.1.first, s32[1,256]{1,0:T(1,128)S(1)} %bitcast.15, bf16[256,640]{1,0:T(8,128)(2,1)S(1)} %bitcast.14, bf16[1024,128]{1,0:T(8,128)(2,1)S(1)} %copy-done.3, bf16[1024,128]{1,0:T(8,128)(2,1)S(1)} %copy-done.4), custom_call_target="tpu_custom_call" | custom-call | tf_op jit(solution)/shard_map/pallas_call | solution.py:174
  26.1 3.7 %all-to-all-start.1 = ((bf16[16,16,768]{2,1,0:T(8,128)(2,1)}), bf16[16,16,768]{2,1,0:T(8,128)(2,1)S(1)}, u32[]{:S(2)}, u32[]{:S(2)}) async-start(bf16[16,16,768]{2,1,0:T(8,128)(2,1)} %bitcast.4), calls=%async_computation.1 | async-start | bytes 786432 | tf_op jit(solution)/shard_map/all_to_all | solution.py:180
  29.8 0.0 copy-done.9
  29.9 9.0 %all-to-all-done.1.parts = bf16[16,16,768]{2,1,0:T(8,128)(2,1)S(1)} async-done(((bf16[16,16,768]{2,1,0:T(8,128)(2,1)}), bf16[16,16,768]{2,1,0:T(8,128)(2,1)S(1)}, u32[]{:S(2)}, u32[]{:S(2)}) %all-to-all-start.1) | async-done | bytes 393248 | tf_op jit(solution)/shard_map/all_to_all | solution.py:180
  38.9 0.0 copy-start.8
  38.9 4.3 %shard_map.119 = (f32[8,5120]{1,0:T(8,128)S(1)}, bf16[8,5120]{1,0:T(8,128)(2,1)S(1)}) custom-call(s32[1]{0:T(128)} %bitcast.core, bf16[16,16,768]{2,1,0:T(8,128)(2,1)S(1)} %all-to-all-done.1.parts, bf16[640,5120]{1,0:T(8,128)(2,1)} %weight.1), custom_call_target="tpu_custom_call" | custom-call | tf_op jit(solution)/shard_map/pallas_call | solution.py:181
  43.1 0.0 collective-permute-start
  43.2 1.3 %collective-permute-done = bf16[8,5120]{1,0:T(8,128)(2,1)S(1)} collective-permute-done((bf16[8,5120]{1,0:T(8,128)(2,1)S(1)}, bf16[8,5120]{1,0:T(8,128)(2,1)S(1)}, u32[]{:S(2)}, u32[]{:S(2)}) %collective-permute-start) | collective-permute-done | bytes 81952 | tf_op jit(solution)/shard_map/ppermute | solution.py:149
  44.4 0.1 fusion.1
  44.5 4.0 %collective-permute-start.3 = (bf16[8,5120]{1,0:T(8,128)(2,1)S(1)}, bf16[8,5120]{1,0:T(8,128)(2,1)S(1)}, u32[]{:S(2)}, u32[]{:S(2)}) collective-permute-start(bf16[8,5120]{1,0:T(8,128)(2,1)S(1)} %fusion.1), channel_id=1, source_target_pairs={{0,4},{1,5},{2,6},{3,7},{4,0},{5,1},{6,2},{7,3},{8,12},{9,13},{10,... | collective-permute-start | bytes 245768 | tf_op jit(solution)/shard_map/ppermute | solution.py:145
  48.5 0.7 collective-permute-start.2
  49.2 1.3 %collective-permute-start.1 = (bf16[8,5120]{1,0:T(8,128)(2,1)S(1)}, bf16[8,5120]{1,0:T(8,128)(2,1)S(1)}, u32[]{:S(2)}, u32[]{:S(2)}) collective-permute-start(bf16[8,5120]{1,0:T(8,128)(2,1)S(1)} %fusion.1), channel_id=1, source_target_pairs={{0,2},{1,3},{2,4},{3,5},{4,6},{5,7},{6,0},{7,1},{8,10},{9,11},{10,... | collective-permute-start | bytes 245768 | tf_op jit(solution)/shard_map/ppermute | solution.py:145
  50.5 0.7 collective-permute-done.3
  51.2 2.5 %collective-permute-done.2 = bf16[8,5120]{1,0:T(8,128)(2,1)S(1)} collective-permute-done((bf16[8,5120]{1,0:T(8,128)(2,1)S(1)}, bf16[8,5120]{1,0:T(8,128)(2,1)S(1)}, u32[]{:S(2)}, u32[]{:S(2)}) %collective-permute-start.2) | collective-permute-done | bytes 81952 | tf_op jit(solution)/shard_map/ppermute | solution.py:145
  53.8 1.1 collective-permute-done.1
  54.8 0.2 multiply_reduce_fusion
  55.1 0.0 copy-done.8
  55.1 0.1 multiply_convert_fusion
  55.2 0.1 broadcast_in_dim.42
  55.3 0.0 copy-start.1
  55.3 22.0 %all_to_all.20 = bf16[16,8,5120]{2,1,0:T(8,128)(2,1)S(1)} all-to-all(bf16[16,8,5120]{2,1,0:T(8,128)(2,1)S(1)} %broadcast_in_dim.42), channel_id=1, replica_groups=mesh['kv'=16,'tp'=8] {'kv'}, dimensions={0} | all-to-all | bytes 2621440 | tf_op jit(solution)/shard_map/all_to_all | solution.py:199
  77.3 0.0 collective-permute-start.4
  77.3 3.0 %collective-permute-done.4.rows = bf16[128,5120]{1,0:T(8,128)(2,1)S(1)} collective-permute-done((bf16[128,5120]{1,0:T(8,128)(2,1)S(1)}, bf16[128,5120]{1,0:T(8,128)(2,1)S(1)}, u32[]{:S(2)}, u32[]{:S(2)}) %collective-permute-start.4) | collective-permute-done | bytes 1310752 | tf_op jit(solution)/shard_map/ppermute | solution.py:149
  80.4 0.0 copy-done.1
  80.4 0.0 copy-start.2
  80.4 4.6 %shard_map.122 = bf16[128,5120]{1,0:T(8,128)(2,1)S(1)} custom-call(bf16[128,5120]{1,0:T(8,128)(2,1)S(1)} %collective-permute-done.4.rows, bf16[216,5120]{1,0:T(8,128)(2,1)S(1)} %bitcast.8, bf16[216,5120]{1,0:T(8,128)(2,1)} %bitcast.10, bf16[216,5120]{1,0:T(8,128)(2,1)} %down.3), custom_call_target="tpu_custom_call" | custom-call | tf_op jit(solution)/shard_map/pallas_call | solution.py:202
  84.9 0.2 collective-permute-start.5
  85.2 0.0 copy-done.2
  85.2 0.0 copy-start
  85.2 1.7 %shard_map.120.hidden = bf16[128,216]{1,0:T(8,128)(2,1)S(1)} custom-call(bf16[128,5120]{1,0:T(8,128)(2,1)S(1)} %bitcast.13, bf16[216,5120]{1,0:T(8,128)(2,1)S(1)} %bitcast.9, bf16[216,5120]{1,0:T(8,128)(2,1)S(1)} %bitcast.11), custom_call_target="tpu_custom_call" | custom-call | tf_op jit(solution)/shard_map/pallas_call | solution.py:201
  86.8 0.0 copy-done
  86.9 0.5 shard_map.121
  87.4 0.7 collective-permute-done.5
  88.1 0.3 add_convert_fusion
  88.3 1.4 %reshape.44 = bf16[64,2,5120]{2,1,0:T(2,128)(2,1)} reshape(bf16[128,5120]{1,0:T(8,128)(2,1)S(1)} %add_convert_fusion) | data formatting | bytes 2621440 | tf_op jit(solution)/shard_map/reshape | solution.py:205
  89.7 7.2 %all-to-all-start.3 = ((bf16[64,2,5120]{2,1,0:T(2,128)(2,1)}), bf16[64,2,5120]{2,1,0:T(2,128)(2,1)S(1)}, u32[]{:S(2)}, u32[]{:S(2)}) async-start(bf16[64,2,5120]{2,1,0:T(2,128)(2,1)} %reshape.44), calls=%async_computation.3 | async-start | bytes 2621440 | tf_op jit(solution)/shard_map/all_to_all | solution.py:207
  96.9 21.8 %all-to-all-done.3 = bf16[64,2,5120]{2,1,0:T(2,128)(2,1)S(1)} async-done(((bf16[64,2,5120]{2,1,0:T(2,128)(2,1)}), bf16[64,2,5120]{2,1,0:T(2,128)(2,1)S(1)}, u32[]{:S(2)}, u32[]{:S(2)}) %all-to-all-start.3) | async-done | bytes 1310752 | tf_op jit(solution)/shard_map/all_to_all | solution.py:207
  118.7 1.1 convert_reduce_fusion
  119.7 0.6 add_convert_fusion.2
  (4 shorter events, 0.1 us)
Async XLA Ops:
  1.5 28.3 %copy-start.9 = (bf16[2,5120]{1,0:T(2,128)(2,1)S(1)}, bf16[2,5120]{1,0:T(2,128)(2,1)}, u32[]{:S(2)}) copy-start(bf16[2,5120]{1,0:T(2,128)(2,1)} %param.12) | copy-start | bytes 61444
  1.5 16.4 %all-to-all-start = ((bf16[16,16,640]{2,1,0:T(8,128)(2,1)}), bf16[16,16,640]{2,1,0:T(8,128)(2,1)S(1)}, u32[]{:S(2)}, u32[]{:S(2)}) async-start(bf16[16,16,640]{2,1,0:T(8,128)(2,1)} %broadcast_in_dim.39), calls=%async_computation | async-start | bytes 655360 | tf_op jit(solution)/shard_map/all_to_all | solution.py:173
  17.9 1.0 copy-start.3
  18.9 0.9 copy-start.4
  19.8 0.7 copy-start.5
  20.5 0.7 copy-start.6
  21.1 0.7 copy-start.7
  26.1 12.8 %all-to-all-start.1 = ((bf16[16,16,768]{2,1,0:T(8,128)(2,1)}), bf16[16,16,768]{2,1,0:T(8,128)(2,1)S(1)}, u32[]{:S(2)}, u32[]{:S(2)}) async-start(bf16[16,16,768]{2,1,0:T(8,128)(2,1)} %bitcast.4), calls=%async_computation.1 | async-start | bytes 786432 | tf_op jit(solution)/shard_map/all_to_all | solution.py:180
  38.9 16.2 %copy-start.8 = (f32[5120]{0:T(1024)S(1)}, f32[5120]{0:T(1024)}, u32[]{:S(2)}) copy-start(f32[5120]{0:T(1024)} %param.20) | copy-start | bytes 61444
  43.1 1.3 %collective-permute-start = (bf16[8,5120]{1,0:T(8,128)(2,1)S(1)}, bf16[8,5120]{1,0:T(8,128)(2,1)S(1)}, u32[]{:S(2)}, u32[]{:S(2)}) collective-permute-start(bf16[8,5120]{1,0:T(8,128)(2,1)S(1)} %get-tuple-element.8), channel_id=1, source_target_pairs={{0,1},{1,0},{2,3},{3,2},{4,5},{5,4},{6,7},{7,6},{8,9},{9,8},{10,11... | collective-permute-start | bytes 245768 | tf_op jit(solution)/shard_map/ppermute | solution.py:149
  44.5 6.7 %collective-permute-start.3 = (bf16[8,5120]{1,0:T(8,128)(2,1)S(1)}, bf16[8,5120]{1,0:T(8,128)(2,1)S(1)}, u32[]{:S(2)}, u32[]{:S(2)}) collective-permute-start(bf16[8,5120]{1,0:T(8,128)(2,1)S(1)} %fusion.1), channel_id=1, source_target_pairs={{0,4},{1,5},{2,6},{3,7},{4,0},{5,1},{6,2},{7,3},{8,12},{9,13},{10,... | collective-permute-start | bytes 245768 | tf_op jit(solution)/shard_map/ppermute | solution.py:145
  48.5 5.3 %collective-permute-start.2 = (bf16[8,5120]{1,0:T(8,128)(2,1)S(1)}, bf16[8,5120]{1,0:T(8,128)(2,1)S(1)}, u32[]{:S(2)}, u32[]{:S(2)}) collective-permute-start(bf16[8,5120]{1,0:T(8,128)(2,1)S(1)} %fusion.1), channel_id=1, source_target_pairs={{0,6},{1,7},{2,0},{3,1},{4,2},{5,3},{6,4},{7,5},{8,14},{9,15},{10,... | collective-permute-start | bytes 245768 | tf_op jit(solution)/shard_map/ppermute | solution.py:145
  49.2 5.7 %collective-permute-start.1 = (bf16[8,5120]{1,0:T(8,128)(2,1)S(1)}, bf16[8,5120]{1,0:T(8,128)(2,1)S(1)}, u32[]{:S(2)}, u32[]{:S(2)}) collective-permute-start(bf16[8,5120]{1,0:T(8,128)(2,1)S(1)} %fusion.1), channel_id=1, source_target_pairs={{0,2},{1,3},{2,4},{3,5},{4,6},{5,7},{6,0},{7,1},{8,10},{9,11},{10,... | collective-permute-start | bytes 245768 | tf_op jit(solution)/shard_map/ppermute | solution.py:145
  55.3 25.0 %copy-start.1 = (bf16[5120,216]{0,1:T(8,128)(2,1)S(1)}, bf16[5120,216]{0,1:T(8,128)(2,1)}, u32[]{:S(2)}) copy-start(bf16[5120,216]{0,1:T(8,128)(2,1)} %param.21) | copy-start | bytes 6635524
  77.3 3.0 %collective-permute-start.4 = (bf16[128,5120]{1,0:T(8,128)(2,1)S(1)}, bf16[128,5120]{1,0:T(8,128)(2,1)S(1)}, u32[]{:S(2)}, u32[]{:S(2)}) collective-permute-start(bf16[128,5120]{1,0:T(8,128)(2,1)S(1)} %bitcast.12), channel_id=1, source_target_pairs={{0,1},{1,0},{2,3},{3,2},{4,5},{5,4},{6,7},{7,6},{8,9},{9,8},{10,11... | collective-permute-start | bytes 3932168 | tf_op jit(solution)/shard_map/ppermute | solution.py:149
  80.4 4.8 %copy-start.2 = (bf16[5120,216]{0,1:T(8,128)(2,1)S(1)}, bf16[5120,216]{0,1:T(8,128)(2,1)}, u32[]{:S(2)}) copy-start(bf16[5120,216]{0,1:T(8,128)(2,1)} %param.22) | copy-start | bytes 6635524
  84.9 3.1 %collective-permute-start.5 = (bf16[128,5120]{1,0:T(8,128)(2,1)S(1)}, bf16[128,5120]{1,0:T(8,128)(2,1)S(1)}, u32[]{:S(2)}, u32[]{:S(2)}) collective-permute-start(bf16[128,5120]{1,0:T(8,128)(2,1)S(1)} %shard_map.122), channel_id=1, source_target_pairs={{0,1},{1,0},{2,3},{3,2},{4,5},{5,4},{6,7},{7,6},{8,9},{9,8},{10,11... | collective-permute-start | bytes 3932168 | tf_op jit(solution)/shard_map/ppermute | solution.py:149
  85.2 1.7 %copy-start = (bf16[216,5120]{1,0:T(8,128)(2,1)S(1)}, bf16[216,5120]{1,0:T(8,128)(2,1)}, u32[]{:S(2)}) copy-start(bf16[216,5120]{1,0:T(8,128)(2,1)} %down.3) | copy-start | bytes 6635524
  89.7 29.0 %all-to-all-start.3 = ((bf16[64,2,5120]{2,1,0:T(2,128)(2,1)}), bf16[64,2,5120]{2,1,0:T(2,128)(2,1)S(1)}, u32[]{:S(2)}, u32[]{:S(2)}) async-start(bf16[64,2,5120]{2,1,0:T(2,128)(2,1)} %reshape.44), calls=%async_computation.3 | async-start | bytes 2621440 | tf_op jit(solution)/shard_map/all_to_all | solution.py:207

commit v3 on v2

--- a/solution.py
+++ b/solution.py
@@ -22,7 +22,7 @@
 SM = pltpu.SMEM
 
 
-def call(kernel, out_shape, in_spaces, scratch=(), limit=48 << 20, **kw):
+def call(kernel, out_shape, in_spaces, scratch=(), limit=12 << 20, **kw):
     outs = out_shape if isinstance(out_shape, (list, tuple)) else [out_shape]
     specs = [pl.BlockSpec(memory_space=VM) for _ in outs]
     return pl.pallas_call(
@@ -44,10 +44,10 @@
     return lax.dot_general(a, b, (((1,), (0,)), ((), ())), preferred_element_type=F32)
 
 
-def attend_kernel(lengths, parents, first, leaf, q, keys, values, out, starts):
+def prepare_kernel(lengths, parents, first, leaf, keys, values, keys_wide, values_out, onehot, starts):
     nodes = lengths.shape[0]
     slots = keys.shape[0]
-    tokens = q.shape[0]
+    tokens = leaf.shape[1]
     running = jnp.int32(0)
     for n in range(nodes):
         starts[n] = running
@@ -69,17 +69,21 @@
         | ((slot >= own_lo) & (slot < own_hi))
         | ((slot >= up_lo) & (slot < up_hi))
     )
-    bias = jnp.where(seen, 0.0, LOWEST).astype(BF)
+    keys_wide[:, :HEAD_WIDTH] = keys[...]
+    keys_wide[:, HEAD_WIDTH:] = jnp.where(seen, 0.0, LOWEST).astype(BF)
+    values_out[...] = values[...]
     node = lax.broadcasted_iota(jnp.int32, (128, tokens), 0)
-    onehot = jnp.where(node == leaf[...], 1.0, 0.0).astype(F32).T.astype(BF)
-    keys_wide = jnp.concatenate([keys[...], bias], axis=1)
-
+    onehot[...] = jnp.where(node == leaf[...], 1.0, 0.0).astype(F32).T.astype(BF)
+
+
+def attend_kernel(q, keys_wide, values, onehot, out):
+    tokens = q.shape[0]
     lane_t = lax.broadcasted_iota(jnp.int32, (tokens, 128), 1)
     stats = jnp.zeros((tokens, 128), F32)
     for g in range(GROUP):
         cols = pl.ds(g * HEAD_WIDTH, HEAD_WIDTH)
-        q_wide = jnp.concatenate([q[:, cols], onehot], axis=1)
-        scores = nt(q_wide, keys_wide)
+        q_wide = jnp.concatenate([q[:, cols], onehot[...]], axis=1)
+        scores = nt(q_wide, keys_wide[...])
         top = jnp.max(scores, axis=1, keepdims=True).astype(BF).astype(F32)
         weights = jnp.exp((scores - top) * SCALE)
         mass = jnp.sum(weights, axis=1, keepdims=True)
@@ -91,7 +95,9 @@
     out[:, GROUP * HEAD_WIDTH :] = stats.astype(BF)
 
 
-def project_kernel(core, parts, weight, own, other):
+def project_kernel(core, parts, weight_far, own, other, weight, sem):
+    copy = pltpu.make_async_copy(weight_far, weight, sem)
+    copy.start()
     sources = parts.shape[0]
     width = GROUP * HEAD_WIDTH
     stats = [parts[s, :, width:].astype(F32) for s in range(sources)]
@@ -117,6 +123,7 @@
     source = (row % 8) // 2 * 4 + half * 2 + row % 2
     pick = jnp.where(col == source, 1.0, 0.0).astype(BF)
     context = mm(pick, context).astype(BF)
+    copy.wait()
     result = mm(context, weight[...])
     own[...] = result[:8]
     other[...] = result[8:].astype(BF)
@@ -128,16 +135,12 @@
     return (g / (1.0 + jnp.exp(-g)) * u).astype(BF)
 
 
-def hidden_kernel(rows, gate, up, out):
-    out[...] = hidden_of(rows[...], gate[...], up[...])
-
-
 def mlp_kernel(rows, gate, up, down, out):
     out[...] = mm(hidden_of(rows[...], gate[...], up[...]), down[...]).astype(out.dtype)
 
 
-def down_kernel(hidden, down, out):
-    out[...] = mm(hidden[...], down[...]).astype(out.dtype)
+def mlp_after_kernel(rows, gate, up, down, earlier, out):
+    mlp_kernel(rows, gate, up, down, out)
 
 
 def move_z(value, k):
@@ -171,16 +174,22 @@
     shape = jax.ShapeDtypeStruct
 
     q = lax.all_to_all(jnp.broadcast_to(queries[None], (16, 16, 640)), "kv", 0, 0)
-    packed = call(
-        attend_kernel,
-        shape((256, 768), BF),
-        [SM, SM, SM, VM, VM, VM, VM],
+    keys_wide, values_in, onehot = call(
+        prepare_kernel,
+        [shape((slots, 256), BF), shape((slots, 128), BF), shape((256, 128), BF)],
+        [SM, SM, SM, VM, VM, VM],
         [pltpu.SMEM((16,), jnp.int32)],
-    )(node_lengths, parents, (kv * slots)[None], token_leaf[None, :], q.reshape(256, 640), keys, values)
+    )(node_lengths, parents, (kv * slots)[None], token_leaf[None, :], keys, values)
+    packed = call(attend_kernel, shape((256, 768), BF), [VM] * 4, limit=12 << 20)(
+        q.reshape(256, 640), keys_wide, values_in, onehot
+    )
     parts = lax.all_to_all(packed.reshape(16, 16, 768), "kv", 0, 0)
-    own, other = call(project_kernel, [shape((8, D), F32), shape((8, D), BF)], [SM, VM, VM])(
-        c[None], parts, out_weight
-    )
+    own, other = call(
+        project_kernel,
+        [shape((8, D), F32), shape((8, D), BF)],
+        [SM, VM, pltpu.HBM],
+        [pltpu.VMEM(out_weight.shape, BF), pltpu.SemaphoreType.DMA],
+    )(c[None], parts, out_weight)
 
     mine = (jnp.arange(8) // 2 == z)[:, None]
     act = jnp.where(mine, jnp.tile(activations, (4, 1)), 0).astype(F32)
@@ -198,15 +207,16 @@
 
     rows = lax.all_to_all(jnp.broadcast_to(normed[None], (16, 8, D)), "kv", 0, 0).reshape(128, D)
     rows_other = move_core(rows)
-    hidden = call(hidden_kernel, shape((128, 216), BF), [VM, VM, VM])(rows, gate_t, up_t)
-    y_other = call(mlp_kernel, shape((128, D), BF), [VM, VM, VM, VM])(rows_other, gate_t, up_t, down_weight)
-    back = move_core(y_other)
-    y_own = call(down_kernel, shape((128, D), F32), [VM, VM])(hidden, down_weight)
-    mixed = (y_own + back.astype(F32)).astype(BF).reshape(64, 2, D)
+    y_own = call(mlp_kernel, shape((128, D), F32), [VM] * 4, limit=12 << 20)(rows, gate_t, up_t, down_weight)
+    y_other = call(mlp_after_kernel, shape((128, D), BF), [VM] * 4 + [pl.ANY], limit=12 << 20)(
+        rows_other, gate_t, up_t, down_weight, y_own
+    )
+    mixed = (y_own + move_core(y_other).astype(F32)).astype(BF).reshape(64, 2, D)
+    keep = lax.dynamic_slice_in_dim(widened, z * 2, 2, 0)
+    mixed, keep = lax.optimization_barrier((mixed, keep))
     groups = [[i for i in range(128) if i % 2 == k] for k in range(2)]
     mixed = lax.all_to_all(mixed, ("kv", "tp"), 0, 0, axis_index_groups=groups)
-    final = lax.dynamic_slice_in_dim(widened, z * 2, 2, 0) + jnp.sum(mixed.astype(F32), axis=0)
-    return final.astype(BF)
+    return (keep + jnp.sum(mixed.astype(F32), axis=0)).astype(BF)
 
 
 def solution(mesh):

time: 121 us -> 120 us (level)
  blocking collectives: 22 us -> 50.9 us
  waiting for transfers between devices: 49.2 us -> 23 us
  starting transfers between devices: 24.3 us -> 17 us
  local copies, waits for them, and re-layouts: 6.97 us -> 11.5 us
  Pallas kernels: 15.3 us -> 11.7 us
  other arithmetic: 2.38 us -> 4.77 us
    all_to_all x0 -> x1, blocking collectives: none -> 28.8 us  [local(): mixed = lax.all_to_all(mixed, ('kv', 'tp'), 0, 0, axis_index_groups=groups)]
    all_to_all x1 -> x0, waiting for transfers between devices: 21.8 us -> none  [local(): mixed = lax.all_to_all(mixed, ('kv', 'tp'), 0, 0, axis_index_groups=groups)]
    all_to_all x1 -> x0, starting transfers between devices: 7.19 us -> none  [local(): mixed = lax.all_to_all(mixed, ('kv', 'tp'), 0, 0, axis_index_groups=groups)]
    all_to_all x1, waiting for transfers between devices: 9.16 us -> 4.29 us  [local(): lax.all_to_all(jnp.broadcast_to(queries[None], (16, 16, 640)), 'kv', 0, 0)]
    pallas_call x5, Pallas kernels: 15.3 us -> 11.7 us  [the longest x1 3.46 us: local(): call(attend_kernel, shape((256, 768), BF), [VM] * 4, limit=12 << 20)]
    unnamed x20 -> x22, local copies, waits for them, and re-layouts: 3.91 us -> 6.77 us
    convert_element_type x2, other arithmetic: 0.88 us -> 3.27 us  [the longest x1 2.64 us: local(): (y_own + move_core(y_other).astype(F32)).astype(BF).reshape(64, 2, D)]
    reshape x1, local copies, waits for them, and re-layouts: 1.38 us -> 3 us  [local(): (y_own + move_core(y_other).astype(F32)).astype(BF).reshape(64, 2, D)]
  transfers between devices with their start and end apart: 9 -> 8, of which waited for: 9 -> 8; matrix products, arithmetic and copies ran while one was open for 0% -> 0% of each run, Pallas kernels for 2% -> 3%
where the time goes in v3:
time: 120 us; the launch traced here: 119 us
  blocking collectives  50.9 us (42%)
  waiting for transfers between devices  23 us (19%)
  starting transfers between devices  17 us (14%)
  Pallas kernels  11.7 us (10%)
  local copies, waits for them, and re-layouts  11.5 us (10%)
  other arithmetic  4.77 us (4%)
    all_to_all x1, blocking collectives, local(): mixed = lax.all_to_all(mixed, ('kv', 'tp'), 0, 0, axis_index_groups=groups)  28.8 us
    all_to_all x1, blocking collectives, local(): lax.all_to_all(jnp.broadcast_to(normed[None], (16, 8, D)), 'kv', 0, 0)  22.1 us
    all_to_all x1, waiting for transfers between devices, local(): parts = lax.all_to_all(packed.reshape(16, 16, 768), 'kv', 0, 0)  8.99 us
    all_to_all x1, starting transfers between devices, local(): lax.all_to_all(jnp.broadcast_to(queries[None], (16, 16, 640)), 'kv', 0, 0)  7.12 us
    unnamed x22, local copies, waits for them, and re-layouts  6.77 us
    ppermute x3, starting transfers between devices, move_z(): return lax.ppermute(value, 'tp', pairs)  5.98 us
    ppermute x3, waiting for transfers between devices, move_core(): return lax.ppermute(value, 'tp', [(i, i ^ 1) for i in range(8)])  5.35 us
    ppermute x3, waiting for transfers between devices, move_z(): return lax.ppermute(value, 'tp', pairs)  4.34 us
  transfers between devices with their start and end apart: 8, of which 8 were waited for; matrix products, arithmetic and copies ran while one was open for 0% of the time, Pallas kernels for 3%

profile of v3, /device:TPU:0, one launch (start us, length us, event | category | flops | bytes accessed | tf_op | source)
XLA Modules:
  0.0 119.0 jit_solution(12964189481985786768)
XLA Ops:
  0.0 1.5 %broadcast_in_dim.37 = bf16[16,16,640]{2,1,0:T(8,128)(2,1)} broadcast(bf16[16,640]{1,0:T(8,128)(2,1)} %param.13), dimensions={1,2} | broadcast | bytes 348160 | tf_op jit(solution)/shard_map/broadcast_in_dim | solution.py:176
  1.5 7.1 %all-to-all-start = ((bf16[16,16,640]{2,1,0:T(8,128)(2,1)}), bf16[16,16,640]{2,1,0:T(8,128)(2,1)S(1)}, u32[]{:S(2)}, u32[]{:S(2)}) async-start(bf16[16,16,640]{2,1,0:T(8,128)(2,1)} %broadcast_in_dim.37), calls=%async_computation | async-start | bytes 655360 | tf_op jit(solution)/shard_map/all_to_all | solution.py:176
  8.6 0.0 copy-start.4
  8.6 0.9 copy-done.4
  9.6 0.0 copy-start.5
  9.6 0.9 copy-done.5
  10.5 0.0 copy-start.6
  10.5 0.7 copy-done.6
  11.2 0.0 copy-start.7
  11.2 0.7 copy-done.7
  11.8 0.0 copy-start.8
  11.9 0.7 copy-done.8
  12.5 1.0 shard_map.118
  13.5 0.0 copy-start.10
  13.5 4.3 %all-to-all-done = bf16[16,16,640]{2,1,0:T(8,128)(2,1)S(1)} async-done(((bf16[16,16,640]{2,1,0:T(8,128)(2,1)}), bf16[16,16,640]{2,1,0:T(8,128)(2,1)S(1)}, u32[]{:S(2)}, u32[]{:S(2)}) %all-to-all-start) | async-done | bytes 327712 | tf_op jit(solution)/shard_map/all_to_all | solution.py:176
  17.8 3.5 %shard_map.119 = bf16[256,768]{1,0:T(8,128)(2,1)} custom-call(bf16[256,640]{1,0:T(8,128)(2,1)S(1)} %bitcast.14, bf16[1024,256]{1,0:T(8,128)(2,1)S(1)} %get-tuple-element.12.keys_wide, bf16[1024,128]{1,0:T(8,128)(2,1)S(1)} %get-tuple-element.13.values, bf16[256,128]{1,0:T(8,128)(2,1)S(1)} %get-tuple-element.14.onehot), custom_call_target="tpu_custom_call" | custom-call | tf_op jit(solution)/shard_map/pallas_call | solution.py:183
  21.2 3.7 %all-to-all-start.1 = ((bf16[16,16,768]{2,1,0:T(8,128)(2,1)}), bf16[16,16,768]{2,1,0:T(8,128)(2,1)S(1)}, u32[]{:S(2)}, u32[]{:S(2)}) async-start(bf16[16,16,768]{2,1,0:T(8,128)(2,1)} %bitcast.4), calls=%async_computation.1 | async-start | bytes 786432 | tf_op jit(solution)/shard_map/all_to_all | solution.py:186
  24.9 0.0 copy-done.10
  25.0 9.0 %all-to-all-done.1.parts = bf16[16,16,768]{2,1,0:T(8,128)(2,1)S(1)} async-done(((bf16[16,16,768]{2,1,0:T(8,128)(2,1)}), bf16[16,16,768]{2,1,0:T(8,128)(2,1)S(1)}, u32[]{:S(2)}, u32[]{:S(2)}) %all-to-all-start.1) | async-done | bytes 393248 | tf_op jit(solution)/shard_map/all_to_all | solution.py:186
  34.0 0.0 copy-start.3
  34.0 2.9 %copy-done.3 = bf16[640,5120]{1,0:T(8,128)(2,1)S(1)} copy-done((bf16[640,5120]{1,0:T(8,128)(2,1)S(1)}, bf16[640,5120]{1,0:T(8,128)(2,1)}, u32[]{:S(2)}) %copy-start.3) | copy-done | bytes 6553624
  36.9 0.0 copy-start.9
  36.9 0.0 copy-start.2
  36.9 1.9 %shard_map.120 = (f32[8,5120]{1,0:T(8,128)S(1)}, bf16[8,5120]{1,0:T(8,128)(2,1)S(1)}) custom-call(s32[1]{0:T(128)} %bitcast.core, bf16[16,16,768]{2,1,0:T(8,128)(2,1)S(1)} %all-to-all-done.1.parts, bf16[640,5120]{1,0:T(8,128)(2,1)S(1)} %copy-done.3), custom_call_target="tpu_custom_call" | custom-call | tf_op jit(solution)/shard_map/pallas_call | solution.py:187
  38.9 0.1 collective-permute-start
  39.0 1.3 %collective-permute-done = bf16[8,5120]{1,0:T(8,128)(2,1)S(1)} collective-permute-done((bf16[8,5120]{1,0:T(8,128)(2,1)S(1)}, bf16[8,5120]{1,0:T(8,128)(2,1)S(1)}, u32[]{:S(2)}, u32[]{:S(2)}) %collective-permute-start) | collective-permute-done | bytes 81952 | tf_op jit(solution)/shard_map/ppermute | solution.py:152
  40.2 0.1 fusion.1
  40.3 4.0 %collective-permute-start.3 = (bf16[8,5120]{1,0:T(8,128)(2,1)S(1)}, bf16[8,5120]{1,0:T(8,128)(2,1)S(1)}, u32[]{:S(2)}, u32[]{:S(2)}) collective-permute-start(bf16[8,5120]{1,0:T(8,128)(2,1)S(1)} %fusion.1), channel_id=1, source_target_pairs={{0,4},{1,5},{2,6},{3,7},{4,0},{5,1},{6,2},{7,3},{8,12},{9,13},{10,... | collective-permute-start | bytes 245768 | tf_op jit(solution)/shard_map/ppermute | solution.py:148
  44.3 0.7 collective-permute-start.2
  45.0 1.3 %collective-permute-start.1 = (bf16[8,5120]{1,0:T(8,128)(2,1)S(1)}, bf16[8,5120]{1,0:T(8,128)(2,1)S(1)}, u32[]{:S(2)}, u32[]{:S(2)}) collective-permute-start(bf16[8,5120]{1,0:T(8,128)(2,1)S(1)} %fusion.1), channel_id=1, source_target_pairs={{0,2},{1,3},{2,4},{3,5},{4,6},{5,7},{6,0},{7,1},{8,10},{9,11},{10,... | collective-permute-start | bytes 245768 | tf_op jit(solution)/shard_map/ppermute | solution.py:148
  46.3 0.7 collective-permute-done.3
  47.0 2.5 %collective-permute-done.2 = bf16[8,5120]{1,0:T(8,128)(2,1)S(1)} collective-permute-done((bf16[8,5120]{1,0:T(8,128)(2,1)S(1)}, bf16[8,5120]{1,0:T(8,128)(2,1)S(1)}, u32[]{:S(2)}, u32[]{:S(2)}) %collective-permute-start.2) | collective-permute-done | bytes 81952 | tf_op jit(solution)/shard_map/ppermute | solution.py:148
  49.6 1.1 collective-permute-done.1
  50.6 0.0 copy-start.1
  50.6 0.2 multiply_reduce_fusion
  50.9 0.0 copy-done.9
  50.9 0.1 multiply_convert_fusion
  51.0 0.1 broadcast_in_dim.42
  51.1 0.0 copy-start
  51.1 22.1 %all_to_all.20 = bf16[16,8,5120]{2,1,0:T(8,128)(2,1)S(1)} all-to-all(bf16[16,8,5120]{2,1,0:T(8,128)(2,1)S(1)} %broadcast_in_dim.42), channel_id=1, replica_groups=mesh['kv'=16,'tp'=8] {'kv'}, dimensions={0} | all-to-all | bytes 2621440 | tf_op jit(solution)/shard_map/all_to_all | solution.py:208
  73.3 0.0 collective-permute-start.4
  73.3 0.0 copy-done.2
  73.3 0.0 copy-done.1
  73.3 0.0 copy-done
  73.3 2.1 %shard_map.121.earlier = f32[128,5120]{1,0:T(8,128)S(1)} custom-call(bf16[128,5120]{1,0:T(8,128)(2,1)S(1)} %bitcast.13, bf16[216,5120]{1,0:T(8,128)(2,1)S(1)} %bitcast.8, bf16[216,5120]{1,0:T(8,128)(2,1)S(1)} %bitcast.10, bf16[216,5120]{1,0:T(8,128)(2,1)S(1)} %copy-done.2), custom_call_target="tpu_custom_call" | custom-call | tf_op jit(solution)/shard_map/pallas_call | solution.py:210
  75.4 0.9 collective-permute-done.4.rows
  76.3 3.2 %shard_map.122 = bf16[128,5120]{1,0:T(8,128)(2,1)} custom-call(bf16[128,5120]{1,0:T(8,128)(2,1)S(1)} %collective-permute-done.4.rows, bf16[216,5120]{1,0:T(8,128)(2,1)S(1)} %bitcast.9, bf16[216,5120]{1,0:T(8,128)(2,1)S(1)} %bitcast.11, bf16[216,5120]{1,0:T(8,128)(2,1)S(1)} %copy-done.2, f32[128,5120]{1,0:T(8,128)S(1)} %shard_map.121.earlier), custom_call_target="tpu_custom_call" | custom-call | tf_op jit(solution)/shard_map/pallas_call | solution.py:211
  79.5 0.1 collective-permute-start.5
  79.7 3.2 %collective-permute-done.5 = bf16[128,5120]{1,0:T(8,128)(2,1)} collective-permute-done((bf16[128,5120]{1,0:T(8,128)(2,1)}, bf16[128,5120]{1,0:T(8,128)(2,1)}, u32[]{:S(2)}, u32[]{:S(2)}) %collective-permute-start.5) | collective-permute-done | bytes 1310752 | tf_op jit(solution)/shard_map/ppermute | solution.py:152
  82.9 2.6 %add_convert_fusion = bf16[128,5120]{1,0:T(8,128)(2,1)} fusion(f32[128,5120]{1,0:T(8,128)S(1)} %shard_map.121.earlier, bf16[128,5120]{1,0:T(8,128)(2,1)} %collective-permute-done.5), kind=kLoop, calls=%fused_computation.1 | loop fusion | flops 1966080 | bytes 5242880 | tf_op jit(solution)/shard_map/convert_element_type | solution.py:214
  85.5 3.0 %reshape.44 = bf16[64,2,5120]{2,1,0:T(2,128)(2,1)S(1)} reshape(bf16[128,5120]{1,0:T(8,128)(2,1)} %add_convert_fusion) | data formatting | bytes 2621440 | tf_op jit(solution)/shard_map/reshape | solution.py:214
  88.5 28.8 %all_to_all.21 = bf16[64,2,5120]{2,1,0:T(2,128)(2,1)S(1)} all-to-all(bf16[64,2,5120]{2,1,0:T(2,128)(2,1)S(1)} %reshape.44), channel_id=1, replica_groups={{0,2,4,6,8,10,12,14,16,18,20,22,24,26,28,30,32,34,36,38,40,42,44,46,48,..., dimensions={0} | all-to-all | bytes 2621440 | tf_op jit(solution)/shard_map/all_to_all | solution.py:218
  117.3 1.1 convert_reduce_fusion
  118.4 0.6 add_convert_fusion.2
  (5 shorter events, 0.1 us)
Async XLA Ops:
  1.5 16.3 %all-to-all-start = ((bf16[16,16,640]{2,1,0:T(8,128)(2,1)}), bf16[16,16,640]{2,1,0:T(8,128)(2,1)S(1)}, u32[]{:S(2)}, u32[]{:S(2)}) async-start(bf16[16,16,640]{2,1,0:T(8,128)(2,1)} %broadcast_in_dim.37), calls=%async_computation | async-start | bytes 655360 | tf_op jit(solution)/shard_map/all_to_all | solution.py:176
  8.6 1.0 copy-start.4
  9.6 0.9 copy-start.5
  10.5 0.7 copy-start.6
  11.2 0.7 copy-start.7
  11.8 0.7 copy-start.8
  13.5 11.5 %copy-start.10 = (bf16[2,5120]{1,0:T(2,128)(2,1)S(1)}, bf16[2,5120]{1,0:T(2,128)(2,1)}, u32[]{:S(2)}) copy-start(bf16[2,5120]{1,0:T(2,128)(2,1)} %param.12) | copy-start | bytes 61444
  21.2 12.8 %all-to-all-start.1 = ((bf16[16,16,768]{2,1,0:T(8,128)(2,1)}), bf16[16,16,768]{2,1,0:T(8,128)(2,1)S(1)}, u32[]{:S(2)}, u32[]{:S(2)}) async-start(bf16[16,16,768]{2,1,0:T(8,128)(2,1)} %bitcast.4), calls=%async_computation.1 | async-start | bytes 786432 | tf_op jit(solution)/shard_map/all_to_all | solution.py:186
  34.0 2.9 %copy-start.3 = (bf16[640,5120]{1,0:T(8,128)(2,1)S(1)}, bf16[640,5120]{1,0:T(8,128)(2,1)}, u32[]{:S(2)}) copy-start(bf16[640,5120]{1,0:T(8,128)(2,1)} %weight_far.1) | copy-start | bytes 19660804
  36.9 14.0 %copy-start.9 = (f32[5120]{0:T(1024)S(1)}, f32[5120]{0:T(1024)}, u32[]{:S(2)}) copy-start(f32[5120]{0:T(1024)} %param.20) | copy-start | bytes 61444
  36.9 36.4 %copy-start.2 = (bf16[216,5120]{1,0:T(8,128)(2,1)S(1)}, bf16[216,5120]{1,0:T(8,128)(2,1)}, u32[]{:S(2)}) copy-start(bf16[216,5120]{1,0:T(8,128)(2,1)} %down.3) | copy-start | bytes 6635524
  38.9 1.4 %collective-permute-start = (bf16[8,5120]{1,0:T(8,128)(2,1)S(1)}, bf16[8,5120]{1,0:T(8,128)(2,1)S(1)}, u32[]{:S(2)}, u32[]{:S(2)}) collective-permute-start(bf16[8,5120]{1,0:T(8,128)(2,1)S(1)} %get-tuple-element.16), channel_id=1, source_target_pairs={{0,1},{1,0},{2,3},{3,2},{4,5},{5,4},{6,7},{7,6},{8,9},{9,8},{10,11... | collective-permute-start | bytes 245768 | tf_op jit(solution)/shard_map/ppermute | solution.py:152
  40.3 6.7 %collective-permute-start.3 = (bf16[8,5120]{1,0:T(8,128)(2,1)S(1)}, bf16[8,5120]{1,0:T(8,128)(2,1)S(1)}, u32[]{:S(2)}, u32[]{:S(2)}) collective-permute-start(bf16[8,5120]{1,0:T(8,128)(2,1)S(1)} %fusion.1), channel_id=1, source_target_pairs={{0,4},{1,5},{2,6},{3,7},{4,0},{5,1},{6,2},{7,3},{8,12},{9,13},{10,... | collective-permute-start | bytes 245768 | tf_op jit(solution)/shard_map/ppermute | solution.py:148
  44.3 5.3 %collective-permute-start.2 = (bf16[8,5120]{1,0:T(8,128)(2,1)S(1)}, bf16[8,5120]{1,0:T(8,128)(2,1)S(1)}, u32[]{:S(2)}, u32[]{:S(2)}) collective-permute-start(bf16[8,5120]{1,0:T(8,128)(2,1)S(1)} %fusion.1), channel_id=1, source_target_pairs={{0,6},{1,7},{2,0},{3,1},{4,2},{5,3},{6,4},{7,5},{8,14},{9,15},{10,... | collective-permute-start | bytes 245768 | tf_op jit(solution)/shard_map/ppermute | solution.py:148
  45.0 5.7 %collective-permute-start.1 = (bf16[8,5120]{1,0:T(8,128)(2,1)S(1)}, bf16[8,5120]{1,0:T(8,128)(2,1)S(1)}, u32[]{:S(2)}, u32[]{:S(2)}) collective-permute-start(bf16[8,5120]{1,0:T(8,128)(2,1)S(1)} %fusion.1), channel_id=1, source_target_pairs={{0,2},{1,3},{2,4},{3,5},{4,6},{5,7},{6,0},{7,1},{8,10},{9,11},{10,... | collective-permute-start | bytes 245768 | tf_op jit(solution)/shard_map/ppermute | solution.py:148
  50.6 22.6 %copy-start.1 = (bf16[5120,216]{0,1:T(8,128)(2,1)S(1)}, bf16[5120,216]{0,1:T(8,128)(2,1)}, u32[]{:S(2)}) copy-start(bf16[5120,216]{0,1:T(8,128)(2,1)} %param.22) | copy-start | bytes 6635524
  51.1 22.2 %copy-start = (bf16[5120,216]{0,1:T(8,128)(2,1)S(1)}, bf16[5120,216]{0,1:T(8,128)(2,1)}, u32[]{:S(2)}) copy-start(bf16[5120,216]{0,1:T(8,128)(2,1)} %param.21) | copy-start | bytes 6635524
  73.3 3.0 %collective-permute-start.4 = (bf16[128,5120]{1,0:T(8,128)(2,1)S(1)}, bf16[128,5120]{1,0:T(8,128)(2,1)S(1)}, u32[]{:S(2)}, u32[]{:S(2)}) collective-permute-start(bf16[128,5120]{1,0:T(8,128)(2,1)S(1)} %bitcast.12), channel_id=1, source_target_pairs={{0,1},{1,0},{2,3},{3,2},{4,5},{5,4},{6,7},{7,6},{8,9},{9,8},{10,11... | collective-permute-start | bytes 3932168 | tf_op jit(solution)/shard_map/ppermute | solution.py:152
  79.5 3.4 %collective-permute-start.5 = (bf16[128,5120]{1,0:T(8,128)(2,1)}, bf16[128,5120]{1,0:T(8,128)(2,1)}, u32[]{:S(2)}, u32[]{:S(2)}) collective-permute-start(bf16[128,5120]{1,0:T(8,128)(2,1)} %shard_map.122), channel_id=1, source_target_pairs={{0,1},{1,0},{2,3},{3,2},{4,5},{5,4},{6,7},{7,6},{8,9},{9,8},{10,11... | collective-permute-start | bytes 3932168 | tf_op jit(solution)/shard_map/ppermute | solution.py:152

commit v4 on v3

--- a/solution.py
+++ b/solution.py
@@ -44,7 +44,7 @@
     return lax.dot_general(a, b, (((1,), (0,)), ((), ())), preferred_element_type=F32)
 
 
-def prepare_kernel(lengths, parents, first, leaf, keys, values, keys_wide, values_out, onehot, starts):
+def prepare_kernel(lengths, parents, kv, leaf, keys, values, keys_wide, values_out, onehot, starts):
     nodes = lengths.shape[0]
     slots = keys.shape[0]
     tokens = leaf.shape[1]
@@ -63,7 +63,7 @@
         own_hi = jnp.where(here, lo + lengths[n], own_hi)
         up_lo = jnp.where(here, starts[up], up_lo)
         up_hi = jnp.where(here, starts[up] + lengths[up], up_hi)
-    slot = first[0] + lax.broadcasted_iota(jnp.int32, (slots, 128), 0)
+    slot = kv[0] * slots + lax.broadcasted_iota(jnp.int32, (slots, 128), 0)
     seen = (
         (slot < lengths[0])
         | ((slot >= own_lo) & (slot < own_hi))
@@ -95,9 +95,10 @@
     out[:, GROUP * HEAD_WIDTH :] = stats.astype(BF)
 
 
-def project_kernel(core, parts, weight_far, own, other, weight, sem):
+def project_kernel(tp, parts, weight_far, activations, own, other, weight, sem):
     copy = pltpu.make_async_copy(weight_far, weight, sem)
     copy.start()
+    z, core = tp[0] >> 1, tp[0] & 1
     sources = parts.shape[0]
     width = GROUP * HEAD_WIDTH
     stats = [parts[s, :, width:].astype(F32) for s in range(sources)]
@@ -119,13 +120,16 @@
     context = jnp.concatenate(heads, axis=1)
     row = lax.broadcasted_iota(jnp.int32, (16, 16), 0)
     col = lax.broadcasted_iota(jnp.int32, (16, 16), 1)
-    half = jnp.where(row < 8, core[0], 1 - core[0])
+    half = jnp.where(row < 8, core, 1 - core)
     source = (row % 8) // 2 * 4 + half * 2 + row % 2
     pick = jnp.where(col == source, 1.0, 0.0).astype(BF)
     context = mm(pick, context).astype(BF)
     copy.wait()
     result = mm(context, weight[...])
-    own[...] = result[:8]
+    row = lax.broadcasted_iota(jnp.int32, (8, 2), 0)
+    col = lax.broadcasted_iota(jnp.int32, (8, 2), 1)
+    place = jnp.where(row == z * 2 + col, 1.0, 0.0).astype(BF)
+    own[...] = result[:8] + mm(place, activations[...])
     other[...] = result[8:].astype(BF)
 
 
@@ -135,12 +139,29 @@
     return (g / (1.0 + jnp.exp(-g)) * u).astype(BF)
 
 
-def mlp_kernel(rows, gate, up, down, out):
-    out[...] = mm(hidden_of(rows[...], gate[...], up[...]), down[...]).astype(out.dtype)
-
-
-def mlp_after_kernel(rows, gate, up, down, earlier, out):
-    mlp_kernel(rows, gate, up, down, out)
+def ordered(hidden, tp):
+    n = hidden.shape[0]
+    row = lax.broadcasted_iota(jnp.int32, (n, n), 0)
+    col = lax.broadcasted_iota(jnp.int32, (n, n), 1)
+    z = tp[0] >> 1
+    source = (row % 32) // 2 * 8 + (z + 4 - row // 32) % 4 * 2 + row % 2
+    return mm(jnp.where(col == source, 1.0, 0.0).astype(BF), hidden).astype(BF)
+
+
+def hidden_kernel(tp, rows, gate, up, out):
+    out[...] = ordered(hidden_of(rows[...], gate[...], up[...]), tp)
+
+
+def mlp_kernel(tp, rows, gate, up, down, earlier, out):
+    hidden = ordered(hidden_of(rows[...], gate[...], up[...]), tp)
+    out[...] = mm(hidden, down[...]).astype(BF)
+
+
+def down_kernel(hidden, down, back, own, *sent):
+    result = mm(hidden[...], down[...]) + back[...].astype(F32)
+    own[...] = result[:32]
+    for k, ref in enumerate(sent):
+        ref[...] = result[32 * (k + 1) : 32 * (k + 2)].astype(BF)
 
 
 def move_z(value, k):
@@ -166,20 +187,19 @@
     up_weight,
     down_weight,
 ):
-    kv = lax.axis_index("kv")
-    tp = lax.axis_index("tp")
-    z, c = tp // 2, tp % 2
-    slots = keys.shape[0]
+    kv = lax.axis_index("kv")[None]
+    tp = lax.axis_index("tp")[None]
     gate_t, up_t = gate_weight.T, up_weight.T
     shape = jax.ShapeDtypeStruct
+    queries, kv, tp = lax.optimization_barrier((queries, kv, tp))
 
     q = lax.all_to_all(jnp.broadcast_to(queries[None], (16, 16, 640)), "kv", 0, 0)
     keys_wide, values_in, onehot = call(
         prepare_kernel,
-        [shape((slots, 256), BF), shape((slots, 128), BF), shape((256, 128), BF)],
+        [shape((keys.shape[0], 256), BF), shape(values.shape, BF), shape((256, 128), BF)],
         [SM, SM, SM, VM, VM, VM],
         [pltpu.SMEM((16,), jnp.int32)],
-    )(node_lengths, parents, (kv * slots)[None], token_leaf[None, :], keys, values)
+    )(node_lengths, parents, kv, token_leaf[None, :], keys, values)
     packed = call(attend_kernel, shape((256, 768), BF), [VM] * 4, limit=12 << 20)(
         q.reshape(256, 640), keys_wide, values_in, onehot
     )
@@ -187,13 +207,11 @@
     own, other = call(
         project_kernel,
         [shape((8, D), F32), shape((8, D), BF)],
-        [SM, VM, pltpu.HBM],
+        [SM, VM, pl.ANY, VM],
         [pltpu.VMEM(out_weight.shape, BF), pltpu.SemaphoreType.DMA],
-    )(c[None], parts, out_weight)
-
-    mine = (jnp.arange(8) // 2 == z)[:, None]
-    act = jnp.where(mine, jnp.tile(activations, (4, 1)), 0).astype(F32)
-    attended = own + move_core(other).astype(F32) + act
+        limit=56 << 20,
+    )(tp, parts, out_weight, activations)
+    attended = own + move_core(other).astype(F32)
     sent = attended.astype(BF)
     for part in [move_z(sent, k) for k in (1, 3, 2)]:
         attended = attended + part.astype(F32)
@@ -207,15 +225,19 @@
 
     rows = lax.all_to_all(jnp.broadcast_to(normed[None], (16, 8, D)), "kv", 0, 0).reshape(128, D)
     rows_other = move_core(rows)
-    y_own = call(mlp_kernel, shape((128, D), F32), [VM] * 4, limit=12 << 20)(rows, gate_t, up_t, down_weight)
-    y_other = call(mlp_after_kernel, shape((128, D), BF), [VM] * 4 + [pl.ANY], limit=12 << 20)(
-        rows_other, gate_t, up_t, down_weight, y_own
-    )
-    mixed = (y_own + move_core(y_other).astype(F32)).astype(BF).reshape(64, 2, D)
-    keep = lax.dynamic_slice_in_dim(widened, z * 2, 2, 0)
-    mixed, keep = lax.optimization_barrier((mixed, keep))
-    groups = [[i for i in range(128) if i % 2 == k] for k in range(2)]
-    mixed = lax.all_to_all(mixed, ("kv", "tp"), 0, 0, axis_index_groups=groups)
+    hidden = call(hidden_kernel, shape((128, 216), BF), [SM] + [VM] * 3)(tp, rows, gate_t, up_t)
+    y_other = call(mlp_kernel, shape((128, D), BF), [SM] + [VM] * 4 + [pl.ANY])(
+        tp, rows_other, gate_t, up_t, down_weight, hidden
+    )
+    block = shape((32, D), BF)
+    mixed, *sent = call(down_kernel, [shape((32, D), F32), block, block, block], [VM] * 3)(
+        hidden, down_weight, move_core(y_other)
+    )
+    for part in [move_z(sent[k - 1], -k) for k in (1, 3, 2)]:
+        mixed = mixed + part.astype(F32)
+    keep = lax.dynamic_slice_in_dim(widened, (tp[0] >> 1) * 2, 2, 0)
+    mixed, keep = lax.optimization_barrier((mixed.astype(BF).reshape(16, 2, D), keep))
+    mixed = lax.all_to_all(mixed, "kv", 0, 0)
     return (keep + jnp.sum(mixed.astype(F32), axis=0)).astype(BF)
 
 

time: 120 us -> 122 us (1.017)
  waiting for transfers between devices: 23 us -> 29.6 us
  blocking collectives: 50.9 us -> 47.1 us
  local copies, waits for them, and re-layouts: 11.5 us -> 8.06 us
  Pallas kernels: 11.7 us -> 14.9 us
  other arithmetic: 4.77 us -> 3.31 us
    ppermute x3 -> x6, waiting for transfers between devices: 4.34 us -> 19.5 us  [move_z(): return lax.ppermute(value, 'tp', pairs)]
    all_to_all x1 -> x0, waiting for transfers between devices: 8.99 us -> none  [local(): parts = lax.all_to_all(packed.reshape(16, 16, 768), 'kv', 0, 0)]
    ppermute x3 -> x6, starting transfers between devices: 5.98 us -> 10.7 us  [move_z(): return lax.ppermute(value, 'tp', pairs)]
    all_to_all x1 -> x2, blocking collectives: 28.8 us -> 25.1 us  [the longest x1 12.7 us: local(): parts = lax.all_to_all(packed.reshape(16, 16, 768), 'kv', 0, 0)]
    all_to_all x1 -> x0, starting transfers between devices: 3.67 us -> none  [local(): parts = lax.all_to_all(packed.reshape(16, 16, 768), 'kv', 0, 0)]
    pallas_call x1, Pallas kernels: 1.95 us -> 5.56 us  [local(): call(project_kernel, [shape((8, D), F32), shape((8, D), BF)], [SM, VM, pl...]
    reshape x1, local copies, waits for them, and re-layouts: 3 us -> 0.12 us  [local(): mixed.astype(BF).reshape(16, 2, D)]
    convert_element_type x1, other arithmetic: 2.64 us -> 0.14 us  [local(): mixed.astype(BF).reshape(16, 2, D)]
  transfers between devices with their start and end apart: 8 -> 10, of which waited for: 8 -> 9; matrix products, arithmetic and copies ran while one was open for 0% -> 1% of each run, Pallas kernels for 3% -> 2%
where the time goes in v4:
time: 122 us; the launch traced here: 121 us
  blocking collectives  47.1 us (39%)
  waiting for transfers between devices  29.6 us (24%)
  starting transfers between devices  18 us (15%)
  Pallas kernels  14.9 us (12%)
  local copies, waits for them, and re-layouts  8.06 us (7%)
  other arithmetic  3.31 us (3%)
    all_to_all x1, blocking collectives, local(): lax.all_to_all(jnp.broadcast_to(normed[None], (16, 8, D)), 'kv', 0, 0)  22 us
    ppermute x6, waiting for transfers between devices, move_z(): return lax.ppermute(value, 'tp', pairs)  19.5 us
    all_to_all x1, blocking collectives, local(): parts = lax.all_to_all(packed.reshape(16, 16, 768), 'kv', 0, 0)  12.7 us
    all_to_all x1, blocking collectives, local(): mixed = lax.all_to_all(mixed, 'kv', 0, 0)  12.4 us
    ppermute x6, starting transfers between devices, move_z(): return lax.ppermute(value, 'tp', pairs)  10.7 us
    all_to_all x1, starting transfers between devices, local(): lax.all_to_all(jnp.broadcast_to(queries[None], (16, 16, 640)), 'kv', 0, 0)  7.12 us
    ppermute x3, waiting for transfers between devices, move_core(): return lax.ppermute(value, 'tp', [(i, i ^ 1) for i in range(8)])  5.77 us
    pallas_call x1, Pallas kernels, local(): call(project_kernel, [shape((8, D), F32), shape((8, D), BF)], [SM, VM, pl...  5.56 us
  transfers between devices with their start and end apart: 10, of which 9 were waited for; matrix products, arithmetic and copies ran while one was open for 1% of the time, Pallas kernels for 2%

profile of v4, /device:TPU:0, one launch (start us, length us, event | category | flops | bytes accessed | tf_op | source)
XLA Modules:
  0.0 121.2 jit_solution(17491043058363089298)
XLA Ops:
  0.0 1.5 %broadcast_in_dim.12 = bf16[16,16,640]{2,1,0:T(8,128)(2,1)} broadcast(bf16[16,640]{1,0:T(8,128)(2,1)} %param.13), dimensions={1,2} | broadcast | bytes 348160 | tf_op jit(solution)/shard_map/broadcast_in_dim | solution.py:196
  1.5 7.1 %all-to-all-start = ((bf16[16,16,640]{2,1,0:T(8,128)(2,1)}), bf16[16,16,640]{2,1,0:T(8,128)(2,1)S(1)}, u32[]{:S(2)}, u32[]{:S(2)}) async-start(bf16[16,16,640]{2,1,0:T(8,128)(2,1)} %broadcast_in_dim.12), calls=%async_computation | async-start | bytes 655360 | tf_op jit(solution)/shard_map/all_to_all | solution.py:196
  8.6 0.0 copy-start.5
  8.6 0.9 copy-done.5
  9.6 0.0 copy-start.6
  9.6 0.9 copy-done.6
  10.5 0.0 copy-start.7
  10.5 0.7 copy-done.7
  11.2 0.0 copy-start.8
  11.2 0.7 copy-done.8
  11.9 0.0 copy-start.9
  11.9 0.7 copy-done.9
  12.5 1.0 shard_map.118
  13.5 4.3 %all-to-all-done = bf16[16,16,640]{2,1,0:T(8,128)(2,1)S(1)} async-done(((bf16[16,16,640]{2,1,0:T(8,128)(2,1)}), bf16[16,16,640]{2,1,0:T(8,128)(2,1)S(1)}, u32[]{:S(2)}, u32[]{:S(2)}) %all-to-all-start) | async-done | bytes 327712 | tf_op jit(solution)/shard_map/all_to_all | solution.py:196
  17.8 2.7 %shard_map.119 = bf16[256,768]{1,0:T(8,128)(2,1)S(1)} custom-call(bf16[256,640]{1,0:T(8,128)(2,1)S(1)} %bitcast.16, bf16[1024,256]{1,0:T(8,128)(2,1)S(1)} %get-tuple-element.22.keys_wide, bf16[1024,128]{1,0:T(8,128)(2,1)S(1)} %get-tuple-element.23.values, bf16[256,128]{1,0:T(8,128)(2,1)S(1)} %get-tuple-element.24.onehot), custom_call_target="tpu_custom_call" | custom-call | tf_op jit(solution)/shard_map/pallas_call | solution.py:203
  20.5 12.7 %all_to_all.20.parts = bf16[16,16,768]{2,1,0:T(8,128)(2,1)} all-to-all(bf16[16,16,768]{2,1,0:T(8,128)(2,1)S(1)} %bitcast.15), channel_id=1, replica_groups=mesh['kv'=16,'tp'=8] {'kv'}, dimensions={0} | all-to-all | bytes 786432 | tf_op jit(solution)/shard_map/all_to_all | solution.py:206
  33.2 0.0 copy-start.11
  33.2 5.6 %shard_map.120 = (f32[8,5120]{1,0:T(8,128)}, bf16[8,5120]{1,0:T(8,128)(2,1)}) custom-call(s32[1]{0:T(128)} %bitcast.1.tp, bf16[16,16,768]{2,1,0:T(8,128)(2,1)} %all_to_all.20.parts, bf16[640,5120]{1,0:T(8,128)(2,1)} %weight_far.1, bf16[2,5120]{1,0:T(2,128)(2,1)} %activations.1), custom_call_target="tpu_custom_call" | custom-call | tf_op jit(solution)/shard_map/pallas_call | solution.py:207
  38.8 0.1 collective-permute-start
  38.9 1.5 %collective-permute-done = bf16[8,5120]{1,0:T(8,128)(2,1)S(1)} collective-permute-done((bf16[8,5120]{1,0:T(8,128)(2,1)}, bf16[8,5120]{1,0:T(8,128)(2,1)S(1)}, u32[]{:S(2)}, u32[]{:S(2)}) %collective-permute-start) | collective-permute-done | bytes 81952 | tf_op jit(solution)/shard_map/ppermute | solution.py:173
  40.3 0.9 fusion
  41.3 4.0 %collective-permute-start.3 = (bf16[8,5120]{1,0:T(8,128)(2,1)S(1)}, bf16[8,5120]{1,0:T(8,128)(2,1)S(1)}, u32[]{:S(2)}, u32[]{:S(2)}) collective-permute-start(bf16[8,5120]{1,0:T(8,128)(2,1)S(1)} %fusion), channel_id=1, source_target_pairs={{0,4},{1,5},{2,6},{3,7},{4,0},{5,1},{6,2},{7,3},{8,12},{9,13},{10,... | collective-permute-start | bytes 245768 | tf_op jit(solution)/shard_map/ppermute | solution.py:169
  45.2 0.7 collective-permute-start.2
  46.0 1.3 %collective-permute-start.1 = (bf16[8,5120]{1,0:T(8,128)(2,1)S(1)}, bf16[8,5120]{1,0:T(8,128)(2,1)S(1)}, u32[]{:S(2)}, u32[]{:S(2)}) collective-permute-start(bf16[8,5120]{1,0:T(8,128)(2,1)S(1)} %fusion), channel_id=1, source_target_pairs={{0,2},{1,3},{2,4},{3,5},{4,6},{5,7},{6,0},{7,1},{8,10},{9,11},{10,... | collective-permute-start | bytes 245768 | tf_op jit(solution)/shard_map/ppermute | solution.py:169
  47.3 0.7 collective-permute-done.3
  48.0 2.5 %collective-permute-done.2 = bf16[8,5120]{1,0:T(8,128)(2,1)S(1)} collective-permute-done((bf16[8,5120]{1,0:T(8,128)(2,1)S(1)}, bf16[8,5120]{1,0:T(8,128)(2,1)S(1)}, u32[]{:S(2)}, u32[]{:S(2)}) %collective-permute-start.2) | collective-permute-done | bytes 81952 | tf_op jit(solution)/shard_map/ppermute | solution.py:169
  50.5 1.1 collective-permute-done.1
  51.6 0.0 copy-start.1
  51.6 1.2 %multiply_reduce_fusion = (f32[8]{0:T(128)S(1)}, f32[8,5120]{1,0:T(8,128)S(1)}) fusion(bf16[8,5120]{1,0:T(8,128)(2,1)S(1)} %collective-permute-done.3, bf16[8,5120]{1,0:T(8,128)(2,1)S(1)} %collective-permute-done.2, bf16[8,5120]{1,0:T(8,128)(2,1)S(1)} %collective-permute-done.1, f32[8,5120]{1,0:T(8,128)} %get-tuple-element.25, ...), kind=kLoop, calls=%fused_computation.3 | loop fusion | flops 491512 | bytes 655392 | tf_op jit(solution)/shard_map/reduce_sum | solution.py:222
  52.8 0.0 copy-start.10
  52.9 0.6 copy-done.10
  53.5 0.0 copy-done.11
  53.5 0.1 multiply_convert_fusion
  53.6 0.1 broadcast_in_dim.27
  53.7 0.0 copy-start
  53.7 22.0 %all_to_all.21 = bf16[16,8,5120]{2,1,0:T(8,128)(2,1)S(1)} all-to-all(bf16[16,8,5120]{2,1,0:T(8,128)(2,1)S(1)} %broadcast_in_dim.27), channel_id=1, replica_groups=mesh['kv'=16,'tp'=8] {'kv'}, dimensions={0} | all-to-all | bytes 2621440 | tf_op jit(solution)/shard_map/all_to_all | solution.py:226
  75.7 0.0 collective-permute-start.4
  75.7 0.0 copy-done.1
  75.7 0.0 copy-done
  75.8 0.0 copy-start.2
  75.8 1.8 %shard_map.121.earlier.hidden = bf16[128,216]{1,0:T(8,128)(2,1)S(1)} custom-call(s32[1]{0:T(128)} %bitcast.1.tp, bf16[128,5120]{1,0:T(8,128)(2,1)S(1)} %bitcast.14, bf16[216,5120]{1,0:T(8,128)(2,1)S(1)} %bitcast.9, bf16[216,5120]{1,0:T(8,128)(2,1)S(1)} %bitcast.11), custom_call_target="tpu_custom_call" | custom-call | tf_op jit(solution)/shard_map/pallas_call | solution.py:228
  77.6 0.0 copy-start.3
  77.6 1.2 collective-permute-done.4.rows
  78.8 0.0 copy-done.2
  78.8 3.4 %shard_map.122 = bf16[128,5120]{1,0:T(8,128)(2,1)} custom-call(s32[1]{0:T(128)} %bitcast.1.tp, bf16[128,5120]{1,0:T(8,128)(2,1)S(1)} %collective-permute-done.4.rows, bf16[216,5120]{1,0:T(8,128)(2,1)S(1)} %bitcast.10, bf16[216,5120]{1,0:T(8,128)(2,1)S(1)} %bitcast.12, bf16[216,5120]{1,0:T(8,128)(2,1)S(1)} %copy-done.2, ...), custom_call_target="tpu_custom_call" | custom-call | tf_op jit(solution)/shard_map/pallas_call | solution.py:229
  82.2 0.0 copy-done.3
  82.2 0.1 collective-permute-start.5
  82.3 3.1 %collective-permute-done.5.back = bf16[128,5120]{1,0:T(8,128)(2,1)S(1)} collective-permute-done((bf16[128,5120]{1,0:T(8,128)(2,1)}, bf16[128,5120]{1,0:T(8,128)(2,1)S(1)}, u32[]{:S(2)}, u32[]{:S(2)}) %collective-permute-start.5) | collective-permute-done | bytes 1310752 | tf_op jit(solution)/shard_map/ppermute | solution.py:173
  85.4 0.0 copy-start.4
  85.4 0.8 copy-done.4
  86.3 0.5 shard_map.123
  86.8 3.2 %collective-permute-start.6 = (bf16[32,5120]{1,0:T(8,128)(2,1)S(1)}, bf16[32,5120]{1,0:T(8,128)(2,1)S(1)}, u32[]{:S(2)}, u32[]{:S(2)}) collective-permute-start(bf16[32,5120]{1,0:T(8,128)(2,1)S(1)} %get-tuple-element.28), channel_id=1, source_target_pairs={{0,6},{1,7},{2,0},{3,1},{4,2},{5,3},{6,4},{7,5},{8,14},{9,15},{10,... | collective-permute-start | bytes 983048 | tf_op jit(solution)/shard_map/ppermute | solution.py:169
  90.0 0.0 collective-permute-start.7
  90.0 1.5 %collective-permute-start.8 = (bf16[32,5120]{1,0:T(8,128)(2,1)S(1)}, bf16[32,5120]{1,0:T(8,128)(2,1)S(1)}, u32[]{:S(2)}, u32[]{:S(2)}) collective-permute-start(bf16[32,5120]{1,0:T(8,128)(2,1)S(1)} %get-tuple-element.30), channel_id=1, source_target_pairs={{0,4},{1,5},{2,6},{3,7},{4,0},{5,1},{6,2},{7,3},{8,12},{9,13},{10,... | collective-permute-start | bytes 983048 | tf_op jit(solution)/shard_map/ppermute | solution.py:169
  91.5 0.9 constant_dynamic-slice_fusion
  92.4 11.8 %collective-permute-done.6 = bf16[32,5120]{1,0:T(8,128)(2,1)S(1)} collective-permute-done((bf16[32,5120]{1,0:T(8,128)(2,1)S(1)}, bf16[32,5120]{1,0:T(8,128)(2,1)S(1)}, u32[]{:S(2)}, u32[]{:S(2)}) %collective-permute-start.6) | collective-permute-done | bytes 327712 | tf_op jit(solution)/shard_map/ppermute | solution.py:169
  104.2 3.4 %collective-permute-done.7 = bf16[32,5120]{1,0:T(8,128)(2,1)S(1)} collective-permute-done((bf16[32,5120]{1,0:T(8,128)(2,1)S(1)}, bf16[32,5120]{1,0:T(8,128)(2,1)S(1)}, u32[]{:S(2)}, u32[]{:S(2)}) %collective-permute-start.7) | collective-permute-done | bytes 327712 | tf_op jit(solution)/shard_map/ppermute | solution.py:169
  107.6 0.0 collective-permute-done.8
  107.6 0.1 add_convert_fusion
  107.8 0.1 reshape.30
  107.9 12.4 %all_to_all.22 = bf16[16,2,5120]{2,1,0:T(2,128)(2,1)S(1)} all-to-all(bf16[16,2,5120]{2,1,0:T(2,128)(2,1)S(1)} %reshape.30), channel_id=1, replica_groups=mesh['kv'=16,'tp'=8] {'kv'}, dimensions={0} | all-to-all | bytes 655360 | tf_op jit(solution)/shard_map/all_to_all | solution.py:240
  120.3 0.3 convert_reduce_fusion
  120.6 0.6 add_convert_fusion.2
  (1 shorter events, 0.0 us)
Async XLA Ops:
  1.5 16.3 %all-to-all-start = ((bf16[16,16,640]{2,1,0:T(8,128)(2,1)}), bf16[16,16,640]{2,1,0:T(8,128)(2,1)S(1)}, u32[]{:S(2)}, u32[]{:S(2)}) async-start(bf16[16,16,640]{2,1,0:T(8,128)(2,1)} %broadcast_in_dim.12), calls=%async_computation | async-start | bytes 655360 | tf_op jit(solution)/shard_map/all_to_all | solution.py:196
  8.6 1.0 copy-start.5
  9.6 0.9 copy-start.6
  10.5 0.7 copy-start.7
  11.2 0.7 copy-start.8
  11.9 0.7 copy-start.9
  33.2 20.3 %copy-start.11 = (f32[5120]{0:T(1024)S(1)}, f32[5120]{0:T(1024)}, u32[]{:S(2)}) copy-start(f32[5120]{0:T(1024)} %param.20) | copy-start | bytes 61444
  38.8 1.6 %collective-permute-start = (bf16[8,5120]{1,0:T(8,128)(2,1)}, bf16[8,5120]{1,0:T(8,128)(2,1)S(1)}, u32[]{:S(2)}, u32[]{:S(2)}) collective-permute-start(bf16[8,5120]{1,0:T(8,128)(2,1)} %get-tuple-element.26), channel_id=1, source_target_pairs={{0,1},{1,0},{2,3},{3,2},{4,5},{5,4},{6,7},{7,6},{8,9},{9,8},{10,11... | collective-permute-start | bytes 245768 | tf_op jit(solution)/shard_map/ppermute | solution.py:173
  41.3 6.7 %collective-permute-start.3 = (bf16[8,5120]{1,0:T(8,128)(2,1)S(1)}, bf16[8,5120]{1,0:T(8,128)(2,1)S(1)}, u32[]{:S(2)}, u32[]{:S(2)}) collective-permute-start(bf16[8,5120]{1,0:T(8,128)(2,1)S(1)} %fusion), channel_id=1, source_target_pairs={{0,4},{1,5},{2,6},{3,7},{4,0},{5,1},{6,2},{7,3},{8,12},{9,13},{10,... | collective-permute-start | bytes 245768 | tf_op jit(solution)/shard_map/ppermute | solution.py:169
  45.2 5.3 %collective-permute-start.2 = (bf16[8,5120]{1,0:T(8,128)(2,1)S(1)}, bf16[8,5120]{1,0:T(8,128)(2,1)S(1)}, u32[]{:S(2)}, u32[]{:S(2)}) collective-permute-start(bf16[8,5120]{1,0:T(8,128)(2,1)S(1)} %fusion), channel_id=1, source_target_pairs={{0,6},{1,7},{2,0},{3,1},{4,2},{5,3},{6,4},{7,5},{8,14},{9,15},{10,... | collective-permute-start | bytes 245768 | tf_op jit(solution)/shard_map/ppermute | solution.py:169
  46.0 5.7 %collective-permute-start.1 = (bf16[8,5120]{1,0:T(8,128)(2,1)S(1)}, bf16[8,5120]{1,0:T(8,128)(2,1)S(1)}, u32[]{:S(2)}, u32[]{:S(2)}) collective-permute-start(bf16[8,5120]{1,0:T(8,128)(2,1)S(1)} %fusion), channel_id=1, source_target_pairs={{0,2},{1,3},{2,4},{3,5},{4,6},{5,7},{6,0},{7,1},{8,10},{9,11},{10,... | collective-permute-start | bytes 245768 | tf_op jit(solution)/shard_map/ppermute | solution.py:169
  51.6 24.1 %copy-start.1 = (bf16[5120,216]{0,1:T(8,128)(2,1)S(1)}, bf16[5120,216]{0,1:T(8,128)(2,1)}, u32[]{:S(2)}) copy-start(bf16[5120,216]{0,1:T(8,128)(2,1)} %param.22) | copy-start | bytes 6635524
  52.8 0.7 copy-start.10
  53.7 22.0 %copy-start = (bf16[5120,216]{0,1:T(8,128)(2,1)S(1)}, bf16[5120,216]{0,1:T(8,128)(2,1)}, u32[]{:S(2)}) copy-start(bf16[5120,216]{0,1:T(8,128)(2,1)} %param.21) | copy-start | bytes 6635524
  75.7 3.0 %collective-permute-start.4 = (bf16[128,5120]{1,0:T(8,128)(2,1)S(1)}, bf16[128,5120]{1,0:T(8,128)(2,1)S(1)}, u32[]{:S(2)}, u32[]{:S(2)}) collective-permute-start(bf16[128,5120]{1,0:T(8,128)(2,1)S(1)} %bitcast.13), channel_id=1, source_target_pairs={{0,1},{1,0},{2,3},{3,2},{4,5},{5,4},{6,7},{7,6},{8,9},{9,8},{10,11... | collective-permute-start | bytes 3932168 | tf_op jit(solution)/shard_map/ppermute | solution.py:173
  75.8 3.0 %copy-start.2 = (bf16[216,5120]{1,0:T(8,128)(2,1)S(1)}, bf16[216,5120]{1,0:T(8,128)(2,1)}, u32[]{:S(2)}) copy-start(bf16[216,5120]{1,0:T(8,128)(2,1)} %down.3) | copy-start | bytes 6635524
  77.6 4.6 %copy-start.3 = (bf16[128,216]{1,0:T(8,128)(2,1)}, bf16[128,216]{1,0:T(8,128)(2,1)S(1)}, u32[]{:S(2)}) copy-start(bf16[128,216]{1,0:T(8,128)(2,1)S(1)} %shard_map.121.earlier.hidden) | copy-start | bytes 165892
  82.2 3.2 %collective-permute-start.5 = (bf16[128,5120]{1,0:T(8,128)(2,1)}, bf16[128,5120]{1,0:T(8,128)(2,1)S(1)}, u32[]{:S(2)}, u32[]{:S(2)}) collective-permute-start(bf16[128,5120]{1,0:T(8,128)(2,1)} %shard_map.122), channel_id=1, source_target_pairs={{0,1},{1,0},{2,3},{3,2},{4,5},{5,4},{6,7},{7,6},{8,9},{9,8},{10,11... | collective-permute-start | bytes 3932168 | tf_op jit(solution)/shard_map/ppermute | solution.py:173
  85.4 0.8 copy-start.4
  86.8 17.4 %collective-permute-start.6 = (bf16[32,5120]{1,0:T(8,128)(2,1)S(1)}, bf16[32,5120]{1,0:T(8,128)(2,1)S(1)}, u32[]{:S(2)}, u32[]{:S(2)}) collective-permute-start(bf16[32,5120]{1,0:T(8,128)(2,1)S(1)} %get-tuple-element.28), channel_id=1, source_target_pairs={{0,6},{1,7},{2,0},{3,1},{4,2},{5,3},{6,4},{7,5},{8,14},{9,15},{10,... | collective-permute-start | bytes 983048 | tf_op jit(solution)/shard_map/ppermute | solution.py:169
  90.0 17.7 %collective-permute-start.7 = (bf16[32,5120]{1,0:T(8,128)(2,1)S(1)}, bf16[32,5120]{1,0:T(8,128)(2,1)S(1)}, u32[]{:S(2)}, u32[]{:S(2)}) collective-permute-start(bf16[32,5120]{1,0:T(8,128)(2,1)S(1)} %get-tuple-element.29), channel_id=1, source_target_pairs={{0,2},{1,3},{2,4},{3,5},{4,6},{5,7},{6,0},{7,1},{8,10},{9,11},{10,... | collective-permute-start | bytes 983048 | tf_op jit(solution)/shard_map/ppermute | solution.py:169
  90.0 17.7 %collective-permute-start.8 = (bf16[32,5120]{1,0:T(8,128)(2,1)S(1)}, bf16[32,5120]{1,0:T(8,128)(2,1)S(1)}, u32[]{:S(2)}, u32[]{:S(2)}) collective-permute-start(bf16[32,5120]{1,0:T(8,128)(2,1)S(1)} %get-tuple-element.30), channel_id=1, source_target_pairs={{0,4},{1,5},{2,6},{3,7},{4,0},{5,1},{6,2},{7,3},{8,12},{9,13},{10,... | collective-permute-start | bytes 983048 | tf_op jit(solution)/shard_map/ppermute | solution.py:169

commit v5 on v4

--- a/solution.py
+++ b/solution.py
@@ -95,9 +95,7 @@
     out[:, GROUP * HEAD_WIDTH :] = stats.astype(BF)
 
 
-def project_kernel(tp, parts, weight_far, activations, own, other, weight, sem):
-    copy = pltpu.make_async_copy(weight_far, weight, sem)
-    copy.start()
+def project_kernel(tp, parts, weight, activations, own, other):
     z, core = tp[0] >> 1, tp[0] & 1
     sources = parts.shape[0]
     width = GROUP * HEAD_WIDTH
@@ -124,7 +122,6 @@
     source = (row % 8) // 2 * 4 + half * 2 + row % 2
     pick = jnp.where(col == source, 1.0, 0.0).astype(BF)
     context = mm(pick, context).astype(BF)
-    copy.wait()
     result = mm(context, weight[...])
     row = lax.broadcasted_iota(jnp.int32, (8, 2), 0)
     col = lax.broadcasted_iota(jnp.int32, (8, 2), 1)
@@ -139,29 +136,57 @@
     return (g / (1.0 + jnp.exp(-g)) * u).astype(BF)
 
 
-def ordered(hidden, tp):
+def ordered(hidden, kv, tp, other):
     n = hidden.shape[0]
     row = lax.broadcasted_iota(jnp.int32, (n, n), 0)
     col = lax.broadcasted_iota(jnp.int32, (n, n), 1)
-    z = tp[0] >> 1
-    source = (row % 32) // 2 * 8 + (z + 4 - row // 32) % 4 * 2 + row % 2
+    x, z, core = kv[0] >> 2, tp[0] >> 1, tp[0] & 1
+    core = 1 - core if other else core
+    run = row // 16
+    q = (run & 1) * 8 + (row & 15) // 2
+    places = jnp.where(run < 2, 0, jnp.where((run == 2) | (run == 5), 2, jnp.where((run == 3) | (run == 6), 1, 3)))
+    along_z = q * 8 + ((z + places) & 3) * 2
+    along_x = (((x + places) & 3) * 4 + q // 4) * 8 + (q & 3) * 2
+    source = jnp.where(core == 0, along_z, along_x) + (row & 1)
     return mm(jnp.where(col == source, 1.0, 0.0).astype(BF), hidden).astype(BF)
 
 
-def hidden_kernel(tp, rows, gate, up, out):
-    out[...] = ordered(hidden_of(rows[...], gate[...], up[...]), tp)
-
-
-def mlp_kernel(tp, rows, gate, up, down, earlier, out):
-    hidden = ordered(hidden_of(rows[...], gate[...], up[...]), tp)
+def hidden_kernel(kv, tp, rows, gate, up, out):
+    out[...] = ordered(hidden_of(rows[...], gate[...], up[...]), kv, tp, False)
+
+
+def mlp_kernel(kv, tp, rows, gate, up, down, out):
+    hidden = ordered(hidden_of(rows[...], gate[...], up[...]), kv, tp, True)
     out[...] = mm(hidden, down[...]).astype(BF)
 
 
-def down_kernel(hidden, down, back, own, *sent):
+def down_kernel(hidden, down, back, own, ahead, behind, rest_ahead, rest_behind):
     result = mm(hidden[...], down[...]) + back[...].astype(F32)
     own[...] = result[:32]
-    for k, ref in enumerate(sent):
-        ref[...] = result[32 * (k + 1) : 32 * (k + 2)].astype(BF)
+    ahead[...] = result[32:64].astype(BF)
+    behind[...] = result[64:96].astype(BF)
+    rest_ahead[...] = result[96:112]
+    rest_behind[...] = result[112:]
+
+
+def device(x, y, z, c):
+    return (x * 4 + y) * 8 + z * 2 + c
+
+
+def move_ring(value, k):
+    pairs = [
+        (device(x, y, z, c), device(x, y, (z + k) % 4, c) if c == 0 else device((x + k) % 4, y, z, c))
+        for x in range(4)
+        for y in range(4)
+        for z in range(4)
+        for c in range(2)
+    ]
+    return lax.ppermute(value, ("kv", "tp"), pairs)
+
+
+PLANES = [[device(x, y, z, 0) for x in range(4) for y in range(4)] for z in range(4)] + [
+    [device(x, y, z, 1) for y in range(4) for z in range(4)] for x in range(4)
+]
 
 
 def move_z(value, k):
@@ -204,13 +229,9 @@
         q.reshape(256, 640), keys_wide, values_in, onehot
     )
     parts = lax.all_to_all(packed.reshape(16, 16, 768), "kv", 0, 0)
-    own, other = call(
-        project_kernel,
-        [shape((8, D), F32), shape((8, D), BF)],
-        [SM, VM, pl.ANY, VM],
-        [pltpu.VMEM(out_weight.shape, BF), pltpu.SemaphoreType.DMA],
-        limit=56 << 20,
-    )(tp, parts, out_weight, activations)
+    own, other = call(project_kernel, [shape((8, D), F32), shape((8, D), BF)], [SM, VM, VM, VM])(
+        tp, parts, out_weight, activations
+    )
     attended = own + move_core(other).astype(F32)
     sent = attended.astype(BF)
     for part in [move_z(sent, k) for k in (1, 3, 2)]:
@@ -225,19 +246,25 @@
 
     rows = lax.all_to_all(jnp.broadcast_to(normed[None], (16, 8, D)), "kv", 0, 0).reshape(128, D)
     rows_other = move_core(rows)
-    hidden = call(hidden_kernel, shape((128, 216), BF), [SM] + [VM] * 3)(tp, rows, gate_t, up_t)
-    y_other = call(mlp_kernel, shape((128, D), BF), [SM] + [VM] * 4 + [pl.ANY])(
-        tp, rows_other, gate_t, up_t, down_weight, hidden
-    )
-    block = shape((32, D), BF)
-    mixed, *sent = call(down_kernel, [shape((32, D), F32), block, block, block], [VM] * 3)(
-        hidden, down_weight, move_core(y_other)
-    )
-    for part in [move_z(sent[k - 1], -k) for k in (1, 3, 2)]:
-        mixed = mixed + part.astype(F32)
+    hidden = call(hidden_kernel, shape((128, 216), BF), [SM, SM] + [VM] * 3)(kv, tp, rows, gate_t, up_t)
+    rows_other, hidden = lax.optimization_barrier((rows_other, hidden))
+    y_other = call(mlp_kernel, shape((128, D), BF), [SM, SM] + [VM] * 4)(
+        kv, tp, rows_other, gate_t, up_t, down_weight
+    )
+    wide, narrow = shape((32, D), BF), shape((16, D), F32)
+    mixed, ahead, behind, rest_ahead, rest_behind = call(
+        down_kernel, [shape((32, D), F32), wide, wide, narrow, narrow], [VM] * 3
+    )(hidden, down_weight, move_core(y_other))
+    from_behind = move_ring(ahead, 1)
+    from_ahead = move_ring(behind, -1)
+    rest_ahead = move_ring((rest_ahead + from_behind[:16].astype(F32)).astype(BF), 1)
+    rest_behind = move_ring((rest_behind + from_ahead[16:].astype(F32)).astype(BF), -1)
+    first = mixed[:16] + from_ahead[:16].astype(F32) + rest_ahead.astype(F32)
+    second = mixed[16:] + from_behind[16:].astype(F32) + rest_behind.astype(F32)
+    mixed = jnp.concatenate([first.astype(BF).reshape(8, 2, D), second.astype(BF).reshape(8, 2, D)], axis=0)
     keep = lax.dynamic_slice_in_dim(widened, (tp[0] >> 1) * 2, 2, 0)
-    mixed, keep = lax.optimization_barrier((mixed.astype(BF).reshape(16, 2, D), keep))
-    mixed = lax.all_to_all(mixed, "kv", 0, 0)
+    mixed, keep = lax.optimization_barrier((mixed, keep))
+    mixed = lax.all_to_all(mixed, ("kv", "tp"), 0, 0, axis_index_groups=PLANES)
     return (keep + jnp.sum(mixed.astype(F32), axis=0)).astype(BF)
 
 

time: 122 us -> 113 us (0.926)
  Pallas kernels: 14.9 us -> 9.78 us
  waiting for transfers between devices: 29.6 us -> 25 us
  starting transfers between devices: 18 us -> 20.4 us
  other arithmetic: 3.31 us -> 1.76 us
    ppermute x6 -> x3, waiting for transfers between devices: 19.5 us -> 4.33 us  [move_z(): return lax.ppermute(value, 'tp', pairs)]
    ppermute x0 -> x4, waiting for transfers between devices: none -> 11.1 us  [move_ring(): return lax.ppermute(value, ('kv', 'tp'), pairs)]
    ppermute x0 -> x4, starting transfers between devices: none -> 6.99 us  [move_ring(): return lax.ppermute(value, ('kv', 'tp'), pairs)]
    pallas_call x4, Pallas kernels: 11.3 us -> 6.11 us  [the longest x1 2.3 us: local(): call(mlp_kernel, shape((128, D), BF), [SM, SM] + [VM] * 4)]
    ppermute x6 -> x3, starting transfers between devices: 10.7 us -> 5.98 us  [move_z(): return lax.ppermute(value, 'tp', pairs)]
    unnamed x24 -> x22, local copies, waits for them, and re-layouts: 5.4 us -> 6.77 us
  transfers between devices with their start and end apart: 10 -> 11, of which waited for: 9 -> 10; matrix products, arithmetic and copies ran while one was open for 1% -> 0% of each run, Pallas kernels for 2% -> 2%
where the time goes in v5:
time: 113 us
  blocking collectives  47.1 us (42%)
  waiting for transfers between devices  25 us (22%)
  starting transfers between devices  20.4 us (18%)
  Pallas kernels  9.78 us (9%)
  local copies, waits for them, and re-layouts  8.51 us (8%)
  other arithmetic  1.76 us (2%)
    all_to_all x1, blocking collectives, local(): lax.all_to_all(jnp.broadcast_to(normed[None], (16, 8, D)), 'kv', 0, 0)  22.1 us
    all_to_all x1, blocking collectives, local(): parts = lax.all_to_all(packed.reshape(16, 16, 768), 'kv', 0, 0)  12.6 us
    all_to_all x1, blocking collectives, local(): mixed = lax.all_to_all(mixed, ('kv', 'tp'), 0, 0, axis_index_groups=PLANES)  12.4 us
    ppermute x4, waiting for transfers between devices, move_ring(): return lax.ppermute(value, ('kv', 'tp'), pairs)  11.1 us
    all_to_all x1, starting transfers between devices, local(): lax.all_to_all(jnp.broadcast_to(queries[None], (16, 16, 640)), 'kv', 0, 0)  7.12 us
    ppermute x4, starting transfers between devices, move_ring(): return lax.ppermute(value, ('kv', 'tp'), pairs)  6.99 us
    unnamed x22, local copies, waits for them, and re-layouts  6.77 us
    ppermute x3, starting transfers between devices, move_z(): return lax.ppermute(value, 'tp', pairs)  5.98 us
  transfers between devices with their start and end apart: 11, of which 10 were waited for; matrix products, arithmetic and copies ran while one was open for 0% of the time, Pallas kernels for 2%

profile of v5, /device:TPU:0, one launch (start us, length us, event | category | flops | bytes accessed | tf_op | source)
XLA Modules:
  0.0 112.8 jit_solution(16040657523315274360)
XLA Ops:
  0.0 1.5 %broadcast_in_dim.12 = bf16[16,16,640]{2,1,0:T(8,128)(2,1)} broadcast(bf16[16,640]{1,0:T(8,128)(2,1)} %param.13), dimensions={1,2} | broadcast | bytes 348160 | tf_op jit(solution)/shard_map/broadcast_in_dim | solution.py:221
  1.5 7.1 %all-to-all-start = ((bf16[16,16,640]{2,1,0:T(8,128)(2,1)}), bf16[16,16,640]{2,1,0:T(8,128)(2,1)S(1)}, u32[]{:S(2)}, u32[]{:S(2)}) async-start(bf16[16,16,640]{2,1,0:T(8,128)(2,1)} %broadcast_in_dim.12), calls=%async_computation | async-start | bytes 655360 | tf_op jit(solution)/shard_map/all_to_all | solution.py:221
  8.6 0.0 copy-start.4
  8.6 0.9 copy-done.4
  9.6 0.0 copy-start.5
  9.6 0.9 copy-done.5
  10.5 0.0 copy-start.7
  10.5 0.7 copy-done.7
  11.2 0.0 copy-start.8
  11.2 0.7 copy-done.8
  11.8 0.0 copy-start.9
  11.8 0.7 copy-done.9
  12.5 1.0 shard_map.118
  13.5 0.0 copy-start.6
  13.5 4.3 %all-to-all-done = bf16[16,16,640]{2,1,0:T(8,128)(2,1)S(1)} async-done(((bf16[16,16,640]{2,1,0:T(8,128)(2,1)}), bf16[16,16,640]{2,1,0:T(8,128)(2,1)S(1)}, u32[]{:S(2)}, u32[]{:S(2)}) %all-to-all-start) | async-done | bytes 327712 | tf_op jit(solution)/shard_map/all_to_all | solution.py:221
  17.8 2.7 %shard_map.119 = bf16[256,768]{1,0:T(8,128)(2,1)S(1)} custom-call(bf16[256,640]{1,0:T(8,128)(2,1)S(1)} %bitcast.16, bf16[1024,256]{1,0:T(8,128)(2,1)S(1)} %get-tuple-element.25.keys_wide, bf16[1024,128]{1,0:T(8,128)(2,1)S(1)} %get-tuple-element.26.values, bf16[256,128]{1,0:T(8,128)(2,1)S(1)} %get-tuple-element.27.onehot), custom_call_target="tpu_custom_call" | custom-call | tf_op jit(solution)/shard_map/pallas_call | solution.py:228
  20.5 12.6 %all_to_all.20.parts = bf16[16,16,768]{2,1,0:T(8,128)(2,1)S(1)} all-to-all(bf16[16,16,768]{2,1,0:T(8,128)(2,1)S(1)} %bitcast.15), channel_id=1, replica_groups=mesh['kv'=16,'tp'=8] {'kv'}, dimensions={0} | all-to-all | bytes 786432 | tf_op jit(solution)/shard_map/all_to_all | solution.py:231
  33.1 0.0 copy-done.6
  33.1 0.0 copy-start.3
  33.1 2.9 %copy-done.3 = bf16[640,5120]{1,0:T(8,128)(2,1)S(1)} copy-done((bf16[640,5120]{1,0:T(8,128)(2,1)S(1)}, bf16[640,5120]{1,0:T(8,128)(2,1)}, u32[]{:S(2)}) %copy-start.3) | copy-done | bytes 6553624
  35.9 0.0 copy-start.10
  35.9 1.4 %shard_map.120 = (f32[8,5120]{1,0:T(8,128)S(1)}, bf16[8,5120]{1,0:T(8,128)(2,1)S(1)}) custom-call(s32[1]{0:T(128)} %bitcast.1.tp, bf16[16,16,768]{2,1,0:T(8,128)(2,1)S(1)} %all_to_all.20.parts, bf16[640,5120]{1,0:T(8,128)(2,1)S(1)} %copy-done.3, bf16[2,5120]{1,0:T(2,128)(2,1)S(1)} %copy-done.6), custom_call_target="tpu_custom_call" | custom-call | tf_op jit(solution)/shard_map/pallas_call | solution.py:232
  37.4 0.1 collective-permute-start
  37.5 1.3 %collective-permute-done = bf16[8,5120]{1,0:T(8,128)(2,1)S(1)} collective-permute-done((bf16[8,5120]{1,0:T(8,128)(2,1)S(1)}, bf16[8,5120]{1,0:T(8,128)(2,1)S(1)}, u32[]{:S(2)}, u32[]{:S(2)}) %collective-permute-start) | collective-permute-done | bytes 81952 | tf_op jit(solution)/shard_map/ppermute | solution.py:198
  38.8 4.0 %collective-permute-start.3 = (bf16[8,5120]{1,0:T(8,128)(2,1)S(1)}, bf16[8,5120]{1,0:T(8,128)(2,1)S(1)}, u32[]{:S(2)}, u32[]{:S(2)}) collective-permute-start(bf16[8,5120]{1,0:T(8,128)(2,1)S(1)} %fusion), channel_id=1, source_target_pairs={{0,4},{1,5},{2,6},{3,7},{4,0},{5,1},{6,2},{7,3},{8,12},{9,13},{10,... | collective-permute-start | bytes 245768 | tf_op jit(solution)/shard_map/ppermute | solution.py:194
  42.7 0.7 collective-permute-start.2
  43.4 1.3 %collective-permute-start.1 = (bf16[8,5120]{1,0:T(8,128)(2,1)S(1)}, bf16[8,5120]{1,0:T(8,128)(2,1)S(1)}, u32[]{:S(2)}, u32[]{:S(2)}) collective-permute-start(bf16[8,5120]{1,0:T(8,128)(2,1)S(1)} %fusion), channel_id=1, source_target_pairs={{0,2},{1,3},{2,4},{3,5},{4,6},{5,7},{6,0},{7,1},{8,10},{9,11},{10,... | collective-permute-start | bytes 245768 | tf_op jit(solution)/shard_map/ppermute | solution.py:194
  44.8 0.7 collective-permute-done.3
  45.5 2.5 %collective-permute-done.2 = bf16[8,5120]{1,0:T(8,128)(2,1)S(1)} collective-permute-done((bf16[8,5120]{1,0:T(8,128)(2,1)S(1)}, bf16[8,5120]{1,0:T(8,128)(2,1)S(1)}, u32[]{:S(2)}, u32[]{:S(2)}) %collective-permute-start.2) | collective-permute-done | bytes 81952 | tf_op jit(solution)/shard_map/ppermute | solution.py:194
  48.0 1.1 collective-permute-done.1
  49.1 0.0 copy-start.1
  49.1 0.2 multiply_reduce_fusion
  49.3 0.0 copy-done.10
  49.3 0.1 multiply_convert_fusion
  49.4 0.1 broadcast_in_dim.27
  49.5 0.0 copy-start
  49.5 22.1 %all_to_all.21 = bf16[16,8,5120]{2,1,0:T(8,128)(2,1)S(1)} all-to-all(bf16[16,8,5120]{2,1,0:T(8,128)(2,1)S(1)} %broadcast_in_dim.27), channel_id=1, replica_groups=mesh['kv'=16,'tp'=8] {'kv'}, dimensions={0} | all-to-all | bytes 2621440 | tf_op jit(solution)/shard_map/all_to_all | solution.py:247
  71.6 0.0 collective-permute-start.4
  71.6 0.0 copy-done.1
  71.6 0.0 copy-done
  71.7 0.0 copy-start.2
  71.7 1.8 %shard_map.121.hidden = bf16[128,216]{1,0:T(8,128)(2,1)S(1)} custom-call(s32[1]{0:T(128)} %bitcast.kv, s32[1]{0:T(128)} %bitcast.1.tp, bf16[128,5120]{1,0:T(8,128)(2,1)S(1)} %bitcast.14, bf16[216,5120]{1,0:T(8,128)(2,1)S(1)} %bitcast.9, bf16[216,5120]{1,0:T(8,128)(2,1)S(1)} %bitcast.11), custom_call_target="tpu_custom_call" | custom-call | tf_op jit(solution)/shard_map/pallas_call | solution.py:249
  73.5 1.2 %collective-permute-done.4.rows = bf16[128,5120]{1,0:T(8,128)(2,1)S(1)} collective-permute-done((bf16[128,5120]{1,0:T(8,128)(2,1)S(1)}, bf16[128,5120]{1,0:T(8,128)(2,1)S(1)}, u32[]{:S(2)}, u32[]{:S(2)}) %collective-permute-start.4) | collective-permute-done | bytes 1310752 | tf_op jit(solution)/shard_map/ppermute | solution.py:198
  74.7 0.0 copy-done.2
  74.7 2.3 %shard_map.122 = bf16[128,5120]{1,0:T(8,128)(2,1)S(1)} custom-call(s32[1]{0:T(128)} %bitcast.kv, s32[1]{0:T(128)} %bitcast.1.tp, bf16[128,5120]{1,0:T(8,128)(2,1)S(1)} %collective-permute-done.4.rows, bf16[216,5120]{1,0:T(8,128)(2,1)S(1)} %bitcast.10, bf16[216,5120]{1,0:T(8,128)(2,1)S(1)} %bitcast.12, bf16[216,5120]{1,0:T(8,128)(2,1)S(1)} %copy-done.2), custom_call_target="tpu_custom_call" | custom-call | tf_op jit(solution)/shard_map/pallas_call | solution.py:251
  77.0 0.2 collective-permute-start.5
  77.2 2.9 %collective-permute-done.5.back = bf16[128,5120]{1,0:T(8,128)(2,1)S(1)} collective-permute-done((bf16[128,5120]{1,0:T(8,128)(2,1)S(1)}, bf16[128,5120]{1,0:T(8,128)(2,1)S(1)}, u32[]{:S(2)}, u32[]{:S(2)}) %collective-permute-start.5) | collective-permute-done | bytes 1310752 | tf_op jit(solution)/shard_map/ppermute | solution.py:198
  80.1 0.5 shard_map.123
  80.6 3.2 %collective-permute-start.6 = (bf16[32,5120]{1,0:T(8,128)(2,1)S(1)}, bf16[32,5120]{1,0:T(8,128)(2,1)S(1)}, u32[]{:S(2)}, u32[]{:S(2)}) collective-permute-start(bf16[32,5120]{1,0:T(8,128)(2,1)S(1)} %get-tuple-element.33), channel_id=1, source_target_pairs={{0,6},{1,97},{2,0},{3,99},{4,2},{5,101},{6,4},{7,103},{8,14},{9,10... | collective-permute-start | bytes 983048 | tf_op jit(solution)/shard_map/ppermute | solution.py:184
  83.8 0.0 collective-permute-start.7
  83.8 4.6 %collective-permute-done.6 = bf16[32,5120]{1,0:T(8,128)(2,1)S(1)} collective-permute-done((bf16[32,5120]{1,0:T(8,128)(2,1)S(1)}, bf16[32,5120]{1,0:T(8,128)(2,1)S(1)}, u32[]{:S(2)}, u32[]{:S(2)}) %collective-permute-start.6) | collective-permute-done | bytes 327712 | tf_op jit(solution)/shard_map/ppermute | solution.py:184
  88.4 3.8 %collective-permute-start.9 = (bf16[16,5120]{1,0:T(8,128)(2,1)S(1)}, bf16[16,5120]{1,0:T(8,128)(2,1)S(1)}, u32[]{:S(2)}, u32[]{:S(2)}) collective-permute-start(bf16[16,5120]{1,0:T(8,128)(2,1)S(1)} %add_convert_fusion.1), channel_id=1, source_target_pairs={{0,6},{1,97},{2,0},{3,99},{4,2},{5,101},{6,4},{7,103},{8,14},{9,10... | collective-permute-start | bytes 491528 | tf_op jit(solution)/shard_map/ppermute | solution.py:184
  92.2 0.0 collective-permute-done.7
  92.2 0.1 collective-permute-start.8
  92.3 2.7 %collective-permute-done.9 = bf16[16,5120]{1,0:T(8,128)(2,1)S(1)} collective-permute-done((bf16[16,5120]{1,0:T(8,128)(2,1)S(1)}, bf16[16,5120]{1,0:T(8,128)(2,1)S(1)}, u32[]{:S(2)}, u32[]{:S(2)}) %collective-permute-start.9) | collective-permute-done | bytes 163872 | tf_op jit(solution)/shard_map/ppermute | solution.py:184
  95.0 3.8 %collective-permute-done.8 = bf16[16,5120]{1,0:T(8,128)(2,1)S(1)} collective-permute-done((bf16[16,5120]{1,0:T(8,128)(2,1)S(1)}, bf16[16,5120]{1,0:T(8,128)(2,1)S(1)}, u32[]{:S(2)}, u32[]{:S(2)}) %collective-permute-start.8) | collective-permute-done | bytes 163872 | tf_op jit(solution)/shard_map/ppermute | solution.py:184
  98.8 0.1 add_convert_fusion.2
  98.9 0.1 reshape.33
  99.0 0.1 reshape.34
  99.1 0.4 pad_maximum_fusion
  99.5 12.4 %all_to_all.22 = bf16[16,2,5120]{2,1,0:T(2,128)(2,1)S(1)} all-to-all(bf16[16,2,5120]{2,1,0:T(2,128)(2,1)S(1)} %pad_maximum_fusion), channel_id=1, replica_groups={{0,8,16,24,32,40,48,56,64,72,80,88,96,104,112,120},{2,10,18,26,34,42,50..., dimensions={0} | all-to-all | bytes 655360 | tf_op jit(solution)/shard_map/all_to_all | solution.py:267
  111.9 0.3 convert_reduce_fusion
  112.1 0.6 add_convert_fusion.5
  (5 shorter events, 0.1 us)
Async XLA Ops:
  1.5 16.3 %all-to-all-start = ((bf16[16,16,640]{2,1,0:T(8,128)(2,1)}), bf16[16,16,640]{2,1,0:T(8,128)(2,1)S(1)}, u32[]{:S(2)}, u32[]{:S(2)}) async-start(bf16[16,16,640]{2,1,0:T(8,128)(2,1)} %broadcast_in_dim.12), calls=%async_computation | async-start | bytes 655360 | tf_op jit(solution)/shard_map/all_to_all | solution.py:221
  8.6 1.0 copy-start.4
  9.6 0.9 copy-start.5
  10.5 0.7 copy-start.7
  11.2 0.7 copy-start.8
  11.8 0.7 copy-start.9
  13.5 19.6 %copy-start.6 = (bf16[2,5120]{1,0:T(2,128)(2,1)S(1)}, bf16[2,5120]{1,0:T(2,128)(2,1)}, u32[]{:S(2)}) copy-start(bf16[2,5120]{1,0:T(2,128)(2,1)} %activations.1) | copy-start | bytes 61444
  33.1 2.9 %copy-start.3 = (bf16[640,5120]{1,0:T(8,128)(2,1)S(1)}, bf16[640,5120]{1,0:T(8,128)(2,1)}, u32[]{:S(2)}) copy-start(bf16[640,5120]{1,0:T(8,128)(2,1)} %weight.1) | copy-start | bytes 19660804
  35.9 13.3 %copy-start.10 = (f32[5120]{0:T(1024)S(1)}, f32[5120]{0:T(1024)}, u32[]{:S(2)}) copy-start(f32[5120]{0:T(1024)} %param.20) | copy-start | bytes 61444
  37.4 1.4 %collective-permute-start = (bf16[8,5120]{1,0:T(8,128)(2,1)S(1)}, bf16[8,5120]{1,0:T(8,128)(2,1)S(1)}, u32[]{:S(2)}, u32[]{:S(2)}) collective-permute-start(bf16[8,5120]{1,0:T(8,128)(2,1)S(1)} %get-tuple-element.29), channel_id=1, source_target_pairs={{0,1},{1,0},{2,3},{3,2},{4,5},{5,4},{6,7},{7,6},{8,9},{9,8},{10,11... | collective-permute-start | bytes 245768 | tf_op jit(solution)/shard_map/ppermute | solution.py:198
  38.8 6.7 %collective-permute-start.3 = (bf16[8,5120]{1,0:T(8,128)(2,1)S(1)}, bf16[8,5120]{1,0:T(8,128)(2,1)S(1)}, u32[]{:S(2)}, u32[]{:S(2)}) collective-permute-start(bf16[8,5120]{1,0:T(8,128)(2,1)S(1)} %fusion), channel_id=1, source_target_pairs={{0,4},{1,5},{2,6},{3,7},{4,0},{5,1},{6,2},{7,3},{8,12},{9,13},{10,... | collective-permute-start | bytes 245768 | tf_op jit(solution)/shard_map/ppermute | solution.py:194
  42.7 5.3 %collective-permute-start.2 = (bf16[8,5120]{1,0:T(8,128)(2,1)S(1)}, bf16[8,5120]{1,0:T(8,128)(2,1)S(1)}, u32[]{:S(2)}, u32[]{:S(2)}) collective-permute-start(bf16[8,5120]{1,0:T(8,128)(2,1)S(1)} %fusion), channel_id=1, source_target_pairs={{0,6},{1,7},{2,0},{3,1},{4,2},{5,3},{6,4},{7,5},{8,14},{9,15},{10,... | collective-permute-start | bytes 245768 | tf_op jit(solution)/shard_map/ppermute | solution.py:194
  43.4 5.7 %collective-permute-start.1 = (bf16[8,5120]{1,0:T(8,128)(2,1)S(1)}, bf16[8,5120]{1,0:T(8,128)(2,1)S(1)}, u32[]{:S(2)}, u32[]{:S(2)}) collective-permute-start(bf16[8,5120]{1,0:T(8,128)(2,1)S(1)} %fusion), channel_id=1, source_target_pairs={{0,2},{1,3},{2,4},{3,5},{4,6},{5,7},{6,0},{7,1},{8,10},{9,11},{10,... | collective-permute-start | bytes 245768 | tf_op jit(solution)/shard_map/ppermute | solution.py:194
  49.1 22.6 %copy-start.1 = (bf16[5120,216]{0,1:T(8,128)(2,1)S(1)}, bf16[5120,216]{0,1:T(8,128)(2,1)}, u32[]{:S(2)}) copy-start(bf16[5120,216]{0,1:T(8,128)(2,1)} %param.22) | copy-start | bytes 6635524
  49.5 22.1 %copy-start = (bf16[5120,216]{0,1:T(8,128)(2,1)S(1)}, bf16[5120,216]{0,1:T(8,128)(2,1)}, u32[]{:S(2)}) copy-start(bf16[5120,216]{0,1:T(8,128)(2,1)} %param.21) | copy-start | bytes 6635524
  71.6 3.0 %collective-permute-start.4 = (bf16[128,5120]{1,0:T(8,128)(2,1)S(1)}, bf16[128,5120]{1,0:T(8,128)(2,1)S(1)}, u32[]{:S(2)}, u32[]{:S(2)}) collective-permute-start(bf16[128,5120]{1,0:T(8,128)(2,1)S(1)} %bitcast.13), channel_id=1, source_target_pairs={{0,1},{1,0},{2,3},{3,2},{4,5},{5,4},{6,7},{7,6},{8,9},{9,8},{10,11... | collective-permute-start | bytes 3932168 | tf_op jit(solution)/shard_map/ppermute | solution.py:198
  71.7 3.0 %copy-start.2 = (bf16[216,5120]{1,0:T(8,128)(2,1)S(1)}, bf16[216,5120]{1,0:T(8,128)(2,1)}, u32[]{:S(2)}) copy-start(bf16[216,5120]{1,0:T(8,128)(2,1)} %down.3) | copy-start | bytes 6635524
  77.0 3.1 %collective-permute-start.5 = (bf16[128,5120]{1,0:T(8,128)(2,1)S(1)}, bf16[128,5120]{1,0:T(8,128)(2,1)S(1)}, u32[]{:S(2)}, u32[]{:S(2)}) collective-permute-start(bf16[128,5120]{1,0:T(8,128)(2,1)S(1)} %shard_map.122), channel_id=1, source_target_pairs={{0,1},{1,0},{2,3},{3,2},{4,5},{5,4},{6,7},{7,6},{8,9},{9,8},{10,11... | collective-permute-start | bytes 3932168 | tf_op jit(solution)/shard_map/ppermute | solution.py:198
  80.6 7.8 %collective-permute-start.6 = (bf16[32,5120]{1,0:T(8,128)(2,1)S(1)}, bf16[32,5120]{1,0:T(8,128)(2,1)S(1)}, u32[]{:S(2)}, u32[]{:S(2)}) collective-permute-start(bf16[32,5120]{1,0:T(8,128)(2,1)S(1)} %get-tuple-element.33), channel_id=1, source_target_pairs={{0,6},{1,97},{2,0},{3,99},{4,2},{5,101},{6,4},{7,103},{8,14},{9,10... | collective-permute-start | bytes 983048 | tf_op jit(solution)/shard_map/ppermute | solution.py:184
  83.8 8.4 %collective-permute-start.7 = (bf16[32,5120]{1,0:T(8,128)(2,1)S(1)}, bf16[32,5120]{1,0:T(8,128)(2,1)S(1)}, u32[]{:S(2)}, u32[]{:S(2)}) collective-permute-start(bf16[32,5120]{1,0:T(8,128)(2,1)S(1)} %get-tuple-element.35), channel_id=1, source_target_pairs={{0,2},{1,33},{2,4},{3,35},{4,6},{5,37},{6,0},{7,39},{8,10},{9,41},... | collective-permute-start | bytes 983048 | tf_op jit(solution)/shard_map/ppermute | solution.py:184
  88.4 6.6 %collective-permute-start.9 = (bf16[16,5120]{1,0:T(8,128)(2,1)S(1)}, bf16[16,5120]{1,0:T(8,128)(2,1)S(1)}, u32[]{:S(2)}, u32[]{:S(2)}) collective-permute-start(bf16[16,5120]{1,0:T(8,128)(2,1)S(1)} %add_convert_fusion.1), channel_id=1, source_target_pairs={{0,6},{1,97},{2,0},{3,99},{4,2},{5,101},{6,4},{7,103},{8,14},{9,10... | collective-permute-start | bytes 491528 | tf_op jit(solution)/shard_map/ppermute | solution.py:184
  92.2 6.6 %collective-permute-start.8 = (bf16[16,5120]{1,0:T(8,128)(2,1)S(1)}, bf16[16,5120]{1,0:T(8,128)(2,1)S(1)}, u32[]{:S(2)}, u32[]{:S(2)}) collective-permute-start(bf16[16,5120]{1,0:T(8,128)(2,1)S(1)} %add_convert_fusion.3), channel_id=1, source_target_pairs={{0,2},{1,33},{2,4},{3,35},{4,6},{5,37},{6,0},{7,39},{8,10},{9,41},... | collective-permute-start | bytes 491528 | tf_op jit(solution)/shard_map/ppermute | solution.py:184

commit v6 on v5

--- a/solution.py
+++ b/solution.py
@@ -95,7 +95,9 @@
     out[:, GROUP * HEAD_WIDTH :] = stats.astype(BF)
 
 
-def project_kernel(tp, parts, weight, activations, own, other):
+def project_kernel(tp, parts, weight_far, activations, own, other, weight, sem):
+    copy = pltpu.make_async_copy(weight_far, weight, sem)
+    copy.start()
     z, core = tp[0] >> 1, tp[0] & 1
     sources = parts.shape[0]
     width = GROUP * HEAD_WIDTH
@@ -122,6 +124,7 @@
     source = (row % 8) // 2 * 4 + half * 2 + row % 2
     pick = jnp.where(col == source, 1.0, 0.0).astype(BF)
     context = mm(pick, context).astype(BF)
+    copy.wait()
     result = mm(context, weight[...])
     row = lax.broadcasted_iota(jnp.int32, (8, 2), 0)
     col = lax.broadcasted_iota(jnp.int32, (8, 2), 1)
@@ -136,12 +139,11 @@
     return (g / (1.0 + jnp.exp(-g)) * u).astype(BF)
 
 
-def ordered(hidden, kv, tp, other):
+def ordered(hidden, kv, tp):
     n = hidden.shape[0]
     row = lax.broadcasted_iota(jnp.int32, (n, n), 0)
     col = lax.broadcasted_iota(jnp.int32, (n, n), 1)
     x, z, core = kv[0] >> 2, tp[0] >> 1, tp[0] & 1
-    core = 1 - core if other else core
     run = row // 16
     q = (run & 1) * 8 + (row & 15) // 2
     places = jnp.where(run < 2, 0, jnp.where((run == 2) | (run == 5), 2, jnp.where((run == 3) | (run == 6), 1, 3)))
@@ -151,17 +153,12 @@
     return mm(jnp.where(col == source, 1.0, 0.0).astype(BF), hidden).astype(BF)
 
 
-def hidden_kernel(kv, tp, rows, gate, up, out):
-    out[...] = ordered(hidden_of(rows[...], gate[...], up[...]), kv, tp, False)
-
-
-def mlp_kernel(kv, tp, rows, gate, up, down, out):
-    hidden = ordered(hidden_of(rows[...], gate[...], up[...]), kv, tp, True)
-    out[...] = mm(hidden, down[...]).astype(BF)
-
-
-def down_kernel(hidden, down, back, own, ahead, behind, rest_ahead, rest_behind):
-    result = mm(hidden[...], down[...]) + back[...].astype(F32)
+def mlp_kernel(
+    kv, tp, rows, gate, up, down, gate_far, up_far, down_far, own, ahead, behind, rest_ahead, rest_behind
+):
+    near = ordered(hidden_of(rows[...], gate[...], up[...]), kv, tp)
+    far = ordered(hidden_of(rows[...], gate_far[...], up_far[...]), kv, tp)
+    result = mm(near, down[...]) + mm(far, down_far[...])
     own[...] = result[:32]
     ahead[...] = result[32:64].astype(BF)
     behind[...] = result[64:96].astype(BF)
@@ -216,6 +213,7 @@
     tp = lax.axis_index("tp")[None]
     gate_t, up_t = gate_weight.T, up_weight.T
     shape = jax.ShapeDtypeStruct
+    far = [move_core(w) for w in (gate_t, up_t, down_weight)]
     queries, kv, tp = lax.optimization_barrier((queries, kv, tp))
 
     q = lax.all_to_all(jnp.broadcast_to(queries[None], (16, 16, 640)), "kv", 0, 0)
@@ -229,9 +227,13 @@
         q.reshape(256, 640), keys_wide, values_in, onehot
     )
     parts = lax.all_to_all(packed.reshape(16, 16, 768), "kv", 0, 0)
-    own, other = call(project_kernel, [shape((8, D), F32), shape((8, D), BF)], [SM, VM, VM, VM])(
-        tp, parts, out_weight, activations
-    )
+    own, other = call(
+        project_kernel,
+        [shape((8, D), F32), shape((8, D), BF)],
+        [SM, VM, pl.ANY, VM],
+        [pltpu.VMEM(out_weight.shape, BF), pltpu.SemaphoreType.DMA],
+        limit=48 << 20,
+    )(tp, parts, out_weight, activations)
     attended = own + move_core(other).astype(F32)
     sent = attended.astype(BF)
     for part in [move_z(sent, k) for k in (1, 3, 2)]:
@@ -245,16 +247,10 @@
     ).astype(BF)
 
     rows = lax.all_to_all(jnp.broadcast_to(normed[None], (16, 8, D)), "kv", 0, 0).reshape(128, D)
-    rows_other = move_core(rows)
-    hidden = call(hidden_kernel, shape((128, 216), BF), [SM, SM] + [VM] * 3)(kv, tp, rows, gate_t, up_t)
-    rows_other, hidden = lax.optimization_barrier((rows_other, hidden))
-    y_other = call(mlp_kernel, shape((128, D), BF), [SM, SM] + [VM] * 4)(
-        kv, tp, rows_other, gate_t, up_t, down_weight
-    )
     wide, narrow = shape((32, D), BF), shape((16, D), F32)
     mixed, ahead, behind, rest_ahead, rest_behind = call(
-        down_kernel, [shape((32, D), F32), wide, wide, narrow, narrow], [VM] * 3
-    )(hidden, down_weight, move_core(y_other))
+        mlp_kernel, [shape((32, D), F32), wide, wide, narrow, narrow], [SM, SM] + [VM] * 7, limit=28 << 20
+    )(kv, tp, rows, gate_t, up_t, down_weight, *far)
     from_behind = move_ring(ahead, 1)
     from_ahead = move_ring(behind, -1)
     rest_ahead = move_ring((rest_ahead + from_behind[:16].astype(F32)).astype(BF), 1)

time: 113 us -> 108 us (0.956)
  waiting for transfers between devices: 25 us -> 20.5 us
  local copies, waits for them, and re-layouts: 8.51 us -> 5.66 us
  Pallas kernels: 9.78 us -> 12.4 us
    ppermute x3 -> x4, waiting for transfers between devices: 5.32 us -> 1.27 us  [move_core(): return lax.ppermute(value, 'tp', [(i, i ^ 1) for i in range(8)])]
    unnamed x22 -> x20, local copies, waits for them, and re-layouts: 6.77 us -> 3.9 us
    pallas_call x4 -> x2, Pallas kernels: 6.11 us -> 8.72 us  [the longest x1 4.45 us: local(): call(project_kernel, [shape((8, D), F32), shape((8, D), BF)], [SM, VM, pl...]
  transfers between devices with their start and end apart: 11 -> 12, of which waited for: 10 -> 8; matrix products, arithmetic and copies ran while one was open for 0% -> 0% of each run, Pallas kernels for 2% -> 1%
where the time goes in v6:
time: 108 us
  blocking collectives  46.8 us (43%)
  starting transfers between devices  20.7 us (19%)
  waiting for transfers between devices  20.5 us (19%)
  Pallas kernels  12.4 us (11%)
  local copies, waits for them, and re-layouts  5.66 us (5%)
  other arithmetic  1.76 us (2%)
    all_to_all x1, blocking collectives, local(): lax.all_to_all(jnp.broadcast_to(normed[None], (16, 8, D)), 'kv', 0, 0)  21.9 us
    all_to_all x1, blocking collectives, local(): parts = lax.all_to_all(packed.reshape(16, 16, 768), 'kv', 0, 0)  12.6 us
    all_to_all x1, blocking collectives, local(): mixed = lax.all_to_all(mixed, ('kv', 'tp'), 0, 0, axis_index_groups=PLANES)  12.4 us
    ppermute x4, waiting for transfers between devices, move_ring(): return lax.ppermute(value, ('kv', 'tp'), pairs)  11.1 us
    all_to_all x1, starting transfers between devices, local(): lax.all_to_all(jnp.broadcast_to(queries[None], (16, 16, 640)), 'kv', 0, 0)  7.12 us
    ppermute x4, starting transfers between devices, move_ring(): return lax.ppermute(value, ('kv', 'tp'), pairs)  7.01 us
    ppermute x3, starting transfers between devices, move_z(): return lax.ppermute(value, 'tp', pairs)  5.98 us
    pallas_call x1, Pallas kernels, local(): call(project_kernel, [shape((8, D), F32), shape((8, D), BF)], [SM, VM, pl...  4.45 us
  transfers between devices with their start and end apart: 12, of which 8 were waited for; matrix products, arithmetic and copies ran while one was open for 0% of the time, Pallas kernels for 1%

profile of v6, /device:TPU:0, one launch (start us, length us, event | category | flops | bytes accessed | tf_op | source)
XLA Modules:
  0.0 108.0 jit_solution(6486956787770370240)
XLA Ops:
  0.0 0.0 copy-start.5
  0.0 1.5 %broadcast_in_dim.12 = bf16[16,16,640]{2,1,0:T(8,128)(2,1)} broadcast(bf16[16,640]{1,0:T(8,128)(2,1)} %param.13), dimensions={1,2} | broadcast | bytes 348160 | tf_op jit(solution)/shard_map/broadcast_in_dim | solution.py:219
  1.5 7.1 %all-to-all-start = ((bf16[16,16,640]{2,1,0:T(8,128)(2,1)}), bf16[16,16,640]{2,1,0:T(8,128)(2,1)S(1)}, u32[]{:S(2)}, u32[]{:S(2)}) async-start(bf16[16,16,640]{2,1,0:T(8,128)(2,1)} %broadcast_in_dim.12), calls=%async_computation | async-start | bytes 655360 | tf_op jit(solution)/shard_map/all_to_all | solution.py:219
  8.6 0.0 copy-start.3
  8.6 0.9 copy-done.3
  9.6 0.0 copy-start.4
  9.6 0.9 copy-done.4
  10.5 0.0 copy-start.6
  10.5 0.7 copy-done.6
  11.2 0.0 copy-start.7
  11.2 0.7 copy-done.7
  11.9 0.0 copy-start.8
  11.9 0.7 copy-done.8
  12.5 1.0 shard_map.118
  13.5 4.3 %all-to-all-done = bf16[16,16,640]{2,1,0:T(8,128)(2,1)S(1)} async-done(((bf16[16,16,640]{2,1,0:T(8,128)(2,1)}), bf16[16,16,640]{2,1,0:T(8,128)(2,1)S(1)}, u32[]{:S(2)}, u32[]{:S(2)}) %all-to-all-start) | async-done | bytes 327712 | tf_op jit(solution)/shard_map/all_to_all | solution.py:219
  17.8 2.7 %shard_map.119 = bf16[256,768]{1,0:T(8,128)(2,1)S(1)} custom-call(bf16[256,640]{1,0:T(8,128)(2,1)S(1)} %bitcast.15, bf16[1024,256]{1,0:T(8,128)(2,1)S(1)} %get-tuple-element.23.keys_wide, bf16[1024,128]{1,0:T(8,128)(2,1)S(1)} %get-tuple-element.24.values, bf16[256,128]{1,0:T(8,128)(2,1)S(1)} %get-tuple-element.25.onehot), custom_call_target="tpu_custom_call" | custom-call | tf_op jit(solution)/shard_map/pallas_call | solution.py:226
  20.5 12.6 %all_to_all.20.parts = bf16[16,16,768]{2,1,0:T(8,128)(2,1)S(1)} all-to-all(bf16[16,16,768]{2,1,0:T(8,128)(2,1)S(1)} %bitcast.14), channel_id=1, replica_groups=mesh['kv'=16,'tp'=8] {'kv'}, dimensions={0} | all-to-all | bytes 786432 | tf_op jit(solution)/shard_map/all_to_all | solution.py:229
  33.1 0.0 copy-done.5
  33.1 0.0 copy-start
  33.1 0.0 copy-start.1
  33.1 0.0 copy-start.2
  33.1 0.0 copy-start.9
  33.1 4.5 %shard_map.120 = (f32[8,5120]{1,0:T(8,128)S(1)}, bf16[8,5120]{1,0:T(8,128)(2,1)S(1)}) custom-call(s32[1]{0:T(128)} %bitcast.1.tp, bf16[16,16,768]{2,1,0:T(8,128)(2,1)S(1)} %all_to_all.20.parts, bf16[640,5120]{1,0:T(8,128)(2,1)} %weight_far.1, bf16[2,5120]{1,0:T(2,128)(2,1)S(1)} %copy-done.5), custom_call_target="tpu_custom_call" | custom-call | tf_op jit(solution)/shard_map/pallas_call | solution.py:230
  37.6 0.1 collective-permute-start
  37.7 1.3 %collective-permute-done = bf16[8,5120]{1,0:T(8,128)(2,1)S(1)} collective-permute-done((bf16[8,5120]{1,0:T(8,128)(2,1)S(1)}, bf16[8,5120]{1,0:T(8,128)(2,1)S(1)}, u32[]{:S(2)}, u32[]{:S(2)}) %collective-permute-start) | collective-permute-done | bytes 81952 | tf_op jit(solution)/shard_map/ppermute | solution.py:195
  39.0 4.0 %collective-permute-start.3 = (bf16[8,5120]{1,0:T(8,128)(2,1)S(1)}, bf16[8,5120]{1,0:T(8,128)(2,1)S(1)}, u32[]{:S(2)}, u32[]{:S(2)}) collective-permute-start(bf16[8,5120]{1,0:T(8,128)(2,1)S(1)} %fusion), channel_id=1, source_target_pairs={{0,4},{1,5},{2,6},{3,7},{4,0},{5,1},{6,2},{7,3},{8,12},{9,13},{10,... | collective-permute-start | bytes 245768 | tf_op jit(solution)/shard_map/ppermute | solution.py:191
  42.9 0.7 collective-permute-start.2
  43.6 1.3 %collective-permute-start.1 = (bf16[8,5120]{1,0:T(8,128)(2,1)S(1)}, bf16[8,5120]{1,0:T(8,128)(2,1)S(1)}, u32[]{:S(2)}, u32[]{:S(2)}) collective-permute-start(bf16[8,5120]{1,0:T(8,128)(2,1)S(1)} %fusion), channel_id=1, source_target_pairs={{0,2},{1,3},{2,4},{3,5},{4,6},{5,7},{6,0},{7,1},{8,10},{9,11},{10,... | collective-permute-start | bytes 245768 | tf_op jit(solution)/shard_map/ppermute | solution.py:191
  44.9 0.0 copy-done
  44.9 0.0 collective-permute-start.4
  45.0 0.0 copy-done.1
  45.0 0.5 collective-permute-start.5
  45.5 0.2 collective-permute-done.3
  45.7 0.0 copy-done.2
  45.7 0.0 collective-permute-start.6
  45.7 2.5 %collective-permute-done.2 = bf16[8,5120]{1,0:T(8,128)(2,1)S(1)} collective-permute-done((bf16[8,5120]{1,0:T(8,128)(2,1)S(1)}, bf16[8,5120]{1,0:T(8,128)(2,1)S(1)}, u32[]{:S(2)}, u32[]{:S(2)}) %collective-permute-start.2) | collective-permute-done | bytes 81952 | tf_op jit(solution)/shard_map/ppermute | solution.py:191
  48.2 1.1 collective-permute-done.1
  49.3 0.2 multiply_reduce_fusion
  49.5 0.0 copy-done.9
  49.5 0.1 multiply_convert_fusion
  49.6 0.1 broadcast_in_dim.27
  49.7 21.9 %all_to_all.21 = bf16[16,8,5120]{2,1,0:T(8,128)(2,1)S(1)} all-to-all(bf16[16,8,5120]{2,1,0:T(8,128)(2,1)S(1)} %broadcast_in_dim.27), channel_id=1, replica_groups=mesh['kv'=16,'tp'=8] {'kv'}, dimensions={0} | all-to-all | bytes 2621440 | tf_op jit(solution)/shard_map/all_to_all | solution.py:249
  71.5 0.0 collective-permute-done.4.gate_far
  71.5 0.0 collective-permute-done.5.up_far
  71.6 0.0 collective-permute-done.6.down_far
  71.6 4.3 %shard_map.121 = (f32[32,5120]{1,0:T(8,128)S(1)}, bf16[32,5120]{1,0:T(8,128)(2,1)S(1)}, bf16[32,5120]{1,0:T(8,128)(2,1)S(1)}, f32[16,5120]{1,0:T(8,128)S(1)}, f32[16,5120]{1,0:T(8,128)S(1)}) custom-call(s32[1]{0:T(128)} %bitcast.kv, s32[1]{0:T(128)} %bitcast.1.tp, bf16[128,5120]{1,0:T(8,128)(2,1)S(1)} %bitcast.9, bf16[216,5120]{1,0:T(8,128)(2,1)S(1)} %bitcast.11, ...), custom_call_target="tpu_custom_call" | custom-call | tf_op jit(solution)/shard_map/pallas_call | solution.py:251
  75.8 3.2 %collective-permute-start.7 = (bf16[32,5120]{1,0:T(8,128)(2,1)S(1)}, bf16[32,5120]{1,0:T(8,128)(2,1)S(1)}, u32[]{:S(2)}, u32[]{:S(2)}) collective-permute-start(bf16[32,5120]{1,0:T(8,128)(2,1)S(1)} %get-tuple-element.29), channel_id=1, source_target_pairs={{0,6},{1,97},{2,0},{3,99},{4,2},{5,101},{6,4},{7,103},{8,14},{9,10... | collective-permute-start | bytes 983048 | tf_op jit(solution)/shard_map/ppermute | solution.py:181
  79.0 0.0 collective-permute-start.8
  79.0 4.6 %collective-permute-done.7 = bf16[32,5120]{1,0:T(8,128)(2,1)S(1)} collective-permute-done((bf16[32,5120]{1,0:T(8,128)(2,1)S(1)}, bf16[32,5120]{1,0:T(8,128)(2,1)S(1)}, u32[]{:S(2)}, u32[]{:S(2)}) %collective-permute-start.7) | collective-permute-done | bytes 327712 | tf_op jit(solution)/shard_map/ppermute | solution.py:181
  83.6 3.8 %collective-permute-start.10 = (bf16[16,5120]{1,0:T(8,128)(2,1)S(1)}, bf16[16,5120]{1,0:T(8,128)(2,1)S(1)}, u32[]{:S(2)}, u32[]{:S(2)}) collective-permute-start(bf16[16,5120]{1,0:T(8,128)(2,1)S(1)} %add_convert_fusion.1), channel_id=1, source_target_pairs={{0,6},{1,97},{2,0},{3,99},{4,2},{5,101},{6,4},{7,103},{8,14},{9,10... | collective-permute-start | bytes 491528 | tf_op jit(solution)/shard_map/ppermute | solution.py:181
  87.4 0.0 collective-permute-done.8
  87.4 0.1 collective-permute-start.9
  87.5 2.7 %collective-permute-done.10 = bf16[16,5120]{1,0:T(8,128)(2,1)S(1)} collective-permute-done((bf16[16,5120]{1,0:T(8,128)(2,1)S(1)}, bf16[16,5120]{1,0:T(8,128)(2,1)S(1)}, u32[]{:S(2)}, u32[]{:S(2)}) %collective-permute-start.10) | collective-permute-done | bytes 163872 | tf_op jit(solution)/shard_map/ppermute | solution.py:181
  90.2 3.8 %collective-permute-done.9 = bf16[16,5120]{1,0:T(8,128)(2,1)S(1)} collective-permute-done((bf16[16,5120]{1,0:T(8,128)(2,1)S(1)}, bf16[16,5120]{1,0:T(8,128)(2,1)S(1)}, u32[]{:S(2)}, u32[]{:S(2)}) %collective-permute-start.9) | collective-permute-done | bytes 163872 | tf_op jit(solution)/shard_map/ppermute | solution.py:181
  94.0 0.1 add_convert_fusion.2
  94.1 0.1 reshape.33
  94.2 0.1 reshape.34
  94.3 0.4 pad_maximum_fusion
  94.7 12.4 %all_to_all.22 = bf16[16,2,5120]{2,1,0:T(2,128)(2,1)S(1)} all-to-all(bf16[16,2,5120]{2,1,0:T(2,128)(2,1)S(1)} %pad_maximum_fusion), channel_id=1, replica_groups={{0,8,16,24,32,40,48,56,64,72,80,88,96,104,112,120},{2,10,18,26,34,42,50..., dimensions={0} | all-to-all | bytes 655360 | tf_op jit(solution)/shard_map/all_to_all | solution.py:263
  107.1 0.3 convert_reduce_fusion
  107.4 0.6 add_convert_fusion.5
  (5 shorter events, 0.1 us)
Async XLA Ops:
  0.0 33.1 %copy-start.5 = (bf16[2,5120]{1,0:T(2,128)(2,1)S(1)}, bf16[2,5120]{1,0:T(2,128)(2,1)}, u32[]{:S(2)}) copy-start(bf16[2,5120]{1,0:T(2,128)(2,1)} %activations.1) | copy-start | bytes 61444
  1.5 16.3 %all-to-all-start = ((bf16[16,16,640]{2,1,0:T(8,128)(2,1)}), bf16[16,16,640]{2,1,0:T(8,128)(2,1)S(1)}, u32[]{:S(2)}, u32[]{:S(2)}) async-start(bf16[16,16,640]{2,1,0:T(8,128)(2,1)} %broadcast_in_dim.12), calls=%async_computation | async-start | bytes 655360 | tf_op jit(solution)/shard_map/all_to_all | solution.py:219
  8.6 1.0 copy-start.3
  9.6 0.9 copy-start.4
  10.5 0.7 copy-start.6
  11.2 0.7 copy-start.7
  11.9 0.7 copy-start.8
  33.1 11.8 %copy-start = (bf16[5120,216]{0,1:T(8,128)(2,1)S(1)}, bf16[5120,216]{0,1:T(8,128)(2,1)}, u32[]{:S(2)}) copy-start(bf16[5120,216]{0,1:T(8,128)(2,1)} %param.21) | copy-start | bytes 6635524
  33.1 11.9 %copy-start.1 = (bf16[5120,216]{0,1:T(8,128)(2,1)S(1)}, bf16[5120,216]{0,1:T(8,128)(2,1)}, u32[]{:S(2)}) copy-start(bf16[5120,216]{0,1:T(8,128)(2,1)} %param.22) | copy-start | bytes 6635524
  33.1 12.6 %copy-start.2 = (bf16[216,5120]{1,0:T(8,128)(2,1)S(1)}, bf16[216,5120]{1,0:T(8,128)(2,1)}, u32[]{:S(2)}) copy-start(bf16[216,5120]{1,0:T(8,128)(2,1)} %down.1) | copy-start | bytes 6635524
  33.1 16.3 %copy-start.9 = (f32[5120]{0:T(1024)S(1)}, f32[5120]{0:T(1024)}, u32[]{:S(2)}) copy-start(f32[5120]{0:T(1024)} %param.20) | copy-start | bytes 61444
  37.6 1.4 %collective-permute-start = (bf16[8,5120]{1,0:T(8,128)(2,1)S(1)}, bf16[8,5120]{1,0:T(8,128)(2,1)S(1)}, u32[]{:S(2)}, u32[]{:S(2)}) collective-permute-start(bf16[8,5120]{1,0:T(8,128)(2,1)S(1)} %get-tuple-element.27), channel_id=1, source_target_pairs={{0,1},{1,0},{2,3},{3,2},{4,5},{5,4},{6,7},{7,6},{8,9},{9,8},{10,11... | collective-permute-start | bytes 245768 | tf_op jit(solution)/shard_map/ppermute | solution.py:195
  39.0 6.7 %collective-permute-start.3 = (bf16[8,5120]{1,0:T(8,128)(2,1)S(1)}, bf16[8,5120]{1,0:T(8,128)(2,1)S(1)}, u32[]{:S(2)}, u32[]{:S(2)}) collective-permute-start(bf16[8,5120]{1,0:T(8,128)(2,1)S(1)} %fusion), channel_id=1, source_target_pairs={{0,4},{1,5},{2,6},{3,7},{4,0},{5,1},{6,2},{7,3},{8,12},{9,13},{10,... | collective-permute-start | bytes 245768 | tf_op jit(solution)/shard_map/ppermute | solution.py:191
  42.9 5.3 %collective-permute-start.2 = (bf16[8,5120]{1,0:T(8,128)(2,1)S(1)}, bf16[8,5120]{1,0:T(8,128)(2,1)S(1)}, u32[]{:S(2)}, u32[]{:S(2)}) collective-permute-start(bf16[8,5120]{1,0:T(8,128)(2,1)S(1)} %fusion), channel_id=1, source_target_pairs={{0,6},{1,7},{2,0},{3,1},{4,2},{5,3},{6,4},{7,5},{8,14},{9,15},{10,... | collective-permute-start | bytes 245768 | tf_op jit(solution)/shard_map/ppermute | solution.py:191
  43.6 5.7 %collective-permute-start.1 = (bf16[8,5120]{1,0:T(8,128)(2,1)S(1)}, bf16[8,5120]{1,0:T(8,128)(2,1)S(1)}, u32[]{:S(2)}, u32[]{:S(2)}) collective-permute-start(bf16[8,5120]{1,0:T(8,128)(2,1)S(1)} %fusion), channel_id=1, source_target_pairs={{0,2},{1,3},{2,4},{3,5},{4,6},{5,7},{6,0},{7,1},{8,10},{9,11},{10,... | collective-permute-start | bytes 245768 | tf_op jit(solution)/shard_map/ppermute | solution.py:191
  44.9 26.6 %collective-permute-start.4 = (bf16[216,5120]{1,0:T(8,128)(2,1)S(1)}, bf16[216,5120]{1,0:T(8,128)(2,1)S(1)}, u32[]{:S(2)}, u32[]{:S(2)}) collective-permute-start(bf16[216,5120]{1,0:T(8,128)(2,1)S(1)} %bitcast.10), channel_id=1, source_target_pairs={{0,1},{1,0},{2,3},{3,2},{4,5},{5,4},{6,7},{7,6},{8,9},{9,8},{10,11... | collective-permute-start | bytes 6635528 | tf_op jit(solution)/shard_map/ppermute | solution.py:195
  45.0 26.6 %collective-permute-start.5 = (bf16[216,5120]{1,0:T(8,128)(2,1)S(1)}, bf16[216,5120]{1,0:T(8,128)(2,1)S(1)}, u32[]{:S(2)}, u32[]{:S(2)}) collective-permute-start(bf16[216,5120]{1,0:T(8,128)(2,1)S(1)} %bitcast.12), channel_id=1, source_target_pairs={{0,1},{1,0},{2,3},{3,2},{4,5},{5,4},{6,7},{7,6},{8,9},{9,8},{10,11... | collective-permute-start | bytes 6635528 | tf_op jit(solution)/shard_map/ppermute | solution.py:195
  45.7 25.9 %collective-permute-start.6 = (bf16[216,5120]{1,0:T(8,128)(2,1)S(1)}, bf16[216,5120]{1,0:T(8,128)(2,1)S(1)}, u32[]{:S(2)}, u32[]{:S(2)}) collective-permute-start(bf16[216,5120]{1,0:T(8,128)(2,1)S(1)} %copy-done.2), channel_id=1, source_target_pairs={{0,1},{1,0},{2,3},{3,2},{4,5},{5,4},{6,7},{7,6},{8,9},{9,8},{10,11... | collective-permute-start | bytes 6635528 | tf_op jit(solution)/shard_map/ppermute | solution.py:195
  75.8 7.8 %collective-permute-start.7 = (bf16[32,5120]{1,0:T(8,128)(2,1)S(1)}, bf16[32,5120]{1,0:T(8,128)(2,1)S(1)}, u32[]{:S(2)}, u32[]{:S(2)}) collective-permute-start(bf16[32,5120]{1,0:T(8,128)(2,1)S(1)} %get-tuple-element.29), channel_id=1, source_target_pairs={{0,6},{1,97},{2,0},{3,99},{4,2},{5,101},{6,4},{7,103},{8,14},{9,10... | collective-permute-start | bytes 983048 | tf_op jit(solution)/shard_map/ppermute | solution.py:181
  79.0 8.4 %collective-permute-start.8 = (bf16[32,5120]{1,0:T(8,128)(2,1)S(1)}, bf16[32,5120]{1,0:T(8,128)(2,1)S(1)}, u32[]{:S(2)}, u32[]{:S(2)}) collective-permute-start(bf16[32,5120]{1,0:T(8,128)(2,1)S(1)} %get-tuple-element.31), channel_id=1, source_target_pairs={{0,2},{1,33},{2,4},{3,35},{4,6},{5,37},{6,0},{7,39},{8,10},{9,41},... | collective-permute-start | bytes 983048 | tf_op jit(solution)/shard_map/ppermute | solution.py:181
  83.6 6.6 %collective-permute-start.10 = (bf16[16,5120]{1,0:T(8,128)(2,1)S(1)}, bf16[16,5120]{1,0:T(8,128)(2,1)S(1)}, u32[]{:S(2)}, u32[]{:S(2)}) collective-permute-start(bf16[16,5120]{1,0:T(8,128)(2,1)S(1)} %add_convert_fusion.1), channel_id=1, source_target_pairs={{0,6},{1,97},{2,0},{3,99},{4,2},{5,101},{6,4},{7,103},{8,14},{9,10... | collective-permute-start | bytes 491528 | tf_op jit(solution)/shard_map/ppermute | solution.py:181
  87.4 6.6 %collective-permute-start.9 = (bf16[16,5120]{1,0:T(8,128)(2,1)S(1)}, bf16[16,5120]{1,0:T(8,128)(2,1)S(1)}, u32[]{:S(2)}, u32[]{:S(2)}) collective-permute-start(bf16[16,5120]{1,0:T(8,128)(2,1)S(1)} %add_convert_fusion.3), channel_id=1, source_target_pairs={{0,2},{1,33},{2,4},{3,35},{4,6},{5,37},{6,0},{7,39},{8,10},{9,41},... | collective-permute-start | bytes 491528 | tf_op jit(solution)/shard_map/ppermute | solution.py:181

commit v7 on v6

--- a/solution.py
+++ b/solution.py
@@ -96,8 +96,11 @@
 
 
 def project_kernel(tp, parts, weight_far, activations, own, other, weight, sem):
-    copy = pltpu.make_async_copy(weight_far, weight, sem)
-    copy.start()
+    copies = []
+    for g in range(GROUP):
+        piece = pl.ds(g * HEAD_WIDTH, HEAD_WIDTH)
+        copies.append(pltpu.make_async_copy(weight_far.at[piece], weight.at[piece], sem.at[g]))
+        copies[g].start()
     z, core = tp[0] >> 1, tp[0] & 1
     sources = parts.shape[0]
     width = GROUP * HEAD_WIDTH
@@ -124,7 +127,8 @@
     source = (row % 8) // 2 * 4 + half * 2 + row % 2
     pick = jnp.where(col == source, 1.0, 0.0).astype(BF)
     context = mm(pick, context).astype(BF)
-    copy.wait()
+    for copy in copies:
+        copy.wait()
     result = mm(context, weight[...])
     row = lax.broadcasted_iota(jnp.int32, (8, 2), 0)
     col = lax.broadcasted_iota(jnp.int32, (8, 2), 1)
@@ -144,26 +148,22 @@
     row = lax.broadcasted_iota(jnp.int32, (n, n), 0)
     col = lax.broadcasted_iota(jnp.int32, (n, n), 1)
     x, z, core = kv[0] >> 2, tp[0] >> 1, tp[0] & 1
-    run = row // 16
-    q = (run & 1) * 8 + (row & 15) // 2
-    places = jnp.where(run < 2, 0, jnp.where((run == 2) | (run == 5), 2, jnp.where((run == 3) | (run == 6), 1, 3)))
+    block = row // 32
+    q = (row & 31) // 2
+    places = jnp.where(block == 0, 0, jnp.where(block == 1, 2, jnp.where(block == 2, 1, 3)))
     along_z = q * 8 + ((z + places) & 3) * 2
     along_x = (((x + places) & 3) * 4 + q // 4) * 8 + (q & 3) * 2
     source = jnp.where(core == 0, along_z, along_x) + (row & 1)
     return mm(jnp.where(col == source, 1.0, 0.0).astype(BF), hidden).astype(BF)
 
 
-def mlp_kernel(
-    kv, tp, rows, gate, up, down, gate_far, up_far, down_far, own, ahead, behind, rest_ahead, rest_behind
-):
+def mlp_kernel(kv, tp, rows, gate, up, down, gate_far, up_far, down_far, own, *sent):
     near = ordered(hidden_of(rows[...], gate[...], up[...]), kv, tp)
     far = ordered(hidden_of(rows[...], gate_far[...], up_far[...]), kv, tp)
     result = mm(near, down[...]) + mm(far, down_far[...])
     own[...] = result[:32]
-    ahead[...] = result[32:64].astype(BF)
-    behind[...] = result[64:96].astype(BF)
-    rest_ahead[...] = result[96:112]
-    rest_behind[...] = result[112:]
+    for k, ref in enumerate(sent):
+        ref[...] = result[32 * (k + 1) : 32 * (k + 2)].astype(BF)
 
 
 def device(x, y, z, c):
@@ -231,7 +231,7 @@
         project_kernel,
         [shape((8, D), F32), shape((8, D), BF)],
         [SM, VM, pl.ANY, VM],
-        [pltpu.VMEM(out_weight.shape, BF), pltpu.SemaphoreType.DMA],
+        [pltpu.VMEM(out_weight.shape, BF), pltpu.SemaphoreType.DMA((GROUP,))],
         limit=48 << 20,
     )(tp, parts, out_weight, activations)
     attended = own + move_core(other).astype(F32)
@@ -247,17 +247,13 @@
     ).astype(BF)
 
     rows = lax.all_to_all(jnp.broadcast_to(normed[None], (16, 8, D)), "kv", 0, 0).reshape(128, D)
-    wide, narrow = shape((32, D), BF), shape((16, D), F32)
-    mixed, ahead, behind, rest_ahead, rest_behind = call(
-        mlp_kernel, [shape((32, D), F32), wide, wide, narrow, narrow], [SM, SM] + [VM] * 7, limit=28 << 20
+    block = shape((32, D), BF)
+    mixed, *sent = call(
+        mlp_kernel, [shape((32, D), F32), block, block, block], [SM, SM] + [VM] * 7, limit=28 << 20
     )(kv, tp, rows, gate_t, up_t, down_weight, *far)
-    from_behind = move_ring(ahead, 1)
-    from_ahead = move_ring(behind, -1)
-    rest_ahead = move_ring((rest_ahead + from_behind[:16].astype(F32)).astype(BF), 1)
-    rest_behind = move_ring((rest_behind + from_ahead[16:].astype(F32)).astype(BF), -1)
-    first = mixed[:16] + from_ahead[:16].astype(F32) + rest_ahead.astype(F32)
-    second = mixed[16:] + from_behind[16:].astype(F32) + rest_behind.astype(F32)
-    mixed = jnp.concatenate([first.astype(BF).reshape(8, 2, D), second.astype(BF).reshape(8, 2, D)], axis=0)
+    for part in [move_ring(value, k) for value, k in zip(sent, (2, 1, 3))]:
+        mixed = mixed + part.astype(F32)
+    mixed = mixed.astype(BF).reshape(16, 2, D)
     keep = lax.dynamic_slice_in_dim(widened, (tp[0] >> 1) * 2, 2, 0)
     mixed, keep = lax.optimization_barrier((mixed, keep))
     mixed = lax.all_to_all(mixed, ("kv", "tp"), 0, 0, axis_index_groups=PLANES)

time: 108 us -> 110 us (1.019)
  blocking collectives: 46.8 us -> 24.9 us
  waiting for transfers between devices: 20.5 us -> 34.5 us
  Pallas kernels: 12.4 us -> 16.6 us
  starting transfers between devices: 20.7 us -> 23.6 us
  local copies, waits for them, and re-layouts: 5.66 us -> 8.32 us
    all_to_all x1 -> x0, blocking collectives: 21.9 us -> none  [local(): lax.all_to_all(jnp.broadcast_to(normed[None], (16, 8, D)), 'kv', 0, 0)]
    all_to_all x0 -> x1, waiting for transfers between devices: none -> 19.2 us  [local(): lax.all_to_all(jnp.broadcast_to(normed[None], (16, 8, D)), 'kv', 0, 0)]
    ppermute x4 -> x3, waiting for transfers between devices: 11.1 us -> 5.95 us  [move_ring(): return lax.ppermute(value, ('kv', 'tp'), pairs)]
    pallas_call x1, Pallas kernels: 4.27 us -> 8.44 us  [local(): call(mlp_kernel, [shape((32, D), F32), block, block, block], [SM, SM] + [...]
    all_to_all x0 -> x1, starting transfers between devices: none -> 3.72 us  [local(): lax.all_to_all(jnp.broadcast_to(normed[None], (16, 8, D)), 'kv', 0, 0)]
    ppermute x4 -> x3, starting transfers between devices: 7.01 us -> 6.13 us  [move_ring(): return lax.ppermute(value, ('kv', 'tp'), pairs)]
    unnamed x20 -> x18, local copies, waits for them, and re-layouts: 3.9 us -> 4.57 us
  transfers between devices with their start and end apart: 12 -> 12, of which waited for: 8 -> 9; matrix products, arithmetic and copies ran while one was open for 0% -> 2% of each run, Pallas kernels for 1% -> 1%
where the time goes in v7:
time: 110 us; the launch traced here: 109 us
  waiting for transfers between devices  34.5 us (31%)
  blocking collectives  24.9 us (23%)
  starting transfers between devices  23.6 us (21%)
  Pallas kernels  16.6 us (15%)
  local copies, waits for them, and re-layouts  8.32 us (8%)
  other arithmetic  1.31 us (1%)
    all_to_all x1, waiting for transfers between devices, local(): lax.all_to_all(jnp.broadcast_to(normed[None], (16, 8, D)), 'kv', 0, 0)  19.2 us
    all_to_all x1, blocking collectives, local(): parts = lax.all_to_all(packed.reshape(16, 16, 768), 'kv', 0, 0)  12.6 us
    all_to_all x1, blocking collectives, local(): mixed = lax.all_to_all(mixed, ('kv', 'tp'), 0, 0, axis_index_groups=PLANES)  12.3 us
    pallas_call x1, Pallas kernels, local(): call(mlp_kernel, [shape((32, D), F32), block, block, block], [SM, SM] + [...  8.44 us
    all_to_all x1, starting transfers between devices, local(): lax.all_to_all(jnp.broadcast_to(queries[None], (16, 16, 640)), 'kv', 0, 0)  7.12 us
    ppermute x3, starting transfers between devices, move_ring(): return lax.ppermute(value, ('kv', 'tp'), pairs)  6.13 us
    ppermute x3, starting transfers between devices, move_z(): return lax.ppermute(value, 'tp', pairs)  5.98 us
    ppermute x3, waiting for transfers between devices, move_ring(): return lax.ppermute(value, ('kv', 'tp'), pairs)  5.95 us
  transfers between devices with their start and end apart: 12, of which 9 were waited for; matrix products, arithmetic and copies ran while one was open for 2% of the time, Pallas kernels for 1%

profile of v7, /device:TPU:0, one launch (start us, length us, event | category | flops | bytes accessed | tf_op | source)
XLA Modules:
  0.0 109.4 jit_solution(9722698632260237935)
XLA Ops:
  0.0 0.0 copy-start.3
  0.0 1.5 %broadcast_in_dim.12 = bf16[16,16,640]{2,1,0:T(8,128)(2,1)} broadcast(bf16[16,640]{1,0:T(8,128)(2,1)} %param.13), dimensions={1,2} | broadcast | bytes 348160 | tf_op jit(solution)/shard_map/broadcast_in_dim | solution.py:219
  1.5 7.1 %all-to-all-start = ((bf16[16,16,640]{2,1,0:T(8,128)(2,1)}), bf16[16,16,640]{2,1,0:T(8,128)(2,1)S(1)}, u32[]{:S(2)}, u32[]{:S(2)}) async-start(bf16[16,16,640]{2,1,0:T(8,128)(2,1)} %broadcast_in_dim.12), calls=%async_computation | async-start | bytes 655360 | tf_op jit(solution)/shard_map/all_to_all | solution.py:219
  8.6 0.0 copy-start.1
  8.6 0.9 copy-done.1
  9.6 0.0 copy-start.2
  9.6 0.9 copy-done.2
  10.5 0.0 copy-start.4
  10.5 0.7 copy-done.4
  11.2 0.0 copy-start.5
  11.2 0.7 copy-done.5
  11.9 0.0 copy-start.6
  11.9 0.7 copy-done.6
  12.5 1.0 shard_map.118
  13.5 4.3 %all-to-all-done = bf16[16,16,640]{2,1,0:T(8,128)(2,1)S(1)} async-done(((bf16[16,16,640]{2,1,0:T(8,128)(2,1)}), bf16[16,16,640]{2,1,0:T(8,128)(2,1)S(1)}, u32[]{:S(2)}, u32[]{:S(2)}) %all-to-all-start) | async-done | bytes 327712 | tf_op jit(solution)/shard_map/all_to_all | solution.py:219
  17.8 2.7 %shard_map.119 = bf16[256,768]{1,0:T(8,128)(2,1)S(1)} custom-call(bf16[256,640]{1,0:T(8,128)(2,1)S(1)} %bitcast.13, bf16[1024,256]{1,0:T(8,128)(2,1)S(1)} %get-tuple-element.22.keys_wide, bf16[1024,128]{1,0:T(8,128)(2,1)S(1)} %get-tuple-element.23.values, bf16[256,128]{1,0:T(8,128)(2,1)S(1)} %get-tuple-element.24.onehot), custom_call_target="tpu_custom_call" | custom-call | tf_op jit(solution)/shard_map/pallas_call | solution.py:226
  20.5 12.6 %all_to_all.20.parts = bf16[16,16,768]{2,1,0:T(8,128)(2,1)S(1)} all-to-all(bf16[16,16,768]{2,1,0:T(8,128)(2,1)S(1)} %bitcast.12), channel_id=1, replica_groups=mesh['kv'=16,'tp'=8] {'kv'}, dimensions={0} | all-to-all | bytes 786432 | tf_op jit(solution)/shard_map/all_to_all | solution.py:229
  33.1 0.0 copy-done.3
  33.1 0.0 copy-start
  33.1 0.0 copy-start.8
  33.1 4.5 %shard_map.120 = (f32[8,5120]{1,0:T(8,128)S(1)}, bf16[8,5120]{1,0:T(8,128)(2,1)S(1)}) custom-call(s32[1]{0:T(128)} %bitcast.1.tp, bf16[16,16,768]{2,1,0:T(8,128)(2,1)S(1)} %all_to_all.20.parts, bf16[640,5120]{1,0:T(8,128)(2,1)} %weight_far.1, bf16[2,5120]{1,0:T(2,128)(2,1)S(1)} %copy-done.3), custom_call_target="tpu_custom_call" | custom-call | tf_op jit(solution)/shard_map/pallas_call | solution.py:230
  37.6 0.1 collective-permute-start
  37.7 1.3 %collective-permute-done = bf16[8,5120]{1,0:T(8,128)(2,1)S(1)} collective-permute-done((bf16[8,5120]{1,0:T(8,128)(2,1)S(1)}, bf16[8,5120]{1,0:T(8,128)(2,1)S(1)}, u32[]{:S(2)}, u32[]{:S(2)}) %collective-permute-start) | collective-permute-done | bytes 81952 | tf_op jit(solution)/shard_map/ppermute | solution.py:195
  39.0 4.0 %collective-permute-start.3 = (bf16[8,5120]{1,0:T(8,128)(2,1)S(1)}, bf16[8,5120]{1,0:T(8,128)(2,1)S(1)}, u32[]{:S(2)}, u32[]{:S(2)}) collective-permute-start(bf16[8,5120]{1,0:T(8,128)(2,1)S(1)} %fusion), channel_id=1, source_target_pairs={{0,4},{1,5},{2,6},{3,7},{4,0},{5,1},{6,2},{7,3},{8,12},{9,13},{10,... | collective-permute-start | bytes 245768 | tf_op jit(solution)/shard_map/ppermute | solution.py:191
  42.9 0.7 collective-permute-start.2
  43.7 1.3 %collective-permute-start.1 = (bf16[8,5120]{1,0:T(8,128)(2,1)S(1)}, bf16[8,5120]{1,0:T(8,128)(2,1)S(1)}, u32[]{:S(2)}, u32[]{:S(2)}) collective-permute-start(bf16[8,5120]{1,0:T(8,128)(2,1)S(1)} %fusion), channel_id=1, source_target_pairs={{0,2},{1,3},{2,4},{3,5},{4,6},{5,7},{6,0},{7,1},{8,10},{9,11},{10,... | collective-permute-start | bytes 245768 | tf_op jit(solution)/shard_map/ppermute | solution.py:191
  45.0 0.0 copy-done
  45.0 0.0 collective-permute-start.4
  45.0 0.5 collective-permute-start.5
  45.5 0.2 collective-permute-done.3
  45.7 0.0 collective-permute-start.6
  45.7 2.5 %collective-permute-done.2 = bf16[8,5120]{1,0:T(8,128)(2,1)S(1)} collective-permute-done((bf16[8,5120]{1,0:T(8,128)(2,1)S(1)}, bf16[8,5120]{1,0:T(8,128)(2,1)S(1)}, u32[]{:S(2)}, u32[]{:S(2)}) %collective-permute-start.2) | collective-permute-done | bytes 81952 | tf_op jit(solution)/shard_map/ppermute | solution.py:191
  48.2 1.1 collective-permute-done.1
  49.3 0.2 multiply_reduce_fusion
  49.5 0.0 copy-start.7
  49.5 0.7 copy-done.7
  50.2 0.0 copy-done.8
  50.2 0.1 multiply_convert_fusion
  50.3 1.2 %broadcast_in_dim.27 = bf16[16,8,5120]{2,1,0:T(8,128)(2,1)} broadcast(bf16[8,5120]{1,0:T(8,128)(2,1)S(1)} %multiply_convert_fusion), dimensions={1,2} | broadcast | bytes 1392640 | tf_op jit(solution)/shard_map/broadcast_in_dim | solution.py:249
  51.5 3.7 %all-to-all-start.2 = ((bf16[16,8,5120]{2,1,0:T(8,128)(2,1)}), bf16[16,8,5120]{2,1,0:T(8,128)(2,1)S(1)}, u32[]{:S(2)}, u32[]{:S(2)}) async-start(bf16[16,8,5120]{2,1,0:T(8,128)(2,1)} %broadcast_in_dim.27), calls=%async_computation.2 | async-start | bytes 2621440 | tf_op jit(solution)/shard_map/all_to_all | solution.py:249
  55.2 19.2 %all-to-all-done.2 = bf16[16,8,5120]{2,1,0:T(8,128)(2,1)S(1)} async-done(((bf16[16,8,5120]{2,1,0:T(8,128)(2,1)}), bf16[16,8,5120]{2,1,0:T(8,128)(2,1)S(1)}, u32[]{:S(2)}, u32[]{:S(2)}) %all-to-all-start.2) | async-done | bytes 1310752 | tf_op jit(solution)/shard_map/all_to_all | solution.py:249
  74.4 0.0 collective-permute-done.4.gate_far
  74.4 0.0 collective-permute-done.5.up_far
  74.4 0.0 collective-permute-done.6.down_far
  74.4 8.4 %shard_map.121 = (f32[32,5120]{1,0:T(8,128)S(1)}, bf16[32,5120]{1,0:T(8,128)(2,1)S(1)}, bf16[32,5120]{1,0:T(8,128)(2,1)S(1)}, bf16[32,5120]{1,0:T(8,128)(2,1)S(1)}) custom-call(s32[1]{0:T(128)} %bitcast.kv, s32[1]{0:T(128)} %bitcast.1.tp, bf16[128,5120]{1,0:T(8,128)(2,1)S(1)} %bitcast.9, bf16[216,5120]{1,0:T(8,128)(2,1)S(1)} %bitcast.11, ...), custom_call_target="tpu_custom_call" | custom-call | tf_op jit(solution)/shard_map/pallas_call | solution.py:251
  82.8 2.9 %collective-permute-start.7 = (bf16[32,5120]{1,0:T(8,128)(2,1)S(1)}, bf16[32,5120]{1,0:T(8,128)(2,1)S(1)}, u32[]{:S(2)}, u32[]{:S(2)}) collective-permute-start(bf16[32,5120]{1,0:T(8,128)(2,1)S(1)} %get-tuple-element.28), channel_id=1, source_target_pairs={{0,4},{1,65},{2,6},{3,67},{4,0},{5,69},{6,2},{7,71},{8,12},{9,73},... | collective-permute-start | bytes 983048 | tf_op jit(solution)/shard_map/ppermute | solution.py:181
  85.7 1.6 %collective-permute-start.8 = (bf16[32,5120]{1,0:T(8,128)(2,1)S(1)}, bf16[32,5120]{1,0:T(8,128)(2,1)S(1)}, u32[]{:S(2)}, u32[]{:S(2)}) collective-permute-start(bf16[32,5120]{1,0:T(8,128)(2,1)S(1)} %get-tuple-element.29), channel_id=1, source_target_pairs={{0,2},{1,33},{2,4},{3,35},{4,6},{5,37},{6,0},{7,39},{8,10},{9,41},... | collective-permute-start | bytes 983048 | tf_op jit(solution)/shard_map/ppermute | solution.py:181
  87.3 1.7 %collective-permute-start.9 = (bf16[32,5120]{1,0:T(8,128)(2,1)S(1)}, bf16[32,5120]{1,0:T(8,128)(2,1)S(1)}, u32[]{:S(2)}, u32[]{:S(2)}) collective-permute-start(bf16[32,5120]{1,0:T(8,128)(2,1)S(1)} %get-tuple-element.30), channel_id=1, source_target_pairs={{0,6},{1,97},{2,0},{3,99},{4,2},{5,101},{6,4},{7,103},{8,14},{9,10... | collective-permute-start | bytes 983048 | tf_op jit(solution)/shard_map/ppermute | solution.py:181
  89.0 0.9 constant_dynamic-slice_fusion
  89.9 1.7 %collective-permute-done.7 = bf16[32,5120]{1,0:T(8,128)(2,1)S(1)} collective-permute-done((bf16[32,5120]{1,0:T(8,128)(2,1)S(1)}, bf16[32,5120]{1,0:T(8,128)(2,1)S(1)}, u32[]{:S(2)}, u32[]{:S(2)}) %collective-permute-start.7) | collective-permute-done | bytes 327712 | tf_op jit(solution)/shard_map/ppermute | solution.py:181
  91.6 3.4 %collective-permute-done.8 = bf16[32,5120]{1,0:T(8,128)(2,1)S(1)} collective-permute-done((bf16[32,5120]{1,0:T(8,128)(2,1)S(1)}, bf16[32,5120]{1,0:T(8,128)(2,1)S(1)}, u32[]{:S(2)}, u32[]{:S(2)}) %collective-permute-start.8) | collective-permute-done | bytes 327712 | tf_op jit(solution)/shard_map/ppermute | solution.py:181
  95.0 0.8 collective-permute-done.9
  95.9 0.1 add_convert_fusion
  96.0 0.1 reshape.30
  96.1 12.3 %all_to_all.21 = bf16[16,2,5120]{2,1,0:T(2,128)(2,1)S(1)} all-to-all(bf16[16,2,5120]{2,1,0:T(2,128)(2,1)S(1)} %reshape.30), channel_id=1, replica_groups={{0,8,16,24,32,40,48,56,64,72,80,88,96,104,112,120},{2,10,18,26,34,42,50..., dimensions={0} | all-to-all | bytes 655360 | tf_op jit(solution)/shard_map/all_to_all | solution.py:259
  108.5 0.3 convert_reduce_fusion
  108.7 0.6 add_convert_fusion.2
  (2 shorter events, 0.0 us)
Async XLA Ops:
  0.0 33.1 %copy-start.3 = (bf16[2,5120]{1,0:T(2,128)(2,1)S(1)}, bf16[2,5120]{1,0:T(2,128)(2,1)}, u32[]{:S(2)}) copy-start(bf16[2,5120]{1,0:T(2,128)(2,1)} %activations.1) | copy-start | bytes 61444
  1.5 16.3 %all-to-all-start = ((bf16[16,16,640]{2,1,0:T(8,128)(2,1)}), bf16[16,16,640]{2,1,0:T(8,128)(2,1)S(1)}, u32[]{:S(2)}, u32[]{:S(2)}) async-start(bf16[16,16,640]{2,1,0:T(8,128)(2,1)} %broadcast_in_dim.12), calls=%async_computation | async-start | bytes 655360 | tf_op jit(solution)/shard_map/all_to_all | solution.py:219
  8.6 1.0 copy-start.1
  9.6 0.9 copy-start.2
  10.5 0.7 copy-start.4
  11.2 0.7 copy-start.5
  11.9 0.7 copy-start.6
  33.1 11.9 %copy-start = (bf16[5120,216]{0,1:T(8,128)(2,1)S(1)}, bf16[5120,216]{0,1:T(8,128)(2,1)}, u32[]{:S(2)}) copy-start(bf16[5120,216]{0,1:T(8,128)(2,1)} %param.21) | copy-start | bytes 6635524
  33.1 17.1 %copy-start.8 = (f32[5120]{0:T(1024)S(1)}, f32[5120]{0:T(1024)}, u32[]{:S(2)}) copy-start(f32[5120]{0:T(1024)} %param.20) | copy-start | bytes 61444
  37.6 1.4 %collective-permute-start = (bf16[8,5120]{1,0:T(8,128)(2,1)S(1)}, bf16[8,5120]{1,0:T(8,128)(2,1)S(1)}, u32[]{:S(2)}, u32[]{:S(2)}) collective-permute-start(bf16[8,5120]{1,0:T(8,128)(2,1)S(1)} %get-tuple-element.26), channel_id=1, source_target_pairs={{0,1},{1,0},{2,3},{3,2},{4,5},{5,4},{6,7},{7,6},{8,9},{9,8},{10,11... | collective-permute-start | bytes 245768 | tf_op jit(solution)/shard_map/ppermute | solution.py:195
  39.0 6.7 %collective-permute-start.3 = (bf16[8,5120]{1,0:T(8,128)(2,1)S(1)}, bf16[8,5120]{1,0:T(8,128)(2,1)S(1)}, u32[]{:S(2)}, u32[]{:S(2)}) collective-permute-start(bf16[8,5120]{1,0:T(8,128)(2,1)S(1)} %fusion), channel_id=1, source_target_pairs={{0,4},{1,5},{2,6},{3,7},{4,0},{5,1},{6,2},{7,3},{8,12},{9,13},{10,... | collective-permute-start | bytes 245768 | tf_op jit(solution)/shard_map/ppermute | solution.py:191
  42.9 5.3 %collective-permute-start.2 = (bf16[8,5120]{1,0:T(8,128)(2,1)S(1)}, bf16[8,5120]{1,0:T(8,128)(2,1)S(1)}, u32[]{:S(2)}, u32[]{:S(2)}) collective-permute-start(bf16[8,5120]{1,0:T(8,128)(2,1)S(1)} %fusion), channel_id=1, source_target_pairs={{0,6},{1,7},{2,0},{3,1},{4,2},{5,3},{6,4},{7,5},{8,14},{9,15},{10,... | collective-permute-start | bytes 245768 | tf_op jit(solution)/shard_map/ppermute | solution.py:191
  43.7 5.7 %collective-permute-start.1 = (bf16[8,5120]{1,0:T(8,128)(2,1)S(1)}, bf16[8,5120]{1,0:T(8,128)(2,1)S(1)}, u32[]{:S(2)}, u32[]{:S(2)}) collective-permute-start(bf16[8,5120]{1,0:T(8,128)(2,1)S(1)} %fusion), channel_id=1, source_target_pairs={{0,2},{1,3},{2,4},{3,5},{4,6},{5,7},{6,0},{7,1},{8,10},{9,11},{10,... | collective-permute-start | bytes 245768 | tf_op jit(solution)/shard_map/ppermute | solution.py:191
  45.0 29.4 %collective-permute-start.4 = (bf16[216,5120]{1,0:T(8,128)(2,1)S(1)}, bf16[216,5120]{1,0:T(8,128)(2,1)}, u32[]{:S(2)}, u32[]{:S(2)}) collective-permute-start(bf16[216,5120]{1,0:T(8,128)(2,1)S(1)} %bitcast.10), channel_id=1, source_target_pairs={{0,1},{1,0},{2,3},{3,2},{4,5},{5,4},{6,7},{7,6},{8,9},{9,8},{10,11... | collective-permute-start | bytes 6635528 | tf_op jit(solution)/shard_map/ppermute | solution.py:195
  45.0 29.4 %collective-permute-start.5 = (bf16[216,5120]{1,0:T(8,128)(2,1)}, bf16[216,5120]{1,0:T(8,128)(2,1)}, u32[]{:S(2)}, u32[]{:S(2)}) collective-permute-start(bf16[216,5120]{1,0:T(8,128)(2,1)} %bitcast.7.up), channel_id=1, source_target_pairs={{0,1},{1,0},{2,3},{3,2},{4,5},{5,4},{6,7},{7,6},{8,9},{9,8},{10,11... | collective-permute-start | bytes 6635528 | tf_op jit(solution)/shard_map/ppermute | solution.py:195
  45.7 28.7 %collective-permute-start.6 = (bf16[216,5120]{1,0:T(8,128)(2,1)}, bf16[216,5120]{1,0:T(8,128)(2,1)}, u32[]{:S(2)}, u32[]{:S(2)}) collective-permute-start(bf16[216,5120]{1,0:T(8,128)(2,1)} %down.1), channel_id=1, source_target_pairs={{0,1},{1,0},{2,3},{3,2},{4,5},{5,4},{6,7},{7,6},{8,9},{9,8},{10,11... | collective-permute-start | bytes 6635528 | tf_op jit(solution)/shard_map/ppermute | solution.py:195
  49.5 0.7 copy-start.7
  51.5 22.9 %all-to-all-start.2 = ((bf16[16,8,5120]{2,1,0:T(8,128)(2,1)}), bf16[16,8,5120]{2,1,0:T(8,128)(2,1)S(1)}, u32[]{:S(2)}, u32[]{:S(2)}) async-start(bf16[16,8,5120]{2,1,0:T(8,128)(2,1)} %broadcast_in_dim.27), calls=%async_computation.2 | async-start | bytes 2621440 | tf_op jit(solution)/shard_map/all_to_all | solution.py:249
  82.8 8.8 %collective-permute-start.7 = (bf16[32,5120]{1,0:T(8,128)(2,1)S(1)}, bf16[32,5120]{1,0:T(8,128)(2,1)S(1)}, u32[]{:S(2)}, u32[]{:S(2)}) collective-permute-start(bf16[32,5120]{1,0:T(8,128)(2,1)S(1)} %get-tuple-element.28), channel_id=1, source_target_pairs={{0,4},{1,65},{2,6},{3,67},{4,0},{5,69},{6,2},{7,71},{8,12},{9,73},... | collective-permute-start | bytes 983048 | tf_op jit(solution)/shard_map/ppermute | solution.py:181
  85.7 9.3 %collective-permute-start.8 = (bf16[32,5120]{1,0:T(8,128)(2,1)S(1)}, bf16[32,5120]{1,0:T(8,128)(2,1)S(1)}, u32[]{:S(2)}, u32[]{:S(2)}) collective-permute-start(bf16[32,5120]{1,0:T(8,128)(2,1)S(1)} %get-tuple-element.29), channel_id=1, source_target_pairs={{0,2},{1,33},{2,4},{3,35},{4,6},{5,37},{6,0},{7,39},{8,10},{9,41},... | collective-permute-start | bytes 983048 | tf_op jit(solution)/shard_map/ppermute | solution.py:181
  87.3 8.6 %collective-permute-start.9 = (bf16[32,5120]{1,0:T(8,128)(2,1)S(1)}, bf16[32,5120]{1,0:T(8,128)(2,1)S(1)}, u32[]{:S(2)}, u32[]{:S(2)}) collective-permute-start(bf16[32,5120]{1,0:T(8,128)(2,1)S(1)} %get-tuple-element.30), channel_id=1, source_target_pairs={{0,6},{1,97},{2,0},{3,99},{4,2},{5,101},{6,4},{7,103},{8,14},{9,10... | collective-permute-start | bytes 983048 | tf_op jit(solution)/shard_map/ppermute | solution.py:181

commit v8 on v7

--- a/solution.py
+++ b/solution.py
@@ -76,7 +76,7 @@
     onehot[...] = jnp.where(node == leaf[...], 1.0, 0.0).astype(F32).T.astype(BF)
 
 
-def attend_kernel(q, keys_wide, values, onehot, out):
+def attend_kernel(q, keys_wide, values, onehot, weight, out):
     tokens = q.shape[0]
     lane_t = lax.broadcasted_iota(jnp.int32, (tokens, 128), 1)
     stats = jnp.zeros((tokens, 128), F32)
@@ -95,12 +95,7 @@
     out[:, GROUP * HEAD_WIDTH :] = stats.astype(BF)
 
 
-def project_kernel(tp, parts, weight_far, activations, own, other, weight, sem):
-    copies = []
-    for g in range(GROUP):
-        piece = pl.ds(g * HEAD_WIDTH, HEAD_WIDTH)
-        copies.append(pltpu.make_async_copy(weight_far.at[piece], weight.at[piece], sem.at[g]))
-        copies[g].start()
+def project_kernel(tp, parts, weight, activations, own, other):
     z, core = tp[0] >> 1, tp[0] & 1
     sources = parts.shape[0]
     width = GROUP * HEAD_WIDTH
@@ -127,8 +122,6 @@
     source = (row % 8) // 2 * 4 + half * 2 + row % 2
     pick = jnp.where(col == source, 1.0, 0.0).astype(BF)
     context = mm(pick, context).astype(BF)
-    for copy in copies:
-        copy.wait()
     result = mm(context, weight[...])
     row = lax.broadcasted_iota(jnp.int32, (8, 2), 0)
     col = lax.broadcasted_iota(jnp.int32, (8, 2), 1)
@@ -164,6 +157,16 @@
     own[...] = result[:32]
     for k, ref in enumerate(sent):
         ref[...] = result[32 * (k + 1) : 32 * (k + 2)].astype(BF)
+
+
+def finish_kernel(tp, residual, parts, out):
+    row = lax.broadcasted_iota(jnp.int32, (2, 8), 0)
+    col = lax.broadcasted_iota(jnp.int32, (2, 8), 1)
+    pick = jnp.where(col == (tp[0] >> 1) * 2 + row, 1.0, 0.0).astype(BF)
+    total = mm(pick, residual[...])
+    for k in range(parts.shape[0]):
+        total = total + parts[k].astype(F32)
+    out[...] = total.astype(BF)
 
 
 def device(x, y, z, c):
@@ -223,17 +226,13 @@
         [SM, SM, SM, VM, VM, VM],
         [pltpu.SMEM((16,), jnp.int32)],
     )(node_lengths, parents, kv, token_leaf[None, :], keys, values)
-    packed = call(attend_kernel, shape((256, 768), BF), [VM] * 4, limit=12 << 20)(
-        q.reshape(256, 640), keys_wide, values_in, onehot
+    packed = call(attend_kernel, shape((256, 768), BF), [VM] * 4 + [pl.ANY], limit=48 << 20)(
+        q.reshape(256, 640), keys_wide, values_in, onehot, out_weight
     )
     parts = lax.all_to_all(packed.reshape(16, 16, 768), "kv", 0, 0)
-    own, other = call(
-        project_kernel,
-        [shape((8, D), F32), shape((8, D), BF)],
-        [SM, VM, pl.ANY, VM],
-        [pltpu.VMEM(out_weight.shape, BF), pltpu.SemaphoreType.DMA((GROUP,))],
-        limit=48 << 20,
-    )(tp, parts, out_weight, activations)
+    own, other = call(project_kernel, [shape((8, D), F32), shape((8, D), BF)], [SM, VM, VM, VM])(
+        tp, parts, out_weight, activations
+    )
     attended = own + move_core(other).astype(F32)
     sent = attended.astype(BF)
     for part in [move_z(sent, k) for k in (1, 3, 2)]:
@@ -254,10 +253,8 @@
     for part in [move_ring(value, k) for value, k in zip(sent, (2, 1, 3))]:
         mixed = mixed + part.astype(F32)
     mixed = mixed.astype(BF).reshape(16, 2, D)
-    keep = lax.dynamic_slice_in_dim(widened, (tp[0] >> 1) * 2, 2, 0)
-    mixed, keep = lax.optimization_barrier((mixed, keep))
     mixed = lax.all_to_all(mixed, ("kv", "tp"), 0, 0, axis_index_groups=PLANES)
-    return (keep + jnp.sum(mixed.astype(F32), axis=0)).astype(BF)
+    return call(finish_kernel, shape((2, D), BF), [SM, VM, VM])(tp, residual, mixed)
 
 
 def solution(mesh):

time: 110 us -> 99.4 us (0.904)
  blocking collectives: 24.9 us -> 46.8 us
  waiting for transfers between devices: 34.5 us -> 16.3 us
  Pallas kernels: 16.6 us -> 10.3 us
  starting transfers between devices: 23.6 us -> 19.4 us
  local copies, waits for them, and re-layouts: 8.32 us -> 5.64 us
    all_to_all x0 -> x1, blocking collectives: none -> 21.9 us  [local(): lax.all_to_all(jnp.broadcast_to(normed[None], (16, 8, D)), 'kv', 0, 0)]
    all_to_all x1 -> x0, waiting for transfers between devices: 19.2 us -> none  [local(): lax.all_to_all(jnp.broadcast_to(normed[None], (16, 8, D)), 'kv', 0, 0)]
    pallas_call x1, Pallas kernels: 8.44 us -> 4.24 us  [local(): call(mlp_kernel, [shape((32, D), F32), block, block, block], [SM, SM] + [...]
    all_to_all x1 -> x0, starting transfers between devices: 3.72 us -> none  [local(): lax.all_to_all(jnp.broadcast_to(normed[None], (16, 8, D)), 'kv', 0, 0)]
    pallas_call x2 -> x3, Pallas kernels: 7.2 us -> 5.08 us  [the longest x1 2.71 us: local(): call(attend_kernel, shape((256, 768), BF), [VM] * 4 + [pl.ANY], limit=48...]
    unnamed x18 -> x22, local copies, waits for them, and re-layouts: 4.57 us -> 3.91 us
  transfers between devices with their start and end apart: 12 -> 11, of which waited for: 9 -> 8; matrix products, arithmetic and copies ran while one was open for 2% -> 0% of each run, Pallas kernels for 1% -> 1%
where the time goes in v8:
time: 99.4 us; the launch traced here: 99 us
  blocking collectives  46.8 us (47%)
  starting transfers between devices  19.4 us (20%)
  waiting for transfers between devices  16.3 us (16%)
  Pallas kernels  10.3 us (10%)
  local copies, waits for them, and re-layouts  5.64 us (6%)
    all_to_all x1, blocking collectives, local(): lax.all_to_all(jnp.broadcast_to(normed[None], (16, 8, D)), 'kv', 0, 0)  21.9 us
    all_to_all x1, blocking collectives, local(): parts = lax.all_to_all(packed.reshape(16, 16, 768), 'kv', 0, 0)  12.6 us
    all_to_all x1, blocking collectives, local(): mixed = lax.all_to_all(mixed, ('kv', 'tp'), 0, 0, axis_index_groups=PLANES)  12.4 us
    all_to_all x1, starting transfers between devices, local(): lax.all_to_all(jnp.broadcast_to(queries[None], (16, 16, 640)), 'kv', 0, 0)  7.12 us
    ppermute x3, waiting for transfers between devices, move_ring(): return lax.ppermute(value, ('kv', 'tp'), pairs)  6.9 us
    ppermute x3, starting transfers between devices, move_z(): return lax.ppermute(value, 'tp', pairs)  5.98 us
    ppermute x3, starting transfers between devices, move_ring(): return lax.ppermute(value, ('kv', 'tp'), pairs)  5.68 us
    all_to_all x1, waiting for transfers between devices, local(): lax.all_to_all(jnp.broadcast_to(queries[None], (16, 16, 640)), 'kv', 0, 0)  4.3 us
  transfers between devices with their start and end apart: 11, of which 8 were waited for; matrix products, arithmetic and copies ran while one was open for 0% of the time, Pallas kernels for 1%

profile of v8, /device:TPU:0, one launch (start us, length us, event | category | flops | bytes accessed | tf_op | source)
XLA Modules:
  0.0 99.0 jit_solution(1756266845857914660)
XLA Ops:
  0.0 1.5 %broadcast_in_dim.12 = bf16[16,16,640]{2,1,0:T(8,128)(2,1)} broadcast(bf16[16,640]{1,0:T(8,128)(2,1)} %param.13), dimensions={1,2} | broadcast | bytes 348160 | tf_op jit(solution)/shard_map/broadcast_in_dim | solution.py:222
  1.5 7.1 %all-to-all-start = ((bf16[16,16,640]{2,1,0:T(8,128)(2,1)}), bf16[16,16,640]{2,1,0:T(8,128)(2,1)S(1)}, u32[]{:S(2)}, u32[]{:S(2)}) async-start(bf16[16,16,640]{2,1,0:T(8,128)(2,1)} %broadcast_in_dim.12), calls=%async_computation | async-start | bytes 655360 | tf_op jit(solution)/shard_map/all_to_all | solution.py:222
  8.6 0.0 copy-start.4
  8.6 0.9 copy-done.4
  9.6 0.0 copy-start.5
  9.6 0.9 copy-done.5
  10.5 0.0 copy-start.7
  10.5 0.7 copy-done.7
  11.2 0.0 copy-start.8
  11.2 0.7 copy-done.8
  11.8 0.0 copy-start.9
  11.9 0.7 copy-done.9
  12.5 1.0 shard_map.118
  13.5 4.3 %all-to-all-done = bf16[16,16,640]{2,1,0:T(8,128)(2,1)S(1)} async-done(((bf16[16,16,640]{2,1,0:T(8,128)(2,1)}), bf16[16,16,640]{2,1,0:T(8,128)(2,1)S(1)}, u32[]{:S(2)}, u32[]{:S(2)}) %all-to-all-start) | async-done | bytes 327712 | tf_op jit(solution)/shard_map/all_to_all | solution.py:222
  17.8 0.0 copy-start
  17.8 0.0 copy-start.6
  17.8 2.7 %shard_map.119 = bf16[256,768]{1,0:T(8,128)(2,1)S(1)} custom-call(bf16[256,640]{1,0:T(8,128)(2,1)S(1)} %bitcast.14, bf16[1024,256]{1,0:T(8,128)(2,1)S(1)} %get-tuple-element.20.keys_wide, bf16[1024,128]{1,0:T(8,128)(2,1)S(1)} %get-tuple-element.21.values, bf16[256,128]{1,0:T(8,128)(2,1)S(1)} %get-tuple-element.22.onehot, bf16[640,5120]{1,0:T(8,128)(2,1)} %weight.3), custom_call_target="tpu_custom_call" | custom-call | tf_op jit(solution)/shard_map/pallas_call | solution.py:229
  20.5 12.6 %all_to_all.20.parts = bf16[16,16,768]{2,1,0:T(8,128)(2,1)S(1)} all-to-all(bf16[16,16,768]{2,1,0:T(8,128)(2,1)S(1)} %bitcast.13), channel_id=1, replica_groups=mesh['kv'=16,'tp'=8] {'kv'}, dimensions={0} | all-to-all | bytes 786432 | tf_op jit(solution)/shard_map/all_to_all | solution.py:232
  33.1 0.0 copy-done
  33.1 0.0 copy-done.6
  33.1 0.0 copy-start.1
  33.1 0.0 copy-start.2
  33.1 0.0 copy-start.3
  33.1 0.0 copy-start.10
  33.1 1.5 %shard_map.120 = (f32[8,5120]{1,0:T(8,128)S(1)}, bf16[8,5120]{1,0:T(8,128)(2,1)S(1)}) custom-call(s32[1]{0:T(128)} %bitcast.1.tp, bf16[16,16,768]{2,1,0:T(8,128)(2,1)S(1)} %all_to_all.20.parts, bf16[640,5120]{1,0:T(8,128)(2,1)S(1)} %copy-done, bf16[2,5120]{1,0:T(2,128)(2,1)S(1)} %copy-done.6), custom_call_target="tpu_custom_call" | custom-call | tf_op jit(solution)/shard_map/pallas_call | solution.py:233
  34.6 0.1 collective-permute-start
  34.7 1.3 %collective-permute-done = bf16[8,5120]{1,0:T(8,128)(2,1)S(1)} collective-permute-done((bf16[8,5120]{1,0:T(8,128)(2,1)S(1)}, bf16[8,5120]{1,0:T(8,128)(2,1)S(1)}, u32[]{:S(2)}, u32[]{:S(2)}) %collective-permute-start) | collective-permute-done | bytes 81952 | tf_op jit(solution)/shard_map/ppermute | solution.py:198
  36.0 4.0 %collective-permute-start.3 = (bf16[8,5120]{1,0:T(8,128)(2,1)S(1)}, bf16[8,5120]{1,0:T(8,128)(2,1)S(1)}, u32[]{:S(2)}, u32[]{:S(2)}) collective-permute-start(bf16[8,5120]{1,0:T(8,128)(2,1)S(1)} %fusion.3), channel_id=1, source_target_pairs={{0,4},{1,5},{2,6},{3,7},{4,0},{5,1},{6,2},{7,3},{8,12},{9,13},{10,... | collective-permute-start | bytes 245768 | tf_op jit(solution)/shard_map/ppermute | solution.py:194
  39.9 0.7 collective-permute-start.2
  40.6 1.3 %collective-permute-start.1 = (bf16[8,5120]{1,0:T(8,128)(2,1)S(1)}, bf16[8,5120]{1,0:T(8,128)(2,1)S(1)}, u32[]{:S(2)}, u32[]{:S(2)}) collective-permute-start(bf16[8,5120]{1,0:T(8,128)(2,1)S(1)} %fusion.3), channel_id=1, source_target_pairs={{0,2},{1,3},{2,4},{3,5},{4,6},{5,7},{6,0},{7,1},{8,10},{9,11},{10,... | collective-permute-start | bytes 245768 | tf_op jit(solution)/shard_map/ppermute | solution.py:194
  41.9 0.0 copy-done.1
  41.9 0.0 collective-permute-start.4
  41.9 0.0 copy-done.2
  42.0 0.5 collective-permute-start.5
  42.5 0.2 collective-permute-done.3
  42.7 0.0 copy-done.3
  42.7 0.0 collective-permute-start.6
  42.7 2.5 %collective-permute-done.2 = bf16[8,5120]{1,0:T(8,128)(2,1)S(1)} collective-permute-done((bf16[8,5120]{1,0:T(8,128)(2,1)S(1)}, bf16[8,5120]{1,0:T(8,128)(2,1)S(1)}, u32[]{:S(2)}, u32[]{:S(2)}) %collective-permute-start.2) | collective-permute-done | bytes 81952 | tf_op jit(solution)/shard_map/ppermute | solution.py:194
  45.2 1.1 %collective-permute-done.1 = bf16[8,5120]{1,0:T(8,128)(2,1)S(1)} collective-permute-done((bf16[8,5120]{1,0:T(8,128)(2,1)S(1)}, bf16[8,5120]{1,0:T(8,128)(2,1)S(1)}, u32[]{:S(2)}, u32[]{:S(2)}) %collective-permute-start.1) | collective-permute-done | bytes 81952 | tf_op jit(solution)/shard_map/ppermute | solution.py:194
  46.3 0.2 fusion
  46.5 0.0 copy-done.10
  46.5 0.1 fusion.2
  46.6 0.1 broadcast_in_dim.27
  46.7 21.9 %all_to_all.21 = bf16[16,8,5120]{2,1,0:T(8,128)(2,1)S(1)} all-to-all(bf16[16,8,5120]{2,1,0:T(8,128)(2,1)S(1)} %broadcast_in_dim.27), channel_id=1, replica_groups=mesh['kv'=16,'tp'=8] {'kv'}, dimensions={0} | all-to-all | bytes 2621440 | tf_op jit(solution)/shard_map/all_to_all | solution.py:248
  68.6 0.0 collective-permute-done.4.gate_far
  68.6 0.0 collective-permute-done.5.up_far
  68.6 0.0 collective-permute-done.6.down_far
  68.6 4.2 %shard_map.121 = (f32[32,5120]{1,0:T(8,128)S(1)}, bf16[32,5120]{1,0:T(8,128)(2,1)S(1)}, bf16[32,5120]{1,0:T(8,128)(2,1)S(1)}, bf16[32,5120]{1,0:T(8,128)(2,1)S(1)}) custom-call(s32[1]{0:T(128)} %bitcast.kv, s32[1]{0:T(128)} %bitcast.1.tp, bf16[128,5120]{1,0:T(8,128)(2,1)S(1)} %bitcast.8, bf16[216,5120]{1,0:T(8,128)(2,1)S(1)} %bitcast.10, ...), custom_call_target="tpu_custom_call" | custom-call | tf_op jit(solution)/shard_map/pallas_call | solution.py:250
  72.8 2.4 %collective-permute-start.7 = (bf16[32,5120]{1,0:T(8,128)(2,1)S(1)}, bf16[32,5120]{1,0:T(8,128)(2,1)S(1)}, u32[]{:S(2)}, u32[]{:S(2)}) collective-permute-start(bf16[32,5120]{1,0:T(8,128)(2,1)S(1)} %get-tuple-element.26), channel_id=1, source_target_pairs={{0,4},{1,65},{2,6},{3,67},{4,0},{5,69},{6,2},{7,71},{8,12},{9,73},... | collective-permute-start | bytes 983048 | tf_op jit(solution)/shard_map/ppermute | solution.py:184
  75.3 1.6 %collective-permute-start.8 = (bf16[32,5120]{1,0:T(8,128)(2,1)S(1)}, bf16[32,5120]{1,0:T(8,128)(2,1)S(1)}, u32[]{:S(2)}, u32[]{:S(2)}) collective-permute-start(bf16[32,5120]{1,0:T(8,128)(2,1)S(1)} %get-tuple-element.27), channel_id=1, source_target_pairs={{0,2},{1,33},{2,4},{3,35},{4,6},{5,37},{6,0},{7,39},{8,10},{9,41},... | collective-permute-start | bytes 983048 | tf_op jit(solution)/shard_map/ppermute | solution.py:184
  76.8 1.7 %collective-permute-start.9 = (bf16[32,5120]{1,0:T(8,128)(2,1)S(1)}, bf16[32,5120]{1,0:T(8,128)(2,1)S(1)}, u32[]{:S(2)}, u32[]{:S(2)}) collective-permute-start(bf16[32,5120]{1,0:T(8,128)(2,1)S(1)} %get-tuple-element.28), channel_id=1, source_target_pairs={{0,6},{1,97},{2,0},{3,99},{4,2},{5,101},{6,4},{7,103},{8,14},{9,10... | collective-permute-start | bytes 983048 | tf_op jit(solution)/shard_map/ppermute | solution.py:184
  78.5 3.1 %collective-permute-done.7 = bf16[32,5120]{1,0:T(8,128)(2,1)S(1)} collective-permute-done((bf16[32,5120]{1,0:T(8,128)(2,1)S(1)}, bf16[32,5120]{1,0:T(8,128)(2,1)S(1)}, u32[]{:S(2)}, u32[]{:S(2)}) %collective-permute-start.7) | collective-permute-done | bytes 327712 | tf_op jit(solution)/shard_map/ppermute | solution.py:184
  81.6 3.4 %collective-permute-done.8 = bf16[32,5120]{1,0:T(8,128)(2,1)S(1)} collective-permute-done((bf16[32,5120]{1,0:T(8,128)(2,1)S(1)}, bf16[32,5120]{1,0:T(8,128)(2,1)S(1)}, u32[]{:S(2)}, u32[]{:S(2)}) %collective-permute-start.8) | collective-permute-done | bytes 327712 | tf_op jit(solution)/shard_map/ppermute | solution.py:184
  85.0 0.4 collective-permute-done.9
  85.4 0.2 add_convert_fusion
  85.6 0.1 reshape.26
  85.7 12.4 %all_to_all.22.parts = bf16[16,2,5120]{2,1,0:T(2,128)(2,1)S(1)} all-to-all(bf16[16,2,5120]{2,1,0:T(2,128)(2,1)S(1)} %reshape.26), channel_id=1, replica_groups={{0,8,16,24,32,40,48,56,64,72,80,88,96,104,112,120},{2,10,18,26,34,42,50..., dimensions={0} | all-to-all | bytes 655360 | tf_op jit(solution)/shard_map/all_to_all | solution.py:256
  98.1 0.9 shard_map.122
  (2 shorter events, 0.0 us)
Async XLA Ops:
  1.5 16.3 %all-to-all-start = ((bf16[16,16,640]{2,1,0:T(8,128)(2,1)}), bf16[16,16,640]{2,1,0:T(8,128)(2,1)S(1)}, u32[]{:S(2)}, u32[]{:S(2)}) async-start(bf16[16,16,640]{2,1,0:T(8,128)(2,1)} %broadcast_in_dim.12), calls=%async_computation | async-start | bytes 655360 | tf_op jit(solution)/shard_map/all_to_all | solution.py:222
  8.6 1.0 copy-start.4
  9.6 0.9 copy-start.5
  10.5 0.7 copy-start.7
  11.2 0.7 copy-start.8
  11.8 0.7 copy-start.9
  17.8 15.3 %copy-start = (bf16[640,5120]{1,0:T(8,128)(2,1)S(1)}, bf16[640,5120]{1,0:T(8,128)(2,1)}, u32[]{:S(2)}) copy-start(bf16[640,5120]{1,0:T(8,128)(2,1)} %weight.3) | copy-start | bytes 19660804
  17.8 15.3 %copy-start.6 = (bf16[2,5120]{1,0:T(2,128)(2,1)S(1)}, bf16[2,5120]{1,0:T(2,128)(2,1)}, u32[]{:S(2)}) copy-start(bf16[2,5120]{1,0:T(2,128)(2,1)} %activations.1) | copy-start | bytes 61444
  33.1 8.8 %copy-start.1 = (bf16[5120,216]{0,1:T(8,128)(2,1)S(1)}, bf16[5120,216]{0,1:T(8,128)(2,1)}, u32[]{:S(2)}) copy-start(bf16[5120,216]{0,1:T(8,128)(2,1)} %param.21) | copy-start | bytes 6635524
  33.1 8.8 %copy-start.2 = (bf16[5120,216]{0,1:T(8,128)(2,1)S(1)}, bf16[5120,216]{0,1:T(8,128)(2,1)}, u32[]{:S(2)}) copy-start(bf16[5120,216]{0,1:T(8,128)(2,1)} %param.22) | copy-start | bytes 6635524
  33.1 9.6 %copy-start.3 = (bf16[216,5120]{1,0:T(8,128)(2,1)S(1)}, bf16[216,5120]{1,0:T(8,128)(2,1)}, u32[]{:S(2)}) copy-start(bf16[216,5120]{1,0:T(8,128)(2,1)} %down.1) | copy-start | bytes 6635524
  33.1 13.3 %copy-start.10 = (f32[5120]{0:T(1024)S(1)}, f32[5120]{0:T(1024)}, u32[]{:S(2)}) copy-start(f32[5120]{0:T(1024)} %param.20) | copy-start | bytes 61444
  34.6 1.4 %collective-permute-start = (bf16[8,5120]{1,0:T(8,128)(2,1)S(1)}, bf16[8,5120]{1,0:T(8,128)(2,1)S(1)}, u32[]{:S(2)}, u32[]{:S(2)}) collective-permute-start(bf16[8,5120]{1,0:T(8,128)(2,1)S(1)} %get-tuple-element.24), channel_id=1, source_target_pairs={{0,1},{1,0},{2,3},{3,2},{4,5},{5,4},{6,7},{7,6},{8,9},{9,8},{10,11... | collective-permute-start | bytes 245768 | tf_op jit(solution)/shard_map/ppermute | solution.py:198
  36.0 6.7 %collective-permute-start.3 = (bf16[8,5120]{1,0:T(8,128)(2,1)S(1)}, bf16[8,5120]{1,0:T(8,128)(2,1)S(1)}, u32[]{:S(2)}, u32[]{:S(2)}) collective-permute-start(bf16[8,5120]{1,0:T(8,128)(2,1)S(1)} %fusion.3), channel_id=1, source_target_pairs={{0,4},{1,5},{2,6},{3,7},{4,0},{5,1},{6,2},{7,3},{8,12},{9,13},{10,... | collective-permute-start | bytes 245768 | tf_op jit(solution)/shard_map/ppermute | solution.py:194
  39.9 5.3 %collective-permute-start.2 = (bf16[8,5120]{1,0:T(8,128)(2,1)S(1)}, bf16[8,5120]{1,0:T(8,128)(2,1)S(1)}, u32[]{:S(2)}, u32[]{:S(2)}) collective-permute-start(bf16[8,5120]{1,0:T(8,128)(2,1)S(1)} %fusion.3), channel_id=1, source_target_pairs={{0,6},{1,7},{2,0},{3,1},{4,2},{5,3},{6,4},{7,5},{8,14},{9,15},{10,... | collective-permute-start | bytes 245768 | tf_op jit(solution)/shard_map/ppermute | solution.py:194
  40.6 5.7 %collective-permute-start.1 = (bf16[8,5120]{1,0:T(8,128)(2,1)S(1)}, bf16[8,5120]{1,0:T(8,128)(2,1)S(1)}, u32[]{:S(2)}, u32[]{:S(2)}) collective-permute-start(bf16[8,5120]{1,0:T(8,128)(2,1)S(1)} %fusion.3), channel_id=1, source_target_pairs={{0,2},{1,3},{2,4},{3,5},{4,6},{5,7},{6,0},{7,1},{8,10},{9,11},{10,... | collective-permute-start | bytes 245768 | tf_op jit(solution)/shard_map/ppermute | solution.py:194
  41.9 26.6 %collective-permute-start.4 = (bf16[216,5120]{1,0:T(8,128)(2,1)S(1)}, bf16[216,5120]{1,0:T(8,128)(2,1)S(1)}, u32[]{:S(2)}, u32[]{:S(2)}) collective-permute-start(bf16[216,5120]{1,0:T(8,128)(2,1)S(1)} %bitcast.9), channel_id=1, source_target_pairs={{0,1},{1,0},{2,3},{3,2},{4,5},{5,4},{6,7},{7,6},{8,9},{9,8},{10,11... | collective-permute-start | bytes 6635528 | tf_op jit(solution)/shard_map/ppermute | solution.py:198
  42.0 26.6 %collective-permute-start.5 = (bf16[216,5120]{1,0:T(8,128)(2,1)S(1)}, bf16[216,5120]{1,0:T(8,128)(2,1)S(1)}, u32[]{:S(2)}, u32[]{:S(2)}) collective-permute-start(bf16[216,5120]{1,0:T(8,128)(2,1)S(1)} %bitcast.11), channel_id=1, source_target_pairs={{0,1},{1,0},{2,3},{3,2},{4,5},{5,4},{6,7},{7,6},{8,9},{9,8},{10,11... | collective-permute-start | bytes 6635528 | tf_op jit(solution)/shard_map/ppermute | solution.py:198
  42.7 25.9 %collective-permute-start.6 = (bf16[216,5120]{1,0:T(8,128)(2,1)S(1)}, bf16[216,5120]{1,0:T(8,128)(2,1)S(1)}, u32[]{:S(2)}, u32[]{:S(2)}) collective-permute-start(bf16[216,5120]{1,0:T(8,128)(2,1)S(1)} %copy-done.3), channel_id=1, source_target_pairs={{0,1},{1,0},{2,3},{3,2},{4,5},{5,4},{6,7},{7,6},{8,9},{9,8},{10,11... | collective-permute-start | bytes 6635528 | tf_op jit(solution)/shard_map/ppermute | solution.py:198
  72.8 8.8 %collective-permute-start.7 = (bf16[32,5120]{1,0:T(8,128)(2,1)S(1)}, bf16[32,5120]{1,0:T(8,128)(2,1)S(1)}, u32[]{:S(2)}, u32[]{:S(2)}) collective-permute-start(bf16[32,5120]{1,0:T(8,128)(2,1)S(1)} %get-tuple-element.26), channel_id=1, source_target_pairs={{0,4},{1,65},{2,6},{3,67},{4,0},{5,69},{6,2},{7,71},{8,12},{9,73},... | collective-permute-start | bytes 983048 | tf_op jit(solution)/shard_map/ppermute | solution.py:184
  75.3 9.7 %collective-permute-start.8 = (bf16[32,5120]{1,0:T(8,128)(2,1)S(1)}, bf16[32,5120]{1,0:T(8,128)(2,1)S(1)}, u32[]{:S(2)}, u32[]{:S(2)}) collective-permute-start(bf16[32,5120]{1,0:T(8,128)(2,1)S(1)} %get-tuple-element.27), channel_id=1, source_target_pairs={{0,2},{1,33},{2,4},{3,35},{4,6},{5,37},{6,0},{7,39},{8,10},{9,41},... | collective-permute-start | bytes 983048 | tf_op jit(solution)/shard_map/ppermute | solution.py:184
  76.8 8.6 %collective-permute-start.9 = (bf16[32,5120]{1,0:T(8,128)(2,1)S(1)}, bf16[32,5120]{1,0:T(8,128)(2,1)S(1)}, u32[]{:S(2)}, u32[]{:S(2)}) collective-permute-start(bf16[32,5120]{1,0:T(8,128)(2,1)S(1)} %get-tuple-element.28), channel_id=1, source_target_pairs={{0,6},{1,97},{2,0},{3,99},{4,2},{5,101},{6,4},{7,103},{8,14},{9,10... | collective-permute-start | bytes 983048 | tf_op jit(solution)/shard_map/ppermute | solution.py:184

commit v9 on v8

--- a/solution.py
+++ b/solution.py
@@ -95,7 +95,8 @@
     out[:, GROUP * HEAD_WIDTH :] = stats.astype(BF)
 
 
-def project_kernel(tp, parts, weight, activations, own, other):
+def project_kernel(tp, parts, weight, activations, *refs):
+    own, other = refs[-2:]
     z, core = tp[0] >> 1, tp[0] & 1
     sources = parts.shape[0]
     width = GROUP * HEAD_WIDTH
@@ -140,23 +141,25 @@
     n = hidden.shape[0]
     row = lax.broadcasted_iota(jnp.int32, (n, n), 0)
     col = lax.broadcasted_iota(jnp.int32, (n, n), 1)
-    x, z, core = kv[0] >> 2, tp[0] >> 1, tp[0] & 1
-    block = row // 32
-    q = (row & 31) // 2
-    places = jnp.where(block == 0, 0, jnp.where(block == 1, 2, jnp.where(block == 2, 1, 3)))
-    along_z = q * 8 + ((z + places) & 3) * 2
-    along_x = (((x + places) & 3) * 4 + q // 4) * 8 + (q & 3) * 2
-    source = jnp.where(core == 0, along_z, along_x) + (row & 1)
+    here = jnp.where((tp[0] & 1) == 0, kv[0] & 3, kv[0] >> 2)
+    places = (here + 4 - (row & 31) // 8) & 3
+    source = row // 32 * 32 + places * 8 + (row & 7)
     return mm(jnp.where(col == source, 1.0, 0.0).astype(BF), hidden).astype(BF)
 
 
-def mlp_kernel(kv, tp, rows, gate, up, down, gate_far, up_far, down_far, own, *sent):
-    near = ordered(hidden_of(rows[...], gate[...], up[...]), kv, tp)
-    far = ordered(hidden_of(rows[...], gate_far[...], up_far[...]), kv, tp)
+def mlp_kernel(kv, tp, gate, up, down, gate_far, up_far, down_far, *refs):
+    blocks = len(refs) // 2
+    rows = jnp.concatenate([ref[...] for ref in refs[:blocks]], axis=0) if blocks > 1 else refs[0][...]
+    near = ordered(hidden_of(rows, gate[...], up[...]), kv, tp)
+    far = ordered(hidden_of(rows, gate_far[...], up_far[...]), kv, tp)
     result = mm(near, down[...]) + mm(far, down_far[...])
-    own[...] = result[:32]
-    for k, ref in enumerate(sent):
-        ref[...] = result[32 * (k + 1) : 32 * (k + 2)].astype(BF)
+    for k, ref in enumerate(refs[blocks:]):
+        ref[...] = result[32 * k : 32 * (k + 1)].astype(ref.dtype)
+
+
+def stack_kernel(*refs):
+    for k, ref in enumerate(refs[:-1]):
+        refs[-1][8 * k : 8 * (k + 1)] = ref[...]
 
 
 def finish_kernel(tp, residual, parts, out):
@@ -173,9 +176,9 @@
     return (x * 4 + y) * 8 + z * 2 + c
 
 
-def move_ring(value, k):
+def move_along(value, k, first):
     pairs = [
-        (device(x, y, z, c), device(x, y, (z + k) % 4, c) if c == 0 else device((x + k) % 4, y, z, c))
+        (device(x, y, z, c), device(x, (y + k) % 4, z, c) if (c == 0) == first else device((x + k) % 4, y, z, c))
         for x in range(4)
         for y in range(4)
         for z in range(4)
@@ -184,8 +187,8 @@
     return lax.ppermute(value, ("kv", "tp"), pairs)
 
 
-PLANES = [[device(x, y, z, 0) for x in range(4) for y in range(4)] for z in range(4)] + [
-    [device(x, y, z, 1) for y in range(4) for z in range(4)] for x in range(4)
+PLANES = [[device(x, y, z, 0) for y in range(4) for z in range(4)] for x in range(4)] + [
+    [device(x, y, z, 1) for x in range(4) for z in range(4)] for y in range(4)
 ]
 
 
@@ -216,7 +219,6 @@
     tp = lax.axis_index("tp")[None]
     gate_t, up_t = gate_weight.T, up_weight.T
     shape = jax.ShapeDtypeStruct
-    far = [move_core(w) for w in (gate_t, up_t, down_weight)]
     queries, kv, tp = lax.optimization_barrier((queries, kv, tp))
 
     q = lax.all_to_all(jnp.broadcast_to(queries[None], (16, 16, 640)), "kv", 0, 0)
@@ -226,12 +228,16 @@
         [SM, SM, SM, VM, VM, VM],
         [pltpu.SMEM((16,), jnp.int32)],
     )(node_lengths, parents, kv, token_leaf[None, :], keys, values)
+    q, keys_wide, values_in, onehot, *far = lax.optimization_barrier(
+        (q, keys_wide, values_in, onehot, gate_t, up_t, down_weight)
+    )
+    far = [move_core(w) for w in far]
     packed = call(attend_kernel, shape((256, 768), BF), [VM] * 4 + [pl.ANY], limit=48 << 20)(
         q.reshape(256, 640), keys_wide, values_in, onehot, out_weight
     )
     parts = lax.all_to_all(packed.reshape(16, 16, 768), "kv", 0, 0)
-    own, other = call(project_kernel, [shape((8, D), F32), shape((8, D), BF)], [SM, VM, VM, VM])(
-        tp, parts, out_weight, activations
+    own, other = call(project_kernel, [shape((8, D), F32), shape((8, D), BF)], [SM, VM, VM, VM] + [pl.ANY] * 3)(
+        tp, parts, out_weight, activations, *far
     )
     attended = own + move_core(other).astype(F32)
     sent = attended.astype(BF)
@@ -245,12 +251,18 @@
         * norm_gain
     ).astype(BF)
 
-    rows = lax.all_to_all(jnp.broadcast_to(normed[None], (16, 8, D)), "kv", 0, 0).reshape(128, D)
-    block = shape((32, D), BF)
-    mixed, *sent = call(
-        mlp_kernel, [shape((32, D), F32), block, block, block], [SM, SM] + [VM] * 7, limit=28 << 20
-    )(kv, tp, rows, gate_t, up_t, down_weight, *far)
-    for part in [move_ring(value, k) for value, k in zip(sent, (2, 1, 3))]:
+    back = {k: move_along(normed, k, True) for k in (2, 1, 3)}
+    rows = call(stack_kernel, shape((32, D), BF), [VM] * 4)(normed, back[1], back[2], back[3])
+    weights = (kv, tp, gate_t, up_t, down_weight, *far)
+    block, wide = shape((32, D), BF), shape((32, D), F32)
+    back = {k: move_along(rows, k, False) for k in (1, 3, 2)}
+    mixed = call(mlp_kernel, wide, [SM, SM] + [VM] * 7, limit=28 << 20)(*weights, rows)
+    near = lax.optimization_barrier((back[1], back[3], mixed))
+    mixed = near[2]
+    ahead, behind = call(mlp_kernel, [block, block], [SM, SM] + [VM] * 8, limit=28 << 20)(*weights, near[0], near[1])
+    opposite, ahead, behind = lax.optimization_barrier((back[2], ahead, behind))
+    opposite = call(mlp_kernel, block, [SM, SM] + [VM] * 7, limit=28 << 20)(*weights, opposite)
+    for part in [move_along(ahead, 3, False), move_along(behind, 1, False), move_along(opposite, 2, False)]:
         mixed = mixed + part.astype(F32)
     mixed = mixed.astype(BF).reshape(16, 2, D)
     mixed = lax.all_to_all(mixed, ("kv", "tp"), 0, 0, axis_index_groups=PLANES)

time: 99.4 us -> 102 us (1.026)
  blocking collectives: 46.8 us -> 26.1 us
  waiting for transfers between devices: 16.3 us -> 29.6 us
  Pallas kernels: 10.3 us -> 17.6 us
  starting transfers between devices: 19.4 us -> 22.4 us
    all_to_all x1 -> x0, blocking collectives: 21.9 us -> none  [local(): lax.all_to_all(jnp.broadcast_to(normed[None], (16, 8, D)), 'kv', 0, 0)]
    ppermute x3 -> x9, waiting for transfers between devices: 6.9 us -> 19.7 us  [move_along(): return lax.ppermute(value, ('kv', 'tp'), pairs)]
    pallas_call x1 -> x4, Pallas kernels: 4.24 us -> 11.6 us  [the longest x1 3.92 us: local(): call(mlp_kernel, [block, block], [SM, SM] + [VM] * 8, limit=28 << 20)]
    ppermute x3 -> x9, starting transfers between devices: 5.68 us -> 8.67 us  [move_along(): return lax.ppermute(value, ('kv', 'tp'), pairs)]
    all_to_all x1, blocking collectives: 12.6 us -> 14 us  [local(): parts = lax.all_to_all(packed.reshape(16, 16, 768), 'kv', 0, 0)]
  transfers between devices with their start and end apart: 11 -> 17, of which waited for: 8 -> 12; matrix products, arithmetic and copies ran while one was open for 0% -> 0% of each run, Pallas kernels for 1% -> 15%
where the time goes in v9:
time: 102 us
  waiting for transfers between devices  29.6 us (29%)
  blocking collectives  26.1 us (26%)
  starting transfers between devices  22.4 us (22%)
  Pallas kernels  17.6 us (17%)
  local copies, waits for them, and re-layouts  5.51 us (5%)
    ppermute x9, waiting for transfers between devices, move_along(): return lax.ppermute(value, ('kv', 'tp'), pairs)  19.7 us
    all_to_all x1, blocking collectives, local(): parts = lax.all_to_all(packed.reshape(16, 16, 768), 'kv', 0, 0)  14 us
    all_to_all x1, blocking collectives, local(): mixed = lax.all_to_all(mixed, ('kv', 'tp'), 0, 0, axis_index_groups=PLANES)  12.2 us
    ppermute x9, starting transfers between devices, move_along(): return lax.ppermute(value, ('kv', 'tp'), pairs)  8.67 us
    all_to_all x1, starting transfers between devices, local(): lax.all_to_all(jnp.broadcast_to(queries[None], (16, 16, 640)), 'kv', 0, 0)  7.12 us
    ppermute x3, starting transfers between devices, move_z(): return lax.ppermute(value, 'tp', pairs)  5.98 us
    ppermute x3, waiting for transfers between devices, move_z(): return lax.ppermute(value, 'tp', pairs)  4.33 us
    all_to_all x1, waiting for transfers between devices, local(): lax.all_to_all(jnp.broadcast_to(queries[None], (16, 16, 640)), 'kv', 0, 0)  4.3 us
  transfers between devices with their start and end apart: 17, of which 12 were waited for; matrix products, arithmetic and copies ran while one was open for 0% of the time, Pallas kernels for 15%

profile of v9, /device:TPU:0, one launch (start us, length us, event | category | flops | bytes accessed | tf_op | source)
XLA Modules:
  0.0 101.9 jit_solution(15453775720278505594)
XLA Ops:
  0.0 1.5 %broadcast_in_dim.19 = bf16[16,16,640]{2,1,0:T(8,128)(2,1)} broadcast(bf16[16,640]{1,0:T(8,128)(2,1)} %param.13), dimensions={1,2} | broadcast | bytes 348160 | tf_op jit(solution)/shard_map/broadcast_in_dim | solution.py:224
  1.5 7.1 %all-to-all-start = ((bf16[16,16,640]{2,1,0:T(8,128)(2,1)}), bf16[16,16,640]{2,1,0:T(8,128)(2,1)S(1)}, u32[]{:S(2)}, u32[]{:S(2)}) async-start(bf16[16,16,640]{2,1,0:T(8,128)(2,1)} %broadcast_in_dim.19), calls=%async_computation | async-start | bytes 655360 | tf_op jit(solution)/shard_map/all_to_all | solution.py:224
  8.6 0.0 copy-start.4
  8.6 0.9 copy-done.4
  9.6 0.9 copy-done.5
  10.5 0.0 copy-start.7
  10.5 0.7 copy-done.7
  11.2 0.7 copy-done.8
  11.8 0.7 copy-done.9
  12.5 1.0 shard_map.118
  13.5 4.3 %all-to-all-done = bf16[16,16,640]{2,1,0:T(8,128)(2,1)S(1)} async-done(((bf16[16,16,640]{2,1,0:T(8,128)(2,1)}), bf16[16,16,640]{2,1,0:T(8,128)(2,1)S(1)}, u32[]{:S(2)}, u32[]{:S(2)}) %all-to-all-start) | async-done | bytes 327712 | tf_op jit(solution)/shard_map/all_to_all | solution.py:224
  17.8 0.0 collective-permute-start
  17.8 0.5 collective-permute-start.1
  18.3 0.0 collective-permute-start.2
  18.3 2.7 %shard_map.119 = bf16[256,768]{1,0:T(8,128)(2,1)S(1)} custom-call(bf16[256,640]{1,0:T(8,128)(2,1)S(1)} %bitcast.16, bf16[1024,256]{1,0:T(8,128)(2,1)S(1)} %get-tuple-element.35.keys_wide, bf16[1024,128]{1,0:T(8,128)(2,1)S(1)} %get-tuple-element.36.values, bf16[256,128]{1,0:T(8,128)(2,1)S(1)} %get-tuple-element.37.onehot, bf16[640,5120]{1,0:T(8,128)(2,1)} %weight.3), custom_call_target="tpu_custom_call" | custom-call | tf_op jit(solution)/shard_map/pallas_call | solution.py:235
  21.0 14.0 %all_to_all.15.parts = bf16[16,16,768]{2,1,0:T(8,128)(2,1)S(1)} all-to-all(bf16[16,16,768]{2,1,0:T(8,128)(2,1)S(1)} %bitcast.15), channel_id=1, replica_groups=mesh['kv'=16,'tp'=8] {'kv'}, dimensions={0} | all-to-all | bytes 786432 | tf_op jit(solution)/shard_map/all_to_all | solution.py:238
  35.0 0.0 collective-permute-done.refs_0_.gate_far
  35.0 0.0 collective-permute-done.1.refs_1_.up_far
  35.0 0.0 collective-permute-done.2.refs_2_.down_far
  35.0 0.0 copy-done
  35.0 0.0 copy-done.6
  35.0 0.0 copy-start.1
  35.0 0.0 copy-start.2
  35.0 0.0 copy-start.3
  35.0 1.4 %shard_map.120 = (f32[8,5120]{1,0:T(8,128)S(1)}, bf16[8,5120]{1,0:T(8,128)(2,1)S(1)}) custom-call(s32[1]{0:T(128)} %bitcast.1.tp, bf16[16,16,768]{2,1,0:T(8,128)(2,1)S(1)} %all_to_all.15.parts, bf16[640,5120]{1,0:T(8,128)(2,1)S(1)} %copy-done, bf16[2,5120]{1,0:T(2,128)(2,1)S(1)} %copy-done.6, bf16[216,5120]{1,0:T(8,128)(2,1)S(1)} %collective-permute-done.refs_0_.gate_far, ...), custom_call_target="tpu_custom_call" | custom-call | tf_op jit(solution)/shard_map/pallas_call | solution.py:239
  36.5 0.1 collective-permute-start.3
  36.6 1.3 %collective-permute-done.3 = bf16[8,5120]{1,0:T(8,128)(2,1)S(1)} collective-permute-done((bf16[8,5120]{1,0:T(8,128)(2,1)S(1)}, bf16[8,5120]{1,0:T(8,128)(2,1)S(1)}, u32[]{:S(2)}, u32[]{:S(2)}) %collective-permute-start.3) | collective-permute-done | bytes 81952 | tf_op jit(solution)/shard_map/ppermute | solution.py:201
  37.9 4.0 %collective-permute-start.6 = (bf16[8,5120]{1,0:T(8,128)(2,1)S(1)}, bf16[8,5120]{1,0:T(8,128)(2,1)S(1)}, u32[]{:S(2)}, u32[]{:S(2)}) collective-permute-start(bf16[8,5120]{1,0:T(8,128)(2,1)S(1)} %fusion.3), channel_id=1, source_target_pairs={{0,4},{1,5},{2,6},{3,7},{4,0},{5,1},{6,2},{7,3},{8,12},{9,13},{10,... | collective-permute-start | bytes 245768 | tf_op jit(solution)/shard_map/ppermute | solution.py:197
  41.8 0.7 collective-permute-start.5
  42.5 1.3 %collective-permute-start.4 = (bf16[8,5120]{1,0:T(8,128)(2,1)S(1)}, bf16[8,5120]{1,0:T(8,128)(2,1)S(1)}, u32[]{:S(2)}, u32[]{:S(2)}) collective-permute-start(bf16[8,5120]{1,0:T(8,128)(2,1)S(1)} %fusion.3), channel_id=1, source_target_pairs={{0,2},{1,3},{2,4},{3,5},{4,6},{5,7},{6,0},{7,1},{8,10},{9,11},{10,... | collective-permute-start | bytes 245768 | tf_op jit(solution)/shard_map/ppermute | solution.py:197
  43.9 0.7 collective-permute-done.6
  44.6 2.5 %collective-permute-done.5 = bf16[8,5120]{1,0:T(8,128)(2,1)S(1)} collective-permute-done((bf16[8,5120]{1,0:T(8,128)(2,1)S(1)}, bf16[8,5120]{1,0:T(8,128)(2,1)S(1)}, u32[]{:S(2)}, u32[]{:S(2)}) %collective-permute-start.5) | collective-permute-done | bytes 81952 | tf_op jit(solution)/shard_map/ppermute | solution.py:197
  47.1 1.1 %collective-permute-done.4 = bf16[8,5120]{1,0:T(8,128)(2,1)S(1)} collective-permute-done((bf16[8,5120]{1,0:T(8,128)(2,1)S(1)}, bf16[8,5120]{1,0:T(8,128)(2,1)S(1)}, u32[]{:S(2)}, u32[]{:S(2)}) %collective-permute-start.4) | collective-permute-done | bytes 81952 | tf_op jit(solution)/shard_map/ppermute | solution.py:197
  48.2 0.2 fusion
  48.4 0.0 copy-done.10
  48.4 0.1 fusion.2.refs_0_
  48.5 0.9 collective-permute-start.9
  49.4 1.6 %collective-permute-start.8 = (bf16[8,5120]{1,0:T(8,128)(2,1)S(1)}, bf16[8,5120]{1,0:T(8,128)(2,1)S(1)}, u32[]{:S(2)}, u32[]{:S(2)}) collective-permute-start(bf16[8,5120]{1,0:T(8,128)(2,1)S(1)} %fusion.2.refs_0_), channel_id=1, source_target_pairs={{0,16},{1,65},{2,18},{3,67},{4,20},{5,69},{6,22},{7,71},{8,24},{9,... | collective-permute-start | bytes 245768 | tf_op jit(solution)/shard_map/ppermute | solution.py:187
  51.1 0.4 collective-permute-start.7
  51.4 1.6 %collective-permute-done.9.refs_3_ = bf16[8,5120]{1,0:T(8,128)(2,1)S(1)} collective-permute-done((bf16[8,5120]{1,0:T(8,128)(2,1)S(1)}, bf16[8,5120]{1,0:T(8,128)(2,1)S(1)}, u32[]{:S(2)}, u32[]{:S(2)}) %collective-permute-start.9) | collective-permute-done | bytes 81952 | tf_op jit(solution)/shard_map/ppermute | solution.py:187
  53.0 2.4 %collective-permute-done.8.refs_2_ = bf16[8,5120]{1,0:T(8,128)(2,1)S(1)} collective-permute-done((bf16[8,5120]{1,0:T(8,128)(2,1)S(1)}, bf16[8,5120]{1,0:T(8,128)(2,1)S(1)}, u32[]{:S(2)}, u32[]{:S(2)}) %collective-permute-start.8) | collective-permute-done | bytes 81952 | tf_op jit(solution)/shard_map/ppermute | solution.py:187
  55.4 1.4 %collective-permute-done.7.refs_1_ = bf16[8,5120]{1,0:T(8,128)(2,1)S(1)} collective-permute-done((bf16[8,5120]{1,0:T(8,128)(2,1)S(1)}, bf16[8,5120]{1,0:T(8,128)(2,1)S(1)}, u32[]{:S(2)}, u32[]{:S(2)}) %collective-permute-start.7) | collective-permute-done | bytes 81952 | tf_op jit(solution)/shard_map/ppermute | solution.py:187
  56.7 1.5 %collective-permute-start.11 = (bf16[32,5120]{1,0:T(8,128)(2,1)S(1)}, bf16[32,5120]{1,0:T(8,128)(2,1)S(1)}, u32[]{:S(2)}, u32[]{:S(2)}) collective-permute-start(bf16[32,5120]{1,0:T(8,128)(2,1)S(1)} %shard_map.121.refs_0_), channel_id=1, source_target_pairs={{0,96},{1,25},{2,98},{3,27},{4,100},{5,29},{6,102},{7,31},{8,104},... | collective-permute-start | bytes 983048 | tf_op jit(solution)/shard_map/ppermute | solution.py:187
  58.2 0.6 collective-permute-start.10
  58.8 1.5 %collective-permute-start.12 = (bf16[32,5120]{1,0:T(8,128)(2,1)S(1)}, bf16[32,5120]{1,0:T(8,128)(2,1)S(1)}, u32[]{:S(2)}, u32[]{:S(2)}) collective-permute-start(bf16[32,5120]{1,0:T(8,128)(2,1)S(1)} %shard_map.121.refs_0_), channel_id=1, source_target_pairs={{0,64},{1,17},{2,66},{3,19},{4,68},{5,21},{6,70},{7,23},{8,72},{9,... | collective-permute-start | bytes 983048 | tf_op jit(solution)/shard_map/ppermute | solution.py:187
  60.3 0.0 copy-done.1
  60.3 0.0 copy-done.2
  60.3 0.0 copy-done.3
  60.3 3.8 %shard_map.122 = f32[32,5120]{1,0:T(8,128)S(1)} custom-call(s32[1]{0:T(128)} %bitcast.kv, s32[1]{0:T(128)} %bitcast.1.tp, bf16[216,5120]{1,0:T(8,128)(2,1)S(1)} %bitcast.8, bf16[216,5120]{1,0:T(8,128)(2,1)S(1)} %bitcast.12, bf16[216,5120]{1,0:T(8,128)(2,1)S(1)} %copy-done.3, bf16[216,5120]{1,0:T(8,128)(2,1)S(1)} %collective-permute-done.refs_0_.gate_far, ...), custom_call_target="tpu_custom_call" | custom-call | tf_op jit(solution)/shard_map/pallas_call | solution.py:259
  64.1 0.0 collective-permute-done.11.refs_1_
  64.1 5.9 %collective-permute-done.10.refs_0_ = bf16[32,5120]{1,0:T(8,128)(2,1)S(1)} collective-permute-done((bf16[32,5120]{1,0:T(8,128)(2,1)S(1)}, bf16[32,5120]{1,0:T(8,128)(2,1)S(1)}, u32[]{:S(2)}, u32[]{:S(2)}) %collective-permute-start.10) | collective-permute-done | bytes 327712 | tf_op jit(solution)/shard_map/ppermute | solution.py:187
  70.0 3.9 %shard_map.123 = (bf16[32,5120]{1,0:T(8,128)(2,1)S(1)}, bf16[32,5120]{1,0:T(8,128)(2,1)S(1)}) custom-call(s32[1]{0:T(128)} %bitcast.kv, s32[1]{0:T(128)} %bitcast.1.tp, bf16[216,5120]{1,0:T(8,128)(2,1)S(1)} %bitcast.9, bf16[216,5120]{1,0:T(8,128)(2,1)S(1)} %bitcast.13, bf16[216,5120]{1,0:T(8,128)(2,1)S(1)} %copy-done.3, ...), custom_call_target="tpu_custom_call" | custom-call | tf_op jit(solution)/shard_map/pallas_call | solution.py:262
  74.0 0.0 collective-permute-done.12.refs_0_
  74.0 0.1 collective-permute-start.13
  74.1 2.0 %collective-permute-start.14 = (bf16[32,5120]{1,0:T(8,128)(2,1)S(1)}, bf16[32,5120]{1,0:T(8,128)(2,1)S(1)}, u32[]{:S(2)}, u32[]{:S(2)}) collective-permute-start(bf16[32,5120]{1,0:T(8,128)(2,1)S(1)} %get-tuple-element.49), channel_id=1, source_target_pairs={{0,32},{1,9},{2,34},{3,11},{4,36},{5,13},{6,38},{7,15},{8,40},{9,1... | collective-permute-start | bytes 983048 | tf_op jit(solution)/shard_map/ppermute | solution.py:187
  76.1 3.8 %shard_map.124 = bf16[32,5120]{1,0:T(8,128)(2,1)S(1)} custom-call(s32[1]{0:T(128)} %bitcast.kv, s32[1]{0:T(128)} %bitcast.1.tp, bf16[216,5120]{1,0:T(8,128)(2,1)S(1)} %bitcast.10, bf16[216,5120]{1,0:T(8,128)(2,1)S(1)} %bitcast.14, bf16[216,5120]{1,0:T(8,128)(2,1)S(1)} %copy-done.3, bf16[216,5120]{1,0:T(8,128)(2,1)S(1)} %collective-permute-done.refs_0_.gate_far, ...), custom_call_target="tpu_custom_call" | custom-call | tf_op jit(solution)/shard_map/pallas_call | solution.py:264
  79.9 0.1 collective-permute-start.15
  80.0 1.2 %collective-permute-done.13 = bf16[32,5120]{1,0:T(8,128)(2,1)S(1)} collective-permute-done((bf16[32,5120]{1,0:T(8,128)(2,1)S(1)}, bf16[32,5120]{1,0:T(8,128)(2,1)S(1)}, u32[]{:S(2)}, u32[]{:S(2)}) %collective-permute-start.13) | collective-permute-done | bytes 327712 | tf_op jit(solution)/shard_map/ppermute | solution.py:187
  81.1 1.3 %collective-permute-done.14 = bf16[32,5120]{1,0:T(8,128)(2,1)S(1)} collective-permute-done((bf16[32,5120]{1,0:T(8,128)(2,1)S(1)}, bf16[32,5120]{1,0:T(8,128)(2,1)S(1)}, u32[]{:S(2)}, u32[]{:S(2)}) %collective-permute-start.14) | collective-permute-done | bytes 327712 | tf_op jit(solution)/shard_map/ppermute | solution.py:187
  82.4 6.1 %collective-permute-done.15 = bf16[32,5120]{1,0:T(8,128)(2,1)S(1)} collective-permute-done((bf16[32,5120]{1,0:T(8,128)(2,1)S(1)}, bf16[32,5120]{1,0:T(8,128)(2,1)S(1)}, u32[]{:S(2)}, u32[]{:S(2)}) %collective-permute-start.15) | collective-permute-done | bytes 327712 | tf_op jit(solution)/shard_map/ppermute | solution.py:187
  88.5 0.2 add_convert_fusion
  88.7 0.1 reshape.21
  88.8 12.2 %all_to_all.16.parts = bf16[16,2,5120]{2,1,0:T(2,128)(2,1)S(1)} all-to-all(bf16[16,2,5120]{2,1,0:T(2,128)(2,1)S(1)} %reshape.21), channel_id=1, replica_groups={{0,2,4,6,8,10,12,14,16,18,20,22,24,26,28,30},{32,34,36,38,40,42,44,46,4..., dimensions={0} | all-to-all | bytes 655360 | tf_op jit(solution)/shard_map/all_to_all | solution.py:268
  101.0 0.9 shard_map.125
  (9 shorter events, 0.1 us)
Async XLA Ops:
  1.5 16.3 %all-to-all-start = ((bf16[16,16,640]{2,1,0:T(8,128)(2,1)}), bf16[16,16,640]{2,1,0:T(8,128)(2,1)S(1)}, u32[]{:S(2)}, u32[]{:S(2)}) async-start(bf16[16,16,640]{2,1,0:T(8,128)(2,1)} %broadcast_in_dim.19), calls=%async_computation | async-start | bytes 655360 | tf_op jit(solution)/shard_map/all_to_all | solution.py:224
  8.6 1.0 copy-start.4
  9.6 0.9 copy-start.5
  10.5 0.7 copy-start.7
  11.2 0.7 copy-start.8
  11.8 0.7 copy-start.9
  17.8 17.2 %collective-permute-start = (bf16[216,5120]{1,0:T(8,128)(2,1)}, bf16[216,5120]{1,0:T(8,128)(2,1)S(1)}, u32[]{:S(2)}, u32[]{:S(2)}) collective-permute-start(bf16[216,5120]{1,0:T(8,128)(2,1)} %bitcast.7), channel_id=1, source_target_pairs={{0,1},{1,0},{2,3},{3,2},{4,5},{5,4},{6,7},{7,6},{8,9},{9,8},{10,11... | collective-permute-start | bytes 6635528 | tf_op jit(solution)/shard_map/ppermute | solution.py:201
  17.8 17.2 %collective-permute-start.1 = (bf16[216,5120]{1,0:T(8,128)(2,1)}, bf16[216,5120]{1,0:T(8,128)(2,1)S(1)}, u32[]{:S(2)}, u32[]{:S(2)}) collective-permute-start(bf16[216,5120]{1,0:T(8,128)(2,1)} %bitcast.11), channel_id=1, source_target_pairs={{0,1},{1,0},{2,3},{3,2},{4,5},{5,4},{6,7},{7,6},{8,9},{9,8},{10,11... | collective-permute-start | bytes 6635528 | tf_op jit(solution)/shard_map/ppermute | solution.py:201
  18.3 16.7 %collective-permute-start.2 = (bf16[216,5120]{1,0:T(8,128)(2,1)}, bf16[216,5120]{1,0:T(8,128)(2,1)S(1)}, u32[]{:S(2)}, u32[]{:S(2)}) collective-permute-start(bf16[216,5120]{1,0:T(8,128)(2,1)} %down.5), channel_id=1, source_target_pairs={{0,1},{1,0},{2,3},{3,2},{4,5},{5,4},{6,7},{7,6},{8,9},{9,8},{10,11... | collective-permute-start | bytes 6635528 | tf_op jit(solution)/shard_map/ppermute | solution.py:201
  18.3 16.7 %copy-start = (bf16[640,5120]{1,0:T(8,128)(2,1)S(1)}, bf16[640,5120]{1,0:T(8,128)(2,1)}, u32[]{:S(2)}) copy-start(bf16[640,5120]{1,0:T(8,128)(2,1)} %weight.3) | copy-start | bytes 19660804
  18.3 16.7 %copy-start.6 = (bf16[2,5120]{1,0:T(2,128)(2,1)S(1)}, bf16[2,5120]{1,0:T(2,128)(2,1)}, u32[]{:S(2)}) copy-start(bf16[2,5120]{1,0:T(2,128)(2,1)} %activations.1) | copy-start | bytes 61444
  35.0 13.4 %copy-start.10 = (f32[5120]{0:T(1024)S(1)}, f32[5120]{0:T(1024)}, u32[]{:S(2)}) copy-start(f32[5120]{0:T(1024)} %param.20) | copy-start | bytes 61444
  35.0 25.3 %copy-start.1 = (bf16[5120,216]{0,1:T(8,128)(2,1)S(1)}, bf16[5120,216]{0,1:T(8,128)(2,1)}, u32[]{:S(2)}) copy-start(bf16[5120,216]{0,1:T(8,128)(2,1)} %param.21) | copy-start | bytes 6635524
  35.0 25.3 %copy-start.2 = (bf16[5120,216]{0,1:T(8,128)(2,1)S(1)}, bf16[5120,216]{0,1:T(8,128)(2,1)}, u32[]{:S(2)}) copy-start(bf16[5120,216]{0,1:T(8,128)(2,1)} %param.22) | copy-start | bytes 6635524
  35.0 25.3 %copy-start.3 = (bf16[216,5120]{1,0:T(8,128)(2,1)S(1)}, bf16[216,5120]{1,0:T(8,128)(2,1)}, u32[]{:S(2)}) copy-start(bf16[216,5120]{1,0:T(8,128)(2,1)} %down.5) | copy-start | bytes 6635524
  36.5 1.4 %collective-permute-start.3 = (bf16[8,5120]{1,0:T(8,128)(2,1)S(1)}, bf16[8,5120]{1,0:T(8,128)(2,1)S(1)}, u32[]{:S(2)}, u32[]{:S(2)}) collective-permute-start(bf16[8,5120]{1,0:T(8,128)(2,1)S(1)} %get-tuple-element.42), channel_id=1, source_target_pairs={{0,1},{1,0},{2,3},{3,2},{4,5},{5,4},{6,7},{7,6},{8,9},{9,8},{10,11... | collective-permute-start | bytes 245768 | tf_op jit(solution)/shard_map/ppermute | solution.py:201
  37.9 6.7 %collective-permute-start.6 = (bf16[8,5120]{1,0:T(8,128)(2,1)S(1)}, bf16[8,5120]{1,0:T(8,128)(2,1)S(1)}, u32[]{:S(2)}, u32[]{:S(2)}) collective-permute-start(bf16[8,5120]{1,0:T(8,128)(2,1)S(1)} %fusion.3), channel_id=1, source_target_pairs={{0,4},{1,5},{2,6},{3,7},{4,0},{5,1},{6,2},{7,3},{8,12},{9,13},{10,... | collective-permute-start | bytes 245768 | tf_op jit(solution)/shard_map/ppermute | solution.py:197
  41.8 5.3 %collective-permute-start.5 = (bf16[8,5120]{1,0:T(8,128)(2,1)S(1)}, bf16[8,5120]{1,0:T(8,128)(2,1)S(1)}, u32[]{:S(2)}, u32[]{:S(2)}) collective-permute-start(bf16[8,5120]{1,0:T(8,128)(2,1)S(1)} %fusion.3), channel_id=1, source_target_pairs={{0,6},{1,7},{2,0},{3,1},{4,2},{5,3},{6,4},{7,5},{8,14},{9,15},{10,... | collective-permute-start | bytes 245768 | tf_op jit(solution)/shard_map/ppermute | solution.py:197
  42.5 5.7 %collective-permute-start.4 = (bf16[8,5120]{1,0:T(8,128)(2,1)S(1)}, bf16[8,5120]{1,0:T(8,128)(2,1)S(1)}, u32[]{:S(2)}, u32[]{:S(2)}) collective-permute-start(bf16[8,5120]{1,0:T(8,128)(2,1)S(1)} %fusion.3), channel_id=1, source_target_pairs={{0,2},{1,3},{2,4},{3,5},{4,6},{5,7},{6,0},{7,1},{8,10},{9,11},{10,... | collective-permute-start | bytes 245768 | tf_op jit(solution)/shard_map/ppermute | solution.py:197
  48.5 4.5 %collective-permute-start.9 = (bf16[8,5120]{1,0:T(8,128)(2,1)S(1)}, bf16[8,5120]{1,0:T(8,128)(2,1)S(1)}, u32[]{:S(2)}, u32[]{:S(2)}) collective-permute-start(bf16[8,5120]{1,0:T(8,128)(2,1)S(1)} %fusion.2.refs_0_), channel_id=1, source_target_pairs={{0,24},{1,97},{2,26},{3,99},{4,28},{5,101},{6,30},{7,103},{8,0},{9... | collective-permute-start | bytes 245768 | tf_op jit(solution)/shard_map/ppermute | solution.py:187
  49.4 5.9 %collective-permute-start.8 = (bf16[8,5120]{1,0:T(8,128)(2,1)S(1)}, bf16[8,5120]{1,0:T(8,128)(2,1)S(1)}, u32[]{:S(2)}, u32[]{:S(2)}) collective-permute-start(bf16[8,5120]{1,0:T(8,128)(2,1)S(1)} %fusion.2.refs_0_), channel_id=1, source_target_pairs={{0,16},{1,65},{2,18},{3,67},{4,20},{5,69},{6,22},{7,71},{8,24},{9,... | collective-permute-start | bytes 245768 | tf_op jit(solution)/shard_map/ppermute | solution.py:187
  51.1 5.7 %collective-permute-start.7 = (bf16[8,5120]{1,0:T(8,128)(2,1)S(1)}, bf16[8,5120]{1,0:T(8,128)(2,1)S(1)}, u32[]{:S(2)}, u32[]{:S(2)}) collective-permute-start(bf16[8,5120]{1,0:T(8,128)(2,1)S(1)} %fusion.2.refs_0_), channel_id=1, source_target_pairs={{0,8},{1,33},{2,10},{3,35},{4,12},{5,37},{6,14},{7,39},{8,16},{9,4... | collective-permute-start | bytes 245768 | tf_op jit(solution)/shard_map/ppermute | solution.py:187
  56.7 7.4 %collective-permute-start.11 = (bf16[32,5120]{1,0:T(8,128)(2,1)S(1)}, bf16[32,5120]{1,0:T(8,128)(2,1)S(1)}, u32[]{:S(2)}, u32[]{:S(2)}) collective-permute-start(bf16[32,5120]{1,0:T(8,128)(2,1)S(1)} %shard_map.121.refs_0_), channel_id=1, source_target_pairs={{0,96},{1,25},{2,98},{3,27},{4,100},{5,29},{6,102},{7,31},{8,104},... | collective-permute-start | bytes 983048 | tf_op jit(solution)/shard_map/ppermute | solution.py:187
  58.2 11.8 %collective-permute-start.10 = (bf16[32,5120]{1,0:T(8,128)(2,1)S(1)}, bf16[32,5120]{1,0:T(8,128)(2,1)S(1)}, u32[]{:S(2)}, u32[]{:S(2)}) collective-permute-start(bf16[32,5120]{1,0:T(8,128)(2,1)S(1)} %shard_map.121.refs_0_), channel_id=1, source_target_pairs={{0,32},{1,9},{2,34},{3,11},{4,36},{5,13},{6,38},{7,15},{8,40},{9,1... | collective-permute-start | bytes 983048 | tf_op jit(solution)/shard_map/ppermute | solution.py:187
  58.8 15.1 %collective-permute-start.12 = (bf16[32,5120]{1,0:T(8,128)(2,1)S(1)}, bf16[32,5120]{1,0:T(8,128)(2,1)S(1)}, u32[]{:S(2)}, u32[]{:S(2)}) collective-permute-start(bf16[32,5120]{1,0:T(8,128)(2,1)S(1)} %shard_map.121.refs_0_), channel_id=1, source_target_pairs={{0,64},{1,17},{2,66},{3,19},{4,68},{5,21},{6,70},{7,23},{8,72},{9,... | collective-permute-start | bytes 983048 | tf_op jit(solution)/shard_map/ppermute | solution.py:187
  74.0 7.1 %collective-permute-start.13 = (bf16[32,5120]{1,0:T(8,128)(2,1)S(1)}, bf16[32,5120]{1,0:T(8,128)(2,1)S(1)}, u32[]{:S(2)}, u32[]{:S(2)}) collective-permute-start(bf16[32,5120]{1,0:T(8,128)(2,1)S(1)} %get-tuple-element.48), channel_id=1, source_target_pairs={{0,96},{1,25},{2,98},{3,27},{4,100},{5,29},{6,102},{7,31},{8,104},... | collective-permute-start | bytes 983048 | tf_op jit(solution)/shard_map/ppermute | solution.py:187
  74.1 8.4 %collective-permute-start.14 = (bf16[32,5120]{1,0:T(8,128)(2,1)S(1)}, bf16[32,5120]{1,0:T(8,128)(2,1)S(1)}, u32[]{:S(2)}, u32[]{:S(2)}) collective-permute-start(bf16[32,5120]{1,0:T(8,128)(2,1)S(1)} %get-tuple-element.49), channel_id=1, source_target_pairs={{0,32},{1,9},{2,34},{3,11},{4,36},{5,13},{6,38},{7,15},{8,40},{9,1... | collective-permute-start | bytes 983048 | tf_op jit(solution)/shard_map/ppermute | solution.py:187
  79.9 8.6 %collective-permute-start.15 = (bf16[32,5120]{1,0:T(8,128)(2,1)S(1)}, bf16[32,5120]{1,0:T(8,128)(2,1)S(1)}, u32[]{:S(2)}, u32[]{:S(2)}) collective-permute-start(bf16[32,5120]{1,0:T(8,128)(2,1)S(1)} %shard_map.124), channel_id=1, source_target_pairs={{0,64},{1,17},{2,66},{3,19},{4,68},{5,21},{6,70},{7,23},{8,72},{9,... | collective-permute-start | bytes 983048 | tf_op jit(solution)/shard_map/ppermute | solution.py:187

commit v10 on v9

--- a/solution.py
+++ b/solution.py
@@ -95,8 +95,7 @@
     out[:, GROUP * HEAD_WIDTH :] = stats.astype(BF)
 
 
-def project_kernel(tp, parts, weight, activations, *refs):
-    own, other = refs[-2:]
+def project_kernel(tp, parts, weight, activations, own, other):
     z, core = tp[0] >> 1, tp[0] & 1
     sources = parts.shape[0]
     width = GROUP * HEAD_WIDTH
@@ -228,19 +227,16 @@
         [SM, SM, SM, VM, VM, VM],
         [pltpu.SMEM((16,), jnp.int32)],
     )(node_lengths, parents, kv, token_leaf[None, :], keys, values)
-    q, keys_wide, values_in, onehot, *far = lax.optimization_barrier(
-        (q, keys_wide, values_in, onehot, gate_t, up_t, down_weight)
-    )
-    far = [move_core(w) for w in far]
     packed = call(attend_kernel, shape((256, 768), BF), [VM] * 4 + [pl.ANY], limit=48 << 20)(
         q.reshape(256, 640), keys_wide, values_in, onehot, out_weight
     )
     parts = lax.all_to_all(packed.reshape(16, 16, 768), "kv", 0, 0)
-    own, other = call(project_kernel, [shape((8, D), F32), shape((8, D), BF)], [SM, VM, VM, VM] + [pl.ANY] * 3)(
-        tp, parts, out_weight, activations, *far
+    own, other = call(project_kernel, [shape((8, D), F32), shape((8, D), BF)], [SM, VM, VM, VM])(
+        tp, parts, out_weight, activations
     )
     attended = own + move_core(other).astype(F32)
-    sent = attended.astype(BF)
+    sent, gate_far = lax.optimization_barrier((attended.astype(BF), gate_t))
+    gate_far = move_core(gate_far)
     for part in [move_z(sent, k) for k in (1, 3, 2)]:
         attended = attended + part.astype(F32)
     residual = attended.astype(BF)
@@ -251,19 +247,23 @@
         * norm_gain
     ).astype(BF)
 
+    normed, gate_far, up_far = lax.optimization_barrier((normed, gate_far, up_t))
+    up_far = move_core(up_far)
     back = {k: move_along(normed, k, True) for k in (2, 1, 3)}
     rows = call(stack_kernel, shape((32, D), BF), [VM] * 4)(normed, back[1], back[2], back[3])
-    weights = (kv, tp, gate_t, up_t, down_weight, *far)
+    rows, up_far, down_far = lax.optimization_barrier((rows, up_far, down_weight))
+    weights = (kv, tp, gate_t, up_t, down_weight, gate_far, up_far, move_core(down_far))
+    cost = pl.CostEstimate(flops=12 * 32 * gate_t.size, transcendentals=0, bytes_accessed=12 * gate_t.size)
     block, wide = shape((32, D), BF), shape((32, D), F32)
     back = {k: move_along(rows, k, False) for k in (1, 3, 2)}
-    mixed = call(mlp_kernel, wide, [SM, SM] + [VM] * 7, limit=28 << 20)(*weights, rows)
-    near = lax.optimization_barrier((back[1], back[3], mixed))
-    mixed = near[2]
-    ahead, behind = call(mlp_kernel, [block, block], [SM, SM] + [VM] * 8, limit=28 << 20)(*weights, near[0], near[1])
+    mixed, ahead, behind = call(mlp_kernel, [wide, block, block], [SM, SM] + [VM] * 9, limit=28 << 20)(
+        *weights, rows, back[1], back[3]
+    )
     opposite, ahead, behind = lax.optimization_barrier((back[2], ahead, behind))
-    opposite = call(mlp_kernel, block, [SM, SM] + [VM] * 7, limit=28 << 20)(*weights, opposite)
-    for part in [move_along(ahead, 3, False), move_along(behind, 1, False), move_along(opposite, 2, False)]:
+    opposite = call(mlp_kernel, block, [SM, SM] + [VM] * 7, limit=28 << 20, cost_estimate=cost)(*weights, opposite)
+    for part in [move_along(ahead, 3, False), move_along(behind, 1, False)]:
         mixed = mixed + part.astype(F32)
+    mixed = lax.optimization_barrier(mixed) + move_along(opposite, 2, False).astype(F32)
     mixed = mixed.astype(BF).reshape(16, 2, D)
     mixed = lax.all_to_all(mixed, ("kv", "tp"), 0, 0, axis_index_groups=PLANES)
     return call(finish_kernel, shape((2, D), BF), [SM, VM, VM])(tp, residual, mixed)

time: 102 us -> 102 us (level)
  starting transfers between devices: 22.4 us -> 26.7 us
  Pallas kernels: 17.6 us -> 13.8 us
  waiting for transfers between devices: 29.6 us -> 27.8 us
    ppermute x9, starting transfers between devices: 8.67 us -> 13.2 us  [move_along(): return lax.ppermute(value, ('kv', 'tp'), pairs)]
    pallas_call x3 -> x2, Pallas kernels: 11.6 us -> 7.74 us  [the longest x1 3.94 us: local(): call(mlp_kernel, [wide, block, block], [SM, SM] + [VM] * 9, limit=28 << 20)]
    all_to_all x1, blocking collectives: 12.2 us -> 14.1 us  [local(): mixed = lax.all_to_all(mixed, ('kv', 'tp'), 0, 0, axis_index_groups=PLANES)]
    ppermute x9, waiting for transfers between devices: 19.7 us -> 18.2 us  [move_along(): return lax.ppermute(value, ('kv', 'tp'), pairs)]
    all_to_all x1, blocking collectives: 14 us -> 12.6 us  [local(): parts = lax.all_to_all(packed.reshape(16, 16, 768), 'kv', 0, 0)]
  transfers between devices with their start and end apart: 17 -> 17, of which waited for: 12 -> 10; matrix products, arithmetic and copies ran while one was open for 0% -> 0% of each run, Pallas kernels for 15% -> 9%
where the time goes in v10:
time: 102 us; the launch traced here: 101 us
  waiting for transfers between devices  27.8 us (27%)
  starting transfers between devices  26.7 us (26%)
  blocking collectives  26.7 us (26%)
  Pallas kernels  13.8 us (14%)
  local copies, waits for them, and re-layouts  5.51 us (5%)
    ppermute x9, waiting for transfers between devices, move_along(): return lax.ppermute(value, ('kv', 'tp'), pairs)  18.2 us
    all_to_all x1, blocking collectives, local(): mixed = lax.all_to_all(mixed, ('kv', 'tp'), 0, 0, axis_index_groups=PLANES)  14.1 us
    ppermute x9, starting transfers between devices, move_along(): return lax.ppermute(value, ('kv', 'tp'), pairs)  13.2 us
    all_to_all x1, blocking collectives, local(): parts = lax.all_to_all(packed.reshape(16, 16, 768), 'kv', 0, 0)  12.6 us
    all_to_all x1, starting transfers between devices, local(): lax.all_to_all(jnp.broadcast_to(queries[None], (16, 16, 640)), 'kv', 0, 0)  7.12 us
    ppermute x3, starting transfers between devices, move_z(): return lax.ppermute(value, 'tp', pairs)  5.91 us
    all_to_all x1, waiting for transfers between devices, local(): lax.all_to_all(jnp.broadcast_to(queries[None], (16, 16, 640)), 'kv', 0, 0)  4.3 us
    ppermute x3, waiting for transfers between devices, move_z(): return lax.ppermute(value, 'tp', pairs)  4.08 us
  transfers between devices with their start and end apart: 17, of which 10 were waited for; matrix products, arithmetic and copies ran while one was open for 0% of the time, Pallas kernels for 9%

profile of v10, /device:TPU:0, one launch (start us, length us, event | category | flops | bytes accessed | tf_op | source)
XLA Modules:
  0.0 101.2 jit_solution(12348434906338673738)
XLA Ops:
  0.0 1.5 %broadcast_in_dim.19 = bf16[16,16,640]{2,1,0:T(8,128)(2,1)} broadcast(bf16[16,640]{1,0:T(8,128)(2,1)} %param.13), dimensions={1,2} | broadcast | bytes 348160 | tf_op jit(solution)/shard_map/broadcast_in_dim | solution.py:223
  1.5 7.1 %all-to-all-start = ((bf16[16,16,640]{2,1,0:T(8,128)(2,1)}), bf16[16,16,640]{2,1,0:T(8,128)(2,1)S(1)}, u32[]{:S(2)}, u32[]{:S(2)}) async-start(bf16[16,16,640]{2,1,0:T(8,128)(2,1)} %broadcast_in_dim.19), calls=%async_computation | async-start | bytes 655360 | tf_op jit(solution)/shard_map/all_to_all | solution.py:223
  8.6 0.0 copy-start.4
  8.6 0.9 copy-done.4
  9.6 0.0 copy-start.5
  9.6 0.9 copy-done.5
  10.5 0.0 copy-start.7
  10.5 0.7 copy-done.7
  11.2 0.7 copy-done.8
  11.8 0.7 copy-done.9
  12.5 1.0 shard_map.118
  13.5 4.3 %all-to-all-done = bf16[16,16,640]{2,1,0:T(8,128)(2,1)S(1)} async-done(((bf16[16,16,640]{2,1,0:T(8,128)(2,1)}), bf16[16,16,640]{2,1,0:T(8,128)(2,1)S(1)}, u32[]{:S(2)}, u32[]{:S(2)}) %all-to-all-start) | async-done | bytes 327712 | tf_op jit(solution)/shard_map/all_to_all | solution.py:223
  17.8 2.7 %shard_map.119 = bf16[256,768]{1,0:T(8,128)(2,1)S(1)} custom-call(bf16[256,640]{1,0:T(8,128)(2,1)S(1)} %bitcast.14, bf16[1024,256]{1,0:T(8,128)(2,1)S(1)} %get-tuple-element.30.keys_wide, bf16[1024,128]{1,0:T(8,128)(2,1)S(1)} %get-tuple-element.31.values, bf16[256,128]{1,0:T(8,128)(2,1)S(1)} %get-tuple-element.32.onehot, bf16[640,5120]{1,0:T(8,128)(2,1)} %weight.3), custom_call_target="tpu_custom_call" | custom-call | tf_op jit(solution)/shard_map/pallas_call | solution.py:230
  20.5 12.6 %all_to_all.15.parts = bf16[16,16,768]{2,1,0:T(8,128)(2,1)S(1)} all-to-all(bf16[16,16,768]{2,1,0:T(8,128)(2,1)S(1)} %bitcast.13), channel_id=1, replica_groups=mesh['kv'=16,'tp'=8] {'kv'}, dimensions={0} | all-to-all | bytes 786432 | tf_op jit(solution)/shard_map/all_to_all | solution.py:233
  33.1 0.0 copy-done
  33.1 0.0 copy-done.6
  33.1 0.0 copy-start.2
  33.1 0.0 copy-start.3
  33.1 1.4 %shard_map.120 = (f32[8,5120]{1,0:T(8,128)S(1)}, bf16[8,5120]{1,0:T(8,128)(2,1)S(1)}) custom-call(s32[1]{0:T(128)} %bitcast.1.tp, bf16[16,16,768]{2,1,0:T(8,128)(2,1)S(1)} %all_to_all.15.parts, bf16[640,5120]{1,0:T(8,128)(2,1)S(1)} %copy-done, bf16[2,5120]{1,0:T(2,128)(2,1)S(1)} %copy-done.6), custom_call_target="tpu_custom_call" | custom-call | tf_op jit(solution)/shard_map/pallas_call | solution.py:234
  34.6 0.1 collective-permute-start
  34.7 1.3 %collective-permute-done = bf16[8,5120]{1,0:T(8,128)(2,1)S(1)} collective-permute-done((bf16[8,5120]{1,0:T(8,128)(2,1)S(1)}, bf16[8,5120]{1,0:T(8,128)(2,1)S(1)}, u32[]{:S(2)}, u32[]{:S(2)}) %collective-permute-start) | collective-permute-done | bytes 81952 | tf_op jit(solution)/shard_map/ppermute | solution.py:200
  36.0 0.0 copy-done.1
  36.0 0.2 collective-permute-start.4
  36.2 1.9 %collective-permute-start.1 = (bf16[8,5120]{1,0:T(8,128)(2,1)S(1)}, bf16[8,5120]{1,0:T(8,128)(2,1)S(1)}, u32[]{:S(2)}, u32[]{:S(2)}) collective-permute-start(bf16[8,5120]{1,0:T(8,128)(2,1)S(1)} %fusion.3), channel_id=1, source_target_pairs={{0,2},{1,3},{2,4},{3,5},{4,6},{5,7},{6,0},{7,1},{8,10},{9,11},{10,... | collective-permute-start | bytes 245768 | tf_op jit(solution)/shard_map/ppermute | solution.py:196
  38.1 2.1 %collective-permute-start.2 = (bf16[8,5120]{1,0:T(8,128)(2,1)S(1)}, bf16[8,5120]{1,0:T(8,128)(2,1)S(1)}, u32[]{:S(2)}, u32[]{:S(2)}) collective-permute-start(bf16[8,5120]{1,0:T(8,128)(2,1)S(1)} %fusion.3), channel_id=1, source_target_pairs={{0,6},{1,7},{2,0},{3,1},{4,2},{5,3},{6,4},{7,5},{8,14},{9,15},{10,... | collective-permute-start | bytes 245768 | tf_op jit(solution)/shard_map/ppermute | solution.py:196
  40.2 1.9 %collective-permute-start.3 = (bf16[8,5120]{1,0:T(8,128)(2,1)S(1)}, bf16[8,5120]{1,0:T(8,128)(2,1)S(1)}, u32[]{:S(2)}, u32[]{:S(2)}) collective-permute-start(bf16[8,5120]{1,0:T(8,128)(2,1)S(1)} %fusion.3), channel_id=1, source_target_pairs={{0,4},{1,5},{2,6},{3,7},{4,0},{5,1},{6,2},{7,3},{8,12},{9,13},{10,... | collective-permute-start | bytes 245768 | tf_op jit(solution)/shard_map/ppermute | solution.py:196
  42.1 1.1 %collective-permute-done.1 = bf16[8,5120]{1,0:T(8,128)(2,1)S(1)} collective-permute-done((bf16[8,5120]{1,0:T(8,128)(2,1)S(1)}, bf16[8,5120]{1,0:T(8,128)(2,1)S(1)}, u32[]{:S(2)}, u32[]{:S(2)}) %collective-permute-start.1) | collective-permute-done | bytes 81952 | tf_op jit(solution)/shard_map/ppermute | solution.py:196
  43.2 0.0 collective-permute-done.2
  43.2 3.0 %collective-permute-done.3 = bf16[8,5120]{1,0:T(8,128)(2,1)S(1)} collective-permute-done((bf16[8,5120]{1,0:T(8,128)(2,1)S(1)}, bf16[8,5120]{1,0:T(8,128)(2,1)S(1)}, u32[]{:S(2)}, u32[]{:S(2)}) %collective-permute-start.3) | collective-permute-done | bytes 81952 | tf_op jit(solution)/shard_map/ppermute | solution.py:196
  46.2 0.2 fusion
  46.4 0.0 copy-done.10
  46.4 0.1 fusion.2.refs_0_
  46.5 0.0 collective-permute-done.4.gate_far
  46.5 0.0 copy-done.2
  46.5 0.1 collective-permute-start.8
  46.6 0.4 collective-permute-start.5
  47.0 2.1 %collective-permute-start.6 = (bf16[8,5120]{1,0:T(8,128)(2,1)S(1)}, bf16[8,5120]{1,0:T(8,128)(2,1)S(1)}, u32[]{:S(2)}, u32[]{:S(2)}) collective-permute-start(bf16[8,5120]{1,0:T(8,128)(2,1)S(1)} %fusion.2.refs_0_), channel_id=1, source_target_pairs={{0,16},{1,65},{2,18},{3,67},{4,20},{5,69},{6,22},{7,71},{8,24},{9,... | collective-permute-start | bytes 245768 | tf_op jit(solution)/shard_map/ppermute | solution.py:186
  49.1 1.7 %collective-permute-start.7 = (bf16[8,5120]{1,0:T(8,128)(2,1)S(1)}, bf16[8,5120]{1,0:T(8,128)(2,1)S(1)}, u32[]{:S(2)}, u32[]{:S(2)}) collective-permute-start(bf16[8,5120]{1,0:T(8,128)(2,1)S(1)} %fusion.2.refs_0_), channel_id=1, source_target_pairs={{0,24},{1,97},{2,26},{3,99},{4,28},{5,101},{6,30},{7,103},{8,0},{9... | collective-permute-start | bytes 245768 | tf_op jit(solution)/shard_map/ppermute | solution.py:186
  50.8 2.4 %collective-permute-done.5.refs_1_ = bf16[8,5120]{1,0:T(8,128)(2,1)S(1)} collective-permute-done((bf16[8,5120]{1,0:T(8,128)(2,1)S(1)}, bf16[8,5120]{1,0:T(8,128)(2,1)S(1)}, u32[]{:S(2)}, u32[]{:S(2)}) %collective-permute-start.5) | collective-permute-done | bytes 81952 | tf_op jit(solution)/shard_map/ppermute | solution.py:186
  53.2 0.0 collective-permute-done.6.refs_2_
  53.2 0.9 collective-permute-done.7.refs_3_
  54.1 0.0 collective-permute-done.8.up_far
  54.1 0.0 copy-done.3
  54.1 0.1 collective-permute-start.9
  54.2 0.1 collective-permute-start.10
  54.3 3.2 %collective-permute-start.11 = (bf16[32,5120]{1,0:T(8,128)(2,1)S(1)}, bf16[32,5120]{1,0:T(8,128)(2,1)S(1)}, u32[]{:S(2)}, u32[]{:S(2)}) collective-permute-start(bf16[32,5120]{1,0:T(8,128)(2,1)S(1)} %shard_map.121.refs_0_), channel_id=1, source_target_pairs={{0,96},{1,25},{2,98},{3,27},{4,100},{5,29},{6,102},{7,31},{8,104},... | collective-permute-start | bytes 983048 | tf_op jit(solution)/shard_map/ppermute | solution.py:186
  57.5 0.2 collective-permute-start.12
  57.7 4.9 %collective-permute-done.10.refs_1_ = bf16[32,5120]{1,0:T(8,128)(2,1)S(1)} collective-permute-done((bf16[32,5120]{1,0:T(8,128)(2,1)S(1)}, bf16[32,5120]{1,0:T(8,128)(2,1)S(1)}, u32[]{:S(2)}, u32[]{:S(2)}) %collective-permute-start.10) | collective-permute-done | bytes 327712 | tf_op jit(solution)/shard_map/ppermute | solution.py:186
  62.5 3.1 %collective-permute-done.11.refs_2_ = bf16[32,5120]{1,0:T(8,128)(2,1)S(1)} collective-permute-done((bf16[32,5120]{1,0:T(8,128)(2,1)S(1)}, bf16[32,5120]{1,0:T(8,128)(2,1)S(1)}, u32[]{:S(2)}, u32[]{:S(2)}) %collective-permute-start.11) | collective-permute-done | bytes 327712 | tf_op jit(solution)/shard_map/ppermute | solution.py:186
  65.6 0.0 collective-permute-done.9.down_far
  65.6 3.9 %shard_map.122 = (f32[32,5120]{1,0:T(8,128)S(1)}, bf16[32,5120]{1,0:T(8,128)(2,1)S(1)}, bf16[32,5120]{1,0:T(8,128)(2,1)S(1)}) custom-call(s32[1]{0:T(128)} %bitcast.kv, s32[1]{0:T(128)} %bitcast.1.tp, bf16[216,5120]{1,0:T(8,128)(2,1)S(1)} %bitcast.8, bf16[216,5120]{1,0:T(8,128)(2,1)S(1)} %bitcast.11, bf16[216,5120]{1,0:T(8,128)(2,1)S(1)} %copy-done.3, ...), custom_call_target="tpu_custom_call" | custom-call | tf_op jit(solution)/shard_map/pallas_call | solution.py:259
  69.5 0.0 collective-permute-done.12.refs_0_
  69.6 3.9 %collective-permute-start.13 = (bf16[32,5120]{1,0:T(8,128)(2,1)S(1)}, bf16[32,5120]{1,0:T(8,128)(2,1)S(1)}, u32[]{:S(2)}, u32[]{:S(2)}) collective-permute-start(bf16[32,5120]{1,0:T(8,128)(2,1)S(1)} %get-tuple-element.46), channel_id=1, source_target_pairs={{0,96},{1,25},{2,98},{3,27},{4,100},{5,29},{6,102},{7,31},{8,104},... | collective-permute-start | bytes 983048 | tf_op jit(solution)/shard_map/ppermute | solution.py:186
  73.5 0.0 collective-permute-start.14
  73.5 3.8 %shard_map.123 = bf16[32,5120]{1,0:T(8,128)(2,1)S(1)} custom-call(s32[1]{0:T(128)} %bitcast.kv, s32[1]{0:T(128)} %bitcast.1.tp, bf16[216,5120]{1,0:T(8,128)(2,1)S(1)} %bitcast.9, bf16[216,5120]{1,0:T(8,128)(2,1)S(1)} %bitcast.12, bf16[216,5120]{1,0:T(8,128)(2,1)S(1)} %copy-done.3, bf16[216,5120]{1,0:T(8,128)(2,1)S(1)} %collective-permute-done.4.gate_far, ...), custom_call_target="tpu_custom_call" | custom-call | flops 424673280 | bytes 13271040 | tf_op jit(solution)/shard_map/pallas_call | solution.py:263
  77.3 1.6 %collective-permute-start.15 = (bf16[32,5120]{1,0:T(8,128)(2,1)S(1)}, bf16[32,5120]{1,0:T(8,128)(2,1)S(1)}, u32[]{:S(2)}, u32[]{:S(2)}) collective-permute-start(bf16[32,5120]{1,0:T(8,128)(2,1)S(1)} %shard_map.123), channel_id=1, source_target_pairs={{0,64},{1,17},{2,66},{3,19},{4,68},{5,21},{6,70},{7,23},{8,72},{9,... | collective-permute-start | bytes 983048 | tf_op jit(solution)/shard_map/ppermute | solution.py:186
  78.9 0.0 collective-permute-done.13
  78.9 2.9 %collective-permute-done.14 = bf16[32,5120]{1,0:T(8,128)(2,1)S(1)} collective-permute-done((bf16[32,5120]{1,0:T(8,128)(2,1)S(1)}, bf16[32,5120]{1,0:T(8,128)(2,1)S(1)}, u32[]{:S(2)}, u32[]{:S(2)}) %collective-permute-start.14) | collective-permute-done | bytes 327712 | tf_op jit(solution)/shard_map/ppermute | solution.py:186
  81.8 0.1 convert_add_fusion
  81.9 4.1 %collective-permute-done.15 = bf16[32,5120]{1,0:T(8,128)(2,1)S(1)} collective-permute-done((bf16[32,5120]{1,0:T(8,128)(2,1)S(1)}, bf16[32,5120]{1,0:T(8,128)(2,1)S(1)}, u32[]{:S(2)}, u32[]{:S(2)}) %collective-permute-start.15) | collective-permute-done | bytes 327712 | tf_op jit(solution)/shard_map/ppermute | solution.py:186
  86.0 0.1 add_convert_fusion
  86.0 0.1 reshape.21
  86.1 14.1 %all_to_all.16.parts = bf16[16,2,5120]{2,1,0:T(2,128)(2,1)S(1)} all-to-all(bf16[16,2,5120]{2,1,0:T(2,128)(2,1)S(1)} %reshape.21), channel_id=1, replica_groups={{0,2,4,6,8,10,12,14,16,18,20,22,24,26,28,30},{32,34,36,38,40,42,44,46,4..., dimensions={0} | all-to-all | bytes 655360 | tf_op jit(solution)/shard_map/all_to_all | solution.py:268
  100.3 0.9 shard_map.124
  (9 shorter events, 0.1 us)
Async XLA Ops:
  1.5 16.3 %all-to-all-start = ((bf16[16,16,640]{2,1,0:T(8,128)(2,1)}), bf16[16,16,640]{2,1,0:T(8,128)(2,1)S(1)}, u32[]{:S(2)}, u32[]{:S(2)}) async-start(bf16[16,16,640]{2,1,0:T(8,128)(2,1)} %broadcast_in_dim.19), calls=%async_computation | async-start | bytes 655360 | tf_op jit(solution)/shard_map/all_to_all | solution.py:223
  8.6 1.0 copy-start.4
  9.6 0.9 copy-start.5
  10.5 0.7 copy-start.7
  11.2 0.7 copy-start.8
  11.8 0.7 copy-start.9
  17.8 15.3 %copy-start = (bf16[640,5120]{1,0:T(8,128)(2,1)S(1)}, bf16[640,5120]{1,0:T(8,128)(2,1)}, u32[]{:S(2)}) copy-start(bf16[640,5120]{1,0:T(8,128)(2,1)} %weight.3) | copy-start | bytes 19660804
  17.8 15.3 %copy-start.6 = (bf16[2,5120]{1,0:T(2,128)(2,1)S(1)}, bf16[2,5120]{1,0:T(2,128)(2,1)}, u32[]{:S(2)}) copy-start(bf16[2,5120]{1,0:T(2,128)(2,1)} %activations.1) | copy-start | bytes 61444
  33.1 2.9 %copy-start.1 = (bf16[5120,216]{0,1:T(8,128)(2,1)S(1)}, bf16[5120,216]{0,1:T(8,128)(2,1)}, u32[]{:S(2)}) copy-start(bf16[5120,216]{0,1:T(8,128)(2,1)} %param.21) | copy-start | bytes 6635524
  33.1 13.3 %copy-start.10 = (f32[5120]{0:T(1024)S(1)}, f32[5120]{0:T(1024)}, u32[]{:S(2)}) copy-start(f32[5120]{0:T(1024)} %param.20) | copy-start | bytes 61444
  33.1 13.4 %copy-start.2 = (bf16[5120,216]{0,1:T(8,128)(2,1)S(1)}, bf16[5120,216]{0,1:T(8,128)(2,1)}, u32[]{:S(2)}) copy-start(bf16[5120,216]{0,1:T(8,128)(2,1)} %param.22) | copy-start | bytes 6635524
  33.1 21.0 %copy-start.3 = (bf16[216,5120]{1,0:T(8,128)(2,1)S(1)}, bf16[216,5120]{1,0:T(8,128)(2,1)}, u32[]{:S(2)}) copy-start(bf16[216,5120]{1,0:T(8,128)(2,1)} %down.3) | copy-start | bytes 6635524
  34.6 1.4 %collective-permute-start = (bf16[8,5120]{1,0:T(8,128)(2,1)S(1)}, bf16[8,5120]{1,0:T(8,128)(2,1)S(1)}, u32[]{:S(2)}, u32[]{:S(2)}) collective-permute-start(bf16[8,5120]{1,0:T(8,128)(2,1)S(1)} %get-tuple-element.34), channel_id=1, source_target_pairs={{0,1},{1,0},{2,3},{3,2},{4,5},{5,4},{6,7},{7,6},{8,9},{9,8},{10,11... | collective-permute-start | bytes 245768 | tf_op jit(solution)/shard_map/ppermute | solution.py:200
  36.0 10.5 %collective-permute-start.4 = (bf16[216,5120]{1,0:T(8,128)(2,1)S(1)}, bf16[216,5120]{1,0:T(8,128)(2,1)S(1)}, u32[]{:S(2)}, u32[]{:S(2)}) collective-permute-start(bf16[216,5120]{1,0:T(8,128)(2,1)S(1)} %bitcast.7), channel_id=1, source_target_pairs={{0,1},{1,0},{2,3},{3,2},{4,5},{5,4},{6,7},{7,6},{8,9},{9,8},{10,11... | collective-permute-start | bytes 6635528 | tf_op jit(solution)/shard_map/ppermute | solution.py:200
  36.2 7.0 %collective-permute-start.1 = (bf16[8,5120]{1,0:T(8,128)(2,1)S(1)}, bf16[8,5120]{1,0:T(8,128)(2,1)S(1)}, u32[]{:S(2)}, u32[]{:S(2)}) collective-permute-start(bf16[8,5120]{1,0:T(8,128)(2,1)S(1)} %fusion.3), channel_id=1, source_target_pairs={{0,2},{1,3},{2,4},{3,5},{4,6},{5,7},{6,0},{7,1},{8,10},{9,11},{10,... | collective-permute-start | bytes 245768 | tf_op jit(solution)/shard_map/ppermute | solution.py:196
  38.1 5.1 %collective-permute-start.2 = (bf16[8,5120]{1,0:T(8,128)(2,1)S(1)}, bf16[8,5120]{1,0:T(8,128)(2,1)S(1)}, u32[]{:S(2)}, u32[]{:S(2)}) collective-permute-start(bf16[8,5120]{1,0:T(8,128)(2,1)S(1)} %fusion.3), channel_id=1, source_target_pairs={{0,6},{1,7},{2,0},{3,1},{4,2},{5,3},{6,4},{7,5},{8,14},{9,15},{10,... | collective-permute-start | bytes 245768 | tf_op jit(solution)/shard_map/ppermute | solution.py:196
  40.2 5.9 %collective-permute-start.3 = (bf16[8,5120]{1,0:T(8,128)(2,1)S(1)}, bf16[8,5120]{1,0:T(8,128)(2,1)S(1)}, u32[]{:S(2)}, u32[]{:S(2)}) collective-permute-start(bf16[8,5120]{1,0:T(8,128)(2,1)S(1)} %fusion.3), channel_id=1, source_target_pairs={{0,4},{1,5},{2,6},{3,7},{4,0},{5,1},{6,2},{7,3},{8,12},{9,13},{10,... | collective-permute-start | bytes 245768 | tf_op jit(solution)/shard_map/ppermute | solution.py:196
  46.5 7.6 %collective-permute-start.8 = (bf16[216,5120]{1,0:T(8,128)(2,1)S(1)}, bf16[216,5120]{1,0:T(8,128)(2,1)S(1)}, u32[]{:S(2)}, u32[]{:S(2)}) collective-permute-start(bf16[216,5120]{1,0:T(8,128)(2,1)S(1)} %bitcast.10), channel_id=1, source_target_pairs={{0,1},{1,0},{2,3},{3,2},{4,5},{5,4},{6,7},{7,6},{8,9},{9,8},{10,11... | collective-permute-start | bytes 6635528 | tf_op jit(solution)/shard_map/ppermute | solution.py:200
  46.6 6.6 %collective-permute-start.5 = (bf16[8,5120]{1,0:T(8,128)(2,1)S(1)}, bf16[8,5120]{1,0:T(8,128)(2,1)S(1)}, u32[]{:S(2)}, u32[]{:S(2)}) collective-permute-start(bf16[8,5120]{1,0:T(8,128)(2,1)S(1)} %fusion.2.refs_0_), channel_id=1, source_target_pairs={{0,8},{1,33},{2,10},{3,35},{4,12},{5,37},{6,14},{7,39},{8,16},{9,4... | collective-permute-start | bytes 245768 | tf_op jit(solution)/shard_map/ppermute | solution.py:186
  47.0 6.2 %collective-permute-start.6 = (bf16[8,5120]{1,0:T(8,128)(2,1)S(1)}, bf16[8,5120]{1,0:T(8,128)(2,1)S(1)}, u32[]{:S(2)}, u32[]{:S(2)}) collective-permute-start(bf16[8,5120]{1,0:T(8,128)(2,1)S(1)} %fusion.2.refs_0_), channel_id=1, source_target_pairs={{0,16},{1,65},{2,18},{3,67},{4,20},{5,69},{6,22},{7,71},{8,24},{9,... | collective-permute-start | bytes 245768 | tf_op jit(solution)/shard_map/ppermute | solution.py:186
  49.1 5.0 %collective-permute-start.7 = (bf16[8,5120]{1,0:T(8,128)(2,1)S(1)}, bf16[8,5120]{1,0:T(8,128)(2,1)S(1)}, u32[]{:S(2)}, u32[]{:S(2)}) collective-permute-start(bf16[8,5120]{1,0:T(8,128)(2,1)S(1)} %fusion.2.refs_0_), channel_id=1, source_target_pairs={{0,24},{1,97},{2,26},{3,99},{4,28},{5,101},{6,30},{7,103},{8,0},{9... | collective-permute-start | bytes 245768 | tf_op jit(solution)/shard_map/ppermute | solution.py:186
  54.1 11.5 %collective-permute-start.9 = (bf16[216,5120]{1,0:T(8,128)(2,1)S(1)}, bf16[216,5120]{1,0:T(8,128)(2,1)S(1)}, u32[]{:S(2)}, u32[]{:S(2)}) collective-permute-start(bf16[216,5120]{1,0:T(8,128)(2,1)S(1)} %copy-done.3), channel_id=1, source_target_pairs={{0,1},{1,0},{2,3},{3,2},{4,5},{5,4},{6,7},{7,6},{8,9},{9,8},{10,11... | collective-permute-start | bytes 6635528 | tf_op jit(solution)/shard_map/ppermute | solution.py:200
  54.2 8.4 %collective-permute-start.10 = (bf16[32,5120]{1,0:T(8,128)(2,1)S(1)}, bf16[32,5120]{1,0:T(8,128)(2,1)S(1)}, u32[]{:S(2)}, u32[]{:S(2)}) collective-permute-start(bf16[32,5120]{1,0:T(8,128)(2,1)S(1)} %shard_map.121.refs_0_), channel_id=1, source_target_pairs={{0,32},{1,9},{2,34},{3,11},{4,36},{5,13},{6,38},{7,15},{8,40},{9,1... | collective-permute-start | bytes 983048 | tf_op jit(solution)/shard_map/ppermute | solution.py:186
  54.3 11.3 %collective-permute-start.11 = (bf16[32,5120]{1,0:T(8,128)(2,1)S(1)}, bf16[32,5120]{1,0:T(8,128)(2,1)S(1)}, u32[]{:S(2)}, u32[]{:S(2)}) collective-permute-start(bf16[32,5120]{1,0:T(8,128)(2,1)S(1)} %shard_map.121.refs_0_), channel_id=1, source_target_pairs={{0,96},{1,25},{2,98},{3,27},{4,100},{5,29},{6,102},{7,31},{8,104},... | collective-permute-start | bytes 983048 | tf_op jit(solution)/shard_map/ppermute | solution.py:186
  57.5 12.1 %collective-permute-start.12 = (bf16[32,5120]{1,0:T(8,128)(2,1)S(1)}, bf16[32,5120]{1,0:T(8,128)(2,1)S(1)}, u32[]{:S(2)}, u32[]{:S(2)}) collective-permute-start(bf16[32,5120]{1,0:T(8,128)(2,1)S(1)} %shard_map.121.refs_0_), channel_id=1, source_target_pairs={{0,64},{1,17},{2,66},{3,19},{4,68},{5,21},{6,70},{7,23},{8,72},{9,... | collective-permute-start | bytes 983048 | tf_op jit(solution)/shard_map/ppermute | solution.py:186
  69.6 9.4 %collective-permute-start.13 = (bf16[32,5120]{1,0:T(8,128)(2,1)S(1)}, bf16[32,5120]{1,0:T(8,128)(2,1)S(1)}, u32[]{:S(2)}, u32[]{:S(2)}) collective-permute-start(bf16[32,5120]{1,0:T(8,128)(2,1)S(1)} %get-tuple-element.46), channel_id=1, source_target_pairs={{0,96},{1,25},{2,98},{3,27},{4,100},{5,29},{6,102},{7,31},{8,104},... | collective-permute-start | bytes 983048 | tf_op jit(solution)/shard_map/ppermute | solution.py:186
  73.5 8.3 %collective-permute-start.14 = (bf16[32,5120]{1,0:T(8,128)(2,1)S(1)}, bf16[32,5120]{1,0:T(8,128)(2,1)S(1)}, u32[]{:S(2)}, u32[]{:S(2)}) collective-permute-start(bf16[32,5120]{1,0:T(8,128)(2,1)S(1)} %get-tuple-element.47), channel_id=1, source_target_pairs={{0,32},{1,9},{2,34},{3,11},{4,36},{5,13},{6,38},{7,15},{8,40},{9,1... | collective-permute-start | bytes 983048 | tf_op jit(solution)/shard_map/ppermute | solution.py:186
  77.3 8.7 %collective-permute-start.15 = (bf16[32,5120]{1,0:T(8,128)(2,1)S(1)}, bf16[32,5120]{1,0:T(8,128)(2,1)S(1)}, u32[]{:S(2)}, u32[]{:S(2)}) collective-permute-start(bf16[32,5120]{1,0:T(8,128)(2,1)S(1)} %shard_map.123), channel_id=1, source_target_pairs={{0,64},{1,17},{2,66},{3,19},{4,68},{5,21},{6,70},{7,23},{8,72},{9,... | collective-permute-start | bytes 983048 | tf_op jit(solution)/shard_map/ppermute | solution.py:186

commit v11 on v8

--- a/solution.py
+++ b/solution.py
@@ -44,28 +44,34 @@
     return lax.dot_general(a, b, (((1,), (0,)), ((), ())), preferred_element_type=F32)
 
 
-def prepare_kernel(lengths, parents, kv, leaf, keys, values, keys_wide, values_out, onehot, starts):
-    nodes = lengths.shape[0]
+def repeat_kernel(rows, out, sem):
+    copies = [pltpu.make_async_copy(rows, out.at[k], sem.at[k]) for k in range(out.shape[0])]
+    for copy in copies:
+        copy.start()
+    for copy in copies:
+        copy.wait()
+
+
+def prepare_kernel(kv, tables, keys, values, keys_wide, values_out, onehot):
     slots = keys.shape[0]
-    tokens = leaf.shape[1]
-    running = jnp.int32(0)
-    for n in range(nodes):
-        starts[n] = running
-        running = running + lengths[n]
-    lane = lax.broadcasted_iota(jnp.int32, (1, 128), 1)
-    zero = jnp.zeros((1, 128), jnp.int32)
-    own_lo, own_hi, up_lo, up_hi = zero, zero, zero, zero
-    for n in range(nodes):
-        lo = starts[n]
-        up = parents[n]
-        here = lane == n
-        own_lo = jnp.where(here, lo, own_lo)
-        own_hi = jnp.where(here, lo + lengths[n], own_hi)
-        up_lo = jnp.where(here, starts[up], up_lo)
-        up_hi = jnp.where(here, starts[up] + lengths[up], up_hi)
+    tokens = onehot.shape[0]
+    row = lax.broadcasted_iota(jnp.int32, (128, 128), 0)
+    col = lax.broadcasted_iota(jnp.int32, (128, 128), 1)
+    leaf = tables[:, :tokens]
+    lengths = tables[:, tokens : tokens + 128]
+    parents = tables[:, tokens + 128 :]
+
+    def upright(lanes):
+        return jnp.sum(jnp.where(row == col, lanes, 0), axis=1, keepdims=True)
+
+    own_lo = jnp.sum(jnp.where(row < col, upright(lengths), 0), axis=0, keepdims=True)
+    own_hi = own_lo + lengths
+    up_lo = jnp.sum(jnp.where(row == parents, upright(own_lo), 0), axis=0, keepdims=True)
+    up_hi = jnp.sum(jnp.where(row == parents, upright(own_hi), 0), axis=0, keepdims=True)
+    root = own_hi[:, :1]
     slot = kv[0] * slots + lax.broadcasted_iota(jnp.int32, (slots, 128), 0)
     seen = (
-        (slot < lengths[0])
+        (slot < root)
         | ((slot >= own_lo) & (slot < own_hi))
         | ((slot >= up_lo) & (slot < up_hi))
     )
@@ -73,7 +79,7 @@
     keys_wide[:, HEAD_WIDTH:] = jnp.where(seen, 0.0, LOWEST).astype(BF)
     values_out[...] = values[...]
     node = lax.broadcasted_iota(jnp.int32, (128, tokens), 0)
-    onehot[...] = jnp.where(node == leaf[...], 1.0, 0.0).astype(F32).T.astype(BF)
+    onehot[...] = jnp.where(node == leaf, 1.0, 0.0).astype(F32).T.astype(BF)
 
 
 def attend_kernel(q, keys_wide, values, onehot, weight, out):
@@ -219,13 +225,22 @@
     far = [move_core(w) for w in (gate_t, up_t, down_weight)]
     queries, kv, tp = lax.optimization_barrier((queries, kv, tp))
 
-    q = lax.all_to_all(jnp.broadcast_to(queries[None], (16, 16, 640)), "kv", 0, 0)
+    padding = 128 - node_lengths.shape[0]
+    tables = jnp.concatenate([token_leaf, jnp.pad(node_lengths, (0, padding)), jnp.pad(parents, (0, padding))])[None, :]
+    repeated = pl.pallas_call(
+        repeat_kernel,
+        out_shape=shape((16, 16, 640), BF),
+        in_specs=[pl.BlockSpec(memory_space=pl.ANY)],
+        out_specs=pl.BlockSpec(memory_space=pl.ANY),
+        scratch_shapes=[pltpu.SemaphoreType.DMA((16,))],
+        compiler_params=pltpu.CompilerParams(vmem_limit_bytes=56 << 20),
+    )(queries)
+    q = lax.all_to_all(repeated, "kv", 0, 0)
     keys_wide, values_in, onehot = call(
         prepare_kernel,
         [shape((keys.shape[0], 256), BF), shape(values.shape, BF), shape((256, 128), BF)],
-        [SM, SM, SM, VM, VM, VM],
-        [pltpu.SMEM((16,), jnp.int32)],
-    )(node_lengths, parents, kv, token_leaf[None, :], keys, values)
+        [SM, VM, VM, VM],
+    )(kv, tables, keys, values)
     packed = call(attend_kernel, shape((256, 768), BF), [VM] * 4 + [pl.ANY], limit=48 << 20)(
         q.reshape(256, 640), keys_wide, values_in, onehot, out_weight
     )
@@ -235,7 +250,7 @@
     )
     attended = own + move_core(other).astype(F32)
     sent = attended.astype(BF)
-    for part in [move_z(sent, k) for k in (1, 3, 2)]:
+    for part in [move_z(sent, k) for k in (2, 1, 3)]:
         attended = attended + part.astype(F32)
     residual = attended.astype(BF)
     widened = residual.astype(F32)

time: 99.4 us -> 110 us (1.11)
  Pallas kernels: 10.3 us -> 21.1 us
  waiting for transfers between devices: 16.3 us -> 20.5 us
  local copies, waits for them, and re-layouts: 5.64 us -> 2.17 us
  starting transfers between devices: 19.4 us -> 17.2 us
    pallas_call x0 -> x1, Pallas kernels: none -> 11.2 us  [local(): pl.pallas_call(repeat_kernel, out_shape=shape((16, 16, 640), BF), in_spec...]
    ppermute x3, starting transfers between devices: 5.68 us -> 3.4 us  [move_ring(): return lax.ppermute(value, ('kv', 'tp'), pairs)]
    unnamed x22 -> x16, local copies, waits for them, and re-layouts: 3.91 us -> 1.93 us
    ppermute x3, waiting for transfers between devices: 6.9 us -> 8.56 us  [move_ring(): return lax.ppermute(value, ('kv', 'tp'), pairs)]
    all_to_all x1, waiting for transfers between devices: 4.3 us -> 5.94 us  [local(): q = lax.all_to_all(repeated, 'kv', 0, 0)]
    broadcast_in_dim x1 -> x0, local copies, waits for them, and re-layouts: 1.48 us -> none  [local(): jnp.broadcast_to(queries[None], (16, 16, 640))]
  transfers between devices with their start and end apart: 11 -> 11, of which waited for: 8 -> 5; matrix products, arithmetic and copies ran while one was open for 0% -> 1% of each run, Pallas kernels for 1% -> 1%
where the time goes in v11:
time: 110 us
  blocking collectives  47.8 us (43%)
  Pallas kernels  21.1 us (19%)
  waiting for transfers between devices  20.5 us (19%)
  starting transfers between devices  17.2 us (16%)
  local copies, waits for them, and re-layouts  2.17 us (2%)
  other arithmetic  1.15 us (1%)
    all_to_all x1, blocking collectives, local(): lax.all_to_all(jnp.broadcast_to(normed[None], (16, 8, D)), 'kv', 0, 0)  22.9 us
    all_to_all x1, blocking collectives, local(): parts = lax.all_to_all(packed.reshape(16, 16, 768), 'kv', 0, 0)  12.6 us
    all_to_all x1, blocking collectives, local(): mixed = lax.all_to_all(mixed, ('kv', 'tp'), 0, 0, axis_index_groups=PLANES)  12.3 us
    pallas_call x1, Pallas kernels, local(): pl.pallas_call(repeat_kernel, out_shape=shape((16, 16, 640), BF), in_spec...  11.2 us
    ppermute x3, waiting for transfers between devices, move_ring(): return lax.ppermute(value, ('kv', 'tp'), pairs)  8.56 us
    all_to_all x1, starting transfers between devices, local(): q = lax.all_to_all(repeated, 'kv', 0, 0)  7.13 us
    ppermute x3, starting transfers between devices, move_z(): return lax.ppermute(value, 'tp', pairs)  5.97 us
    all_to_all x1, waiting for transfers between devices, local(): q = lax.all_to_all(repeated, 'kv', 0, 0)  5.94 us
  transfers between devices with their start and end apart: 11, of which 5 were waited for; matrix products, arithmetic and copies ran while one was open for 1% of the time, Pallas kernels for 1%

profile of v11, /device:TPU:0, one launch (start us, length us, event | category | flops | bytes accessed | tf_op | source)
XLA Modules:
  0.0 110.0 jit_solution(12077679117085353225)
XLA Ops:
  0.0 11.2 %shard_map.118 = bf16[16,16,640]{2,1,0:T(8,128)(2,1)} custom-call(bf16[16,640]{1,0:T(8,128)(2,1)} %rows), custom_call_target="tpu_custom_call" | custom-call | tf_op jit(solution)/shard_map/pallas_call | solution.py:230
  11.2 7.1 %all-to-all-start = ((bf16[16,16,640]{2,1,0:T(8,128)(2,1)}), bf16[16,16,640]{2,1,0:T(8,128)(2,1)S(1)}, u32[]{:S(2)}, u32[]{:S(2)}) async-start(bf16[16,16,640]{2,1,0:T(8,128)(2,1)} %shard_map.118), calls=%async_computation | async-start | bytes 655360 | tf_op jit(solution)/shard_map/all_to_all | solution.py:238
  18.3 0.7 pad_add_fusion
  19.0 0.0 copy-start.4
  19.0 0.9 copy-done.4
  20.0 0.0 copy-start.5
  20.0 0.9 copy-done.5
  20.9 0.6 shard_map.119
  21.5 5.9 %all-to-all-done = bf16[16,16,640]{2,1,0:T(8,128)(2,1)S(1)} async-done(((bf16[16,16,640]{2,1,0:T(8,128)(2,1)}), bf16[16,16,640]{2,1,0:T(8,128)(2,1)S(1)}, u32[]{:S(2)}, u32[]{:S(2)}) %all-to-all-start) | async-done | bytes 327712 | tf_op jit(solution)/shard_map/all_to_all | solution.py:238
  27.5 0.0 copy-start
  27.5 0.0 copy-start.6
  27.5 2.7 %shard_map.120 = bf16[256,768]{1,0:T(8,128)(2,1)S(1)} custom-call(bf16[256,640]{1,0:T(8,128)(2,1)S(1)} %bitcast.14, bf16[1024,256]{1,0:T(8,128)(2,1)S(1)} %get-tuple-element.20.keys_wide, bf16[1024,128]{1,0:T(8,128)(2,1)S(1)} %get-tuple-element.21.values, bf16[256,128]{1,0:T(8,128)(2,1)S(1)} %get-tuple-element.22.onehot, bf16[640,5120]{1,0:T(8,128)(2,1)} %weight.3), custom_call_target="tpu_custom_call" | custom-call | tf_op jit(solution)/shard_map/pallas_call | solution.py:244
  30.2 12.6 %all_to_all.20.parts = bf16[16,16,768]{2,1,0:T(8,128)(2,1)S(1)} all-to-all(bf16[16,16,768]{2,1,0:T(8,128)(2,1)S(1)} %bitcast.13), channel_id=1, replica_groups=mesh['kv'=16,'tp'=8] {'kv'}, dimensions={0} | all-to-all | bytes 786432 | tf_op jit(solution)/shard_map/all_to_all | solution.py:247
  42.8 0.0 copy-done
  42.8 0.0 copy-done.6
  42.8 0.0 copy-start.1
  42.8 0.0 copy-start.2
  42.8 0.0 copy-start.3
  42.8 0.0 copy-start.7
  42.8 1.5 %shard_map.121 = (f32[8,5120]{1,0:T(8,128)S(1)}, bf16[8,5120]{1,0:T(8,128)(2,1)S(1)}) custom-call(s32[1]{0:T(128)} %bitcast.1.tp, bf16[16,16,768]{2,1,0:T(8,128)(2,1)S(1)} %all_to_all.20.parts, bf16[640,5120]{1,0:T(8,128)(2,1)S(1)} %copy-done, bf16[2,5120]{1,0:T(2,128)(2,1)S(1)} %copy-done.6), custom_call_target="tpu_custom_call" | custom-call | tf_op jit(solution)/shard_map/pallas_call | solution.py:248
  44.3 0.1 collective-permute-start
  44.4 1.3 %collective-permute-done = bf16[8,5120]{1,0:T(8,128)(2,1)S(1)} collective-permute-done((bf16[8,5120]{1,0:T(8,128)(2,1)S(1)}, bf16[8,5120]{1,0:T(8,128)(2,1)S(1)}, u32[]{:S(2)}, u32[]{:S(2)}) %collective-permute-start) | collective-permute-done | bytes 81952 | tf_op jit(solution)/shard_map/ppermute | solution.py:204
  45.7 4.1 %collective-permute-start.3 = (bf16[8,5120]{1,0:T(8,128)(2,1)S(1)}, bf16[8,5120]{1,0:T(8,128)(2,1)S(1)}, u32[]{:S(2)}, u32[]{:S(2)}) collective-permute-start(bf16[8,5120]{1,0:T(8,128)(2,1)S(1)} %fusion.3), channel_id=1, source_target_pairs={{0,6},{1,7},{2,0},{3,1},{4,2},{5,3},{6,4},{7,5},{8,14},{9,15},{10,... | collective-permute-start | bytes 245768 | tf_op jit(solution)/shard_map/ppermute | solution.py:200
  49.8 0.0 collective-permute-start.2
  49.8 1.9 %collective-permute-start.1 = (bf16[8,5120]{1,0:T(8,128)(2,1)S(1)}, bf16[8,5120]{1,0:T(8,128)(2,1)S(1)}, u32[]{:S(2)}, u32[]{:S(2)}) collective-permute-start(bf16[8,5120]{1,0:T(8,128)(2,1)S(1)} %fusion.3), channel_id=1, source_target_pairs={{0,4},{1,5},{2,6},{3,7},{4,0},{5,1},{6,2},{7,3},{8,12},{9,13},{10,... | collective-permute-start | bytes 245768 | tf_op jit(solution)/shard_map/ppermute | solution.py:200
  51.6 0.0 copy-done.1
  51.6 0.0 collective-permute-start.4
  51.6 0.0 copy-done.2
  51.7 0.5 collective-permute-start.5
  52.2 0.0 collective-permute-done.3
  52.2 0.0 copy-done.3
  52.2 0.1 collective-permute-start.6
  52.3 4.7 %collective-permute-done.2 = bf16[8,5120]{1,0:T(8,128)(2,1)S(1)} collective-permute-done((bf16[8,5120]{1,0:T(8,128)(2,1)S(1)}, bf16[8,5120]{1,0:T(8,128)(2,1)S(1)}, u32[]{:S(2)}, u32[]{:S(2)}) %collective-permute-start.2) | collective-permute-done | bytes 81952 | tf_op jit(solution)/shard_map/ppermute | solution.py:200
  57.0 0.0 collective-permute-done.1
  57.0 0.2 fusion
  57.1 0.0 copy-done.7
  57.2 0.1 fusion.2
  57.2 0.1 broadcast_in_dim.20
  57.4 22.9 %all_to_all.21 = bf16[16,8,5120]{2,1,0:T(8,128)(2,1)S(1)} all-to-all(bf16[16,8,5120]{2,1,0:T(8,128)(2,1)S(1)} %broadcast_in_dim.20), channel_id=1, replica_groups=mesh['kv'=16,'tp'=8] {'kv'}, dimensions={0} | all-to-all | bytes 2621440 | tf_op jit(solution)/shard_map/all_to_all | solution.py:263
  80.3 0.0 collective-permute-done.4.gate_far
  80.3 0.0 collective-permute-done.5.up_far
  80.3 0.0 collective-permute-done.6.down_far
  80.3 4.2 %shard_map.122 = (f32[32,5120]{1,0:T(8,128)S(1)}, bf16[32,5120]{1,0:T(8,128)(2,1)S(1)}, bf16[32,5120]{1,0:T(8,128)(2,1)S(1)}, bf16[32,5120]{1,0:T(8,128)(2,1)S(1)}) custom-call(s32[1]{0:T(128)} %bitcast.kv, s32[1]{0:T(128)} %bitcast.1.tp, bf16[128,5120]{1,0:T(8,128)(2,1)S(1)} %bitcast.8, bf16[216,5120]{1,0:T(8,128)(2,1)S(1)} %bitcast.10, ...), custom_call_target="tpu_custom_call" | custom-call | tf_op jit(solution)/shard_map/pallas_call | solution.py:265
  84.5 0.1 collective-permute-start.7
  84.6 1.8 %collective-permute-start.8 = (bf16[32,5120]{1,0:T(8,128)(2,1)S(1)}, bf16[32,5120]{1,0:T(8,128)(2,1)S(1)}, u32[]{:S(2)}, u32[]{:S(2)}) collective-permute-start(bf16[32,5120]{1,0:T(8,128)(2,1)S(1)} %get-tuple-element.27), channel_id=1, source_target_pairs={{0,2},{1,33},{2,4},{3,35},{4,6},{5,37},{6,0},{7,39},{8,10},{9,41},... | collective-permute-start | bytes 983048 | tf_op jit(solution)/shard_map/ppermute | solution.py:190
  86.4 1.5 %collective-permute-start.9 = (bf16[32,5120]{1,0:T(8,128)(2,1)S(1)}, bf16[32,5120]{1,0:T(8,128)(2,1)S(1)}, u32[]{:S(2)}, u32[]{:S(2)}) collective-permute-start(bf16[32,5120]{1,0:T(8,128)(2,1)S(1)} %get-tuple-element.28), channel_id=1, source_target_pairs={{0,6},{1,97},{2,0},{3,99},{4,2},{5,101},{6,4},{7,103},{8,14},{9,10... | collective-permute-start | bytes 983048 | tf_op jit(solution)/shard_map/ppermute | solution.py:190
  87.9 5.4 %collective-permute-done.7 = bf16[32,5120]{1,0:T(8,128)(2,1)S(1)} collective-permute-done((bf16[32,5120]{1,0:T(8,128)(2,1)S(1)}, bf16[32,5120]{1,0:T(8,128)(2,1)S(1)}, u32[]{:S(2)}, u32[]{:S(2)}) %collective-permute-start.7) | collective-permute-done | bytes 327712 | tf_op jit(solution)/shard_map/ppermute | solution.py:190
  93.3 3.2 %collective-permute-done.8 = bf16[32,5120]{1,0:T(8,128)(2,1)S(1)} collective-permute-done((bf16[32,5120]{1,0:T(8,128)(2,1)S(1)}, bf16[32,5120]{1,0:T(8,128)(2,1)S(1)}, u32[]{:S(2)}, u32[]{:S(2)}) %collective-permute-start.8) | collective-permute-done | bytes 327712 | tf_op jit(solution)/shard_map/ppermute | solution.py:190
  96.5 0.0 collective-permute-done.9
  96.5 0.1 add_convert_fusion
  96.6 0.1 reshape.25
  96.8 12.3 %all_to_all.22.parts = bf16[16,2,5120]{2,1,0:T(2,128)(2,1)S(1)} all-to-all(bf16[16,2,5120]{2,1,0:T(2,128)(2,1)S(1)} %reshape.25), channel_id=1, replica_groups={{0,8,16,24,32,40,48,56,64,72,80,88,96,104,112,120},{2,10,18,26,34,42,50..., dimensions={0} | all-to-all | bytes 655360 | tf_op jit(solution)/shard_map/all_to_all | solution.py:271
  109.1 0.9 shard_map.123
  (2 shorter events, 0.0 us)
Async XLA Ops:
  11.2 16.3 %all-to-all-start = ((bf16[16,16,640]{2,1,0:T(8,128)(2,1)}), bf16[16,16,640]{2,1,0:T(8,128)(2,1)S(1)}, u32[]{:S(2)}, u32[]{:S(2)}) async-start(bf16[16,16,640]{2,1,0:T(8,128)(2,1)} %shard_map.118), calls=%async_computation | async-start | bytes 655360 | tf_op jit(solution)/shard_map/all_to_all | solution.py:238
  19.0 0.9 copy-start.4
  20.0 0.9 copy-start.5
  27.5 15.3 %copy-start = (bf16[640,5120]{1,0:T(8,128)(2,1)S(1)}, bf16[640,5120]{1,0:T(8,128)(2,1)}, u32[]{:S(2)}) copy-start(bf16[640,5120]{1,0:T(8,128)(2,1)} %weight.3) | copy-start | bytes 19660804
  27.5 15.3 %copy-start.6 = (bf16[2,5120]{1,0:T(2,128)(2,1)S(1)}, bf16[2,5120]{1,0:T(2,128)(2,1)}, u32[]{:S(2)}) copy-start(bf16[2,5120]{1,0:T(2,128)(2,1)} %activations.1) | copy-start | bytes 61444
  42.8 8.8 %copy-start.1 = (bf16[5120,216]{0,1:T(8,128)(2,1)S(1)}, bf16[5120,216]{0,1:T(8,128)(2,1)}, u32[]{:S(2)}) copy-start(bf16[5120,216]{0,1:T(8,128)(2,1)} %param.21) | copy-start | bytes 6635524
  42.8 8.8 %copy-start.2 = (bf16[5120,216]{0,1:T(8,128)(2,1)S(1)}, bf16[5120,216]{0,1:T(8,128)(2,1)}, u32[]{:S(2)}) copy-start(bf16[5120,216]{0,1:T(8,128)(2,1)} %param.22) | copy-start | bytes 6635524
  42.8 9.4 %copy-start.3 = (bf16[216,5120]{1,0:T(8,128)(2,1)S(1)}, bf16[216,5120]{1,0:T(8,128)(2,1)}, u32[]{:S(2)}) copy-start(bf16[216,5120]{1,0:T(8,128)(2,1)} %down.1) | copy-start | bytes 6635524
  42.8 14.3 %copy-start.7 = (f32[5120]{0:T(1024)S(1)}, f32[5120]{0:T(1024)}, u32[]{:S(2)}) copy-start(f32[5120]{0:T(1024)} %param.20) | copy-start | bytes 61444
  44.3 1.4 %collective-permute-start = (bf16[8,5120]{1,0:T(8,128)(2,1)S(1)}, bf16[8,5120]{1,0:T(8,128)(2,1)S(1)}, u32[]{:S(2)}, u32[]{:S(2)}) collective-permute-start(bf16[8,5120]{1,0:T(8,128)(2,1)S(1)} %get-tuple-element.24), channel_id=1, source_target_pairs={{0,1},{1,0},{2,3},{3,2},{4,5},{5,4},{6,7},{7,6},{8,9},{9,8},{10,11... | collective-permute-start | bytes 245768 | tf_op jit(solution)/shard_map/ppermute | solution.py:204
  45.7 6.5 %collective-permute-start.3 = (bf16[8,5120]{1,0:T(8,128)(2,1)S(1)}, bf16[8,5120]{1,0:T(8,128)(2,1)S(1)}, u32[]{:S(2)}, u32[]{:S(2)}) collective-permute-start(bf16[8,5120]{1,0:T(8,128)(2,1)S(1)} %fusion.3), channel_id=1, source_target_pairs={{0,6},{1,7},{2,0},{3,1},{4,2},{5,3},{6,4},{7,5},{8,14},{9,15},{10,... | collective-permute-start | bytes 245768 | tf_op jit(solution)/shard_map/ppermute | solution.py:200
  49.8 7.2 %collective-permute-start.2 = (bf16[8,5120]{1,0:T(8,128)(2,1)S(1)}, bf16[8,5120]{1,0:T(8,128)(2,1)S(1)}, u32[]{:S(2)}, u32[]{:S(2)}) collective-permute-start(bf16[8,5120]{1,0:T(8,128)(2,1)S(1)} %fusion.3), channel_id=1, source_target_pairs={{0,2},{1,3},{2,4},{3,5},{4,6},{5,7},{6,0},{7,1},{8,10},{9,11},{10,... | collective-permute-start | bytes 245768 | tf_op jit(solution)/shard_map/ppermute | solution.py:200
  49.8 7.2 %collective-permute-start.1 = (bf16[8,5120]{1,0:T(8,128)(2,1)S(1)}, bf16[8,5120]{1,0:T(8,128)(2,1)S(1)}, u32[]{:S(2)}, u32[]{:S(2)}) collective-permute-start(bf16[8,5120]{1,0:T(8,128)(2,1)S(1)} %fusion.3), channel_id=1, source_target_pairs={{0,4},{1,5},{2,6},{3,7},{4,0},{5,1},{6,2},{7,3},{8,12},{9,13},{10,... | collective-permute-start | bytes 245768 | tf_op jit(solution)/shard_map/ppermute | solution.py:200
  51.6 28.6 %collective-permute-start.4 = (bf16[216,5120]{1,0:T(8,128)(2,1)S(1)}, bf16[216,5120]{1,0:T(8,128)(2,1)S(1)}, u32[]{:S(2)}, u32[]{:S(2)}) collective-permute-start(bf16[216,5120]{1,0:T(8,128)(2,1)S(1)} %bitcast.9), channel_id=1, source_target_pairs={{0,1},{1,0},{2,3},{3,2},{4,5},{5,4},{6,7},{7,6},{8,9},{9,8},{10,11... | collective-permute-start | bytes 6635528 | tf_op jit(solution)/shard_map/ppermute | solution.py:204
  51.7 28.6 %collective-permute-start.5 = (bf16[216,5120]{1,0:T(8,128)(2,1)S(1)}, bf16[216,5120]{1,0:T(8,128)(2,1)S(1)}, u32[]{:S(2)}, u32[]{:S(2)}) collective-permute-start(bf16[216,5120]{1,0:T(8,128)(2,1)S(1)} %bitcast.11), channel_id=1, source_target_pairs={{0,1},{1,0},{2,3},{3,2},{4,5},{5,4},{6,7},{7,6},{8,9},{9,8},{10,11... | collective-permute-start | bytes 6635528 | tf_op jit(solution)/shard_map/ppermute | solution.py:204
  52.2 28.1 %collective-permute-start.6 = (bf16[216,5120]{1,0:T(8,128)(2,1)S(1)}, bf16[216,5120]{1,0:T(8,128)(2,1)S(1)}, u32[]{:S(2)}, u32[]{:S(2)}) collective-permute-start(bf16[216,5120]{1,0:T(8,128)(2,1)S(1)} %copy-done.3), channel_id=1, source_target_pairs={{0,1},{1,0},{2,3},{3,2},{4,5},{5,4},{6,7},{7,6},{8,9},{9,8},{10,11... | collective-permute-start | bytes 6635528 | tf_op jit(solution)/shard_map/ppermute | solution.py:204
  84.5 8.8 %collective-permute-start.7 = (bf16[32,5120]{1,0:T(8,128)(2,1)S(1)}, bf16[32,5120]{1,0:T(8,128)(2,1)S(1)}, u32[]{:S(2)}, u32[]{:S(2)}) collective-permute-start(bf16[32,5120]{1,0:T(8,128)(2,1)S(1)} %get-tuple-element.26), channel_id=1, source_target_pairs={{0,4},{1,65},{2,6},{3,67},{4,0},{5,69},{6,2},{7,71},{8,12},{9,73},... | collective-permute-start | bytes 983048 | tf_op jit(solution)/shard_map/ppermute | solution.py:190
  84.6 11.9 %collective-permute-start.8 = (bf16[32,5120]{1,0:T(8,128)(2,1)S(1)}, bf16[32,5120]{1,0:T(8,128)(2,1)S(1)}, u32[]{:S(2)}, u32[]{:S(2)}) collective-permute-start(bf16[32,5120]{1,0:T(8,128)(2,1)S(1)} %get-tuple-element.27), channel_id=1, source_target_pairs={{0,2},{1,33},{2,4},{3,35},{4,6},{5,37},{6,0},{7,39},{8,10},{9,41},... | collective-permute-start | bytes 983048 | tf_op jit(solution)/shard_map/ppermute | solution.py:190
  86.4 10.1 %collective-permute-start.9 = (bf16[32,5120]{1,0:T(8,128)(2,1)S(1)}, bf16[32,5120]{1,0:T(8,128)(2,1)S(1)}, u32[]{:S(2)}, u32[]{:S(2)}) collective-permute-start(bf16[32,5120]{1,0:T(8,128)(2,1)S(1)} %get-tuple-element.28), channel_id=1, source_target_pairs={{0,6},{1,97},{2,0},{3,99},{4,2},{5,101},{6,4},{7,103},{8,14},{9,10... | collective-permute-start | bytes 983048 | tf_op jit(solution)/shard_map/ppermute | solution.py:190

commit v12 on v11

--- a/solution.py
+++ b/solution.py
@@ -230,7 +230,7 @@
     repeated = pl.pallas_call(
         repeat_kernel,
         out_shape=shape((16, 16, 640), BF),
-        in_specs=[pl.BlockSpec(memory_space=pl.ANY)],
+        in_specs=[pl.BlockSpec(memory_space=VM)],
         out_specs=pl.BlockSpec(memory_space=pl.ANY),
         scratch_shapes=[pltpu.SemaphoreType.DMA((16,))],
         compiler_params=pltpu.CompilerParams(vmem_limit_bytes=56 << 20),

time: 110 us -> 101 us (0.918)
  Pallas kernels: 21.1 us -> 11.5 us
    pallas_call x1, Pallas kernels: 11.2 us -> 1.6 us  [local(): pl.pallas_call(repeat_kernel, out_shape=shape((16, 16, 640), BF), in_spec...]
where the time goes in v12:
time: 101 us; the launch traced here: 100 us
  blocking collectives  47.8 us (47%)
  waiting for transfers between devices  20.5 us (20%)
  starting transfers between devices  17.2 us (17%)
  Pallas kernels  11.5 us (11%)
  local copies, waits for them, and re-layouts  2.17 us (2%)
  other arithmetic  1.15 us (1%)
    all_to_all x1, blocking collectives, local(): lax.all_to_all(jnp.broadcast_to(normed[None], (16, 8, D)), 'kv', 0, 0)  22.9 us
    all_to_all x1, blocking collectives, local(): parts = lax.all_to_all(packed.reshape(16, 16, 768), 'kv', 0, 0)  12.6 us
    all_to_all x1, blocking collectives, local(): mixed = lax.all_to_all(mixed, ('kv', 'tp'), 0, 0, axis_index_groups=PLANES)  12.3 us
    ppermute x3, waiting for transfers between devices, move_ring(): return lax.ppermute(value, ('kv', 'tp'), pairs)  8.56 us
    all_to_all x1, starting transfers between devices, local(): q = lax.all_to_all(repeated, 'kv', 0, 0)  7.13 us
    ppermute x3, starting transfers between devices, move_z(): return lax.ppermute(value, 'tp', pairs)  5.97 us
    all_to_all x1, waiting for transfers between devices, local(): q = lax.all_to_all(repeated, 'kv', 0, 0)  5.94 us
    ppermute x3, waiting for transfers between devices, move_z(): return lax.ppermute(value, 'tp', pairs)  4.71 us
  transfers between devices with their start and end apart: 11, of which 5 were waited for; matrix products, arithmetic and copies ran while one was open for 1% of the time, Pallas kernels for 1%

profile of v12, /device:TPU:0, one launch (start us, length us, event | category | flops | bytes accessed | tf_op | source)
XLA Modules:
  0.0 100.4 jit_solution(970096179625531932)
XLA Ops:
  0.0 1.6 %shard_map.118 = bf16[16,16,640]{2,1,0:T(8,128)(2,1)} custom-call(bf16[16,640]{1,0:T(8,128)(2,1)} %rows), custom_call_target="tpu_custom_call" | custom-call | tf_op jit(solution)/shard_map/pallas_call | solution.py:230
  1.6 7.1 %all-to-all-start = ((bf16[16,16,640]{2,1,0:T(8,128)(2,1)}), bf16[16,16,640]{2,1,0:T(8,128)(2,1)S(1)}, u32[]{:S(2)}, u32[]{:S(2)}) async-start(bf16[16,16,640]{2,1,0:T(8,128)(2,1)} %shard_map.118), calls=%async_computation | async-start | bytes 655360 | tf_op jit(solution)/shard_map/all_to_all | solution.py:238
  8.7 0.7 pad_add_fusion
  9.5 0.0 copy-start.4
  9.5 0.9 copy-done.4
  10.4 0.0 copy-start.5
  10.4 0.9 copy-done.5
  11.4 0.6 shard_map.119
  12.0 5.9 %all-to-all-done = bf16[16,16,640]{2,1,0:T(8,128)(2,1)S(1)} async-done(((bf16[16,16,640]{2,1,0:T(8,128)(2,1)}), bf16[16,16,640]{2,1,0:T(8,128)(2,1)S(1)}, u32[]{:S(2)}, u32[]{:S(2)}) %all-to-all-start) | async-done | bytes 327712 | tf_op jit(solution)/shard_map/all_to_all | solution.py:238
  17.9 0.0 copy-start
  17.9 0.0 copy-start.6
  17.9 2.7 %shard_map.120 = bf16[256,768]{1,0:T(8,128)(2,1)S(1)} custom-call(bf16[256,640]{1,0:T(8,128)(2,1)S(1)} %bitcast.14, bf16[1024,256]{1,0:T(8,128)(2,1)S(1)} %get-tuple-element.20.keys_wide, bf16[1024,128]{1,0:T(8,128)(2,1)S(1)} %get-tuple-element.21.values, bf16[256,128]{1,0:T(8,128)(2,1)S(1)} %get-tuple-element.22.onehot, bf16[640,5120]{1,0:T(8,128)(2,1)} %weight.3), custom_call_target="tpu_custom_call" | custom-call | tf_op jit(solution)/shard_map/pallas_call | solution.py:244
  20.6 12.6 %all_to_all.20.parts = bf16[16,16,768]{2,1,0:T(8,128)(2,1)S(1)} all-to-all(bf16[16,16,768]{2,1,0:T(8,128)(2,1)S(1)} %bitcast.13), channel_id=1, replica_groups=mesh['kv'=16,'tp'=8] {'kv'}, dimensions={0} | all-to-all | bytes 786432 | tf_op jit(solution)/shard_map/all_to_all | solution.py:247
  33.2 0.0 copy-done
  33.2 0.0 copy-done.6
  33.2 0.0 copy-start.1
  33.2 0.0 copy-start.2
  33.2 0.0 copy-start.3
  33.3 0.0 copy-start.7
  33.3 1.5 %shard_map.121 = (f32[8,5120]{1,0:T(8,128)S(1)}, bf16[8,5120]{1,0:T(8,128)(2,1)S(1)}) custom-call(s32[1]{0:T(128)} %bitcast.1.tp, bf16[16,16,768]{2,1,0:T(8,128)(2,1)S(1)} %all_to_all.20.parts, bf16[640,5120]{1,0:T(8,128)(2,1)S(1)} %copy-done, bf16[2,5120]{1,0:T(2,128)(2,1)S(1)} %copy-done.6), custom_call_target="tpu_custom_call" | custom-call | tf_op jit(solution)/shard_map/pallas_call | solution.py:248
  34.7 0.1 collective-permute-start
  34.8 1.3 %collective-permute-done = bf16[8,5120]{1,0:T(8,128)(2,1)S(1)} collective-permute-done((bf16[8,5120]{1,0:T(8,128)(2,1)S(1)}, bf16[8,5120]{1,0:T(8,128)(2,1)S(1)}, u32[]{:S(2)}, u32[]{:S(2)}) %collective-permute-start) | collective-permute-done | bytes 81952 | tf_op jit(solution)/shard_map/ppermute | solution.py:204
  36.1 4.1 %collective-permute-start.3 = (bf16[8,5120]{1,0:T(8,128)(2,1)S(1)}, bf16[8,5120]{1,0:T(8,128)(2,1)S(1)}, u32[]{:S(2)}, u32[]{:S(2)}) collective-permute-start(bf16[8,5120]{1,0:T(8,128)(2,1)S(1)} %fusion.3), channel_id=1, source_target_pairs={{0,6},{1,7},{2,0},{3,1},{4,2},{5,3},{6,4},{7,5},{8,14},{9,15},{10,... | collective-permute-start | bytes 245768 | tf_op jit(solution)/shard_map/ppermute | solution.py:200
  40.2 0.0 collective-permute-start.2
  40.2 1.9 %collective-permute-start.1 = (bf16[8,5120]{1,0:T(8,128)(2,1)S(1)}, bf16[8,5120]{1,0:T(8,128)(2,1)S(1)}, u32[]{:S(2)}, u32[]{:S(2)}) collective-permute-start(bf16[8,5120]{1,0:T(8,128)(2,1)S(1)} %fusion.3), channel_id=1, source_target_pairs={{0,4},{1,5},{2,6},{3,7},{4,0},{5,1},{6,2},{7,3},{8,12},{9,13},{10,... | collective-permute-start | bytes 245768 | tf_op jit(solution)/shard_map/ppermute | solution.py:200
  42.1 0.0 copy-done.1
  42.1 0.0 collective-permute-start.4
  42.1 0.0 copy-done.2
  42.1 0.5 collective-permute-start.5
  42.6 0.0 collective-permute-done.3
  42.6 0.0 copy-done.3
  42.6 0.1 collective-permute-start.6
  42.7 4.7 %collective-permute-done.2 = bf16[8,5120]{1,0:T(8,128)(2,1)S(1)} collective-permute-done((bf16[8,5120]{1,0:T(8,128)(2,1)S(1)}, bf16[8,5120]{1,0:T(8,128)(2,1)S(1)}, u32[]{:S(2)}, u32[]{:S(2)}) %collective-permute-start.2) | collective-permute-done | bytes 81952 | tf_op jit(solution)/shard_map/ppermute | solution.py:200
  47.4 0.0 collective-permute-done.1
  47.4 0.2 fusion
  47.6 0.0 copy-done.7
  47.6 0.1 fusion.2
  47.7 0.1 broadcast_in_dim.20
  47.8 22.9 %all_to_all.21 = bf16[16,8,5120]{2,1,0:T(8,128)(2,1)S(1)} all-to-all(bf16[16,8,5120]{2,1,0:T(8,128)(2,1)S(1)} %broadcast_in_dim.20), channel_id=1, replica_groups=mesh['kv'=16,'tp'=8] {'kv'}, dimensions={0} | all-to-all | bytes 2621440 | tf_op jit(solution)/shard_map/all_to_all | solution.py:263
  70.7 0.0 collective-permute-done.4.gate_far
  70.7 0.0 collective-permute-done.5.up_far
  70.7 0.0 collective-permute-done.6.down_far
  70.7 4.2 %shard_map.122 = (f32[32,5120]{1,0:T(8,128)S(1)}, bf16[32,5120]{1,0:T(8,128)(2,1)S(1)}, bf16[32,5120]{1,0:T(8,128)(2,1)S(1)}, bf16[32,5120]{1,0:T(8,128)(2,1)S(1)}) custom-call(s32[1]{0:T(128)} %bitcast.kv, s32[1]{0:T(128)} %bitcast.1.tp, bf16[128,5120]{1,0:T(8,128)(2,1)S(1)} %bitcast.8, bf16[216,5120]{1,0:T(8,128)(2,1)S(1)} %bitcast.10, ...), custom_call_target="tpu_custom_call" | custom-call | tf_op jit(solution)/shard_map/pallas_call | solution.py:265
  74.9 0.1 collective-permute-start.7
  75.1 1.8 %collective-permute-start.8 = (bf16[32,5120]{1,0:T(8,128)(2,1)S(1)}, bf16[32,5120]{1,0:T(8,128)(2,1)S(1)}, u32[]{:S(2)}, u32[]{:S(2)}) collective-permute-start(bf16[32,5120]{1,0:T(8,128)(2,1)S(1)} %get-tuple-element.27), channel_id=1, source_target_pairs={{0,2},{1,33},{2,4},{3,35},{4,6},{5,37},{6,0},{7,39},{8,10},{9,41},... | collective-permute-start | bytes 983048 | tf_op jit(solution)/shard_map/ppermute | solution.py:190
  76.8 1.5 %collective-permute-start.9 = (bf16[32,5120]{1,0:T(8,128)(2,1)S(1)}, bf16[32,5120]{1,0:T(8,128)(2,1)S(1)}, u32[]{:S(2)}, u32[]{:S(2)}) collective-permute-start(bf16[32,5120]{1,0:T(8,128)(2,1)S(1)} %get-tuple-element.28), channel_id=1, source_target_pairs={{0,6},{1,97},{2,0},{3,99},{4,2},{5,101},{6,4},{7,103},{8,14},{9,10... | collective-permute-start | bytes 983048 | tf_op jit(solution)/shard_map/ppermute | solution.py:190
  78.3 5.4 %collective-permute-done.7 = bf16[32,5120]{1,0:T(8,128)(2,1)S(1)} collective-permute-done((bf16[32,5120]{1,0:T(8,128)(2,1)S(1)}, bf16[32,5120]{1,0:T(8,128)(2,1)S(1)}, u32[]{:S(2)}, u32[]{:S(2)}) %collective-permute-start.7) | collective-permute-done | bytes 327712 | tf_op jit(solution)/shard_map/ppermute | solution.py:190
  83.7 3.2 %collective-permute-done.8 = bf16[32,5120]{1,0:T(8,128)(2,1)S(1)} collective-permute-done((bf16[32,5120]{1,0:T(8,128)(2,1)S(1)}, bf16[32,5120]{1,0:T(8,128)(2,1)S(1)}, u32[]{:S(2)}, u32[]{:S(2)}) %collective-permute-start.8) | collective-permute-done | bytes 327712 | tf_op jit(solution)/shard_map/ppermute | solution.py:190
  86.9 0.0 collective-permute-done.9
  86.9 0.1 add_convert_fusion
  87.1 0.1 reshape.25
  87.2 12.3 %all_to_all.22.parts = bf16[16,2,5120]{2,1,0:T(2,128)(2,1)S(1)} all-to-all(bf16[16,2,5120]{2,1,0:T(2,128)(2,1)S(1)} %reshape.25), channel_id=1, replica_groups={{0,8,16,24,32,40,48,56,64,72,80,88,96,104,112,120},{2,10,18,26,34,42,50..., dimensions={0} | all-to-all | bytes 655360 | tf_op jit(solution)/shard_map/all_to_all | solution.py:271
  99.5 0.9 shard_map.123
  (2 shorter events, 0.0 us)
Async XLA Ops:
  1.6 16.3 %all-to-all-start = ((bf16[16,16,640]{2,1,0:T(8,128)(2,1)}), bf16[16,16,640]{2,1,0:T(8,128)(2,1)S(1)}, u32[]{:S(2)}, u32[]{:S(2)}) async-start(bf16[16,16,640]{2,1,0:T(8,128)(2,1)} %shard_map.118), calls=%async_computation | async-start | bytes 655360 | tf_op jit(solution)/shard_map/all_to_all | solution.py:238
  9.5 0.9 copy-start.4
  10.4 0.9 copy-start.5
  17.9 15.3 %copy-start = (bf16[640,5120]{1,0:T(8,128)(2,1)S(1)}, bf16[640,5120]{1,0:T(8,128)(2,1)}, u32[]{:S(2)}) copy-start(bf16[640,5120]{1,0:T(8,128)(2,1)} %weight.3) | copy-start | bytes 19660804
  17.9 15.3 %copy-start.6 = (bf16[2,5120]{1,0:T(2,128)(2,1)S(1)}, bf16[2,5120]{1,0:T(2,128)(2,1)}, u32[]{:S(2)}) copy-start(bf16[2,5120]{1,0:T(2,128)(2,1)} %activations.1) | copy-start | bytes 61444
  33.2 8.8 %copy-start.1 = (bf16[5120,216]{0,1:T(8,128)(2,1)S(1)}, bf16[5120,216]{0,1:T(8,128)(2,1)}, u32[]{:S(2)}) copy-start(bf16[5120,216]{0,1:T(8,128)(2,1)} %param.21) | copy-start | bytes 6635524
  33.2 8.8 %copy-start.2 = (bf16[5120,216]{0,1:T(8,128)(2,1)S(1)}, bf16[5120,216]{0,1:T(8,128)(2,1)}, u32[]{:S(2)}) copy-start(bf16[5120,216]{0,1:T(8,128)(2,1)} %param.22) | copy-start | bytes 6635524
  33.2 9.4 %copy-start.3 = (bf16[216,5120]{1,0:T(8,128)(2,1)S(1)}, bf16[216,5120]{1,0:T(8,128)(2,1)}, u32[]{:S(2)}) copy-start(bf16[216,5120]{1,0:T(8,128)(2,1)} %down.1) | copy-start | bytes 6635524
  33.3 14.3 %copy-start.7 = (f32[5120]{0:T(1024)S(1)}, f32[5120]{0:T(1024)}, u32[]{:S(2)}) copy-start(f32[5120]{0:T(1024)} %param.20) | copy-start | bytes 61444
  34.7 1.4 %collective-permute-start = (bf16[8,5120]{1,0:T(8,128)(2,1)S(1)}, bf16[8,5120]{1,0:T(8,128)(2,1)S(1)}, u32[]{:S(2)}, u32[]{:S(2)}) collective-permute-start(bf16[8,5120]{1,0:T(8,128)(2,1)S(1)} %get-tuple-element.24), channel_id=1, source_target_pairs={{0,1},{1,0},{2,3},{3,2},{4,5},{5,4},{6,7},{7,6},{8,9},{9,8},{10,11... | collective-permute-start | bytes 245768 | tf_op jit(solution)/shard_map/ppermute | solution.py:204
  36.1 6.5 %collective-permute-start.3 = (bf16[8,5120]{1,0:T(8,128)(2,1)S(1)}, bf16[8,5120]{1,0:T(8,128)(2,1)S(1)}, u32[]{:S(2)}, u32[]{:S(2)}) collective-permute-start(bf16[8,5120]{1,0:T(8,128)(2,1)S(1)} %fusion.3), channel_id=1, source_target_pairs={{0,6},{1,7},{2,0},{3,1},{4,2},{5,3},{6,4},{7,5},{8,14},{9,15},{10,... | collective-permute-start | bytes 245768 | tf_op jit(solution)/shard_map/ppermute | solution.py:200
  40.2 7.2 %collective-permute-start.2 = (bf16[8,5120]{1,0:T(8,128)(2,1)S(1)}, bf16[8,5120]{1,0:T(8,128)(2,1)S(1)}, u32[]{:S(2)}, u32[]{:S(2)}) collective-permute-start(bf16[8,5120]{1,0:T(8,128)(2,1)S(1)} %fusion.3), channel_id=1, source_target_pairs={{0,2},{1,3},{2,4},{3,5},{4,6},{5,7},{6,0},{7,1},{8,10},{9,11},{10,... | collective-permute-start | bytes 245768 | tf_op jit(solution)/shard_map/ppermute | solution.py:200
  40.2 7.2 %collective-permute-start.1 = (bf16[8,5120]{1,0:T(8,128)(2,1)S(1)}, bf16[8,5120]{1,0:T(8,128)(2,1)S(1)}, u32[]{:S(2)}, u32[]{:S(2)}) collective-permute-start(bf16[8,5120]{1,0:T(8,128)(2,1)S(1)} %fusion.3), channel_id=1, source_target_pairs={{0,4},{1,5},{2,6},{3,7},{4,0},{5,1},{6,2},{7,3},{8,12},{9,13},{10,... | collective-permute-start | bytes 245768 | tf_op jit(solution)/shard_map/ppermute | solution.py:200
  42.1 28.6 %collective-permute-start.4 = (bf16[216,5120]{1,0:T(8,128)(2,1)S(1)}, bf16[216,5120]{1,0:T(8,128)(2,1)S(1)}, u32[]{:S(2)}, u32[]{:S(2)}) collective-permute-start(bf16[216,5120]{1,0:T(8,128)(2,1)S(1)} %bitcast.9), channel_id=1, source_target_pairs={{0,1},{1,0},{2,3},{3,2},{4,5},{5,4},{6,7},{7,6},{8,9},{9,8},{10,11... | collective-permute-start | bytes 6635528 | tf_op jit(solution)/shard_map/ppermute | solution.py:204
  42.1 28.6 %collective-permute-start.5 = (bf16[216,5120]{1,0:T(8,128)(2,1)S(1)}, bf16[216,5120]{1,0:T(8,128)(2,1)S(1)}, u32[]{:S(2)}, u32[]{:S(2)}) collective-permute-start(bf16[216,5120]{1,0:T(8,128)(2,1)S(1)} %bitcast.11), channel_id=1, source_target_pairs={{0,1},{1,0},{2,3},{3,2},{4,5},{5,4},{6,7},{7,6},{8,9},{9,8},{10,11... | collective-permute-start | bytes 6635528 | tf_op jit(solution)/shard_map/ppermute | solution.py:204
  42.6 28.1 %collective-permute-start.6 = (bf16[216,5120]{1,0:T(8,128)(2,1)S(1)}, bf16[216,5120]{1,0:T(8,128)(2,1)S(1)}, u32[]{:S(2)}, u32[]{:S(2)}) collective-permute-start(bf16[216,5120]{1,0:T(8,128)(2,1)S(1)} %copy-done.3), channel_id=1, source_target_pairs={{0,1},{1,0},{2,3},{3,2},{4,5},{5,4},{6,7},{7,6},{8,9},{9,8},{10,11... | collective-permute-start | bytes 6635528 | tf_op jit(solution)/shard_map/ppermute | solution.py:204
  74.9 8.8 %collective-permute-start.7 = (bf16[32,5120]{1,0:T(8,128)(2,1)S(1)}, bf16[32,5120]{1,0:T(8,128)(2,1)S(1)}, u32[]{:S(2)}, u32[]{:S(2)}) collective-permute-start(bf16[32,5120]{1,0:T(8,128)(2,1)S(1)} %get-tuple-element.26), channel_id=1, source_target_pairs={{0,4},{1,65},{2,6},{3,67},{4,0},{5,69},{6,2},{7,71},{8,12},{9,73},... | collective-permute-start | bytes 983048 | tf_op jit(solution)/shard_map/ppermute | solution.py:190
  75.1 11.9 %collective-permute-start.8 = (bf16[32,5120]{1,0:T(8,128)(2,1)S(1)}, bf16[32,5120]{1,0:T(8,128)(2,1)S(1)}, u32[]{:S(2)}, u32[]{:S(2)}) collective-permute-start(bf16[32,5120]{1,0:T(8,128)(2,1)S(1)} %get-tuple-element.27), channel_id=1, source_target_pairs={{0,2},{1,33},{2,4},{3,35},{4,6},{5,37},{6,0},{7,39},{8,10},{9,41},... | collective-permute-start | bytes 983048 | tf_op jit(solution)/shard_map/ppermute | solution.py:190
  76.8 10.1 %collective-permute-start.9 = (bf16[32,5120]{1,0:T(8,128)(2,1)S(1)}, bf16[32,5120]{1,0:T(8,128)(2,1)S(1)}, u32[]{:S(2)}, u32[]{:S(2)}) collective-permute-start(bf16[32,5120]{1,0:T(8,128)(2,1)S(1)} %get-tuple-element.28), channel_id=1, source_target_pairs={{0,6},{1,97},{2,0},{3,99},{4,2},{5,101},{6,4},{7,103},{8,14},{9,10... | collective-permute-start | bytes 983048 | tf_op jit(solution)/shard_map/ppermute | solution.py:190

commit v13 on v12

--- a/solution.py
+++ b/solution.py
@@ -42,14 +42,6 @@
 
 def mm(a, b):
     return lax.dot_general(a, b, (((1,), (0,)), ((), ())), preferred_element_type=F32)
-
-
-def repeat_kernel(rows, out, sem):
-    copies = [pltpu.make_async_copy(rows, out.at[k], sem.at[k]) for k in range(out.shape[0])]
-    for copy in copies:
-        copy.start()
-    for copy in copies:
-        copy.wait()
 
 
 def prepare_kernel(kv, tables, keys, values, keys_wide, values_out, onehot):
@@ -136,6 +128,20 @@
     other[...] = result[8:].astype(BF)
 
 
+def normalize_kernel(gain, own, swapped, *refs):
+    residual, repeated = refs[-2:]
+    total = own[...] + swapped[...].astype(F32)
+    for part in refs[:-2]:
+        total = total + part[...].astype(F32)
+    rounded = total.astype(BF)
+    residual[...] = rounded
+    wide = rounded.astype(F32)
+    scale = lax.rsqrt(jnp.mean(wide * wide, axis=1, keepdims=True) + EPSILON)
+    normed = (wide * scale * gain[...]).astype(BF)
+    for k in range(repeated.shape[0]):
+        repeated[k] = normed
+
+
 def hidden_of(rows, gate, up):
     g = nt(rows, gate)
     u = nt(rows, up)
@@ -222,20 +228,11 @@
     tp = lax.axis_index("tp")[None]
     gate_t, up_t = gate_weight.T, up_weight.T
     shape = jax.ShapeDtypeStruct
-    far = [move_core(w) for w in (gate_t, up_t, down_weight)]
     queries, kv, tp = lax.optimization_barrier((queries, kv, tp))
 
     padding = 128 - node_lengths.shape[0]
     tables = jnp.concatenate([token_leaf, jnp.pad(node_lengths, (0, padding)), jnp.pad(parents, (0, padding))])[None, :]
-    repeated = pl.pallas_call(
-        repeat_kernel,
-        out_shape=shape((16, 16, 640), BF),
-        in_specs=[pl.BlockSpec(memory_space=VM)],
-        out_specs=pl.BlockSpec(memory_space=pl.ANY),
-        scratch_shapes=[pltpu.SemaphoreType.DMA((16,))],
-        compiler_params=pltpu.CompilerParams(vmem_limit_bytes=56 << 20),
-    )(queries)
-    q = lax.all_to_all(repeated, "kv", 0, 0)
+    q = lax.all_to_all(jnp.broadcast_to(queries[None], (16, 16, 640)), "kv", 0, 0)
     keys_wide, values_in, onehot = call(
         prepare_kernel,
         [shape((keys.shape[0], 256), BF), shape(values.shape, BF), shape((256, 128), BF)],
@@ -248,19 +245,15 @@
     own, other = call(project_kernel, [shape((8, D), F32), shape((8, D), BF)], [SM, VM, VM, VM])(
         tp, parts, out_weight, activations
     )
-    attended = own + move_core(other).astype(F32)
-    sent = attended.astype(BF)
-    for part in [move_z(sent, k) for k in (2, 1, 3)]:
-        attended = attended + part.astype(F32)
-    residual = attended.astype(BF)
-    widened = residual.astype(F32)
-    normed = (
-        widened
-        * lax.rsqrt(jnp.mean(widened * widened, axis=1, keepdims=True) + EPSILON)
-        * norm_gain
-    ).astype(BF)
-
-    rows = lax.all_to_all(jnp.broadcast_to(normed[None], (16, 8, D)), "kv", 0, 0).reshape(128, D)
+    swapped = move_core(other)
+    sent = (own + swapped.astype(F32)).astype(BF)
+    around = [move_z(sent, k) for k in (2, 1, 3)]
+    residual, repeated = call(normalize_kernel, [shape((8, D), BF), shape((16, 8, D), BF)], [VM] * 6)(
+        norm_gain[None, :], own, swapped, *around
+    )
+    repeated, *far = lax.optimization_barrier((repeated, gate_t, up_t, down_weight))
+    far = [move_core(w) for w in far]
+    rows = lax.all_to_all(repeated, "kv", 0, 0).reshape(128, D)
     block = shape((32, D), BF)
     mixed, *sent = call(
         mlp_kernel, [shape((32, D), F32), block, block, block], [SM, SM] + [VM] * 7, limit=28 << 20

time: 101 us -> 102 us (level)
  local copies, waits for them, and re-layouts: 2.17 us -> 3.52 us
  Pallas kernels: 11.5 us -> 10.2 us
    broadcast_in_dim x1, local copies, waits for them, and re-layouts: 0.12 us -> 1.47 us  [local(): jnp.broadcast_to(queries[None], (16, 16, 640))]
    pallas_call x1, Pallas kernels: 1.6 us -> 0.28 us  [local(): call(normalize_kernel, [shape((8, D), BF), shape((16, 8, D), BF)], [VM] * 6)]
  transfers between devices with their start and end apart: 11 -> 11, of which waited for: 5 -> 6; matrix products, arithmetic and copies ran while one was open for 1% -> 1% of each run, Pallas kernels for 1% -> 1%
where the time goes in v13:
time: 102 us
  blocking collectives  48.7 us (48%)
  waiting for transfers between devices  20.8 us (20%)
  starting transfers between devices  17.8 us (17%)
  Pallas kernels  10.2 us (10%)
  local copies, waits for them, and re-layouts  3.52 us (3%)
    all_to_all x1, blocking collectives, local(): rows = lax.all_to_all(repeated, 'kv', 0, 0).reshape(128, D)  23.8 us
    all_to_all x1, blocking collectives, local(): parts = lax.all_to_all(packed.reshape(16, 16, 768), 'kv', 0, 0)  12.6 us
    all_to_all x1, blocking collectives, local(): mixed = lax.all_to_all(mixed, ('kv', 'tp'), 0, 0, axis_index_groups=PLANES)  12.3 us
    ppermute x3, waiting for transfers between devices, move_ring(): return lax.ppermute(value, ('kv', 'tp'), pairs)  8.24 us
    all_to_all x1, starting transfers between devices, local(): lax.all_to_all(jnp.broadcast_to(queries[None], (16, 16, 640)), 'kv', 0, 0)  7.12 us
    ppermute x3, starting transfers between devices, move_z(): return lax.ppermute(value, 'tp', pairs)  5.97 us
    all_to_all x1, waiting for transfers between devices, local(): lax.all_to_all(jnp.broadcast_to(queries[None], (16, 16, 640)), 'kv', 0, 0)  5.93 us
    ppermute x3, waiting for transfers between devices, move_z(): return lax.ppermute(value, 'tp', pairs)  5.33 us
  transfers between devices with their start and end apart: 11, of which 6 were waited for; matrix products, arithmetic and copies ran while one was open for 1% of the time, Pallas kernels for 1%

profile of v13, /device:TPU:0, one launch (start us, length us, event | category | flops | bytes accessed | tf_op | source)
XLA Modules:
  0.0 102.0 jit_solution(16471969667424794153)
XLA Ops:
  0.0 1.5 %broadcast_in_dim.21 = bf16[16,16,640]{2,1,0:T(8,128)(2,1)} broadcast(bf16[16,640]{1,0:T(8,128)(2,1)} %param.13), dimensions={1,2} | broadcast | bytes 348160 | tf_op jit(solution)/shard_map/broadcast_in_dim | solution.py:235
  1.5 7.1 %all-to-all-start = ((bf16[16,16,640]{2,1,0:T(8,128)(2,1)}), bf16[16,16,640]{2,1,0:T(8,128)(2,1)S(1)}, u32[]{:S(2)}, u32[]{:S(2)}) async-start(bf16[16,16,640]{2,1,0:T(8,128)(2,1)} %broadcast_in_dim.21), calls=%async_computation | async-start | bytes 655360 | tf_op jit(solution)/shard_map/all_to_all | solution.py:235
  8.6 0.7 pad_add_fusion
  9.3 0.0 copy-start.4
  9.3 0.9 copy-done.4
  10.3 0.0 copy-start.5
  10.3 0.9 copy-done.5
  11.2 0.6 shard_map.118
  11.8 5.9 %all-to-all-done = bf16[16,16,640]{2,1,0:T(8,128)(2,1)S(1)} async-done(((bf16[16,16,640]{2,1,0:T(8,128)(2,1)}), bf16[16,16,640]{2,1,0:T(8,128)(2,1)S(1)}, u32[]{:S(2)}, u32[]{:S(2)}) %all-to-all-start) | async-done | bytes 327712 | tf_op jit(solution)/shard_map/all_to_all | solution.py:235
  17.8 0.0 copy-start
  17.8 0.0 copy-start.6
  17.8 2.7 %shard_map.119 = bf16[256,768]{1,0:T(8,128)(2,1)S(1)} custom-call(bf16[256,640]{1,0:T(8,128)(2,1)S(1)} %bitcast.15, bf16[1024,256]{1,0:T(8,128)(2,1)S(1)} %get-tuple-element.26.keys_wide, bf16[1024,128]{1,0:T(8,128)(2,1)S(1)} %get-tuple-element.27.values, bf16[256,128]{1,0:T(8,128)(2,1)S(1)} %get-tuple-element.28.onehot, bf16[640,5120]{1,0:T(8,128)(2,1)} %weight.3), custom_call_target="tpu_custom_call" | custom-call | tf_op jit(solution)/shard_map/pallas_call | solution.py:241
  20.5 12.6 %all_to_all.20.parts = bf16[16,16,768]{2,1,0:T(8,128)(2,1)S(1)} all-to-all(bf16[16,16,768]{2,1,0:T(8,128)(2,1)S(1)} %bitcast.14), channel_id=1, replica_groups=mesh['kv'=16,'tp'=8] {'kv'}, dimensions={0} | all-to-all | bytes 786432 | tf_op jit(solution)/shard_map/all_to_all | solution.py:244
  33.1 0.0 copy-done
  33.1 0.0 copy-done.6
  33.1 0.0 copy-start.7
  33.1 0.0 copy-start.1
  33.1 0.0 copy-start.2
  33.1 0.0 copy-start.3
  33.1 1.5 %shard_map.120 = (f32[8,5120]{1,0:T(8,128)S(1)}, bf16[8,5120]{1,0:T(8,128)(2,1)S(1)}) custom-call(s32[1]{0:T(128)} %bitcast.1.tp, bf16[16,16,768]{2,1,0:T(8,128)(2,1)S(1)} %all_to_all.20.parts, bf16[640,5120]{1,0:T(8,128)(2,1)S(1)} %copy-done, bf16[2,5120]{1,0:T(2,128)(2,1)S(1)} %copy-done.6), custom_call_target="tpu_custom_call" | custom-call | tf_op jit(solution)/shard_map/pallas_call | solution.py:245
  34.6 0.1 collective-permute-start
  34.7 1.3 %collective-permute-done.swapped = bf16[8,5120]{1,0:T(8,128)(2,1)S(1)} collective-permute-done((bf16[8,5120]{1,0:T(8,128)(2,1)S(1)}, bf16[8,5120]{1,0:T(8,128)(2,1)S(1)}, u32[]{:S(2)}, u32[]{:S(2)}) %collective-permute-start) | collective-permute-done | bytes 81952 | tf_op jit(solution)/shard_map/ppermute | solution.py:210
  36.0 4.1 %collective-permute-start.3 = (bf16[8,5120]{1,0:T(8,128)(2,1)S(1)}, bf16[8,5120]{1,0:T(8,128)(2,1)S(1)}, u32[]{:S(2)}, u32[]{:S(2)}) collective-permute-start(bf16[8,5120]{1,0:T(8,128)(2,1)S(1)} %add_convert_fusion.1), channel_id=1, source_target_pairs={{0,6},{1,7},{2,0},{3,1},{4,2},{5,3},{6,4},{7,5},{8,14},{9,15},{10,... | collective-permute-start | bytes 245768 | tf_op jit(solution)/shard_map/ppermute | solution.py:206
  40.1 0.0 collective-permute-start.2
  40.1 1.9 %collective-permute-start.1 = (bf16[8,5120]{1,0:T(8,128)(2,1)S(1)}, bf16[8,5120]{1,0:T(8,128)(2,1)S(1)}, u32[]{:S(2)}, u32[]{:S(2)}) collective-permute-start(bf16[8,5120]{1,0:T(8,128)(2,1)S(1)} %add_convert_fusion.1), channel_id=1, source_target_pairs={{0,4},{1,5},{2,6},{3,7},{4,0},{5,1},{6,2},{7,3},{8,12},{9,13},{10,... | collective-permute-start | bytes 245768 | tf_op jit(solution)/shard_map/ppermute | solution.py:206
  41.9 0.2 collective-permute-done.3.refs_2_
  42.1 5.1 %collective-permute-done.2.refs_1_ = bf16[8,5120]{1,0:T(8,128)(2,1)S(1)} collective-permute-done((bf16[8,5120]{1,0:T(8,128)(2,1)S(1)}, bf16[8,5120]{1,0:T(8,128)(2,1)S(1)}, u32[]{:S(2)}, u32[]{:S(2)}) %collective-permute-start.2) | collective-permute-done | bytes 81952 | tf_op jit(solution)/shard_map/ppermute | solution.py:206
  47.2 0.0 collective-permute-done.1.refs_0_
  47.3 0.0 copy-done.7
  47.3 0.3 shard_map.121
  47.5 0.0 copy-done.1
  47.6 0.1 collective-permute-start.4
  47.6 0.0 copy-done.2
  47.7 0.5 collective-permute-start.5
  48.1 0.0 copy-done.3
  48.1 0.1 collective-permute-start.6
  48.2 23.8 %all_to_all.21 = bf16[16,8,5120]{2,1,0:T(8,128)(2,1)S(1)} all-to-all(bf16[16,8,5120]{2,1,0:T(8,128)(2,1)S(1)} %get-tuple-element.33), channel_id=1, replica_groups=mesh['kv'=16,'tp'=8] {'kv'}, dimensions={0} | all-to-all | bytes 2621440 | tf_op jit(solution)/shard_map/all_to_all | solution.py:256
  72.1 0.0 collective-permute-done.4.gate_far
  72.1 0.0 collective-permute-done.5.up_far
  72.1 0.0 collective-permute-done.6.down_far
  72.1 4.2 %shard_map.122 = (f32[32,5120]{1,0:T(8,128)S(1)}, bf16[32,5120]{1,0:T(8,128)(2,1)S(1)}, bf16[32,5120]{1,0:T(8,128)(2,1)S(1)}, bf16[32,5120]{1,0:T(8,128)(2,1)S(1)}) custom-call(s32[1]{0:T(128)} %bitcast.kv, s32[1]{0:T(128)} %bitcast.1.tp, bf16[128,5120]{1,0:T(8,128)(2,1)S(1)} %bitcast.9, bf16[216,5120]{1,0:T(8,128)(2,1)S(1)} %bitcast.11, ...), custom_call_target="tpu_custom_call" | custom-call | tf_op jit(solution)/shard_map/pallas_call | solution.py:258
  76.3 0.7 collective-permute-start.7
  77.0 2.2 %collective-permute-start.8 = (bf16[32,5120]{1,0:T(8,128)(2,1)S(1)}, bf16[32,5120]{1,0:T(8,128)(2,1)S(1)}, u32[]{:S(2)}, u32[]{:S(2)}) collective-permute-start(bf16[32,5120]{1,0:T(8,128)(2,1)S(1)} %get-tuple-element.39), channel_id=1, source_target_pairs={{0,2},{1,33},{2,4},{3,35},{4,6},{5,37},{6,0},{7,39},{8,10},{9,41},... | collective-permute-start | bytes 983048 | tf_op jit(solution)/shard_map/ppermute | solution.py:196
  79.3 1.0 collective-permute-start.9
  80.3 4.8 %collective-permute-done.7 = bf16[32,5120]{1,0:T(8,128)(2,1)S(1)} collective-permute-done((bf16[32,5120]{1,0:T(8,128)(2,1)S(1)}, bf16[32,5120]{1,0:T(8,128)(2,1)S(1)}, u32[]{:S(2)}, u32[]{:S(2)}) %collective-permute-start.7) | collective-permute-done | bytes 327712 | tf_op jit(solution)/shard_map/ppermute | solution.py:196
  85.1 3.4 %collective-permute-done.8 = bf16[32,5120]{1,0:T(8,128)(2,1)S(1)} collective-permute-done((bf16[32,5120]{1,0:T(8,128)(2,1)S(1)}, bf16[32,5120]{1,0:T(8,128)(2,1)S(1)}, u32[]{:S(2)}, u32[]{:S(2)}) %collective-permute-start.8) | collective-permute-done | bytes 327712 | tf_op jit(solution)/shard_map/ppermute | solution.py:196
  88.5 0.0 collective-permute-done.9
  88.5 0.2 add_convert_fusion
  88.7 0.1 reshape.16
  88.8 12.3 %all_to_all.22.parts = bf16[16,2,5120]{2,1,0:T(2,128)(2,1)S(1)} all-to-all(bf16[16,2,5120]{2,1,0:T(2,128)(2,1)S(1)} %reshape.16), channel_id=1, replica_groups={{0,8,16,24,32,40,48,56,64,72,80,88,96,104,112,120},{2,10,18,26,34,42,50..., dimensions={0} | all-to-all | bytes 655360 | tf_op jit(solution)/shard_map/all_to_all | solution.py:264
  101.1 0.9 shard_map.123
  (1 shorter events, 0.0 us)
Async XLA Ops:
  1.5 16.3 %all-to-all-start = ((bf16[16,16,640]{2,1,0:T(8,128)(2,1)}), bf16[16,16,640]{2,1,0:T(8,128)(2,1)S(1)}, u32[]{:S(2)}, u32[]{:S(2)}) async-start(bf16[16,16,640]{2,1,0:T(8,128)(2,1)} %broadcast_in_dim.21), calls=%async_computation | async-start | bytes 655360 | tf_op jit(solution)/shard_map/all_to_all | solution.py:235
  9.3 0.9 copy-start.4
  10.3 0.9 copy-start.5
  17.8 15.3 %copy-start = (bf16[640,5120]{1,0:T(8,128)(2,1)S(1)}, bf16[640,5120]{1,0:T(8,128)(2,1)}, u32[]{:S(2)}) copy-start(bf16[640,5120]{1,0:T(8,128)(2,1)} %weight.3) | copy-start | bytes 19660804
  17.8 15.3 %copy-start.6 = (bf16[2,5120]{1,0:T(2,128)(2,1)S(1)}, bf16[2,5120]{1,0:T(2,128)(2,1)}, u32[]{:S(2)}) copy-start(bf16[2,5120]{1,0:T(2,128)(2,1)} %activations.1) | copy-start | bytes 61444
  33.1 14.2 %copy-start.7 = (f32[5120]{0:T(1024)S(1)}, f32[5120]{0:T(1024)}, u32[]{:S(2)}) copy-start(f32[5120]{0:T(1024)} %param.20) | copy-start | bytes 61444
  33.1 14.5 %copy-start.1 = (bf16[5120,216]{0,1:T(8,128)(2,1)S(1)}, bf16[5120,216]{0,1:T(8,128)(2,1)}, u32[]{:S(2)}) copy-start(bf16[5120,216]{0,1:T(8,128)(2,1)} %param.21) | copy-start | bytes 6635524
  33.1 14.6 %copy-start.2 = (bf16[5120,216]{0,1:T(8,128)(2,1)S(1)}, bf16[5120,216]{0,1:T(8,128)(2,1)}, u32[]{:S(2)}) copy-start(bf16[5120,216]{0,1:T(8,128)(2,1)} %param.22) | copy-start | bytes 6635524
  33.1 15.0 %copy-start.3 = (bf16[216,5120]{1,0:T(8,128)(2,1)S(1)}, bf16[216,5120]{1,0:T(8,128)(2,1)}, u32[]{:S(2)}) copy-start(bf16[216,5120]{1,0:T(8,128)(2,1)} %down.1) | copy-start | bytes 6635524
  34.6 1.4 %collective-permute-start = (bf16[8,5120]{1,0:T(8,128)(2,1)S(1)}, bf16[8,5120]{1,0:T(8,128)(2,1)S(1)}, u32[]{:S(2)}, u32[]{:S(2)}) collective-permute-start(bf16[8,5120]{1,0:T(8,128)(2,1)S(1)} %get-tuple-element.30), channel_id=1, source_target_pairs={{0,1},{1,0},{2,3},{3,2},{4,5},{5,4},{6,7},{7,6},{8,9},{9,8},{10,11... | collective-permute-start | bytes 245768 | tf_op jit(solution)/shard_map/ppermute | solution.py:210
  36.0 6.2 %collective-permute-start.3 = (bf16[8,5120]{1,0:T(8,128)(2,1)S(1)}, bf16[8,5120]{1,0:T(8,128)(2,1)S(1)}, u32[]{:S(2)}, u32[]{:S(2)}) collective-permute-start(bf16[8,5120]{1,0:T(8,128)(2,1)S(1)} %add_convert_fusion.1), channel_id=1, source_target_pairs={{0,6},{1,7},{2,0},{3,1},{4,2},{5,3},{6,4},{7,5},{8,14},{9,15},{10,... | collective-permute-start | bytes 245768 | tf_op jit(solution)/shard_map/ppermute | solution.py:206
  40.1 7.2 %collective-permute-start.2 = (bf16[8,5120]{1,0:T(8,128)(2,1)S(1)}, bf16[8,5120]{1,0:T(8,128)(2,1)S(1)}, u32[]{:S(2)}, u32[]{:S(2)}) collective-permute-start(bf16[8,5120]{1,0:T(8,128)(2,1)S(1)} %add_convert_fusion.1), channel_id=1, source_target_pairs={{0,2},{1,3},{2,4},{3,5},{4,6},{5,7},{6,0},{7,1},{8,10},{9,11},{10,... | collective-permute-start | bytes 245768 | tf_op jit(solution)/shard_map/ppermute | solution.py:206
  40.1 7.2 %collective-permute-start.1 = (bf16[8,5120]{1,0:T(8,128)(2,1)S(1)}, bf16[8,5120]{1,0:T(8,128)(2,1)S(1)}, u32[]{:S(2)}, u32[]{:S(2)}) collective-permute-start(bf16[8,5120]{1,0:T(8,128)(2,1)S(1)} %add_convert_fusion.1), channel_id=1, source_target_pairs={{0,4},{1,5},{2,6},{3,7},{4,0},{5,1},{6,2},{7,3},{8,12},{9,13},{10,... | collective-permute-start | bytes 245768 | tf_op jit(solution)/shard_map/ppermute | solution.py:206
  47.6 24.5 %collective-permute-start.4 = (bf16[216,5120]{1,0:T(8,128)(2,1)S(1)}, bf16[216,5120]{1,0:T(8,128)(2,1)S(1)}, u32[]{:S(2)}, u32[]{:S(2)}) collective-permute-start(bf16[216,5120]{1,0:T(8,128)(2,1)S(1)} %bitcast.10), channel_id=1, source_target_pairs={{0,1},{1,0},{2,3},{3,2},{4,5},{5,4},{6,7},{7,6},{8,9},{9,8},{10,11... | collective-permute-start | bytes 6635528 | tf_op jit(solution)/shard_map/ppermute | solution.py:210
  47.7 24.4 %collective-permute-start.5 = (bf16[216,5120]{1,0:T(8,128)(2,1)S(1)}, bf16[216,5120]{1,0:T(8,128)(2,1)S(1)}, u32[]{:S(2)}, u32[]{:S(2)}) collective-permute-start(bf16[216,5120]{1,0:T(8,128)(2,1)S(1)} %bitcast.12), channel_id=1, source_target_pairs={{0,1},{1,0},{2,3},{3,2},{4,5},{5,4},{6,7},{7,6},{8,9},{9,8},{10,11... | collective-permute-start | bytes 6635528 | tf_op jit(solution)/shard_map/ppermute | solution.py:210
  48.1 23.9 %collective-permute-start.6 = (bf16[216,5120]{1,0:T(8,128)(2,1)S(1)}, bf16[216,5120]{1,0:T(8,128)(2,1)S(1)}, u32[]{:S(2)}, u32[]{:S(2)}) collective-permute-start(bf16[216,5120]{1,0:T(8,128)(2,1)S(1)} %copy-done.3), channel_id=1, source_target_pairs={{0,1},{1,0},{2,3},{3,2},{4,5},{5,4},{6,7},{7,6},{8,9},{9,8},{10,11... | collective-permute-start | bytes 6635528 | tf_op jit(solution)/shard_map/ppermute | solution.py:210
  76.3 8.8 %collective-permute-start.7 = (bf16[32,5120]{1,0:T(8,128)(2,1)S(1)}, bf16[32,5120]{1,0:T(8,128)(2,1)S(1)}, u32[]{:S(2)}, u32[]{:S(2)}) collective-permute-start(bf16[32,5120]{1,0:T(8,128)(2,1)S(1)} %get-tuple-element.38), channel_id=1, source_target_pairs={{0,4},{1,65},{2,6},{3,67},{4,0},{5,69},{6,2},{7,71},{8,12},{9,73},... | collective-permute-start | bytes 983048 | tf_op jit(solution)/shard_map/ppermute | solution.py:196
  77.0 11.5 %collective-permute-start.8 = (bf16[32,5120]{1,0:T(8,128)(2,1)S(1)}, bf16[32,5120]{1,0:T(8,128)(2,1)S(1)}, u32[]{:S(2)}, u32[]{:S(2)}) collective-permute-start(bf16[32,5120]{1,0:T(8,128)(2,1)S(1)} %get-tuple-element.39), channel_id=1, source_target_pairs={{0,2},{1,33},{2,4},{3,35},{4,6},{5,37},{6,0},{7,39},{8,10},{9,41},... | collective-permute-start | bytes 983048 | tf_op jit(solution)/shard_map/ppermute | solution.py:196
  79.3 9.2 %collective-permute-start.9 = (bf16[32,5120]{1,0:T(8,128)(2,1)S(1)}, bf16[32,5120]{1,0:T(8,128)(2,1)S(1)}, u32[]{:S(2)}, u32[]{:S(2)}) collective-permute-start(bf16[32,5120]{1,0:T(8,128)(2,1)S(1)} %get-tuple-element.40), channel_id=1, source_target_pairs={{0,6},{1,97},{2,0},{3,99},{4,2},{5,101},{6,4},{7,103},{8,14},{9,10... | collective-permute-start | bytes 983048 | tf_op jit(solution)/shard_map/ppermute | solution.py:196

commit v14 on v13

--- a/solution.py
+++ b/solution.py
@@ -245,14 +245,15 @@
     own, other = call(project_kernel, [shape((8, D), F32), shape((8, D), BF)], [SM, VM, VM, VM])(
         tp, parts, out_weight, activations
     )
+    far = [move_core(w) for w in (gate_t, up_t)]
     swapped = move_core(other)
     sent = (own + swapped.astype(F32)).astype(BF)
     around = [move_z(sent, k) for k in (2, 1, 3)]
     residual, repeated = call(normalize_kernel, [shape((8, D), BF), shape((16, 8, D), BF)], [VM] * 6)(
         norm_gain[None, :], own, swapped, *around
     )
-    repeated, *far = lax.optimization_barrier((repeated, gate_t, up_t, down_weight))
-    far = [move_core(w) for w in far]
+    repeated, down_far = lax.optimization_barrier((repeated, down_weight))
+    far.append(move_core(down_far))
     rows = lax.all_to_all(repeated, "kv", 0, 0).reshape(128, D)
     block = shape((32, D), BF)
     mixed, *sent = call(

time: 102 us -> 102 us (level)
  transfers between devices with their start and end apart: 11 -> 11, of which waited for: 6 -> 5; matrix products, arithmetic and copies ran while one was open for 1% -> 1% of each run, Pallas kernels for 1% -> 1%
where the time goes in v14:
time: 102 us; the launch traced here: 101 us
  blocking collectives  48.8 us (48%)
  waiting for transfers between devices  20.3 us (20%)
  starting transfers between devices  17.7 us (17%)
  Pallas kernels  10.2 us (10%)
  local copies, waits for them, and re-layouts  3.52 us (3%)
    all_to_all x1, blocking collectives, local(): rows = lax.all_to_all(repeated, 'kv', 0, 0).reshape(128, D)  23.9 us
    all_to_all x1, blocking collectives, local(): parts = lax.all_to_all(packed.reshape(16, 16, 768), 'kv', 0, 0)  12.6 us
    all_to_all x1, blocking collectives, local(): mixed = lax.all_to_all(mixed, ('kv', 'tp'), 0, 0, axis_index_groups=PLANES)  12.2 us
    ppermute x3, waiting for transfers between devices, move_ring(): return lax.ppermute(value, ('kv', 'tp'), pairs)  8.24 us
    all_to_all x1, starting transfers between devices, local(): lax.all_to_all(jnp.broadcast_to(queries[None], (16, 16, 640)), 'kv', 0, 0)  7.12 us
    ppermute x3, starting transfers between devices, move_z(): return lax.ppermute(value, 'tp', pairs)  5.97 us
    all_to_all x1, waiting for transfers between devices, local(): lax.all_to_all(jnp.broadcast_to(queries[None], (16, 16, 640)), 'kv', 0, 0)  5.93 us
    ppermute x3, waiting for transfers between devices, move_z(): return lax.ppermute(value, 'tp', pairs)  4.81 us
  transfers between devices with their start and end apart: 11, of which 5 were waited for; matrix products, arithmetic and copies ran while one was open for 1% of the time, Pallas kernels for 1%

profile of v14, /device:TPU:0, one launch (start us, length us, event | category | flops | bytes accessed | tf_op | source)
XLA Modules:
  0.0 101.4 jit_solution(4862322681182664103)
XLA Ops:
  0.0 1.5 %broadcast_in_dim.21 = bf16[16,16,640]{2,1,0:T(8,128)(2,1)} broadcast(bf16[16,640]{1,0:T(8,128)(2,1)} %param.13), dimensions={1,2} | broadcast | bytes 348160 | tf_op jit(solution)/shard_map/broadcast_in_dim | solution.py:235
  1.5 7.1 %all-to-all-start = ((bf16[16,16,640]{2,1,0:T(8,128)(2,1)}), bf16[16,16,640]{2,1,0:T(8,128)(2,1)S(1)}, u32[]{:S(2)}, u32[]{:S(2)}) async-start(bf16[16,16,640]{2,1,0:T(8,128)(2,1)} %broadcast_in_dim.21), calls=%async_computation | async-start | bytes 655360 | tf_op jit(solution)/shard_map/all_to_all | solution.py:235
  8.6 0.7 pad_add_fusion
  9.3 0.0 copy-start.4
  9.3 0.9 copy-done.4
  10.3 0.0 copy-start.5
  10.3 0.9 copy-done.5
  11.2 0.6 shard_map.118
  11.8 5.9 %all-to-all-done = bf16[16,16,640]{2,1,0:T(8,128)(2,1)S(1)} async-done(((bf16[16,16,640]{2,1,0:T(8,128)(2,1)}), bf16[16,16,640]{2,1,0:T(8,128)(2,1)S(1)}, u32[]{:S(2)}, u32[]{:S(2)}) %all-to-all-start) | async-done | bytes 327712 | tf_op jit(solution)/shard_map/all_to_all | solution.py:235
  17.8 0.0 copy-start
  17.8 0.0 copy-start.6
  17.8 2.7 %shard_map.119 = bf16[256,768]{1,0:T(8,128)(2,1)S(1)} custom-call(bf16[256,640]{1,0:T(8,128)(2,1)S(1)} %bitcast.15, bf16[1024,256]{1,0:T(8,128)(2,1)S(1)} %get-tuple-element.24.keys_wide, bf16[1024,128]{1,0:T(8,128)(2,1)S(1)} %get-tuple-element.25.values, bf16[256,128]{1,0:T(8,128)(2,1)S(1)} %get-tuple-element.26.onehot, bf16[640,5120]{1,0:T(8,128)(2,1)} %weight.3), custom_call_target="tpu_custom_call" | custom-call | tf_op jit(solution)/shard_map/pallas_call | solution.py:241
  20.5 12.6 %all_to_all.20.parts = bf16[16,16,768]{2,1,0:T(8,128)(2,1)S(1)} all-to-all(bf16[16,16,768]{2,1,0:T(8,128)(2,1)S(1)} %bitcast.14), channel_id=1, replica_groups=mesh['kv'=16,'tp'=8] {'kv'}, dimensions={0} | all-to-all | bytes 786432 | tf_op jit(solution)/shard_map/all_to_all | solution.py:244
  33.1 0.0 copy-done
  33.1 0.0 copy-done.6
  33.1 0.0 copy-start.1
  33.1 0.0 copy-start.2
  33.1 0.0 copy-start.7
  33.1 0.0 copy-start.3
  33.1 1.5 %shard_map.120 = (f32[8,5120]{1,0:T(8,128)S(1)}, bf16[8,5120]{1,0:T(8,128)(2,1)S(1)}) custom-call(s32[1]{0:T(128)} %bitcast.1.tp, bf16[16,16,768]{2,1,0:T(8,128)(2,1)S(1)} %all_to_all.20.parts, bf16[640,5120]{1,0:T(8,128)(2,1)S(1)} %copy-done, bf16[2,5120]{1,0:T(2,128)(2,1)S(1)} %copy-done.6), custom_call_target="tpu_custom_call" | custom-call | tf_op jit(solution)/shard_map/pallas_call | solution.py:245
  34.6 0.1 collective-permute-start
  34.7 1.3 %collective-permute-done.swapped = bf16[8,5120]{1,0:T(8,128)(2,1)S(1)} collective-permute-done((bf16[8,5120]{1,0:T(8,128)(2,1)S(1)}, bf16[8,5120]{1,0:T(8,128)(2,1)S(1)}, u32[]{:S(2)}, u32[]{:S(2)}) %collective-permute-start) | collective-permute-done | bytes 81952 | tf_op jit(solution)/shard_map/ppermute | solution.py:210
  36.0 4.1 %collective-permute-start.3 = (bf16[8,5120]{1,0:T(8,128)(2,1)S(1)}, bf16[8,5120]{1,0:T(8,128)(2,1)S(1)}, u32[]{:S(2)}, u32[]{:S(2)}) collective-permute-start(bf16[8,5120]{1,0:T(8,128)(2,1)S(1)} %add_convert_fusion.1), channel_id=1, source_target_pairs={{0,6},{1,7},{2,0},{3,1},{4,2},{5,3},{6,4},{7,5},{8,14},{9,15},{10,... | collective-permute-start | bytes 245768 | tf_op jit(solution)/shard_map/ppermute | solution.py:206
  40.1 0.0 collective-permute-start.2
  40.1 1.9 %collective-permute-start.1 = (bf16[8,5120]{1,0:T(8,128)(2,1)S(1)}, bf16[8,5120]{1,0:T(8,128)(2,1)S(1)}, u32[]{:S(2)}, u32[]{:S(2)}) collective-permute-start(bf16[8,5120]{1,0:T(8,128)(2,1)S(1)} %add_convert_fusion.1), channel_id=1, source_target_pairs={{0,4},{1,5},{2,6},{3,7},{4,0},{5,1},{6,2},{7,3},{8,12},{9,13},{10,... | collective-permute-start | bytes 245768 | tf_op jit(solution)/shard_map/ppermute | solution.py:206
  41.9 0.0 copy-done.1
  41.9 0.0 collective-permute-start.4
  41.9 0.0 copy-done.2
  41.9 0.5 collective-permute-start.5
  42.4 0.0 collective-permute-done.3.refs_2_
  42.4 4.8 %collective-permute-done.2.refs_1_ = bf16[8,5120]{1,0:T(8,128)(2,1)S(1)} collective-permute-done((bf16[8,5120]{1,0:T(8,128)(2,1)S(1)}, bf16[8,5120]{1,0:T(8,128)(2,1)S(1)}, u32[]{:S(2)}, u32[]{:S(2)}) %collective-permute-start.2) | collective-permute-done | bytes 81952 | tf_op jit(solution)/shard_map/ppermute | solution.py:206
  47.2 0.0 collective-permute-done.1.refs_0_
  47.3 0.0 copy-done.7
  47.3 0.3 shard_map.121
  47.5 0.0 copy-done.3
  47.6 0.1 collective-permute-start.6
  47.6 23.9 %all_to_all.21 = bf16[16,8,5120]{2,1,0:T(8,128)(2,1)S(1)} all-to-all(bf16[16,8,5120]{2,1,0:T(8,128)(2,1)S(1)} %get-tuple-element.31), channel_id=1, replica_groups=mesh['kv'=16,'tp'=8] {'kv'}, dimensions={0} | all-to-all | bytes 2621440 | tf_op jit(solution)/shard_map/all_to_all | solution.py:257
  71.5 0.0 collective-permute-done.4.gate_far
  71.6 0.0 collective-permute-done.5.up_far
  71.6 0.0 collective-permute-done.6.down_far
  71.6 4.2 %shard_map.122 = (f32[32,5120]{1,0:T(8,128)S(1)}, bf16[32,5120]{1,0:T(8,128)(2,1)S(1)}, bf16[32,5120]{1,0:T(8,128)(2,1)S(1)}, bf16[32,5120]{1,0:T(8,128)(2,1)S(1)}) custom-call(s32[1]{0:T(128)} %bitcast.kv, s32[1]{0:T(128)} %bitcast.1.tp, bf16[128,5120]{1,0:T(8,128)(2,1)S(1)} %bitcast.9, bf16[216,5120]{1,0:T(8,128)(2,1)S(1)} %bitcast.11, ...), custom_call_target="tpu_custom_call" | custom-call | tf_op jit(solution)/shard_map/pallas_call | solution.py:259
  75.8 0.7 collective-permute-start.7
  76.5 2.2 %collective-permute-start.8 = (bf16[32,5120]{1,0:T(8,128)(2,1)S(1)}, bf16[32,5120]{1,0:T(8,128)(2,1)S(1)}, u32[]{:S(2)}, u32[]{:S(2)}) collective-permute-start(bf16[32,5120]{1,0:T(8,128)(2,1)S(1)} %get-tuple-element.35), channel_id=1, source_target_pairs={{0,2},{1,33},{2,4},{3,35},{4,6},{5,37},{6,0},{7,39},{8,10},{9,41},... | collective-permute-start | bytes 983048 | tf_op jit(solution)/shard_map/ppermute | solution.py:196
  78.7 1.0 collective-permute-start.9
  79.7 4.8 %collective-permute-done.7 = bf16[32,5120]{1,0:T(8,128)(2,1)S(1)} collective-permute-done((bf16[32,5120]{1,0:T(8,128)(2,1)S(1)}, bf16[32,5120]{1,0:T(8,128)(2,1)S(1)}, u32[]{:S(2)}, u32[]{:S(2)}) %collective-permute-start.7) | collective-permute-done | bytes 327712 | tf_op jit(solution)/shard_map/ppermute | solution.py:196
  84.6 3.4 %collective-permute-done.8 = bf16[32,5120]{1,0:T(8,128)(2,1)S(1)} collective-permute-done((bf16[32,5120]{1,0:T(8,128)(2,1)S(1)}, bf16[32,5120]{1,0:T(8,128)(2,1)S(1)}, u32[]{:S(2)}, u32[]{:S(2)}) %collective-permute-start.8) | collective-permute-done | bytes 327712 | tf_op jit(solution)/shard_map/ppermute | solution.py:196
  88.0 0.0 collective-permute-done.9
  88.0 0.2 add_convert_fusion
  88.1 0.1 reshape.16
  88.3 12.2 %all_to_all.22.parts = bf16[16,2,5120]{2,1,0:T(2,128)(2,1)S(1)} all-to-all(bf16[16,2,5120]{2,1,0:T(2,128)(2,1)S(1)} %reshape.16), channel_id=1, replica_groups={{0,8,16,24,32,40,48,56,64,72,80,88,96,104,112,120},{2,10,18,26,34,42,50..., dimensions={0} | all-to-all | bytes 655360 | tf_op jit(solution)/shard_map/all_to_all | solution.py:265
  100.5 0.9 shard_map.123
  (1 shorter events, 0.0 us)
Async XLA Ops:
  1.5 16.3 %all-to-all-start = ((bf16[16,16,640]{2,1,0:T(8,128)(2,1)}), bf16[16,16,640]{2,1,0:T(8,128)(2,1)S(1)}, u32[]{:S(2)}, u32[]{:S(2)}) async-start(bf16[16,16,640]{2,1,0:T(8,128)(2,1)} %broadcast_in_dim.21), calls=%async_computation | async-start | bytes 655360 | tf_op jit(solution)/shard_map/all_to_all | solution.py:235
  9.3 0.9 copy-start.4
  10.3 0.9 copy-start.5
  17.8 15.3 %copy-start = (bf16[640,5120]{1,0:T(8,128)(2,1)S(1)}, bf16[640,5120]{1,0:T(8,128)(2,1)}, u32[]{:S(2)}) copy-start(bf16[640,5120]{1,0:T(8,128)(2,1)} %weight.3) | copy-start | bytes 19660804
  17.8 15.3 %copy-start.6 = (bf16[2,5120]{1,0:T(2,128)(2,1)S(1)}, bf16[2,5120]{1,0:T(2,128)(2,1)}, u32[]{:S(2)}) copy-start(bf16[2,5120]{1,0:T(2,128)(2,1)} %activations.1) | copy-start | bytes 61444
  33.1 8.8 %copy-start.1 = (bf16[5120,216]{0,1:T(8,128)(2,1)S(1)}, bf16[5120,216]{0,1:T(8,128)(2,1)}, u32[]{:S(2)}) copy-start(bf16[5120,216]{0,1:T(8,128)(2,1)} %param.21) | copy-start | bytes 6635524
  33.1 8.8 %copy-start.2 = (bf16[5120,216]{0,1:T(8,128)(2,1)S(1)}, bf16[5120,216]{0,1:T(8,128)(2,1)}, u32[]{:S(2)}) copy-start(bf16[5120,216]{0,1:T(8,128)(2,1)} %param.22) | copy-start | bytes 6635524
  33.1 14.2 %copy-start.7 = (f32[5120]{0:T(1024)S(1)}, f32[5120]{0:T(1024)}, u32[]{:S(2)}) copy-start(f32[5120]{0:T(1024)} %param.20) | copy-start | bytes 61444
  33.1 14.4 %copy-start.3 = (bf16[216,5120]{1,0:T(8,128)(2,1)S(1)}, bf16[216,5120]{1,0:T(8,128)(2,1)}, u32[]{:S(2)}) copy-start(bf16[216,5120]{1,0:T(8,128)(2,1)} %down.1) | copy-start | bytes 6635524
  34.6 1.4 %collective-permute-start = (bf16[8,5120]{1,0:T(8,128)(2,1)S(1)}, bf16[8,5120]{1,0:T(8,128)(2,1)S(1)}, u32[]{:S(2)}, u32[]{:S(2)}) collective-permute-start(bf16[8,5120]{1,0:T(8,128)(2,1)S(1)} %get-tuple-element.28), channel_id=1, source_target_pairs={{0,1},{1,0},{2,3},{3,2},{4,5},{5,4},{6,7},{7,6},{8,9},{9,8},{10,11... | collective-permute-start | bytes 245768 | tf_op jit(solution)/shard_map/ppermute | solution.py:210
  36.0 6.5 %collective-permute-start.3 = (bf16[8,5120]{1,0:T(8,128)(2,1)S(1)}, bf16[8,5120]{1,0:T(8,128)(2,1)S(1)}, u32[]{:S(2)}, u32[]{:S(2)}) collective-permute-start(bf16[8,5120]{1,0:T(8,128)(2,1)S(1)} %add_convert_fusion.1), channel_id=1, source_target_pairs={{0,6},{1,7},{2,0},{3,1},{4,2},{5,3},{6,4},{7,5},{8,14},{9,15},{10,... | collective-permute-start | bytes 245768 | tf_op jit(solution)/shard_map/ppermute | solution.py:206
  40.1 7.2 %collective-permute-start.2 = (bf16[8,5120]{1,0:T(8,128)(2,1)S(1)}, bf16[8,5120]{1,0:T(8,128)(2,1)S(1)}, u32[]{:S(2)}, u32[]{:S(2)}) collective-permute-start(bf16[8,5120]{1,0:T(8,128)(2,1)S(1)} %add_convert_fusion.1), channel_id=1, source_target_pairs={{0,2},{1,3},{2,4},{3,5},{4,6},{5,7},{6,0},{7,1},{8,10},{9,11},{10,... | collective-permute-start | bytes 245768 | tf_op jit(solution)/shard_map/ppermute | solution.py:206
  40.1 7.2 %collective-permute-start.1 = (bf16[8,5120]{1,0:T(8,128)(2,1)S(1)}, bf16[8,5120]{1,0:T(8,128)(2,1)S(1)}, u32[]{:S(2)}, u32[]{:S(2)}) collective-permute-start(bf16[8,5120]{1,0:T(8,128)(2,1)S(1)} %add_convert_fusion.1), channel_id=1, source_target_pairs={{0,4},{1,5},{2,6},{3,7},{4,0},{5,1},{6,2},{7,3},{8,12},{9,13},{10,... | collective-permute-start | bytes 245768 | tf_op jit(solution)/shard_map/ppermute | solution.py:206
  41.9 29.6 %collective-permute-start.4 = (bf16[216,5120]{1,0:T(8,128)(2,1)S(1)}, bf16[216,5120]{1,0:T(8,128)(2,1)S(1)}, u32[]{:S(2)}, u32[]{:S(2)}) collective-permute-start(bf16[216,5120]{1,0:T(8,128)(2,1)S(1)} %bitcast.10), channel_id=1, source_target_pairs={{0,1},{1,0},{2,3},{3,2},{4,5},{5,4},{6,7},{7,6},{8,9},{9,8},{10,11... | collective-permute-start | bytes 6635528 | tf_op jit(solution)/shard_map/ppermute | solution.py:210
  41.9 29.6 %collective-permute-start.5 = (bf16[216,5120]{1,0:T(8,128)(2,1)S(1)}, bf16[216,5120]{1,0:T(8,128)(2,1)S(1)}, u32[]{:S(2)}, u32[]{:S(2)}) collective-permute-start(bf16[216,5120]{1,0:T(8,128)(2,1)S(1)} %bitcast.12), channel_id=1, source_target_pairs={{0,1},{1,0},{2,3},{3,2},{4,5},{5,4},{6,7},{7,6},{8,9},{9,8},{10,11... | collective-permute-start | bytes 6635528 | tf_op jit(solution)/shard_map/ppermute | solution.py:210
  47.6 24.0 %collective-permute-start.6 = (bf16[216,5120]{1,0:T(8,128)(2,1)S(1)}, bf16[216,5120]{1,0:T(8,128)(2,1)S(1)}, u32[]{:S(2)}, u32[]{:S(2)}) collective-permute-start(bf16[216,5120]{1,0:T(8,128)(2,1)S(1)} %copy-done.3), channel_id=1, source_target_pairs={{0,1},{1,0},{2,3},{3,2},{4,5},{5,4},{6,7},{7,6},{8,9},{9,8},{10,11... | collective-permute-start | bytes 6635528 | tf_op jit(solution)/shard_map/ppermute | solution.py:210
  75.8 8.8 %collective-permute-start.7 = (bf16[32,5120]{1,0:T(8,128)(2,1)S(1)}, bf16[32,5120]{1,0:T(8,128)(2,1)S(1)}, u32[]{:S(2)}, u32[]{:S(2)}) collective-permute-start(bf16[32,5120]{1,0:T(8,128)(2,1)S(1)} %get-tuple-element.34), channel_id=1, source_target_pairs={{0,4},{1,65},{2,6},{3,67},{4,0},{5,69},{6,2},{7,71},{8,12},{9,73},... | collective-permute-start | bytes 983048 | tf_op jit(solution)/shard_map/ppermute | solution.py:196
  76.5 11.5 %collective-permute-start.8 = (bf16[32,5120]{1,0:T(8,128)(2,1)S(1)}, bf16[32,5120]{1,0:T(8,128)(2,1)S(1)}, u32[]{:S(2)}, u32[]{:S(2)}) collective-permute-start(bf16[32,5120]{1,0:T(8,128)(2,1)S(1)} %get-tuple-element.35), channel_id=1, source_target_pairs={{0,2},{1,33},{2,4},{3,35},{4,6},{5,37},{6,0},{7,39},{8,10},{9,41},... | collective-permute-start | bytes 983048 | tf_op jit(solution)/shard_map/ppermute | solution.py:196
  78.7 9.3 %collective-permute-start.9 = (bf16[32,5120]{1,0:T(8,128)(2,1)S(1)}, bf16[32,5120]{1,0:T(8,128)(2,1)S(1)}, u32[]{:S(2)}, u32[]{:S(2)}) collective-permute-start(bf16[32,5120]{1,0:T(8,128)(2,1)S(1)} %get-tuple-element.36), channel_id=1, source_target_pairs={{0,6},{1,97},{2,0},{3,99},{4,2},{5,101},{6,4},{7,103},{8,14},{9,10... | collective-permute-start | bytes 983048 | tf_op jit(solution)/shard_map/ppermute | solution.py:196

commit v15 on v12

--- a/solution.py
+++ b/solution.py
@@ -42,14 +42,6 @@
 
 def mm(a, b):
     return lax.dot_general(a, b, (((1,), (0,)), ((), ())), preferred_element_type=F32)
-
-
-def repeat_kernel(rows, out, sem):
-    copies = [pltpu.make_async_copy(rows, out.at[k], sem.at[k]) for k in range(out.shape[0])]
-    for copy in copies:
-        copy.start()
-    for copy in copies:
-        copy.wait()
 
 
 def prepare_kernel(kv, tables, keys, values, keys_wide, values_out, onehot):
@@ -227,15 +219,7 @@
 
     padding = 128 - node_lengths.shape[0]
     tables = jnp.concatenate([token_leaf, jnp.pad(node_lengths, (0, padding)), jnp.pad(parents, (0, padding))])[None, :]
-    repeated = pl.pallas_call(
-        repeat_kernel,
-        out_shape=shape((16, 16, 640), BF),
-        in_specs=[pl.BlockSpec(memory_space=VM)],
-        out_specs=pl.BlockSpec(memory_space=pl.ANY),
-        scratch_shapes=[pltpu.SemaphoreType.DMA((16,))],
-        compiler_params=pltpu.CompilerParams(vmem_limit_bytes=56 << 20),
-    )(queries)
-    q = lax.all_to_all(repeated, "kv", 0, 0)
+    q = lax.all_to_all(jnp.broadcast_to(queries[None], (16, 16, 640)), "kv", 0, 0)
     keys_wide, values_in, onehot = call(
         prepare_kernel,
         [shape((keys.shape[0], 256), BF), shape(values.shape, BF), shape((256, 128), BF)],
@@ -250,7 +234,7 @@
     )
     attended = own + move_core(other).astype(F32)
     sent = attended.astype(BF)
-    for part in [move_z(sent, k) for k in (2, 1, 3)]:
+    for part in [move_z(sent, k) for k in (1, 3, 2)]:
         attended = attended + part.astype(F32)
     residual = attended.astype(BF)
     widened = residual.astype(F32)

time: 101 us -> 99.4 us (0.984)
  waiting for transfers between devices: 20.5 us -> 17.9 us
  starting transfers between devices: 17.2 us -> 19.4 us
  Pallas kernels: 11.5 us -> 9.92 us
  local copies, waits for them, and re-layouts: 2.17 us -> 3.65 us
    ppermute x3, starting transfers between devices: 3.4 us -> 5.68 us  [move_ring(): return lax.ppermute(value, ('kv', 'tp'), pairs)]
    ppermute x3, waiting for transfers between devices: 8.56 us -> 6.9 us  [move_ring(): return lax.ppermute(value, ('kv', 'tp'), pairs)]
    pallas_call x1 -> x0, Pallas kernels: 1.6 us -> none  [local(): pl.pallas_call(repeat_kernel, out_shape=shape((16, 16, 640), BF), in_spec...]
    broadcast_in_dim x0 -> x1, local copies, waits for them, and re-layouts: none -> 1.48 us  [local(): jnp.broadcast_to(queries[None], (16, 16, 640))]
    all_to_all x1, blocking collectives: 22.9 us -> 21.9 us  [local(): lax.all_to_all(jnp.broadcast_to(normed[None], (16, 8, D)), 'kv', 0, 0)]
  transfers between devices with their start and end apart: 11 -> 11, of which waited for: 5 -> 8; matrix products, arithmetic and copies ran while one was open for 1% -> 1% of each run, Pallas kernels for 1% -> 1%
where the time goes in v15:
time: 99.4 us; the launch traced here: 99 us
  blocking collectives  46.8 us (47%)
  starting transfers between devices  19.4 us (20%)
  waiting for transfers between devices  17.9 us (18%)
  Pallas kernels  9.92 us (10%)
  local copies, waits for them, and re-layouts  3.65 us (4%)
  other arithmetic  1.16 us (1%)
    all_to_all x1, blocking collectives, local(): lax.all_to_all(jnp.broadcast_to(normed[None], (16, 8, D)), 'kv', 0, 0)  21.9 us
    all_to_all x1, blocking collectives, local(): parts = lax.all_to_all(packed.reshape(16, 16, 768), 'kv', 0, 0)  12.6 us
    all_to_all x1, blocking collectives, local(): mixed = lax.all_to_all(mixed, ('kv', 'tp'), 0, 0, axis_index_groups=PLANES)  12.4 us
    all_to_all x1, starting transfers between devices, local(): lax.all_to_all(jnp.broadcast_to(queries[None], (16, 16, 640)), 'kv', 0, 0)  7.12 us
    ppermute x3, waiting for transfers between devices, move_ring(): return lax.ppermute(value, ('kv', 'tp'), pairs)  6.9 us
    ppermute x3, starting transfers between devices, move_z(): return lax.ppermute(value, 'tp', pairs)  5.98 us
    all_to_all x1, waiting for transfers between devices, local(): lax.all_to_all(jnp.broadcast_to(queries[None], (16, 16, 640)), 'kv', 0, 0)  5.93 us
    ppermute x3, starting transfers between devices, move_ring(): return lax.ppermute(value, ('kv', 'tp'), pairs)  5.68 us
  transfers between devices with their start and end apart: 11, of which 8 were waited for; matrix products, arithmetic and copies ran while one was open for 1% of the time, Pallas kernels for 1%

profile of v15, /device:TPU:0, one launch (start us, length us, event | category | flops | bytes accessed | tf_op | source)
XLA Modules:
  0.0 99.0 jit_solution(10522163997400874519)
XLA Ops:
  0.0 1.5 %broadcast_in_dim.12 = bf16[16,16,640]{2,1,0:T(8,128)(2,1)} broadcast(bf16[16,640]{1,0:T(8,128)(2,1)} %param.13), dimensions={1,2} | broadcast | bytes 348160 | tf_op jit(solution)/shard_map/broadcast_in_dim | solution.py:222
  1.5 7.1 %all-to-all-start = ((bf16[16,16,640]{2,1,0:T(8,128)(2,1)}), bf16[16,16,640]{2,1,0:T(8,128)(2,1)S(1)}, u32[]{:S(2)}, u32[]{:S(2)}) async-start(bf16[16,16,640]{2,1,0:T(8,128)(2,1)} %broadcast_in_dim.12), calls=%async_computation | async-start | bytes 655360 | tf_op jit(solution)/shard_map/all_to_all | solution.py:222
  8.6 0.7 pad_add_fusion
  9.3 0.0 copy-start.4
  9.3 0.9 copy-done.4
  10.3 0.0 copy-start.5
  10.3 0.9 copy-done.5
  11.2 0.6 shard_map.118
  11.8 5.9 %all-to-all-done = bf16[16,16,640]{2,1,0:T(8,128)(2,1)S(1)} async-done(((bf16[16,16,640]{2,1,0:T(8,128)(2,1)}), bf16[16,16,640]{2,1,0:T(8,128)(2,1)S(1)}, u32[]{:S(2)}, u32[]{:S(2)}) %all-to-all-start) | async-done | bytes 327712 | tf_op jit(solution)/shard_map/all_to_all | solution.py:222
  17.8 0.0 copy-start
  17.8 0.0 copy-start.6
  17.8 2.7 %shard_map.119 = bf16[256,768]{1,0:T(8,128)(2,1)S(1)} custom-call(bf16[256,640]{1,0:T(8,128)(2,1)S(1)} %bitcast.14, bf16[1024,256]{1,0:T(8,128)(2,1)S(1)} %get-tuple-element.20.keys_wide, bf16[1024,128]{1,0:T(8,128)(2,1)S(1)} %get-tuple-element.21.values, bf16[256,128]{1,0:T(8,128)(2,1)S(1)} %get-tuple-element.22.onehot, bf16[640,5120]{1,0:T(8,128)(2,1)} %weight.3), custom_call_target="tpu_custom_call" | custom-call | tf_op jit(solution)/shard_map/pallas_call | solution.py:228
  20.5 12.6 %all_to_all.20.parts = bf16[16,16,768]{2,1,0:T(8,128)(2,1)S(1)} all-to-all(bf16[16,16,768]{2,1,0:T(8,128)(2,1)S(1)} %bitcast.13), channel_id=1, replica_groups=mesh['kv'=16,'tp'=8] {'kv'}, dimensions={0} | all-to-all | bytes 786432 | tf_op jit(solution)/shard_map/all_to_all | solution.py:231
  33.1 0.0 copy-done
  33.1 0.0 copy-done.6
  33.1 0.0 copy-start.1
  33.1 0.0 copy-start.2
  33.1 0.0 copy-start.3
  33.1 0.0 copy-start.7
  33.1 1.5 %shard_map.120 = (f32[8,5120]{1,0:T(8,128)S(1)}, bf16[8,5120]{1,0:T(8,128)(2,1)S(1)}) custom-call(s32[1]{0:T(128)} %bitcast.1.tp, bf16[16,16,768]{2,1,0:T(8,128)(2,1)S(1)} %all_to_all.20.parts, bf16[640,5120]{1,0:T(8,128)(2,1)S(1)} %copy-done, bf16[2,5120]{1,0:T(2,128)(2,1)S(1)} %copy-done.6), custom_call_target="tpu_custom_call" | custom-call | tf_op jit(solution)/shard_map/pallas_call | solution.py:232
  34.6 0.1 collective-permute-start
  34.7 1.3 %collective-permute-done = bf16[8,5120]{1,0:T(8,128)(2,1)S(1)} collective-permute-done((bf16[8,5120]{1,0:T(8,128)(2,1)S(1)}, bf16[8,5120]{1,0:T(8,128)(2,1)S(1)}, u32[]{:S(2)}, u32[]{:S(2)}) %collective-permute-start) | collective-permute-done | bytes 81952 | tf_op jit(solution)/shard_map/ppermute | solution.py:196
  36.0 4.0 %collective-permute-start.3 = (bf16[8,5120]{1,0:T(8,128)(2,1)S(1)}, bf16[8,5120]{1,0:T(8,128)(2,1)S(1)}, u32[]{:S(2)}, u32[]{:S(2)}) collective-permute-start(bf16[8,5120]{1,0:T(8,128)(2,1)S(1)} %fusion.3), channel_id=1, source_target_pairs={{0,4},{1,5},{2,6},{3,7},{4,0},{5,1},{6,2},{7,3},{8,12},{9,13},{10,... | collective-permute-start | bytes 245768 | tf_op jit(solution)/shard_map/ppermute | solution.py:192
  39.9 0.7 collective-permute-start.2
  40.6 1.3 %collective-permute-start.1 = (bf16[8,5120]{1,0:T(8,128)(2,1)S(1)}, bf16[8,5120]{1,0:T(8,128)(2,1)S(1)}, u32[]{:S(2)}, u32[]{:S(2)}) collective-permute-start(bf16[8,5120]{1,0:T(8,128)(2,1)S(1)} %fusion.3), channel_id=1, source_target_pairs={{0,2},{1,3},{2,4},{3,5},{4,6},{5,7},{6,0},{7,1},{8,10},{9,11},{10,... | collective-permute-start | bytes 245768 | tf_op jit(solution)/shard_map/ppermute | solution.py:192
  41.9 0.0 copy-done.1
  41.9 0.0 collective-permute-start.4
  41.9 0.0 copy-done.2
  42.0 0.5 collective-permute-start.5
  42.5 0.2 collective-permute-done.3
  42.7 0.0 copy-done.3
  42.7 0.0 collective-permute-start.6
  42.7 2.5 %collective-permute-done.2 = bf16[8,5120]{1,0:T(8,128)(2,1)S(1)} collective-permute-done((bf16[8,5120]{1,0:T(8,128)(2,1)S(1)}, bf16[8,5120]{1,0:T(8,128)(2,1)S(1)}, u32[]{:S(2)}, u32[]{:S(2)}) %collective-permute-start.2) | collective-permute-done | bytes 81952 | tf_op jit(solution)/shard_map/ppermute | solution.py:192
  45.2 1.1 %collective-permute-done.1 = bf16[8,5120]{1,0:T(8,128)(2,1)S(1)} collective-permute-done((bf16[8,5120]{1,0:T(8,128)(2,1)S(1)}, bf16[8,5120]{1,0:T(8,128)(2,1)S(1)}, u32[]{:S(2)}, u32[]{:S(2)}) %collective-permute-start.1) | collective-permute-done | bytes 81952 | tf_op jit(solution)/shard_map/ppermute | solution.py:192
  46.3 0.2 fusion
  46.5 0.0 copy-done.7
  46.5 0.1 fusion.2
  46.6 0.1 broadcast_in_dim.27
  46.7 21.9 %all_to_all.21 = bf16[16,8,5120]{2,1,0:T(8,128)(2,1)S(1)} all-to-all(bf16[16,8,5120]{2,1,0:T(8,128)(2,1)S(1)} %broadcast_in_dim.27), channel_id=1, replica_groups=mesh['kv'=16,'tp'=8] {'kv'}, dimensions={0} | all-to-all | bytes 2621440 | tf_op jit(solution)/shard_map/all_to_all | solution.py:247
  68.6 0.0 collective-permute-done.4.gate_far
  68.6 0.0 collective-permute-done.5.up_far
  68.6 0.0 collective-permute-done.6.down_far
  68.6 4.2 %shard_map.121 = (f32[32,5120]{1,0:T(8,128)S(1)}, bf16[32,5120]{1,0:T(8,128)(2,1)S(1)}, bf16[32,5120]{1,0:T(8,128)(2,1)S(1)}, bf16[32,5120]{1,0:T(8,128)(2,1)S(1)}) custom-call(s32[1]{0:T(128)} %bitcast.kv, s32[1]{0:T(128)} %bitcast.1.tp, bf16[128,5120]{1,0:T(8,128)(2,1)S(1)} %bitcast.8, bf16[216,5120]{1,0:T(8,128)(2,1)S(1)} %bitcast.10, ...), custom_call_target="tpu_custom_call" | custom-call | tf_op jit(solution)/shard_map/pallas_call | solution.py:249
  72.8 2.4 %collective-permute-start.7 = (bf16[32,5120]{1,0:T(8,128)(2,1)S(1)}, bf16[32,5120]{1,0:T(8,128)(2,1)S(1)}, u32[]{:S(2)}, u32[]{:S(2)}) collective-permute-start(bf16[32,5120]{1,0:T(8,128)(2,1)S(1)} %get-tuple-element.26), channel_id=1, source_target_pairs={{0,4},{1,65},{2,6},{3,67},{4,0},{5,69},{6,2},{7,71},{8,12},{9,73},... | collective-permute-start | bytes 983048 | tf_op jit(solution)/shard_map/ppermute | solution.py:182
  75.3 1.6 %collective-permute-start.8 = (bf16[32,5120]{1,0:T(8,128)(2,1)S(1)}, bf16[32,5120]{1,0:T(8,128)(2,1)S(1)}, u32[]{:S(2)}, u32[]{:S(2)}) collective-permute-start(bf16[32,5120]{1,0:T(8,128)(2,1)S(1)} %get-tuple-element.27), channel_id=1, source_target_pairs={{0,2},{1,33},{2,4},{3,35},{4,6},{5,37},{6,0},{7,39},{8,10},{9,41},... | collective-permute-start | bytes 983048 | tf_op jit(solution)/shard_map/ppermute | solution.py:182
  76.8 1.7 %collective-permute-start.9 = (bf16[32,5120]{1,0:T(8,128)(2,1)S(1)}, bf16[32,5120]{1,0:T(8,128)(2,1)S(1)}, u32[]{:S(2)}, u32[]{:S(2)}) collective-permute-start(bf16[32,5120]{1,0:T(8,128)(2,1)S(1)} %get-tuple-element.28), channel_id=1, source_target_pairs={{0,6},{1,97},{2,0},{3,99},{4,2},{5,101},{6,4},{7,103},{8,14},{9,10... | collective-permute-start | bytes 983048 | tf_op jit(solution)/shard_map/ppermute | solution.py:182
  78.5 3.1 %collective-permute-done.7 = bf16[32,5120]{1,0:T(8,128)(2,1)S(1)} collective-permute-done((bf16[32,5120]{1,0:T(8,128)(2,1)S(1)}, bf16[32,5120]{1,0:T(8,128)(2,1)S(1)}, u32[]{:S(2)}, u32[]{:S(2)}) %collective-permute-start.7) | collective-permute-done | bytes 327712 | tf_op jit(solution)/shard_map/ppermute | solution.py:182
  81.6 3.4 %collective-permute-done.8 = bf16[32,5120]{1,0:T(8,128)(2,1)S(1)} collective-permute-done((bf16[32,5120]{1,0:T(8,128)(2,1)S(1)}, bf16[32,5120]{1,0:T(8,128)(2,1)S(1)}, u32[]{:S(2)}, u32[]{:S(2)}) %collective-permute-start.8) | collective-permute-done | bytes 327712 | tf_op jit(solution)/shard_map/ppermute | solution.py:182
  85.0 0.4 collective-permute-done.9
  85.4 0.2 add_convert_fusion
  85.6 0.1 reshape.26
  85.7 12.4 %all_to_all.22.parts = bf16[16,2,5120]{2,1,0:T(2,128)(2,1)S(1)} all-to-all(bf16[16,2,5120]{2,1,0:T(2,128)(2,1)S(1)} %reshape.26), channel_id=1, replica_groups={{0,8,16,24,32,40,48,56,64,72,80,88,96,104,112,120},{2,10,18,26,34,42,50..., dimensions={0} | all-to-all | bytes 655360 | tf_op jit(solution)/shard_map/all_to_all | solution.py:255
  98.1 0.9 shard_map.122
  (2 shorter events, 0.0 us)
Async XLA Ops:
  1.5 16.3 %all-to-all-start = ((bf16[16,16,640]{2,1,0:T(8,128)(2,1)}), bf16[16,16,640]{2,1,0:T(8,128)(2,1)S(1)}, u32[]{:S(2)}, u32[]{:S(2)}) async-start(bf16[16,16,640]{2,1,0:T(8,128)(2,1)} %broadcast_in_dim.12), calls=%async_computation | async-start | bytes 655360 | tf_op jit(solution)/shard_map/all_to_all | solution.py:222
  9.3 0.9 copy-start.4
  10.3 0.9 copy-start.5
  17.8 15.3 %copy-start = (bf16[640,5120]{1,0:T(8,128)(2,1)S(1)}, bf16[640,5120]{1,0:T(8,128)(2,1)}, u32[]{:S(2)}) copy-start(bf16[640,5120]{1,0:T(8,128)(2,1)} %weight.3) | copy-start | bytes 19660804
  17.8 15.3 %copy-start.6 = (bf16[2,5120]{1,0:T(2,128)(2,1)S(1)}, bf16[2,5120]{1,0:T(2,128)(2,1)}, u32[]{:S(2)}) copy-start(bf16[2,5120]{1,0:T(2,128)(2,1)} %activations.1) | copy-start | bytes 61444
  33.1 8.8 %copy-start.1 = (bf16[5120,216]{0,1:T(8,128)(2,1)S(1)}, bf16[5120,216]{0,1:T(8,128)(2,1)}, u32[]{:S(2)}) copy-start(bf16[5120,216]{0,1:T(8,128)(2,1)} %param.21) | copy-start | bytes 6635524
  33.1 8.9 %copy-start.2 = (bf16[5120,216]{0,1:T(8,128)(2,1)S(1)}, bf16[5120,216]{0,1:T(8,128)(2,1)}, u32[]{:S(2)}) copy-start(bf16[5120,216]{0,1:T(8,128)(2,1)} %param.22) | copy-start | bytes 6635524
  33.1 9.6 %copy-start.3 = (bf16[216,5120]{1,0:T(8,128)(2,1)S(1)}, bf16[216,5120]{1,0:T(8,128)(2,1)}, u32[]{:S(2)}) copy-start(bf16[216,5120]{1,0:T(8,128)(2,1)} %down.1) | copy-start | bytes 6635524
  33.1 13.3 %copy-start.7 = (f32[5120]{0:T(1024)S(1)}, f32[5120]{0:T(1024)}, u32[]{:S(2)}) copy-start(f32[5120]{0:T(1024)} %param.20) | copy-start | bytes 61444
  34.6 1.4 %collective-permute-start = (bf16[8,5120]{1,0:T(8,128)(2,1)S(1)}, bf16[8,5120]{1,0:T(8,128)(2,1)S(1)}, u32[]{:S(2)}, u32[]{:S(2)}) collective-permute-start(bf16[8,5120]{1,0:T(8,128)(2,1)S(1)} %get-tuple-element.24), channel_id=1, source_target_pairs={{0,1},{1,0},{2,3},{3,2},{4,5},{5,4},{6,7},{7,6},{8,9},{9,8},{10,11... | collective-permute-start | bytes 245768 | tf_op jit(solution)/shard_map/ppermute | solution.py:196
  36.0 6.7 %collective-permute-start.3 = (bf16[8,5120]{1,0:T(8,128)(2,1)S(1)}, bf16[8,5120]{1,0:T(8,128)(2,1)S(1)}, u32[]{:S(2)}, u32[]{:S(2)}) collective-permute-start(bf16[8,5120]{1,0:T(8,128)(2,1)S(1)} %fusion.3), channel_id=1, source_target_pairs={{0,4},{1,5},{2,6},{3,7},{4,0},{5,1},{6,2},{7,3},{8,12},{9,13},{10,... | collective-permute-start | bytes 245768 | tf_op jit(solution)/shard_map/ppermute | solution.py:192
  39.9 5.3 %collective-permute-start.2 = (bf16[8,5120]{1,0:T(8,128)(2,1)S(1)}, bf16[8,5120]{1,0:T(8,128)(2,1)S(1)}, u32[]{:S(2)}, u32[]{:S(2)}) collective-permute-start(bf16[8,5120]{1,0:T(8,128)(2,1)S(1)} %fusion.3), channel_id=1, source_target_pairs={{0,6},{1,7},{2,0},{3,1},{4,2},{5,3},{6,4},{7,5},{8,14},{9,15},{10,... | collective-permute-start | bytes 245768 | tf_op jit(solution)/shard_map/ppermute | solution.py:192
  40.6 5.7 %collective-permute-start.1 = (bf16[8,5120]{1,0:T(8,128)(2,1)S(1)}, bf16[8,5120]{1,0:T(8,128)(2,1)S(1)}, u32[]{:S(2)}, u32[]{:S(2)}) collective-permute-start(bf16[8,5120]{1,0:T(8,128)(2,1)S(1)} %fusion.3), channel_id=1, source_target_pairs={{0,2},{1,3},{2,4},{3,5},{4,6},{5,7},{6,0},{7,1},{8,10},{9,11},{10,... | collective-permute-start | bytes 245768 | tf_op jit(solution)/shard_map/ppermute | solution.py:192
  41.9 26.6 %collective-permute-start.4 = (bf16[216,5120]{1,0:T(8,128)(2,1)S(1)}, bf16[216,5120]{1,0:T(8,128)(2,1)S(1)}, u32[]{:S(2)}, u32[]{:S(2)}) collective-permute-start(bf16[216,5120]{1,0:T(8,128)(2,1)S(1)} %bitcast.9), channel_id=1, source_target_pairs={{0,1},{1,0},{2,3},{3,2},{4,5},{5,4},{6,7},{7,6},{8,9},{9,8},{10,11... | collective-permute-start | bytes 6635528 | tf_op jit(solution)/shard_map/ppermute | solution.py:196
  42.0 26.6 %collective-permute-start.5 = (bf16[216,5120]{1,0:T(8,128)(2,1)S(1)}, bf16[216,5120]{1,0:T(8,128)(2,1)S(1)}, u32[]{:S(2)}, u32[]{:S(2)}) collective-permute-start(bf16[216,5120]{1,0:T(8,128)(2,1)S(1)} %bitcast.11), channel_id=1, source_target_pairs={{0,1},{1,0},{2,3},{3,2},{4,5},{5,4},{6,7},{7,6},{8,9},{9,8},{10,11... | collective-permute-start | bytes 6635528 | tf_op jit(solution)/shard_map/ppermute | solution.py:196
  42.7 25.9 %collective-permute-start.6 = (bf16[216,5120]{1,0:T(8,128)(2,1)S(1)}, bf16[216,5120]{1,0:T(8,128)(2,1)S(1)}, u32[]{:S(2)}, u32[]{:S(2)}) collective-permute-start(bf16[216,5120]{1,0:T(8,128)(2,1)S(1)} %copy-done.3), channel_id=1, source_target_pairs={{0,1},{1,0},{2,3},{3,2},{4,5},{5,4},{6,7},{7,6},{8,9},{9,8},{10,11... | collective-permute-start | bytes 6635528 | tf_op jit(solution)/shard_map/ppermute | solution.py:196
  72.8 8.8 %collective-permute-start.7 = (bf16[32,5120]{1,0:T(8,128)(2,1)S(1)}, bf16[32,5120]{1,0:T(8,128)(2,1)S(1)}, u32[]{:S(2)}, u32[]{:S(2)}) collective-permute-start(bf16[32,5120]{1,0:T(8,128)(2,1)S(1)} %get-tuple-element.26), channel_id=1, source_target_pairs={{0,4},{1,65},{2,6},{3,67},{4,0},{5,69},{6,2},{7,71},{8,12},{9,73},... | collective-permute-start | bytes 983048 | tf_op jit(solution)/shard_map/ppermute | solution.py:182
  75.3 9.7 %collective-permute-start.8 = (bf16[32,5120]{1,0:T(8,128)(2,1)S(1)}, bf16[32,5120]{1,0:T(8,128)(2,1)S(1)}, u32[]{:S(2)}, u32[]{:S(2)}) collective-permute-start(bf16[32,5120]{1,0:T(8,128)(2,1)S(1)} %get-tuple-element.27), channel_id=1, source_target_pairs={{0,2},{1,33},{2,4},{3,35},{4,6},{5,37},{6,0},{7,39},{8,10},{9,41},... | collective-permute-start | bytes 983048 | tf_op jit(solution)/shard_map/ppermute | solution.py:182
  76.8 8.6 %collective-permute-start.9 = (bf16[32,5120]{1,0:T(8,128)(2,1)S(1)}, bf16[32,5120]{1,0:T(8,128)(2,1)S(1)}, u32[]{:S(2)}, u32[]{:S(2)}) collective-permute-start(bf16[32,5120]{1,0:T(8,128)(2,1)S(1)} %get-tuple-element.28), channel_id=1, source_target_pairs={{0,6},{1,97},{2,0},{3,99},{4,2},{5,101},{6,4},{7,103},{8,14},{9,10... | collective-permute-start | bytes 983048 | tf_op jit(solution)/shard_map/ppermute | solution.py:182

commit v16 on v15

--- a/solution.py
+++ b/solution.py
@@ -249,7 +249,7 @@
     mixed, *sent = call(
         mlp_kernel, [shape((32, D), F32), block, block, block], [SM, SM] + [VM] * 7, limit=28 << 20
     )(kv, tp, rows, gate_t, up_t, down_weight, *far)
-    for part in [move_ring(value, k) for value, k in zip(sent, (2, 1, 3))]:
+    for part in [move_ring(value, k) for value, k in ((sent[0], 2), (sent[2], 3), (sent[1], 1))]:
         mixed = mixed + part.astype(F32)
     mixed = mixed.astype(BF).reshape(16, 2, D)
     mixed = lax.all_to_all(mixed, ("kv", "tp"), 0, 0, axis_index_groups=PLANES)

time: 99.4 us -> 99.5 us (level)
  waiting for transfers between devices: 17.9 us -> 19.2 us
  starting transfers between devices: 19.4 us -> 18.2 us
    ppermute x3, waiting for transfers between devices: 6.9 us -> 8.16 us  [move_ring(): return lax.ppermute(value, ('kv', 'tp'), pairs)]
    ppermute x3, starting transfers between devices: 5.68 us -> 4.47 us  [move_ring(): return lax.ppermute(value, ('kv', 'tp'), pairs)]
  transfers between devices with their start and end apart: 11 -> 11, of which waited for: 8 -> 7; matrix products, arithmetic and copies ran while one was open for 1% -> 1% of each run, Pallas kernels for 1% -> 1%
where the time goes in v16:
time: 99.5 us; the launch traced here: 99 us
  blocking collectives  46.8 us (47%)
  waiting for transfers between devices  19.2 us (19%)
  starting transfers between devices  18.2 us (18%)
  Pallas kernels  9.92 us (10%)
  local copies, waits for them, and re-layouts  3.65 us (4%)
  other arithmetic  1.16 us (1%)
    all_to_all x1, blocking collectives, local(): lax.all_to_all(jnp.broadcast_to(normed[None], (16, 8, D)), 'kv', 0, 0)  21.9 us
    all_to_all x1, blocking collectives, local(): parts = lax.all_to_all(packed.reshape(16, 16, 768), 'kv', 0, 0)  12.6 us
    all_to_all x1, blocking collectives, local(): mixed = lax.all_to_all(mixed, ('kv', 'tp'), 0, 0, axis_index_groups=PLANES)  12.4 us
    ppermute x3, waiting for transfers between devices, move_ring(): return lax.ppermute(value, ('kv', 'tp'), pairs)  8.16 us
    all_to_all x1, starting transfers between devices, local(): lax.all_to_all(jnp.broadcast_to(queries[None], (16, 16, 640)), 'kv', 0, 0)  7.12 us
    ppermute x3, starting transfers between devices, move_z(): return lax.ppermute(value, 'tp', pairs)  5.98 us
    all_to_all x1, waiting for transfers between devices, local(): lax.all_to_all(jnp.broadcast_to(queries[None], (16, 16, 640)), 'kv', 0, 0)  5.93 us
    ppermute x3, starting transfers between devices, move_ring(): return lax.ppermute(value, ('kv', 'tp'), pairs)  4.47 us
  transfers between devices with their start and end apart: 11, of which 7 were waited for; matrix products, arithmetic and copies ran while one was open for 1% of the time, Pallas kernels for 1%

profile of v16, /device:TPU:0, one launch (start us, length us, event | category | flops | bytes accessed | tf_op | source)
XLA Modules:
  0.0 99.0 jit_solution(17894627307374336989)
XLA Ops:
  0.0 1.5 %broadcast_in_dim.12 = bf16[16,16,640]{2,1,0:T(8,128)(2,1)} broadcast(bf16[16,640]{1,0:T(8,128)(2,1)} %param.13), dimensions={1,2} | broadcast | bytes 348160 | tf_op jit(solution)/shard_map/broadcast_in_dim | solution.py:222
  1.5 7.1 %all-to-all-start = ((bf16[16,16,640]{2,1,0:T(8,128)(2,1)}), bf16[16,16,640]{2,1,0:T(8,128)(2,1)S(1)}, u32[]{:S(2)}, u32[]{:S(2)}) async-start(bf16[16,16,640]{2,1,0:T(8,128)(2,1)} %broadcast_in_dim.12), calls=%async_computation | async-start | bytes 655360 | tf_op jit(solution)/shard_map/all_to_all | solution.py:222
  8.6 0.7 pad_add_fusion
  9.3 0.0 copy-start.4
  9.3 0.9 copy-done.4
  10.3 0.0 copy-start.5
  10.3 0.9 copy-done.5
  11.2 0.6 shard_map.118
  11.8 5.9 %all-to-all-done = bf16[16,16,640]{2,1,0:T(8,128)(2,1)S(1)} async-done(((bf16[16,16,640]{2,1,0:T(8,128)(2,1)}), bf16[16,16,640]{2,1,0:T(8,128)(2,1)S(1)}, u32[]{:S(2)}, u32[]{:S(2)}) %all-to-all-start) | async-done | bytes 327712 | tf_op jit(solution)/shard_map/all_to_all | solution.py:222
  17.8 0.0 copy-start
  17.8 0.0 copy-start.6
  17.8 2.7 %shard_map.119 = bf16[256,768]{1,0:T(8,128)(2,1)S(1)} custom-call(bf16[256,640]{1,0:T(8,128)(2,1)S(1)} %bitcast.14, bf16[1024,256]{1,0:T(8,128)(2,1)S(1)} %get-tuple-element.20.keys_wide, bf16[1024,128]{1,0:T(8,128)(2,1)S(1)} %get-tuple-element.21.values, bf16[256,128]{1,0:T(8,128)(2,1)S(1)} %get-tuple-element.22.onehot, bf16[640,5120]{1,0:T(8,128)(2,1)} %weight.3), custom_call_target="tpu_custom_call" | custom-call | tf_op jit(solution)/shard_map/pallas_call | solution.py:228
  20.5 12.6 %all_to_all.20.parts = bf16[16,16,768]{2,1,0:T(8,128)(2,1)S(1)} all-to-all(bf16[16,16,768]{2,1,0:T(8,128)(2,1)S(1)} %bitcast.13), channel_id=1, replica_groups=mesh['kv'=16,'tp'=8] {'kv'}, dimensions={0} | all-to-all | bytes 786432 | tf_op jit(solution)/shard_map/all_to_all | solution.py:231
  33.1 0.0 copy-done
  33.1 0.0 copy-done.6
  33.1 0.0 copy-start.1
  33.1 0.0 copy-start.2
  33.1 0.0 copy-start.3
  33.1 0.0 copy-start.7
  33.1 1.5 %shard_map.120 = (f32[8,5120]{1,0:T(8,128)S(1)}, bf16[8,5120]{1,0:T(8,128)(2,1)S(1)}) custom-call(s32[1]{0:T(128)} %bitcast.1.tp, bf16[16,16,768]{2,1,0:T(8,128)(2,1)S(1)} %all_to_all.20.parts, bf16[640,5120]{1,0:T(8,128)(2,1)S(1)} %copy-done, bf16[2,5120]{1,0:T(2,128)(2,1)S(1)} %copy-done.6), custom_call_target="tpu_custom_call" | custom-call | tf_op jit(solution)/shard_map/pallas_call | solution.py:232
  34.6 0.1 collective-permute-start
  34.7 1.3 %collective-permute-done = bf16[8,5120]{1,0:T(8,128)(2,1)S(1)} collective-permute-done((bf16[8,5120]{1,0:T(8,128)(2,1)S(1)}, bf16[8,5120]{1,0:T(8,128)(2,1)S(1)}, u32[]{:S(2)}, u32[]{:S(2)}) %collective-permute-start) | collective-permute-done | bytes 81952 | tf_op jit(solution)/shard_map/ppermute | solution.py:196
  36.0 4.0 %collective-permute-start.3 = (bf16[8,5120]{1,0:T(8,128)(2,1)S(1)}, bf16[8,5120]{1,0:T(8,128)(2,1)S(1)}, u32[]{:S(2)}, u32[]{:S(2)}) collective-permute-start(bf16[8,5120]{1,0:T(8,128)(2,1)S(1)} %fusion.3), channel_id=1, source_target_pairs={{0,4},{1,5},{2,6},{3,7},{4,0},{5,1},{6,2},{7,3},{8,12},{9,13},{10,... | collective-permute-start | bytes 245768 | tf_op jit(solution)/shard_map/ppermute | solution.py:192
  39.9 0.7 collective-permute-start.2
  40.6 1.3 %collective-permute-start.1 = (bf16[8,5120]{1,0:T(8,128)(2,1)S(1)}, bf16[8,5120]{1,0:T(8,128)(2,1)S(1)}, u32[]{:S(2)}, u32[]{:S(2)}) collective-permute-start(bf16[8,5120]{1,0:T(8,128)(2,1)S(1)} %fusion.3), channel_id=1, source_target_pairs={{0,2},{1,3},{2,4},{3,5},{4,6},{5,7},{6,0},{7,1},{8,10},{9,11},{10,... | collective-permute-start | bytes 245768 | tf_op jit(solution)/shard_map/ppermute | solution.py:192
  41.9 0.0 copy-done.1
  41.9 0.0 collective-permute-start.4
  41.9 0.0 copy-done.2
  42.0 0.5 collective-permute-start.5
  42.5 0.2 collective-permute-done.3
  42.7 0.0 copy-done.3
  42.7 0.0 collective-permute-start.6
  42.7 2.5 %collective-permute-done.2 = bf16[8,5120]{1,0:T(8,128)(2,1)S(1)} collective-permute-done((bf16[8,5120]{1,0:T(8,128)(2,1)S(1)}, bf16[8,5120]{1,0:T(8,128)(2,1)S(1)}, u32[]{:S(2)}, u32[]{:S(2)}) %collective-permute-start.2) | collective-permute-done | bytes 81952 | tf_op jit(solution)/shard_map/ppermute | solution.py:192
  45.2 1.1 %collective-permute-done.1 = bf16[8,5120]{1,0:T(8,128)(2,1)S(1)} collective-permute-done((bf16[8,5120]{1,0:T(8,128)(2,1)S(1)}, bf16[8,5120]{1,0:T(8,128)(2,1)S(1)}, u32[]{:S(2)}, u32[]{:S(2)}) %collective-permute-start.1) | collective-permute-done | bytes 81952 | tf_op jit(solution)/shard_map/ppermute | solution.py:192
  46.3 0.2 fusion
  46.5 0.0 copy-done.7
  46.5 0.1 fusion.2
  46.6 0.1 broadcast_in_dim.27
  46.7 21.9 %all_to_all.21 = bf16[16,8,5120]{2,1,0:T(8,128)(2,1)S(1)} all-to-all(bf16[16,8,5120]{2,1,0:T(8,128)(2,1)S(1)} %broadcast_in_dim.27), channel_id=1, replica_groups=mesh['kv'=16,'tp'=8] {'kv'}, dimensions={0} | all-to-all | bytes 2621440 | tf_op jit(solution)/shard_map/all_to_all | solution.py:247
  68.6 0.0 collective-permute-done.4.gate_far
  68.6 0.0 collective-permute-done.5.up_far
  68.6 0.0 collective-permute-done.6.down_far
  68.6 4.2 %shard_map.121 = (f32[32,5120]{1,0:T(8,128)S(1)}, bf16[32,5120]{1,0:T(8,128)(2,1)S(1)}, bf16[32,5120]{1,0:T(8,128)(2,1)S(1)}, bf16[32,5120]{1,0:T(8,128)(2,1)S(1)}) custom-call(s32[1]{0:T(128)} %bitcast.kv, s32[1]{0:T(128)} %bitcast.1.tp, bf16[128,5120]{1,0:T(8,128)(2,1)S(1)} %bitcast.8, bf16[216,5120]{1,0:T(8,128)(2,1)S(1)} %bitcast.10, ...), custom_call_target="tpu_custom_call" | custom-call | tf_op jit(solution)/shard_map/pallas_call | solution.py:249
  72.8 2.4 %collective-permute-start.7 = (bf16[32,5120]{1,0:T(8,128)(2,1)S(1)}, bf16[32,5120]{1,0:T(8,128)(2,1)S(1)}, u32[]{:S(2)}, u32[]{:S(2)}) collective-permute-start(bf16[32,5120]{1,0:T(8,128)(2,1)S(1)} %get-tuple-element.26), channel_id=1, source_target_pairs={{0,4},{1,65},{2,6},{3,67},{4,0},{5,69},{6,2},{7,71},{8,12},{9,73},... | collective-permute-start | bytes 983048 | tf_op jit(solution)/shard_map/ppermute | solution.py:182
  75.3 1.0 collective-permute-start.8
  76.3 1.0 %collective-permute-start.9 = (bf16[32,5120]{1,0:T(8,128)(2,1)S(1)}, bf16[32,5120]{1,0:T(8,128)(2,1)S(1)}, u32[]{:S(2)}, u32[]{:S(2)}) collective-permute-start(bf16[32,5120]{1,0:T(8,128)(2,1)S(1)} %get-tuple-element.28), channel_id=1, source_target_pairs={{0,2},{1,33},{2,4},{3,35},{4,6},{5,37},{6,0},{7,39},{8,10},{9,41},... | collective-permute-start | bytes 983048 | tf_op jit(solution)/shard_map/ppermute | solution.py:182
  77.3 4.2 %collective-permute-done.7 = bf16[32,5120]{1,0:T(8,128)(2,1)S(1)} collective-permute-done((bf16[32,5120]{1,0:T(8,128)(2,1)S(1)}, bf16[32,5120]{1,0:T(8,128)(2,1)S(1)}, u32[]{:S(2)}, u32[]{:S(2)}) %collective-permute-start.7) | collective-permute-done | bytes 327712 | tf_op jit(solution)/shard_map/ppermute | solution.py:182
  81.5 3.9 %collective-permute-done.8 = bf16[32,5120]{1,0:T(8,128)(2,1)S(1)} collective-permute-done((bf16[32,5120]{1,0:T(8,128)(2,1)S(1)}, bf16[32,5120]{1,0:T(8,128)(2,1)S(1)}, u32[]{:S(2)}, u32[]{:S(2)}) %collective-permute-start.8) | collective-permute-done | bytes 327712 | tf_op jit(solution)/shard_map/ppermute | solution.py:182
  85.5 0.0 collective-permute-done.9
  85.5 0.2 add_convert_fusion
  85.6 0.1 reshape.26
  85.7 12.4 %all_to_all.22.parts = bf16[16,2,5120]{2,1,0:T(2,128)(2,1)S(1)} all-to-all(bf16[16,2,5120]{2,1,0:T(2,128)(2,1)S(1)} %reshape.26), channel_id=1, replica_groups={{0,8,16,24,32,40,48,56,64,72,80,88,96,104,112,120},{2,10,18,26,34,42,50..., dimensions={0} | all-to-all | bytes 655360 | tf_op jit(solution)/shard_map/all_to_all | solution.py:255
  98.1 0.9 shard_map.122
  (2 shorter events, 0.0 us)
Async XLA Ops:
  1.5 16.3 %all-to-all-start = ((bf16[16,16,640]{2,1,0:T(8,128)(2,1)}), bf16[16,16,640]{2,1,0:T(8,128)(2,1)S(1)}, u32[]{:S(2)}, u32[]{:S(2)}) async-start(bf16[16,16,640]{2,1,0:T(8,128)(2,1)} %broadcast_in_dim.12), calls=%async_computation | async-start | bytes 655360 | tf_op jit(solution)/shard_map/all_to_all | solution.py:222
  9.3 0.9 copy-start.4
  10.3 0.9 copy-start.5
  17.8 15.3 %copy-start = (bf16[640,5120]{1,0:T(8,128)(2,1)S(1)}, bf16[640,5120]{1,0:T(8,128)(2,1)}, u32[]{:S(2)}) copy-start(bf16[640,5120]{1,0:T(8,128)(2,1)} %weight.3) | copy-start | bytes 19660804
  17.8 15.3 %copy-start.6 = (bf16[2,5120]{1,0:T(2,128)(2,1)S(1)}, bf16[2,5120]{1,0:T(2,128)(2,1)}, u32[]{:S(2)}) copy-start(bf16[2,5120]{1,0:T(2,128)(2,1)} %activations.1) | copy-start | bytes 61444
  33.1 8.8 %copy-start.1 = (bf16[5120,216]{0,1:T(8,128)(2,1)S(1)}, bf16[5120,216]{0,1:T(8,128)(2,1)}, u32[]{:S(2)}) copy-start(bf16[5120,216]{0,1:T(8,128)(2,1)} %param.21) | copy-start | bytes 6635524
  33.1 8.9 %copy-start.2 = (bf16[5120,216]{0,1:T(8,128)(2,1)S(1)}, bf16[5120,216]{0,1:T(8,128)(2,1)}, u32[]{:S(2)}) copy-start(bf16[5120,216]{0,1:T(8,128)(2,1)} %param.22) | copy-start | bytes 6635524
  33.1 9.6 %copy-start.3 = (bf16[216,5120]{1,0:T(8,128)(2,1)S(1)}, bf16[216,5120]{1,0:T(8,128)(2,1)}, u32[]{:S(2)}) copy-start(bf16[216,5120]{1,0:T(8,128)(2,1)} %down.1) | copy-start | bytes 6635524
  33.1 13.3 %copy-start.7 = (f32[5120]{0:T(1024)S(1)}, f32[5120]{0:T(1024)}, u32[]{:S(2)}) copy-start(f32[5120]{0:T(1024)} %param.20) | copy-start | bytes 61444
  34.6 1.4 %collective-permute-start = (bf16[8,5120]{1,0:T(8,128)(2,1)S(1)}, bf16[8,5120]{1,0:T(8,128)(2,1)S(1)}, u32[]{:S(2)}, u32[]{:S(2)}) collective-permute-start(bf16[8,5120]{1,0:T(8,128)(2,1)S(1)} %get-tuple-element.24), channel_id=1, source_target_pairs={{0,1},{1,0},{2,3},{3,2},{4,5},{5,4},{6,7},{7,6},{8,9},{9,8},{10,11... | collective-permute-start | bytes 245768 | tf_op jit(solution)/shard_map/ppermute | solution.py:196
  36.0 6.7 %collective-permute-start.3 = (bf16[8,5120]{1,0:T(8,128)(2,1)S(1)}, bf16[8,5120]{1,0:T(8,128)(2,1)S(1)}, u32[]{:S(2)}, u32[]{:S(2)}) collective-permute-start(bf16[8,5120]{1,0:T(8,128)(2,1)S(1)} %fusion.3), channel_id=1, source_target_pairs={{0,4},{1,5},{2,6},{3,7},{4,0},{5,1},{6,2},{7,3},{8,12},{9,13},{10,... | collective-permute-start | bytes 245768 | tf_op jit(solution)/shard_map/ppermute | solution.py:192
  39.9 5.3 %collective-permute-start.2 = (bf16[8,5120]{1,0:T(8,128)(2,1)S(1)}, bf16[8,5120]{1,0:T(8,128)(2,1)S(1)}, u32[]{:S(2)}, u32[]{:S(2)}) collective-permute-start(bf16[8,5120]{1,0:T(8,128)(2,1)S(1)} %fusion.3), channel_id=1, source_target_pairs={{0,6},{1,7},{2,0},{3,1},{4,2},{5,3},{6,4},{7,5},{8,14},{9,15},{10,... | collective-permute-start | bytes 245768 | tf_op jit(solution)/shard_map/ppermute | solution.py:192
  40.6 5.7 %collective-permute-start.1 = (bf16[8,5120]{1,0:T(8,128)(2,1)S(1)}, bf16[8,5120]{1,0:T(8,128)(2,1)S(1)}, u32[]{:S(2)}, u32[]{:S(2)}) collective-permute-start(bf16[8,5120]{1,0:T(8,128)(2,1)S(1)} %fusion.3), channel_id=1, source_target_pairs={{0,2},{1,3},{2,4},{3,5},{4,6},{5,7},{6,0},{7,1},{8,10},{9,11},{10,... | collective-permute-start | bytes 245768 | tf_op jit(solution)/shard_map/ppermute | solution.py:192
  41.9 26.6 %collective-permute-start.4 = (bf16[216,5120]{1,0:T(8,128)(2,1)S(1)}, bf16[216,5120]{1,0:T(8,128)(2,1)S(1)}, u32[]{:S(2)}, u32[]{:S(2)}) collective-permute-start(bf16[216,5120]{1,0:T(8,128)(2,1)S(1)} %bitcast.9), channel_id=1, source_target_pairs={{0,1},{1,0},{2,3},{3,2},{4,5},{5,4},{6,7},{7,6},{8,9},{9,8},{10,11... | collective-permute-start | bytes 6635528 | tf_op jit(solution)/shard_map/ppermute | solution.py:196
  42.0 26.6 %collective-permute-start.5 = (bf16[216,5120]{1,0:T(8,128)(2,1)S(1)}, bf16[216,5120]{1,0:T(8,128)(2,1)S(1)}, u32[]{:S(2)}, u32[]{:S(2)}) collective-permute-start(bf16[216,5120]{1,0:T(8,128)(2,1)S(1)} %bitcast.11), channel_id=1, source_target_pairs={{0,1},{1,0},{2,3},{3,2},{4,5},{5,4},{6,7},{7,6},{8,9},{9,8},{10,11... | collective-permute-start | bytes 6635528 | tf_op jit(solution)/shard_map/ppermute | solution.py:196
  42.7 25.9 %collective-permute-start.6 = (bf16[216,5120]{1,0:T(8,128)(2,1)S(1)}, bf16[216,5120]{1,0:T(8,128)(2,1)S(1)}, u32[]{:S(2)}, u32[]{:S(2)}) collective-permute-start(bf16[216,5120]{1,0:T(8,128)(2,1)S(1)} %copy-done.3), channel_id=1, source_target_pairs={{0,1},{1,0},{2,3},{3,2},{4,5},{5,4},{6,7},{7,6},{8,9},{9,8},{10,11... | collective-permute-start | bytes 6635528 | tf_op jit(solution)/shard_map/ppermute | solution.py:196
  72.8 8.7 %collective-permute-start.7 = (bf16[32,5120]{1,0:T(8,128)(2,1)S(1)}, bf16[32,5120]{1,0:T(8,128)(2,1)S(1)}, u32[]{:S(2)}, u32[]{:S(2)}) collective-permute-start(bf16[32,5120]{1,0:T(8,128)(2,1)S(1)} %get-tuple-element.26), channel_id=1, source_target_pairs={{0,4},{1,65},{2,6},{3,67},{4,0},{5,69},{6,2},{7,71},{8,12},{9,73},... | collective-permute-start | bytes 983048 | tf_op jit(solution)/shard_map/ppermute | solution.py:182
  75.3 10.2 %collective-permute-start.8 = (bf16[32,5120]{1,0:T(8,128)(2,1)S(1)}, bf16[32,5120]{1,0:T(8,128)(2,1)S(1)}, u32[]{:S(2)}, u32[]{:S(2)}) collective-permute-start(bf16[32,5120]{1,0:T(8,128)(2,1)S(1)} %get-tuple-element.27), channel_id=1, source_target_pairs={{0,6},{1,97},{2,0},{3,99},{4,2},{5,101},{6,4},{7,103},{8,14},{9,10... | collective-permute-start | bytes 983048 | tf_op jit(solution)/shard_map/ppermute | solution.py:182
  76.3 9.2 %collective-permute-start.9 = (bf16[32,5120]{1,0:T(8,128)(2,1)S(1)}, bf16[32,5120]{1,0:T(8,128)(2,1)S(1)}, u32[]{:S(2)}, u32[]{:S(2)}) collective-permute-start(bf16[32,5120]{1,0:T(8,128)(2,1)S(1)} %get-tuple-element.28), channel_id=1, source_target_pairs={{0,2},{1,33},{2,4},{3,35},{4,6},{5,37},{6,0},{7,39},{8,10},{9,41},... | collective-permute-start | bytes 983048 | tf_op jit(solution)/shard_map/ppermute | solution.py:182
